TPU v7x, 32 devices: a whole 2x2x4 slice. The times are simulated.
32 devices in a mesh: dp: 8 (over z, x), tensor: 4 (over y, core).
Axes of the slice: x: 2, y: 2, z: 4, core: 2. Of those that a mesh axis runs over, the one named last changes fastest.
Arguments:
- hidden_in: bfloat16 [10240, 2048], P(('dp', 'tensor')), may hold values from -6 to 6
- cotangent: bfloat16 [10240, 2048], P(('dp', 'tensor')), may hold values from -6 to 6
- gain_attn: float32 [2048], replicated, may hold values from 0.1 to 1.9
- w_query: bfloat16 [2048, 2048], P(None, 'tensor'), may hold values from -0.125 to 0.125
- w_key: bfloat16 [2048, 2048], P(None, 'tensor'), may hold values from -0.125 to 0.125
- w_value: bfloat16 [2048, 2048], P(None, 'tensor'), may hold values from -0.125 to 0.125
- w_out: bfloat16 [2048, 2048], P('tensor'), may hold values from -1 to 1
- gain_mlp: float32 [2048], replicated, may hold values from 0.1 to 1.9
- w_gate: bfloat16 [2048, 5632], P(None, 'tensor'), may hold values from -0.125 to 0.125
- w_up: bfloat16 [2048, 5632], P(None, 'tensor'), may hold values from -0.125 to 0.125
- w_down: bfloat16 [5632, 2048], P('tensor'), may hold values from -0.078125 to 0.078125
- doc_lengths: int32 [8, 3], P('dp'), may hold values from 1 to 1024, as said below
- doc_groups: int32 [8, 3], P('dp'), may hold values from 0 to 7
- pad_mask: int32 [8, 1280], P('dp'), may hold values from 0 to 1, as said below
Outputs:
- output: bfloat16 [10240, 2048], P(('dp', 'tensor'))
- grad_input: float32 [10240, 2048], P(('dp', 'tensor'))
- grad_gain_attn: float32 [2048], P('dp')
- grad_w_query: float32 [2048, 2048], P('dp', 'tensor')
- grad_w_key: float32 [2048, 2048], P('dp', 'tensor')
- grad_w_value: float32 [2048, 2048], P('dp', 'tensor')
- grad_w_out: float32 [2048, 2048], P('tensor', 'dp')
- grad_gain_mlp: float32 [2048], P('dp')
- grad_w_gate: float32 [2048, 5632], P('dp', 'tensor')
- grad_w_up: float32 [2048, 5632], P('dp', 'tensor')
- grad_w_down: float32 [5632, 2048], P('tensor', 'dp')
Inputs may be any that keep to these rules, and one draw needn't show every extreme that they name: `doc_lengths`: A row's document lengths sum to 1280; every row holds one document of exactly 1024 tokens and the others are shorter. `pad_mask`: the first token of every document is real; padding lies only at a document's end, fewer than half of its tokens.
All inputs are finite; a program needn't handle non-finite values.
Results may differ from a plain program's by a relative error of at most 0.015.
Values may be sent and summed in bfloat16 or wider, within the bound.
A program may use at most 320 MiB of HBM per device.

v0:
```python
import jax
import jax.numpy as jnp
from jax import lax
from jax.sharding import PartitionSpec as P

HEAD_DIM = 128
ROWS = 1280
QBLOCK = 640
DOCS = 3
GROUPS = 8


epsilon = 1e-05
masked_score = -1e30
rope_base = 10000.0


def row_tables(length_row, group_row):
    starts = jnp.cumsum(length_row) - length_row
    token_idx = jnp.arange(ROWS, dtype=jnp.int32)
    doc_index = jnp.sum((token_idx[:, None] >= starts[None, 1:]).astype(jnp.int32), axis=1)
    onehot = doc_index[:, None] == jnp.arange(DOCS, dtype=jnp.int32)[None, :]
    inside = token_idx - jnp.sum(jnp.where(onehot, starts[None, :], 0), axis=1)
    group_tok = jnp.sum(jnp.where(onehot, group_row[None, :], 0), axis=1)
    return (doc_index, inside, group_tok)


def rope_tables(inside):
    freq = rope_base ** (-jnp.arange(0, HEAD_DIM // 2, dtype=jnp.float32) * 2.0 / HEAD_DIM)
    angle = inside.astype(jnp.float32)[:, None] * freq[None, :]
    return (jnp.cos(angle)[:, None, :], jnp.sin(angle)[:, None, :])


def rotate(values, cosine, sine):
    half = values.shape[-1] // 2
    first, second = (values[..., :half], values[..., half:])
    return jnp.concatenate(
        [first * cosine - second * sine, second * cosine + first * sine], axis=-1
    )


def rotate_back(values, cosine, sine):
    half = values.shape[-1] // 2
    first, second = (values[..., :half], values[..., half:])
    return jnp.concatenate(
        [first * cosine + second * sine, second * cosine - first * sine], axis=-1
    )


def rows_dot(left, right):
    return jnp.dot(left, right, preferred_element_type=jnp.float32)


def rows_dot_t(left, right):
    return lax.dot_general(
        left, right, (((1,), (1,)), ((), ())), preferred_element_type=jnp.float32
    )


def cross_rows(left, right):
    return lax.dot_general(
        left, right, (((0,), (0,)), ((), ())), preferred_element_type=jnp.float32
    )


def block_scores(query_blk, key_part, query_doc, key_doc, key_mask, row_first):
    score_scale = HEAD_DIM ** (-0.5)
    raw = jnp.einsum("qhd,khd->hqk", query_blk, key_part, preferred_element_type=jnp.float32)
    query_tok = row_first + jnp.arange(query_blk.shape[0], dtype=jnp.int32)
    key_tok = jnp.arange(key_part.shape[0], dtype=jnp.int32)
    allowed = (
        (query_doc[:, None] == key_doc[None, :])
        & (query_tok[:, None] >= key_tok[None, :])
        & (key_mask[None, :] > 0.5)
    )
    return jnp.where(allowed[None], raw * score_scale, masked_score)


def shards(
    hidden_in,
    cotangent,
    gain_attn,
    w_query,
    w_key,
    w_value,
    w_out,
    gain_mlp,
    w_gate,
    w_up,
    w_down,
    doc_lengths,
    doc_groups,
    pad_mask,
):
    rows_local = hidden_in.shape[0]
    heads_local = w_query.shape[1] // HEAD_DIM
    width_local = w_query.shape[1]
    row_offset = lax.axis_index("tensor") * rows_local
    score_scale = HEAD_DIM ** (-0.5)
    doc_index, inside, group_tok = row_tables(doc_lengths[0], doc_groups[0])
    real_tok = pad_mask[0].astype(jnp.float32)
    onehot_g = group_tok[:, None] == jnp.arange(GROUPS, dtype=jnp.int32)[None, :]
    counts_local = jnp.sum(jnp.where(onehot_g, real_tok[:, None], 0.0), axis=0)
    counts = lax.psum(counts_local, "dp")
    live = jnp.sum(counts)
    group_scale = jnp.sqrt(live / (GROUPS * jnp.maximum(counts, 1.0)))
    token_weight = real_tok * jnp.sum(jnp.where(onehot_g, group_scale[None, :], 0.0), axis=-1)
    weight_local = lax.dynamic_slice_in_dim(token_weight, row_offset, rows_local)
    x_f = hidden_in.astype(jnp.float32)
    inv_a = lax.rsqrt(jnp.mean(x_f * x_f, axis=-1, keepdims=True) + epsilon)
    scaled_a = x_f * inv_a
    normed_a = (scaled_a * gain_attn).astype(jnp.bfloat16)
    gathered_a = lax.all_gather(normed_a, "tensor", axis=0, tiled=True)
    cosine, sine = rope_tables(inside)
    query = rotate(
        rows_dot(gathered_a, w_query).reshape(ROWS, heads_local, HEAD_DIM), cosine, sine
    ).astype(jnp.bfloat16)
    key_vec = rotate(
        rows_dot(gathered_a, w_key).reshape(ROWS, heads_local, HEAD_DIM), cosine, sine
    ).astype(jnp.bfloat16)
    value = rows_dot(gathered_a, w_value).astype(jnp.bfloat16).reshape(ROWS, heads_local, HEAD_DIM)
    num_blocks = ROWS // QBLOCK
    head_blocks = []
    log_totals = []
    for block_idx in range(num_blocks):
        row_first = block_idx * QBLOCK
        row_end = row_first + QBLOCK
        scores = block_scores(
            query[row_first:row_end],
            key_vec[:row_end],
            doc_index[row_first:row_end],
            doc_index[:row_end],
            real_tok[:row_end],
            row_first,
        )
        top_val = jnp.max(scores, axis=-1, keepdims=True)
        log_total = top_val + jnp.log(jnp.sum(jnp.exp(scores - top_val), axis=-1, keepdims=True))
        prob = jnp.exp(scores - log_total).astype(jnp.bfloat16)
        heads_out = jnp.einsum(
            "hqk,khd->qhd", prob, value[:row_end], preferred_element_type=jnp.float32
        )
        head_blocks.append(heads_out.astype(jnp.bfloat16))
        log_totals.append(log_total)
    attn_heads = jnp.concatenate(head_blocks, axis=0).reshape(ROWS, width_local)
    mid_h = x_f + lax.psum_scatter(
        rows_dot(attn_heads, w_out), "tensor", scatter_dimension=0, tiled=True
    )
    inv_b = lax.rsqrt(jnp.mean(mid_h * mid_h, axis=-1, keepdims=True) + epsilon)
    scaled_b = mid_h * inv_b
    normed_b = (scaled_b * gain_mlp).astype(jnp.bfloat16)
    gathered_b = lax.all_gather(normed_b, "tensor", axis=0, tiled=True)
    gate = rows_dot(gathered_b, w_gate)
    up_val = rows_dot(gathered_b, w_up)
    sigma = jax.nn.sigmoid(gate)
    activated = gate * sigma
    mlp_mid = (activated * up_val).astype(jnp.bfloat16)
    output = (
        mid_h
        + lax.psum_scatter(
            rows_dot(mlp_mid, w_down).astype(jnp.bfloat16),
            "tensor",
            scatter_dimension=0,
            tiled=True,
        ).astype(jnp.float32)
    ).astype(jnp.bfloat16)
    weighted = cotangent.astype(jnp.float32) * weight_local[:, None]
    grad_rows = lax.all_gather(weighted.astype(jnp.bfloat16), "tensor", axis=0, tiled=True)
    grad_down_t = cross_rows(grad_rows, mlp_mid)
    d_mid = rows_dot_t(grad_rows, w_down)
    d_gate = (d_mid * up_val * sigma * (1.0 + gate * (1.0 - sigma))).astype(jnp.bfloat16)
    d_up = (d_mid * activated).astype(jnp.bfloat16)
    d_normed_b = lax.psum_scatter(
        rows_dot_t(d_gate, w_gate) + rows_dot_t(d_up, w_up),
        "tensor",
        scatter_dimension=0,
        tiled=True,
    )
    grad_gate = cross_rows(gathered_b, d_gate)
    grad_upw = cross_rows(gathered_b, d_up)
    gain_mlp_part = jnp.sum(d_normed_b * scaled_b, axis=0)
    e_term = d_normed_b * gain_mlp
    d_hidden = weighted + inv_b * (
        e_term - scaled_b * jnp.mean(e_term * scaled_b, axis=-1, keepdims=True)
    )
    grad_attn_rows = lax.all_gather(d_hidden.astype(jnp.bfloat16), "tensor", axis=0, tiled=True)
    grad_out_t = cross_rows(grad_attn_rows, attn_heads)
    d_heads = (
        rows_dot_t(grad_attn_rows, w_out).astype(jnp.bfloat16).reshape(ROWS, heads_local, HEAD_DIM)
    )
    query_grads = []
    key_grad = jnp.zeros((ROWS, heads_local, HEAD_DIM), jnp.float32)
    value_grad = jnp.zeros((ROWS, heads_local, HEAD_DIM), jnp.float32)
    for block_idx in range(num_blocks):
        row_first = block_idx * QBLOCK
        row_end = row_first + QBLOCK
        scores = block_scores(
            query[row_first:row_end],
            key_vec[:row_end],
            doc_index[row_first:row_end],
            doc_index[:row_end],
            real_tok[:row_end],
            row_first,
        )
        prob = jnp.exp(scores - log_totals[block_idx])
        d_prob = jnp.einsum(
            "qhd,khd->hqk",
            d_heads[row_first:row_end],
            value[:row_end],
            preferred_element_type=jnp.float32,
        )
        row_dot = jnp.sum(prob * d_prob, axis=-1, keepdims=True)
        d_score = (prob * (d_prob - row_dot) * score_scale).astype(jnp.bfloat16)
        query_grads.append(
            jnp.einsum(
                "hqk,khd->qhd", d_score, key_vec[:row_end], preferred_element_type=jnp.float32
            )
        )
        key_grad = key_grad.at[:row_end].add(
            jnp.einsum(
                "hqk,qhd->khd",
                d_score,
                query[row_first:row_end],
                preferred_element_type=jnp.float32,
            )
        )
        value_grad = value_grad.at[:row_end].add(
            jnp.einsum(
                "hqk,qhd->khd",
                prob.astype(jnp.bfloat16),
                d_heads[row_first:row_end],
                preferred_element_type=jnp.float32,
            )
        )
    query_pre = (
        rotate_back(jnp.concatenate(query_grads, axis=0), cosine, sine)
        .astype(jnp.bfloat16)
        .reshape(ROWS, width_local)
    )
    key_pre = rotate_back(key_grad, cosine, sine).astype(jnp.bfloat16).reshape(ROWS, width_local)
    value_pre = value_grad.astype(jnp.bfloat16).reshape(ROWS, width_local)
    grad_query = cross_rows(gathered_a, query_pre)
    grad_keyw = cross_rows(gathered_a, key_pre)
    grad_valuew = cross_rows(gathered_a, value_pre)
    total = rows_dot_t(query_pre, w_query)
    total = total + rows_dot_t(key_pre, w_key)
    d_normed_a = lax.psum_scatter(
        (total + rows_dot_t(value_pre, w_value)).astype(jnp.bfloat16),
        "tensor",
        scatter_dimension=0,
        tiled=True,
    ).astype(jnp.float32)
    gain_attn_part = jnp.sum(d_normed_a * scaled_a, axis=0)
    e_attn = d_normed_a * gain_attn
    grad_input = d_hidden + inv_a * (
        e_attn - scaled_a * jnp.mean(e_attn * scaled_a, axis=-1, keepdims=True)
    )
    all_sums = (
        lax.psum_scatter(grad_query, "dp", scatter_dimension=0, tiled=True),
        lax.psum_scatter(grad_keyw, "dp", scatter_dimension=0, tiled=True),
        lax.psum_scatter(grad_valuew, "dp", scatter_dimension=0, tiled=True),
        lax.psum_scatter(grad_out_t, "dp", scatter_dimension=0, tiled=True),
        lax.psum_scatter(grad_gate, "dp", scatter_dimension=0, tiled=True),
        lax.psum_scatter(grad_upw, "dp", scatter_dimension=0, tiled=True),
        lax.psum_scatter(grad_down_t, "dp", scatter_dimension=0, tiled=True),
        lax.psum_scatter(gain_attn_part, "dp", scatter_dimension=0, tiled=True),
        lax.psum_scatter(gain_mlp_part, "dp", scatter_dimension=0, tiled=True),
    )
    (
        sum_query,
        sum_key,
        sum_value,
        sum_out_t,
        sum_gate,
        sum_up,
        sum_down_t,
        sum_gain_attn,
        sum_gain_mlp,
    ) = all_sums
    gain_attn_grad, gain_mlp_grad = lax.psum((sum_gain_attn, sum_gain_mlp), "tensor")
    return (
        output,
        grad_input,
        gain_attn_grad,
        sum_query,
        sum_key,
        sum_value,
        sum_out_t.T,
        gain_mlp_grad,
        sum_gate,
        sum_up,
        sum_down_t.T,
    )


def solution(mesh):
    in_specs = (
        P(("dp", "tensor"), None),
        P(("dp", "tensor"), None),
        P(),
        P(None, "tensor"),
        P(None, "tensor"),
        P(None, "tensor"),
        P("tensor", None),
        P(),
        P(None, "tensor"),
        P(None, "tensor"),
        P("tensor", None),
        P("dp", None),
        P("dp", None),
        P("dp", None),
    )
    out_specs = (
        P(("dp", "tensor"), None),
        P(("dp", "tensor"), None),
        P("dp"),
        P("dp", "tensor"),
        P("dp", "tensor"),
        P("dp", "tensor"),
        P("tensor", "dp"),
        P("dp"),
        P("dp", "tensor"),
        P("dp", "tensor"),
        P("tensor", "dp"),
    )
    return jax.shard_map(shards, mesh=mesh, in_specs=in_specs, out_specs=out_specs, check_vma=False)
```

profile of v0, /device:TPU:0, one launch (start us, length us, event | category | flops | bytes accessed | tf_op | source)
XLA Modules:
  0.0 1554.5 jit_solution(6701316542190648984)
XLA Ops:
  18.2 37.6 %all-gather.5.cloned.1.call-done = bf16[1280,2048]{1,0:T(8,128)(2,1)} async-done(((bf16[320,2048]{1,0:T(8,128)(2,1)}), bf16[1280,2048]{1,0:T(8,128)(2,1)}) %all-gather.5.cloned.1.call-update) | async-done | bytes 5242896 | tf_op jit(solution)/shard_map/all_gather | solution.py:113
  55.7 6.2 convolution_convert_fusion.2
  73.9 6.2 fusion.130
  87.8 5.5 subtract_convert_fusion.2
  99.2 6.6 fusion.5
  105.9 9.1 exponential_reduce_fusion
  119.1 8.4 fusion.90
  128.7 5.5 fusion.132
  134.3 84.5 %reduce-scatter.12.cloned.1.call-done = f32[320,2048]{1,0:T(8,128)} async-done(((f32[1280,2048]{1,0:T(8,128)}), f32[320,2048]{1,0:T(8,128)}) %reduce-scatter.12.cloned.1.call-update) | async-done | bytes 2621456 | tf_op jit(solution)/shard_map/reduce_scatter | solution.py:145
  224.1 21.4 %psum.21 = f32[8]{0:T(128)S(1)} all-reduce(f32[8]{0:T(128)S(1)} %select_reduce_fusion.1), channel_id=1, replica_groups=mesh['dp'=8,'tensor'=4] {'dp'}, use_global_device_ids=true, to_apply=%region_13.14 | all-reduce | flops 8 | bytes 64 | tf_op jit(solution)/shard_map/psum | solution.py:104
  248.5 15.9 %all-gather.7.cloned.1.call-done = bf16[1280,2048]{1,0:T(8,128)(2,1)} async-done(((bf16[320,2048]{1,0:T(8,128)(2,1)}), bf16[1280,2048]{1,0:T(8,128)(2,1)}) %all-gather.7.cloned.1.call-update) | async-done | bytes 5242896 | tf_op jit(solution)/shard_map/all_gather | solution.py:151
  264.4 13.8 fusion.134
  278.2 12.2 fusion.133
  290.4 16.4 %all-gather.9.cloned.1.call-done = bf16[1280,2048]{1,0:T(8,128)(2,1)} async-done(((bf16[320,2048]{1,0:T(8,128)(2,1)}), bf16[1280,2048]{1,0:T(8,128)(2,1)}) %all-gather.9.cloned.1.call-update) | async-done | bytes 5242896 | tf_op jit(solution)/shard_map/all_gather | solution.py:167
  306.9 19.9 %multiply_convert_fusion.1 = (bf16[1280,1408]{1,0:T(8,128)(2,1)}, bf16[1280,1408]{1,0:T(8,128)(2,1)}, bf16[1280,1408]{1,0:T(8,128)(2,1)}) fusion(f32[1280,1408]{1,0:T(8,128)} %fusion.133, f32[1280,1408]{1,0:T(8,128)} %fusion.134, bf16[1280,2048]{1,0:T(8,128)(2,1)} %all-gather.9.cloned.1.call-done, bf16[1408,2048]{1,0:T(8,128)(2,1)} %param.36), kind=kOutput, calls=%fused_computation.12 | convolution fusion | flops 7409008640 | bytes 36241408 | tf_op jit(solution)/shard_map/dot_general | solution.py:55
  326.7 11.9 fusion.135
  338.6 13.9 convolution_add_fusion
  352.5 13.5 convolution_convert_fusion
  366.1 70.9 %reduce-scatter.16.cloned.1.call-done = f32[320,2048]{1,0:T(8,128)} async-done(((f32[1280,2048]{1,0:T(8,128)}), f32[320,2048]{1,0:T(8,128)}) %reduce-scatter.16.cloned.1.call-update) | async-done | bytes 2621456 | tf_op jit(solution)/shard_map/reduce_scatter | solution.py:172
  440.9 50.0 %reduce-scatter.14.cloned.1.call-done = bf16[320,2048]{1,0:T(8,128)(2,1)} async-done(((bf16[1280,2048]{1,0:T(8,128)(2,1)}), bf16[320,2048]{1,0:T(8,128)(2,1)}) %reduce-scatter.14.cloned.1.call-update) | async-done | bytes 1310736 | tf_op jit(solution)/shard_map/reduce_scatter | solution.py:159
  490.8 6.3 fusion.125
  497.2 13.9 fusion.146
  511.2 26.5 %all-gather.11.cloned.1.call-done = bf16[1280,2048]{1,0:T(8,128)(2,1)} async-done(((bf16[320,2048]{1,0:T(8,128)(2,1)}), bf16[1280,2048]{1,0:T(8,128)(2,1)}) %all-gather.11.cloned.1.call-update) | async-done | bytes 5242896 | tf_op jit(solution)/shard_map/all_gather | solution.py:185
  537.7 7.1 fusion.143
  556.0 14.7 fusion.84
  570.6 15.2 fusion.81
  585.8 7.7 fusion.137
  593.5 33.6 %fusion.66 = f32[1280,4,128]{2,0,1:T(8,128)} fusion(bf16[640,4,128]{2,0,1:T(8,128)(2,1)} %copy-done.19, f32[4,640,1280]{2,1,0:T(8,128)} %fusion.137, f32[4,640,1280]{2,1,0:T(8,128)} %get-tuple-element.160, f32[4,640]{1,0:T(4,128)S(1)} %copy-done.39, pred[640,1280]{1,0:T(8,128)(4,1)} %copy-done.11, f32[640,4,128]{2,0,1:T(8,128)} %fusion.84), kind=kOutput, calls=%fused_computation.58 | convolution fusion | flops 875564800 | bytes 31631360 | tf_op jit(solution)/shard_map/hqk,qhd->khd/dot_general | solution.py:219
  627.1 31.8 %fusion.87 = f32[640,4,128]{2,0,1:T(8,128)} fusion(f32[4,640,1280]{2,1,0:T(8,128)} %fusion.137, f32[4,640,1280]{2,1,0:T(8,128)} %get-tuple-element.160, f32[4,640]{1,0:T(4,128)S(1)} %copy-done.39, pred[640,1280]{1,0:T(8,128)(4,1)} %copy-done.11, bf16[1280,4,64]{2,0,1:T(8,128)(2,1)} %copy-done.7, bf16[1280,4,64]{2,0,1:T(8,128)(2,1)S(1)} %copy-done.6), kind=kOutput, calls=%fused_computation.95 | convolution fusion | flops 877530880 | bytes 29665280 | tf_op jit(solution)/shard_map/hqk,khd->qhd/dot_general | solution.py:214
  658.8 8.2 add_convert_fusion.1
  676.1 5.5 convolution_bitcast_fusion.1
  681.6 7.9 fusion.139
  689.5 5.7 fusion.138
  699.4 11.2 add_convert_fusion
  710.7 14.1 fusion.145
  724.9 14.0 fusion.144
  739.0 7.1 fusion.142
  747.4 7.1 fusion.141
  755.9 7.4 fusion.140
  768.1 57.0 %reduce-scatter.26.cloned.1.call-done = f32[256,512]{1,0:T(8,128)} async-done(((f32[2048,512]{1,0:T(8,128)}), f32[256,512]{1,0:T(8,128)}) %reduce-scatter.26.cloned.1.call-update) | async-done | bytes 524304 | tf_op jit(solution)/shard_map/reduce_scatter | solution.py:261
  827.2 51.4 %reduce-scatter.18.cloned.1.call-done = bf16[320,2048]{1,0:T(8,128)(2,1)} async-done(((bf16[1280,2048]{1,0:T(8,128)(2,1)}), bf16[320,2048]{1,0:T(8,128)(2,1)}) %reduce-scatter.18.cloned.1.call-update) | async-done | bytes 1310736 | tf_op jit(solution)/shard_map/reduce_scatter | solution.py:246
  880.9 39.1 %all-reduce.4 = (f32[2048]{0:T(1024)S(1)}, f32[2048]{0:T(1024)S(1)}) all-reduce(f32[2048]{0:T(1024)S(1)} %get-tuple-element.121, f32[2048]{0:T(1024)S(1)} %copy-done.34), channel_id=6, replica_groups=mesh['dp'=8,'tensor'=4] {'dp'}, use_global_device_ids=true, to_apply=%region_23.24.clone | all-reduce | flops 4096 | bytes 32768
  920.1 6.6 all-reduce.5
  931.1 144.8 %reduce-scatter.30.cloned.1.call-done = f32[256,1408]{1,0:T(8,128)} async-done(((f32[2048,1408]{1,0:T(8,128)}), f32[256,1408]{1,0:T(8,128)}) %reduce-scatter.30.cloned.1.call-update) | async-done | bytes 1441808 | tf_op jit(solution)/shard_map/reduce_scatter | solution.py:263
  1075.9 196.0 %reduce-scatter.28.cloned.1.call-done = f32[256,1408]{1,0:T(8,128)} async-done(((f32[2048,1408]{1,0:T(8,128)}), f32[256,1408]{1,0:T(8,128)}) %reduce-scatter.28.cloned.1.call-update) | async-done | bytes 1441808 | tf_op jit(solution)/shard_map/reduce_scatter | solution.py:262
  1271.8 91.7 %reduce-scatter.24.cloned.1.call-done = f32[256,512]{1,0:T(8,128)} async-done(((f32[2048,512]{1,0:T(8,128)}), f32[256,512]{1,0:T(8,128)}) %reduce-scatter.24.cloned.1.call-update) | async-done | bytes 524304 | tf_op jit(solution)/shard_map/reduce_scatter | solution.py:260
  1363.5 92.0 %reduce-scatter.22.cloned.1.call-done = f32[256,512]{1,0:T(8,128)} async-done(((f32[2048,512]{1,0:T(8,128)}), f32[256,512]{1,0:T(8,128)}) %reduce-scatter.22.cloned.1.call-update) | async-done | bytes 524304 | tf_op jit(solution)/shard_map/reduce_scatter | solution.py:259
  1455.5 92.0 %reduce-scatter.20.cloned.1.call-done = f32[256,512]{1,0:T(8,128)} async-done(((f32[2048,512]{1,0:T(8,128)}), f32[256,512]{1,0:T(8,128)}) %reduce-scatter.20.cloned.1.call-update) | async-done | bytes 524304 | tf_op jit(solution)/shard_map/reduce_scatter | solution.py:258
  (196 shorter events, 94.1 us)
Async XLA Ops:
  7.2 121.5 %copy-start = (bf16[512,2048]{1,0:T(8,128)(2,1)S(1)}, bf16[512,2048]{1,0:T(8,128)(2,1)}, u32[]{:S(2)}) copy-start(bf16[512,2048]{1,0:T(8,128)(2,1)} %param.32) | copy-start | bytes 6291460
  7.2 5.3 copy-start.45
  7.2 5.5 copy-start.32
  7.2 5.7 copy-start.40
  7.2 48.5 %all-gather.5.cloned.1.call-start = ((), (), s32[]{:S(2)}) async-start(), calls=%async_computation.11 | async-start | bytes 6553600 | tf_op jit(solution)/shard_map/all_gather | solution.py:113
  12.4 206.4 %reduce-scatter.12.cloned.1.call-start = ((), (), s32[]{:S(2)}) async-start(), calls=%async_computation.12 | async-start | bytes 13107200 | tf_op jit(solution)/shard_map/reduce_scatter | solution.py:145
  13.4 102.3 %copy-start.18 = (pred[640,640]{0,1:T(8,128)(4,1)}, pred[640,640]{0,1:T(8,128)(4,1)S(1)}, u32[]{:S(2)}) copy-start(pred[640,640]{0,1:T(8,128)(4,1)S(1)} %fusion.80) | copy-start | bytes 1228804
  18.1 100.9 %copy-start.11 = (pred[640,1280]{1,0:T(8,128)(4,1)}, pred[640,1280]{1,0:T(8,128)(4,1)S(1)}, u32[]{:S(2)}) copy-start(pred[640,1280]{1,0:T(8,128)(4,1)S(1)} %fusion.58) | copy-start | bytes 2457604
  55.7 7.2 copy-start.41
  55.7 7.2 copy-start.43
  93.3 5.9 copy-start.5
  93.3 5.9 copy-start.7
  94.1 5.2 copy-start.19
  96.6 19.0 %copy-start.4 = (f32[4,640,640]{1,2,0:T(8,128)}, f32[4,640,640]{1,2,0:T(8,128)S(1)}, u32[]{:S(2)}) copy-start(f32[4,640,640]{1,2,0:T(8,128)S(1)} %get-tuple-element.162) | copy-start | bytes 19660804
  134.2 84.6 %copy-start.2 = (bf16[320,2048]{1,0:T(8,128)(2,1)S(1)}, bf16[320,2048]{1,0:T(8,128)(2,1)}, u32[]{:S(2)}) copy-start(bf16[320,2048]{1,0:T(8,128)(2,1)} %param.26) | copy-start | bytes 3932164
  134.2 88.2 %copy-start.30 = (f32[2048]{0:T(1024)S(1)}, f32[2048]{0:T(1024)}, u32[]{:S(2)}) copy-start(f32[2048]{0:T(1024)} %param.33) | copy-start | bytes 24580
  134.3 130.2 %all-gather.7.cloned.1.call-start = ((), (), s32[]{:S(2)}) async-start(), calls=%async_computation.13 | async-start | bytes 6553600 | tf_op jit(solution)/shard_map/all_gather | solution.py:151
  222.5 24.4 %copy-start.13 = (bf16[320,2048]{1,0:T(8,128)(2,1)S(1)}, bf16[320,2048]{1,0:T(8,128)(2,1)}, u32[]{:S(2)}) copy-start(bf16[320,2048]{1,0:T(8,128)(2,1)} %param.27) | copy-start | bytes 3932164
  223.9 83.0 %all-gather.9.cloned.1.call-start = ((), (), s32[]{:S(2)}) async-start(), calls=%async_computation.15 | async-start | bytes 6553600 | tf_op jit(solution)/shard_map/all_gather | solution.py:167
  248.3 188.8 %reduce-scatter.16.cloned.1.call-start = ((), (), s32[]{:S(2)}) async-start(), calls=%async_computation.16 | async-start | bytes 13107200 | tf_op jit(solution)/shard_map/reduce_scatter | solution.py:172
  264.4 13.8 copy-start.42
  352.5 138.3 %reduce-scatter.14.cloned.1.call-start = ((), (), s32[]{:S(2)}) async-start(), calls=%async_computation.14 | async-start | bytes 6553600 | tf_op jit(solution)/shard_map/reduce_scatter | solution.py:159
  366.1 171.6 %all-gather.11.cloned.1.call-start = ((), (), s32[]{:S(2)}) async-start(), calls=%async_computation.17 | async-start | bytes 6553600 | tf_op jit(solution)/shard_map/all_gather | solution.py:185
  497.1 268.1 %reduce-scatter.32.cloned.1.call-start = ((), (), s32[]{:S(2)}) async-start(), calls=%async_computation.25 | async-start | bytes 12976128 | tf_op jit(solution)/shard_map/reduce_scatter | solution.py:264
  511.1 26.6 %copy-start.25 = (bf16[1280,4,128]{0,2,1:T(8,128)(2,1)S(1)}, bf16[1280,4,128]{0,2,1:T(8,128)(2,1)}, u32[]{:S(2)}) copy-start(bf16[1280,4,128]{0,2,1:T(8,128)(2,1)} %copy-done.24) | copy-start | bytes 3932164
  511.1 314.0 %reduce-scatter.26.cloned.1.call-start = ((), (), s32[]{:S(2)}) async-start(), calls=%async_computation.22 | async-start | bytes 4718592 | tf_op jit(solution)/shard_map/reduce_scatter | solution.py:261
  544.8 333.8 %reduce-scatter.18.cloned.1.call-start = ((), (), s32[]{:S(2)}) async-start(), calls=%async_computation.18 | async-start | bytes 6553600 | tf_op jit(solution)/shard_map/reduce_scatter | solution.py:246
  570.6 15.2 copy-start.16
  585.8 7.7 copy-start.39
  593.5 33.6 %copy-start.6 = (bf16[1280,4,64]{2,0,1:T(8,128)(2,1)S(1)}, bf16[1280,4,64]{2,0,1:T(8,128)(2,1)}, u32[]{:S(2)}) copy-start(bf16[1280,4,64]{2,0,1:T(8,128)(2,1)} %copy-done.5) | copy-start | bytes 1966084
  676.1 13.4 copy-start.26
  676.1 5.5 copy-start.28
  676.1 19.1 %slice-start = ((s8[13107200]{0:T(1024)(128)(4,1)}), s8[4194304]{0:T(1024)(128)(4,1)S(1)}, s32[]{:S(2)}) async-start(s8[13107200]{0:T(1024)(128)(4,1)} %bitcast.101), calls=%async_computation.26 | async-start | bytes 8388608
  676.1 19.1 %slice-start.1 = ((s8[13107200]{0:T(1024)(128)(4,1)}), s8[4194304]{0:T(1024)(128)(4,1)S(1)}, s32[]{:S(2)}) async-start(s8[13107200]{0:T(1024)(128)(4,1)} %bitcast.101), calls=%async_computation.27 | async-start | bytes 8388608
  681.6 7.9 copy-start.44
  681.6 13.6 slice-start.2
  689.5 5.7 slice-start.3
  689.5 5.7 copy-start.12
  689.5 5.7 copy-start.17
  710.7 365.2 %reduce-scatter.30.cloned.1.call-start = ((), (), s32[]{:S(2)}) async-start(), calls=%async_computation.24 | async-start | bytes 12976128 | tf_op jit(solution)/shard_map/reduce_scatter | solution.py:263
  724.8 547.0 %reduce-scatter.28.cloned.1.call-start = ((), (), s32[]{:S(2)}) async-start(), calls=%async_computation.23 | async-start | bytes 12976128 | tf_op jit(solution)/shard_map/reduce_scatter | solution.py:262
  738.9 624.6 %reduce-scatter.24.cloned.1.call-start = ((), (), s32[]{:S(2)}) async-start(), calls=%async_computation.21 | async-start | bytes 4718592 | tf_op jit(solution)/shard_map/reduce_scatter | solution.py:260
  746.1 709.3 %reduce-scatter.22.cloned.1.call-start = ((), (), s32[]{:S(2)}) async-start(), calls=%async_computation.20 | async-start | bytes 4718592 | tf_op jit(solution)/shard_map/reduce_scatter | solution.py:259
  754.6 792.9 %reduce-scatter.20.cloned.1.call-start = ((), (), s32[]{:S(2)}) async-start(), calls=%async_computation.19 | async-start | bytes 4718592 | tf_op jit(solution)/shard_map/reduce_scatter | solution.py:258
  763.3 115.2 %copy-start.3 = (bf16[320,2048]{1,0:T(8,128)(2,1)S(1)}, bf16[320,2048]{1,0:T(8,128)(2,1)}, u32[]{:S(2)}) copy-start(bf16[320,2048]{1,0:T(8,128)(2,1)} %param.26) | copy-start | bytes 3932164
  763.3 115.2 %copy-start.31 = (f32[2048]{0:T(1024)S(1)}, f32[2048]{0:T(1024)}, u32[]{:S(2)}) copy-start(f32[2048]{0:T(1024)} %param.28) | copy-start | bytes 24580
  763.3 115.2 %copy-start.36 = (f32[320]{0:T(512)S(1)}, f32[320]{0:T(512)}, u32[]{:S(2)}) copy-start(f32[320]{0:T(512)} %copy-done.35) | copy-start | bytes 3844
  765.2 115.7 %copy-start.34 = (f32[2048]{0:T(1024)S(1)}, f32[2048]{0:T(1024)}, u32[]{:S(2)}) copy-start(f32[2048]{0:T(1024)} %get-tuple-element.119) | copy-start | bytes 24580
  (18 other events, 38.4 us)
Sparse Core Ops, SparseCore 0:
  12.5 43.1 all-gather.4
  134.4 84.3 reduce-scatter.11
  224.0 40.4 all-gather.6
  266.4 40.3 all-gather.8
  352.6 84.3 reduce-scatter.15
  439.4 51.3 reduce-scatter.13
  497.3 40.3 all-gather.10
  541.3 192.7 reduce-scatter.31
  737.7 87.4 reduce-scatter.25
  827.5 50.9 reduce-scatter.17
  882.7 193.0 reduce-scatter.29
  1079.9 191.8 reduce-scatter.27
  1276.0 87.4 reduce-scatter.23
  1367.5 87.8 reduce-scatter.21
  1459.5 87.9 reduce-scatter.19
where the time goes:
time: 1560 us; the launch traced here: 1550 us
  waiting for transfers between devices  1030 us (66%)
  matrix products  343 us (22%)
  blocking collectives  67.1 us (4%)
  other arithmetic  65 us (4%)
  local copies, waits for them, and re-layouts  35.5 us (2%)
  between operations  15.7 us (1%)
    reduce_scatter x1, waiting for transfers between devices, shards(): lax.psum_scatter(grad_gate, 'dp', scatter_dimension=0, tiled=True)  196 us
    reduce_scatter x1, waiting for transfers between devices, shards(): lax.psum_scatter(grad_upw, 'dp', scatter_dimension=0, tiled=True)  145 us
    reduce_scatter x1, waiting for transfers between devices, shards(): lax.psum_scatter(grad_query, 'dp', scatter_dimension=0, tiled=True)  92 us
    reduce_scatter x1, waiting for transfers between devices, shards(): lax.psum_scatter(grad_keyw, 'dp', scatter_dimension=0, tiled=True)  92 us
    reduce_scatter x1, waiting for transfers between devices, shards(): lax.psum_scatter(grad_valuew, 'dp', scatter_dimension=0, tiled=True)  91.7 us
    reduce_scatter x1, waiting for transfers between devices, shards(): lax.psum_scatter(rows_dot(attn_heads, w_out), 'tensor', scatter_dimension...  84.5 us
    dot_general x7, matrix products, rows_dot_t(): lax.dot_general(left, right, (((1,), (1,)), ((), ())), preferred_element_...  75.8 us
    reduce_scatter x1, waiting for transfers between devices, shards(): lax.psum_scatter(rows_dot_t(d_gate, w_gate) + rows_dot_t(d_up, w_up), 'te...  70.9 us
  transfers between devices with their start and end apart: 15, of which 14 were waited for; matrix products, arithmetic and copies ran while one was open for 19% of the time, Pallas kernels for 0%

commit v1 on v0

--- a/solution.py
+++ b/solution.py
@@ -74,6 +74,40 @@
         & (key_mask[None, :] > 0.5)
     )
     return jnp.where(allowed[None], raw * score_scale, masked_score)
+
+
+def exchange(values, axis, bit):
+    size = lax.axis_size(axis)
+    return lax.ppermute(values, axis, [(rank, rank ^ bit) for rank in range(size)])
+
+
+def halve(values, axis_rank, bit):
+    pairs = values.reshape((values.shape[0] // 2, 2) + values.shape[1:])
+    own = lax.dynamic_index_in_dim(pairs, axis_rank, axis=1, keepdims=False)
+    other = lax.dynamic_index_in_dim(pairs, 1 - axis_rank, axis=1, keepdims=False)
+    return own, other
+
+
+def scatter_sum(values, axis, link_dtype):
+    size = lax.axis_size(axis)
+    rank = lax.axis_index(axis)
+    kept = values.reshape((size, values.shape[0] // size) + values.shape[1:])
+    bit = 1
+    while bit < size:
+        own, other = halve(kept, (rank // bit) % 2, bit)
+        received = exchange(other.astype(link_dtype), axis, bit)
+        kept = own.astype(jnp.float32) + received.astype(jnp.float32)
+        bit *= 2
+    return kept[0]
+
+
+def butterfly_sum(values, axis):
+    size = lax.axis_size(axis)
+    bit = 1
+    while bit < size:
+        values = values + exchange(values, axis, bit)
+        bit *= 2
+    return values
 
 
 def shards(
@@ -101,7 +135,7 @@
     real_tok = pad_mask[0].astype(jnp.float32)
     onehot_g = group_tok[:, None] == jnp.arange(GROUPS, dtype=jnp.int32)[None, :]
     counts_local = jnp.sum(jnp.where(onehot_g, real_tok[:, None], 0.0), axis=0)
-    counts = lax.psum(counts_local, "dp")
+    counts = butterfly_sum(counts_local, "dp")
     live = jnp.sum(counts)
     group_scale = jnp.sqrt(live / (GROUPS * jnp.maximum(counts, 1.0)))
     token_weight = real_tok * jnp.sum(jnp.where(onehot_g, group_scale[None, :], 0.0), axis=-1)
@@ -143,8 +177,11 @@
         log_totals.append(log_total)
     attn_heads = jnp.concatenate(head_blocks, axis=0).reshape(ROWS, width_local)
     mid_h = x_f + lax.psum_scatter(
-        rows_dot(attn_heads, w_out), "tensor", scatter_dimension=0, tiled=True
-    )
+        rows_dot(attn_heads, w_out).astype(jnp.bfloat16),
+        "tensor",
+        scatter_dimension=0,
+        tiled=True,
+    ).astype(jnp.float32)
     inv_b = lax.rsqrt(jnp.mean(mid_h * mid_h, axis=-1, keepdims=True) + epsilon)
     scaled_b = mid_h * inv_b
     normed_b = (scaled_b * gain_mlp).astype(jnp.bfloat16)
@@ -170,11 +207,11 @@
     d_gate = (d_mid * up_val * sigma * (1.0 + gate * (1.0 - sigma))).astype(jnp.bfloat16)
     d_up = (d_mid * activated).astype(jnp.bfloat16)
     d_normed_b = lax.psum_scatter(
-        rows_dot_t(d_gate, w_gate) + rows_dot_t(d_up, w_up),
+        (rows_dot_t(d_gate, w_gate) + rows_dot_t(d_up, w_up)).astype(jnp.bfloat16),
         "tensor",
         scatter_dimension=0,
         tiled=True,
-    )
+    ).astype(jnp.float32)
     grad_gate = cross_rows(gathered_b, d_gate)
     grad_upw = cross_rows(gathered_b, d_up)
     gain_mlp_part = jnp.sum(d_normed_b * scaled_b, axis=0)
@@ -254,16 +291,19 @@
     grad_input = d_hidden + inv_a * (
         e_attn - scaled_a * jnp.mean(e_attn * scaled_a, axis=-1, keepdims=True)
     )
-    all_sums = (
-        lax.psum_scatter(grad_query, "dp", scatter_dimension=0, tiled=True),
-        lax.psum_scatter(grad_keyw, "dp", scatter_dimension=0, tiled=True),
-        lax.psum_scatter(grad_valuew, "dp", scatter_dimension=0, tiled=True),
-        lax.psum_scatter(grad_out_t, "dp", scatter_dimension=0, tiled=True),
-        lax.psum_scatter(grad_gate, "dp", scatter_dimension=0, tiled=True),
-        lax.psum_scatter(grad_upw, "dp", scatter_dimension=0, tiled=True),
-        lax.psum_scatter(grad_down_t, "dp", scatter_dimension=0, tiled=True),
-        lax.psum_scatter(gain_attn_part, "dp", scatter_dimension=0, tiled=True),
-        lax.psum_scatter(gain_mlp_part, "dp", scatter_dimension=0, tiled=True),
+    all_sums = tuple(
+        scatter_sum(grad, "dp", jnp.bfloat16)
+        for grad in (
+            grad_query,
+            grad_keyw,
+            grad_valuew,
+            grad_out_t,
+            grad_gate,
+            grad_upw,
+            grad_down_t,
+        )
+    ) + tuple(
+        scatter_sum(part, "dp", jnp.float32) for part in (gain_attn_part, gain_mlp_part)
     )
     (
         sum_query,
@@ -276,7 +316,8 @@
         sum_gain_attn,
         sum_gain_mlp,
     ) = all_sums
-    gain_attn_grad, gain_mlp_grad = lax.psum((sum_gain_attn, sum_gain_mlp), "tensor")
+    gain_attn_grad = butterfly_sum(sum_gain_attn, "tensor")
+    gain_mlp_grad = butterfly_sum(sum_gain_mlp, "tensor")
     return (
         output,
         grad_input,

time: 1560 us -> 1090 us (0.70)
  waiting for transfers between devices: 1030 us -> 530 us
  blocking collectives: 67.1 us -> 0 us
  local copies, waits for them, and re-layouts: 35.5 us -> 76.2 us
  starting transfers between devices: 0.98 us -> 37.6 us
  other arithmetic: 65 us -> 99 us
  matrix products: 343 us -> 319 us
    reduce_scatter x9 -> x2, waiting for transfers between devices: 829 us -> 103 us  [the longest x1 51.5 us: shards(): lax.psum_scatter((rows_dot_t(d_gate, w_gate) + rows_dot_t(d_up, w_up)).as...]
    ppermute x0 -> x34, waiting for transfers between devices: none -> 309 us  [exchange(): lax.ppermute(values, axis, [(rank, rank ^ bit) for rank in range(size)])]
    reduce_scatter x1, waiting for transfers between devices: 51.4 us -> 0.01 us  [shards(): lax.psum_scatter((total + rows_dot_t(value_pre, w_value)).astype(jnp.bflo...]
    reduce_scatter x1, waiting for transfers between devices: 50 us -> 0.01 us  [shards(): lax.psum_scatter(rows_dot(mlp_mid, w_down).astype(jnp.bfloat16), 'tensor'...]
    unnamed x1 -> x0, blocking collectives: 39.1 us -> none
    ppermute x0 -> x34, starting transfers between devices: none -> 36.7 us  [exchange(): lax.ppermute(values, axis, [(rank, rank ^ bit) for rank in range(size)])]
    add x0 -> x27, other arithmetic: none -> 33.1 us  [the longest x20 23.7 us: scatter_sum(): kept = own.astype(jnp.float32) + received.astype(jnp.float32)]
    psum x2 -> x0, blocking collectives: 28 us -> none  [the longest x1 21.4 us: shards(): counts = lax.psum(counts_local, 'dp')]
  transfers between devices with their start and end apart: 15 -> 42, of which waited for: 14 -> 24; matrix products, arithmetic and copies ran while one was open for 19% -> 16% of each run, Pallas kernels for 0% -> 0%
where the time goes in v1:
time: 1090 us; the launch traced here: 1080 us
  waiting for transfers between devices  530 us (49%)
  matrix products  319 us (29%)
  other arithmetic  99 us (9%)
  local copies, waits for them, and re-layouts  76.2 us (7%)
  starting transfers between devices  37.6 us (3%)
  between operations  15.7 us (1%)
    ppermute x34, waiting for transfers between devices, exchange(): lax.ppermute(values, axis, [(rank, rank ^ bit) for rank in range(size)])  309 us
    dot_general x7, matrix products, rows_dot_t(): lax.dot_general(left, right, (((1,), (1,)), ((), ())), preferred_element_...  74.8 us
    dot_general x7, matrix products, rows_dot(): return jnp.dot(left, right, preferred_element_type=jnp.float32)  56.7 us
    reduce_scatter x1, waiting for transfers between devices, shards(): lax.psum_scatter((rows_dot_t(d_gate, w_gate) + rows_dot_t(d_up, w_up)).as...  51.5 us
    reduce_scatter x1, waiting for transfers between devices, shards(): lax.psum_scatter(rows_dot(attn_heads, w_out).astype(jnp.bfloat16), 'tenso...  51.4 us
    dot_general x2, matrix products, shards(): jnp.einsum('hqk,qhd->khd', d_score, query[row_first:row_end], preferred_e...  48.9 us
    dot_general x7, matrix products, cross_rows(): lax.dot_general(left, right, (((0,), (0,)), ((), ())), preferred_element_...  46.9 us
    dot_general x2, matrix products, shards(): jnp.einsum('hqk,khd->qhd', d_score, key_vec[:row_end], preferred_element_...  45.6 us
  transfers between devices with their start and end apart: 42, of which 24 were waited for; matrix products, arithmetic and copies ran while one was open for 16% of the time, Pallas kernels for 0%

profile of v1, /device:TPU:0, one launch (start us, length us, event | category | flops | bytes accessed | tf_op | source)
XLA Modules:
  0.0 1078.0 jit_solution(9692189030716969883)
XLA Ops:
  18.2 37.5 %all-gather.5.cloned.1.call-done = bf16[1280,2048]{1,0:T(8,128)(2,1)} async-done(((bf16[320,2048]{1,0:T(8,128)(2,1)}), bf16[1280,2048]{1,0:T(8,128)(2,1)}) %all-gather.5.cloned.1.call-update) | async-done | bytes 5242896 | tf_op jit(solution)/shard_map/all_gather | solution.py:147
  55.7 6.2 convolution_convert_fusion.3
  73.8 6.2 fusion.152
  87.8 5.5 subtract_convert_fusion
  99.3 6.6 fusion.5
  105.9 9.1 exponential_reduce_fusion
  119.1 8.4 fusion.103
  133.5 51.4 %reduce-scatter.5.cloned.1.call-done = bf16[320,2048]{1,0:T(8,128)(2,1)} async-done(((bf16[1280,2048]{1,0:T(8,128)(2,1)}), bf16[320,2048]{1,0:T(8,128)(2,1)}) %reduce-scatter.5.cloned.1.call-update) | async-done | bytes 1310736 | tf_op jit(solution)/shard_map/reduce_scatter | solution.py:179
  204.9 24.3 %all-gather.7.cloned.1.call-done = bf16[1280,2048]{1,0:T(8,128)(2,1)} async-done(((bf16[320,2048]{1,0:T(8,128)(2,1)}), bf16[1280,2048]{1,0:T(8,128)(2,1)}) %all-gather.7.cloned.1.call-update) | async-done | bytes 5242896 | tf_op jit(solution)/shard_map/all_gather | solution.py:188
  229.2 13.8 %fusion.155 = f32[1280,1408]{1,0:T(8,128)} fusion(bf16[1280,2048]{1,0:T(8,128)(2,1)} %all-gather.7.cloned.1.call-done, bf16[2048,1408]{1,0:T(8,128)(2,1)} %param.35), kind=kOutput, calls=%fused_computation.247 | convolution fusion | flops 7381975040 | bytes 18219008 | tf_op jit(solution)/shard_map/dot_general | solution.py:51
  243.0 12.3 %fusion.154 = f32[1280,1408]{1,0:T(8,128)} fusion(bf16[1280,2048]{1,0:T(8,128)(2,1)S(1)} %copy-done.75, bf16[2048,1408]{1,0:T(8,128)(2,1)} %param.34), kind=kOutput, calls=%fused_computation.246 | convolution fusion | flops 7381975040 | bytes 18219008 | tf_op jit(solution)/shard_map/dot_general | solution.py:51
  255.3 16.3 %all-gather.9.cloned.1.call-done = bf16[1280,2048]{1,0:T(8,128)(2,1)} async-done(((bf16[320,2048]{1,0:T(8,128)(2,1)}), bf16[1280,2048]{1,0:T(8,128)(2,1)}) %all-gather.9.cloned.1.call-update) | async-done | bytes 5242896 | tf_op jit(solution)/shard_map/all_gather | solution.py:204
  271.6 19.8 %multiply_convert_fusion.1 = (bf16[1280,1408]{1,0:T(8,128)(2,1)}, bf16[1280,1408]{1,0:T(8,128)(2,1)}, bf16[1280,1408]{1,0:T(8,128)(2,1)}) fusion(f32[1280,1408]{1,0:T(8,128)} %fusion.154, f32[1280,1408]{1,0:T(8,128)} %fusion.155, bf16[1280,2048]{1,0:T(8,128)(2,1)} %all-gather.9.cloned.1.call-done, bf16[1408,2048]{1,0:T(8,128)(2,1)} %param.36), kind=kOutput, calls=%fused_computation.13 | convolution fusion | flops 7409008640 | bytes 36241408 | tf_op jit(solution)/shard_map/dot_general | solution.py:55
  291.4 11.7 %fusion.156 = f32[1280,2048]{1,0:T(8,128)S(1)} fusion(bf16[1280,1408]{1,0:T(8,128)(2,1)} %get-tuple-element.104, bf16[2048,1408]{1,0:T(8,128)(2,1)} %param.34), kind=kOutput, calls=%fused_computation.248 | convolution fusion | flops 7381975040 | bytes 19857408 | tf_op jit(solution)/shard_map/dot_general | solution.py:55
  303.1 13.2 %add_convert_fusion.1 = bf16[1280,2048]{1,0:T(8,128)(2,1)} fusion(f32[1280,2048]{1,0:T(8,128)S(1)} %fusion.156, bf16[1280,1408]{1,0:T(8,128)(2,1)} %get-tuple-element.103, bf16[2048,1408]{1,0:T(8,128)(2,1)} %param.35), kind=kOutput, calls=%fused_computation.9 | convolution fusion | flops 7387217920 | bytes 25100288 | tf_op jit(solution)/shard_map/dot_general | solution.py:55
  316.3 51.5 %reduce-scatter.9.cloned.1.call-done = bf16[320,2048]{1,0:T(8,128)(2,1)} async-done(((bf16[1280,2048]{1,0:T(8,128)(2,1)}), bf16[320,2048]{1,0:T(8,128)(2,1)}) %reduce-scatter.9.cloned.1.call-update) | async-done | bytes 1310736 | tf_op jit(solution)/shard_map/reduce_scatter | solution.py:209
  374.6 40.1 %all-gather.11.cloned.1.call-done = bf16[1280,2048]{1,0:T(8,128)(2,1)} async-done(((bf16[320,2048]{1,0:T(8,128)(2,1)}), bf16[1280,2048]{1,0:T(8,128)(2,1)}) %all-gather.11.cloned.1.call-update) | async-done | bytes 5242896 | tf_op jit(solution)/shard_map/all_gather | solution.py:222
  414.7 5.4 convolution_convert_fusion.2
  421.1 5.9 convolution_bitcast_fusion.1
  430.8 14.8 %fusion.97 = f32[640,4,128]{2,0,1:T(8,128)} fusion(f32[4,640,640]{1,2,0:T(8,128)} %fusion.157, f32[4,640,640]{1,2,0:T(8,128)} %copy-done.6, f32[4,640]{1,0:T(4,128)S(1)} %copy-done.73, pred[640,640]{0,1:T(8,128)(4,1)} %copy-done.36, bf16[1280,4,64]{2,0,1:T(8,128)(2,1)S(1)} %copy-done.15, bf16[1280,4,64]{2,0,1:T(8,128)(2,1)S(1)} %copy-done.13), kind=kOutput, calls=%fused_computation.134 | convolution fusion | flops 438766720 | bytes 30986240 | tf_op jit(solution)/shard_map/hqk,qhd->khd/dot_general | solution.py:256
  445.6 15.0 %fusion.94 = f32[640,4,128]{2,0,1:T(8,128)} fusion(bf16[640,4,128]{2,0,1:T(8,128)(2,1)} %copy-done.41, f32[4,640,640]{1,2,0:T(8,128)} %fusion.157, f32[4,640,640]{1,2,0:T(8,128)} %copy-done.6, f32[4,640]{1,0:T(4,128)S(1)} %copy-done.73, pred[640,640]{0,1:T(8,128)(4,1)} %copy-done.36), kind=kOutput, calls=%fused_computation.133 | convolution fusion | flops 437456000 | bytes 15493120 | tf_op jit(solution)/shard_map/hqk,khd->qhd/dot_general | solution.py:251
  460.6 6.6 fusion.158
  467.3 9.9 fusion.73
  477.2 30.6 %fusion.100 = f32[640,4,128]{2,0,1:T(8,128)} fusion(f32[4,640,1280]{2,1,0:T(8,128)} %fusion.158, f32[4,640,1280]{2,1,0:T(8,128)} %get-tuple-element.139, f32[4,640]{1,0:T(4,128)S(1)} %copy-done.72, pred[640,1280]{1,0:T(8,128)(4,1)} %copy-done.21, bf16[1280,4,64]{2,0,1:T(8,128)(2,1)S(1)} %copy-done.11, bf16[1280,4,64]{2,0,1:T(8,128)(2,1)S(1)} %copy-done.9), kind=kOutput, calls=%fused_computation.136 | convolution fusion | flops 877530880 | bytes 29665280 | tf_op jit(solution)/shard_map/hqk,khd->qhd/dot_general | solution.py:251
  507.8 34.1 %fusion.66 = f32[1280,4,128]{2,0,1:T(8,128)} fusion(bf16[640,4,128]{2,0,1:T(8,128)(2,1)S(1)} %copy-done.40, f32[4,640,1280]{2,1,0:T(8,128)} %fusion.158, f32[4,640,1280]{2,1,0:T(8,128)} %get-tuple-element.139, f32[4,640]{1,0:T(4,128)S(1)} %copy-done.72, pred[640,1280]{1,0:T(8,128)(4,1)} %copy-done.21, f32[640,4,128]{2,0,1:T(8,128)} %fusion.97), kind=kOutput, calls=%fused_computation.67 | convolution fusion | flops 875564800 | bytes 31631360 | tf_op jit(solution)/shard_map/hqk,qhd->khd/dot_general | solution.py:256
  541.9 8.2 multiply_add_fusion
  557.7 8.2 fusion.159
  565.9 5.7 fusion.160
  571.6 10.9 %add_convert_fusion = bf16[1280,2048]{1,0:T(8,128)(2,1)} fusion(f32[1280,2048]{1,0:T(8,128)} %fusion.159, f32[1280,2048]{1,0:T(8,128)} %fusion.160, bf16[1280,512]{0,1:T(8,128)(2,1)S(1)} %bitcast.279, bf16[2048,512]{1,0:T(8,128)(2,1)S(1)} %copy-done.48), kind=kOutput, calls=%fused_computation.8 | convolution fusion | flops 2692218880 | bytes 29622272 | tf_op jit(solution)/shard_map/dot_general | solution.py:55
  582.7 8.1 copy.159
  590.8 13.0 %fusion.167 = f32[2048,1408]{1,0:T(8,128)S(1)} fusion(bf16[1280,2048]{1,0:T(8,128)(2,1)} %all-gather.9.cloned.1.call-done, bf16[1280,1408]{1,0:T(8,128)(2,1)} %get-tuple-element.105), kind=kOutput, calls=%fused_computation.259 | convolution fusion | flops 7381975040 | bytes 20381696 | tf_op jit(solution)/shard_map/dot_general | solution.py:61
  611.6 8.6 fusion.166
  626.8 9.1 fusion.165
  643.7 10.2 convolution_convert_fusion.1
  653.8 21.7 %collective-permute-done.31 = bf16[4,256,1408]{2,1,0:T(8,128)(2,1)} collective-permute-done((bf16[4,256,1408]{2,1,0:T(8,128)(2,1)}, bf16[4,256,1408]{2,1,0:T(8,128)(2,1)}, u32[]{:S(2)}, u32[]{:S(2)}) %collective-permute-start.31) | collective-permute-done | bytes 2883616 | tf_op jit(solution)/shard_map/ppermute | solution.py:81
  681.5 55.8 %collective-permute-done.28 = bf16[4,256,1408]{2,1,0:T(8,128)(2,1)} collective-permute-done((bf16[4,256,1408]{2,1,0:T(8,128)(2,1)}, bf16[4,256,1408]{2,1,0:T(8,128)(2,1)}, u32[]{:S(2)}, u32[]{:S(2)}) %collective-permute-start.28) | collective-permute-done | bytes 2883616 | tf_op jit(solution)/shard_map/ppermute | solution.py:81
  743.3 55.1 %collective-permute-done.25 = bf16[4,256,1408]{2,1,0:T(8,128)(2,1)} collective-permute-done((bf16[4,256,1408]{2,1,0:T(8,128)(2,1)}, bf16[4,256,1408]{2,1,0:T(8,128)(2,1)}, u32[]{:S(2)}, u32[]{:S(2)}) %collective-permute-start.25) | collective-permute-done | bytes 2883616 | tf_op jit(solution)/shard_map/ppermute | solution.py:81
  813.6 50.6 %collective-permute-done.26 = bf16[2,256,1408]{2,1,0:T(8,128)(2,1)S(1)} collective-permute-done((bf16[2,256,1408]{2,1,0:T(8,128)(2,1)S(1)}, bf16[2,256,1408]{2,1,0:T(8,128)(2,1)S(1)}, u32[]{:S(2)}, u32[]{:S(2)}) %collective-permute-start.26) | collective-permute-done | bytes 1441824 | tf_op jit(solution)/shard_map/ppermute | solution.py:81
  874.2 28.4 %collective-permute-done.22 = f32[1,256]{1,0:T(1,128)S(1)} collective-permute-done((f32[1,256]{1,0:T(1,128)S(1)}, f32[1,256]{1,0:T(1,128)S(1)}, u32[]{:S(2)}, u32[]{:S(2)}) %collective-permute-start.22) | collective-permute-done | bytes 1056 | tf_op jit(solution)/shard_map/ppermute | solution.py:81
  910.0 4.9 fusion.163
  917.5 8.0 copy.157
  925.5 5.2 fusion.164
  945.9 19.0 %collective-permute-done.17 = bf16[4,256,512]{2,1,0:T(8,128)(2,1)S(1)} collective-permute-done((bf16[4,256,512]{2,1,0:T(8,128)(2,1)S(1)}, bf16[4,256,512]{2,1,0:T(8,128)(2,1)S(1)}, u32[]{:S(2)}, u32[]{:S(2)}) %collective-permute-start.17) | collective-permute-done | bytes 1048608 | tf_op jit(solution)/shard_map/ppermute | solution.py:81
  967.0 20.5 %collective-permute-done.8 = bf16[4,256,512]{2,1,0:T(8,128)(2,1)} collective-permute-done((bf16[4,256,512]{2,1,0:T(8,128)(2,1)}, bf16[4,256,512]{2,1,0:T(8,128)(2,1)}, u32[]{:S(2)}, u32[]{:S(2)}) %collective-permute-start.8) | collective-permute-done | bytes 1048608 | tf_op jit(solution)/shard_map/ppermute | solution.py:81
  989.9 19.3 %collective-permute-done.11 = bf16[4,256,512]{2,1,0:T(8,128)(2,1)} collective-permute-done((bf16[4,256,512]{2,1,0:T(8,128)(2,1)}, bf16[4,256,512]{2,1,0:T(8,128)(2,1)}, u32[]{:S(2)}, u32[]{:S(2)}) %collective-permute-start.11) | collective-permute-done | bytes 1048608 | tf_op jit(solution)/shard_map/ppermute | solution.py:81
  1020.0 13.6 %collective-permute-done.12 = bf16[2,256,512]{2,1,0:T(8,128)(2,1)S(1)} collective-permute-done((bf16[2,256,512]{2,1,0:T(8,128)(2,1)S(1)}, bf16[2,256,512]{2,1,0:T(8,128)(2,1)S(1)}, u32[]{:S(2)}, u32[]{:S(2)}) %collective-permute-start.12) | collective-permute-done | bytes 524320 | tf_op jit(solution)/shard_map/ppermute | solution.py:81
  1039.3 11.4 %collective-permute-done.19 = bf16[1,256,512]{1,2,0:T(8,128)(2,1)} collective-permute-done((bf16[1,256,512]{1,2,0:T(8,128)(2,1)}, bf16[1,256,512]{1,2,0:T(8,128)(2,1)}, u32[]{:S(2)}, u32[]{:S(2)}) %collective-permute-start.19) | collective-permute-done | bytes 262176 | tf_op jit(solution)/shard_map/ppermute | solution.py:81
  1064.9 5.5 fusion.78
  (387 shorter events, 205.1 us)
Async XLA Ops:
  7.2 121.6 %copy-start = (bf16[512,2048]{1,0:T(8,128)(2,1)S(1)}, bf16[512,2048]{1,0:T(8,128)(2,1)}, u32[]{:S(2)}) copy-start(bf16[512,2048]{1,0:T(8,128)(2,1)} %param.32) | copy-start | bytes 6291460
  7.2 48.5 %all-gather.5.cloned.1.call-start = ((), (), s32[]{:S(2)}) async-start(), calls=%async_computation.4 | async-start | bytes 6553600 | tf_op jit(solution)/shard_map/all_gather | solution.py:147
  12.4 172.5 %reduce-scatter.5.cloned.1.call-start = ((), (), s32[]{:S(2)}) async-start(), calls=%async_computation.5 | async-start | bytes 6553600 | tf_op jit(solution)/shard_map/reduce_scatter | solution.py:179
  13.4 102.4 %copy-start.36 = (pred[640,640]{0,1:T(8,128)(4,1)}, pred[640,640]{0,1:T(8,128)(4,1)S(1)}, u32[]{:S(2)}) copy-start(pred[640,640]{0,1:T(8,128)(4,1)S(1)} %fusion.90) | copy-start | bytes 1228804
  18.2 100.9 %copy-start.21 = (pred[640,1280]{1,0:T(8,128)(4,1)}, pred[640,1280]{1,0:T(8,128)(4,1)S(1)}, u32[]{:S(2)}) copy-start(pred[640,1280]{1,0:T(8,128)(4,1)S(1)} %fusion.58) | copy-start | bytes 2457604
  133.5 53.4 %copy-start.57 = (f32[2048]{0:T(1024)S(1)}, f32[2048]{0:T(1024)}, u32[]{:S(2)}) copy-start(f32[2048]{0:T(1024)} %param.33) | copy-start | bytes 24580
  133.5 95.7 %all-gather.7.cloned.1.call-start = ((), (), s32[]{:S(2)}) async-start(), calls=%async_computation.6 | async-start | bytes 6553600 | tf_op jit(solution)/shard_map/all_gather | solution.py:188
  186.9 184.4 %copy-start.60 = (f32[320]{0:T(512)}, f32[320]{0:T(512)S(1)}, u32[]{:S(2)}) copy-start(f32[320]{0:T(512)S(1)} %add_rsqrt_fusion) | copy-start | bytes 3844
  188.6 83.0 %all-gather.9.cloned.1.call-start = ((), (), s32[]{:S(2)}) async-start(), calls=%async_computation.8 | async-start | bytes 6553600 | tf_op jit(solution)/shard_map/all_gather | solution.py:204
  189.0 3.6 collective-permute-start
  192.6 3.6 collective-permute-start.1
  196.2 4.5 collective-permute-start.2
  202.1 169.2 %copy-start.67 = (f32[320]{0:T(512)}, f32[320]{0:T(512)S(1)}, u32[]{:S(2)}) copy-start(f32[320]{0:T(512)S(1)} %dynamic-slice_multiply_fusion) | copy-start | bytes 3844
  204.8 163.0 %reduce-scatter.9.cloned.1.call-start = ((), (), s32[]{:S(2)}) async-start(), calls=%async_computation.9 | async-start | bytes 6553600 | tf_op jit(solution)/shard_map/reduce_scatter | solution.py:209
  316.3 98.4 %all-gather.11.cloned.1.call-start = ((), (), s32[]{:S(2)}) async-start(), calls=%async_computation.10 | async-start | bytes 6553600 | tf_op jit(solution)/shard_map/all_gather | solution.py:222
  374.1 661.3 %reduce-scatter.11.cloned.1.call-start = ((), (), s32[]{:S(2)}) async-start(), calls=%async_computation.11 | async-start | bytes 6553600 | tf_op jit(solution)/shard_map/reduce_scatter | solution.py:283
  582.6 482.3 %reduce-scatter.7.cloned.1.call-start = ((), (), s32[]{:S(2)}) async-start(), calls=%async_computation.7 | async-start | bytes 6553600 | tf_op jit(solution)/shard_map/reduce_scatter | solution.py:196
  609.8 65.7 %collective-permute-start.31 = (bf16[4,256,1408]{2,1,0:T(8,128)(2,1)}, bf16[4,256,1408]{2,1,0:T(8,128)(2,1)}, u32[]{:S(2)}, u32[]{:S(2)}) collective-permute-start(bf16[4,256,1408]{2,1,0:T(8,128)(2,1)} %fusion.76), channel_id=1, source_target_pairs={{0,4},{4,0},{8,12},{12,8},{16,20},{20,16},{24,28},{28,24},{1,5},{5... | collective-permute-start | bytes 8650760 | tf_op jit(solution)/shard_map/ppermute | solution.py:81
  626.5 110.8 %collective-permute-start.28 = (bf16[4,256,1408]{2,1,0:T(8,128)(2,1)}, bf16[4,256,1408]{2,1,0:T(8,128)(2,1)}, u32[]{:S(2)}, u32[]{:S(2)}) collective-permute-start(bf16[4,256,1408]{2,1,0:T(8,128)(2,1)} %fusion.75), channel_id=1, source_target_pairs={{0,4},{4,0},{8,12},{12,8},{16,20},{20,16},{24,28},{28,24},{1,5},{5... | collective-permute-start | bytes 8650760 | tf_op jit(solution)/shard_map/ppermute | solution.py:81
  641.9 156.5 %collective-permute-start.25 = (bf16[4,256,1408]{2,1,0:T(8,128)(2,1)}, bf16[4,256,1408]{2,1,0:T(8,128)(2,1)}, u32[]{:S(2)}, u32[]{:S(2)}) collective-permute-start(bf16[4,256,1408]{2,1,0:T(8,128)(2,1)} %fusion.74), channel_id=1, source_target_pairs={{0,4},{4,0},{8,12},{12,8},{16,20},{20,16},{24,28},{28,24},{1,5},{5... | collective-permute-start | bytes 8650760 | tf_op jit(solution)/shard_map/ppermute | solution.py:81
  679.7 124.7 %collective-permute-start.32 = (bf16[2,256,1408]{2,1,0:T(8,128)(2,1)S(1)}, bf16[2,256,1408]{2,1,0:T(8,128)(2,1)S(1)}, u32[]{:S(2)}, u32[]{:S(2)}) collective-permute-start(bf16[2,256,1408]{2,1,0:T(8,128)(2,1)S(1)} %fusion.93), channel_id=1, source_target_pairs={{0,8},{4,12},{8,0},{12,4},{16,24},{20,28},{24,16},{28,20},{1,9},{5... | collective-permute-start | bytes 4325384 | tf_op jit(solution)/shard_map/ppermute | solution.py:81
  741.5 67.0 %collective-permute-start.29 = (bf16[2,256,1408]{2,1,0:T(8,128)(2,1)S(1)}, bf16[2,256,1408]{2,1,0:T(8,128)(2,1)S(1)}, u32[]{:S(2)}, u32[]{:S(2)}) collective-permute-start(bf16[2,256,1408]{2,1,0:T(8,128)(2,1)S(1)} %fusion.92), channel_id=1, source_target_pairs={{0,8},{4,12},{8,0},{12,4},{16,24},{20,28},{24,16},{28,20},{1,9},{5... | collective-permute-start | bytes 4325384 | tf_op jit(solution)/shard_map/ppermute | solution.py:81
  802.6 61.6 %collective-permute-start.26 = (bf16[2,256,1408]{2,1,0:T(8,128)(2,1)S(1)}, bf16[2,256,1408]{2,1,0:T(8,128)(2,1)S(1)}, u32[]{:S(2)}, u32[]{:S(2)}) collective-permute-start(bf16[2,256,1408]{2,1,0:T(8,128)(2,1)S(1)} %fusion.91), channel_id=1, source_target_pairs={{0,8},{4,12},{8,0},{12,4},{16,24},{20,28},{24,16},{28,20},{1,9},{5... | collective-permute-start | bytes 4325384 | tf_op jit(solution)/shard_map/ppermute | solution.py:81
  805.9 66.6 %collective-permute-start.33 = (bf16[1,256,1408]{2,1,0:T(8,128)(2,1)}, bf16[1,256,1408]{2,1,0:T(8,128)(2,1)}, u32[]{:S(2)}, u32[]{:S(2)}) collective-permute-start(bf16[1,256,1408]{2,1,0:T(8,128)(2,1)} %dynamic-slice_convert_fusion.7), channel_id=1, source_target_pairs={{0,16},{4,20},{8,24},{12,28},{16,0},{20,4},{24,8},{28,12},{1,17},{... | collective-permute-start | bytes 2162696 | tf_op jit(solution)/shard_map/ppermute | solution.py:81
  811.2 91.5 %collective-permute-start.30 = (bf16[1,256,1408]{2,1,0:T(8,128)(2,1)}, bf16[1,256,1408]{2,1,0:T(8,128)(2,1)}, u32[]{:S(2)}, u32[]{:S(2)}) collective-permute-start(bf16[1,256,1408]{2,1,0:T(8,128)(2,1)} %dynamic-slice_convert_fusion.8), channel_id=1, source_target_pairs={{0,16},{4,20},{8,24},{12,28},{16,0},{20,4},{24,8},{28,12},{1,17},{... | collective-permute-start | bytes 2162696 | tf_op jit(solution)/shard_map/ppermute | solution.py:81
  812.1 55.8 %collective-permute-start.20 = (f32[4,256]{1,0:T(4,128)S(1)}, f32[4,256]{1,0:T(4,128)S(1)}, u32[]{:S(2)}, u32[]{:S(2)}) collective-permute-start(f32[4,256]{1,0:T(4,128)S(1)} %bitcast.292), channel_id=1, source_target_pairs={{0,4},{4,0},{8,12},{12,8},{16,20},{20,16},{24,28},{28,24},{1,5},{5... | collective-permute-start | bytes 12296 | tf_op jit(solution)/shard_map/ppermute | solution.py:81
  867.9 3.7 collective-permute-start.21
  869.4 37.3 %collective-permute-start.27 = (bf16[1,256,1408]{2,1,0:T(8,128)(2,1)S(1)}, bf16[1,256,1408]{2,1,0:T(8,128)(2,1)S(1)}, u32[]{:S(2)}, u32[]{:S(2)}) collective-permute-start(bf16[1,256,1408]{2,1,0:T(8,128)(2,1)S(1)} %dynamic-slice_convert_fusion.9), channel_id=1, source_target_pairs={{0,16},{4,20},{8,24},{12,28},{16,0},{20,4},{24,8},{28,12},{1,17},{... | collective-permute-start | bytes 2162696 | tf_op jit(solution)/shard_map/ppermute | solution.py:81
  871.6 31.1 %collective-permute-start.22 = (f32[1,256]{1,0:T(1,128)S(1)}, f32[1,256]{1,0:T(1,128)S(1)}, u32[]{:S(2)}, u32[]{:S(2)}) collective-permute-start(f32[1,256]{1,0:T(1,128)S(1)} %constant_dynamic-slice_fusion), channel_id=1, source_target_pairs={{0,16},{4,20},{8,24},{12,28},{16,0},{20,4},{24,8},{28,12},{1,17},{... | collective-permute-start | bytes 3080 | tf_op jit(solution)/shard_map/ppermute | solution.py:81
  902.7 2.8 collective-permute-start.23
  905.5 4.0 collective-permute-start.24
  916.2 26.6 %collective-permute-start.14 = (bf16[4,256,512]{2,1,0:T(8,128)(2,1)}, bf16[4,256,512]{2,1,0:T(8,128)(2,1)}, u32[]{:S(2)}, u32[]{:S(2)}) collective-permute-start(bf16[4,256,512]{2,1,0:T(8,128)(2,1)} %fusion.107), channel_id=1, source_target_pairs={{0,4},{4,0},{8,12},{12,8},{16,20},{20,16},{24,28},{28,24},{1,5},{5... | collective-permute-start | bytes 3145736 | tf_op jit(solution)/shard_map/ppermute | solution.py:81
  930.9 34.0 %collective-permute-start.17 = (bf16[4,256,512]{2,1,0:T(8,128)(2,1)S(1)}, bf16[4,256,512]{2,1,0:T(8,128)(2,1)S(1)}, u32[]{:S(2)}, u32[]{:S(2)}) collective-permute-start(bf16[4,256,512]{2,1,0:T(8,128)(2,1)S(1)} %fusion.108), channel_id=1, source_target_pairs={{0,4},{4,0},{8,12},{12,8},{16,20},{20,16},{24,28},{28,24},{1,5},{5... | collective-permute-start | bytes 3145736 | tf_op jit(solution)/shard_map/ppermute | solution.py:81
  936.3 51.2 %collective-permute-start.8 = (bf16[4,256,512]{2,1,0:T(8,128)(2,1)}, bf16[4,256,512]{2,1,0:T(8,128)(2,1)}, u32[]{:S(2)}, u32[]{:S(2)}) collective-permute-start(bf16[4,256,512]{2,1,0:T(8,128)(2,1)} %fusion.105), channel_id=1, source_target_pairs={{0,4},{4,0},{8,12},{12,8},{16,20},{20,16},{24,28},{28,24},{1,5},{5... | collective-permute-start | bytes 3145736 | tf_op jit(solution)/shard_map/ppermute | solution.py:81
  941.8 67.4 %collective-permute-start.11 = (bf16[4,256,512]{2,1,0:T(8,128)(2,1)}, bf16[4,256,512]{2,1,0:T(8,128)(2,1)}, u32[]{:S(2)}, u32[]{:S(2)}) collective-permute-start(bf16[4,256,512]{2,1,0:T(8,128)(2,1)} %fusion.106), channel_id=1, source_target_pairs={{0,4},{4,0},{8,12},{12,8},{16,20},{20,16},{24,28},{28,24},{1,5},{5... | collective-permute-start | bytes 3145736 | tf_op jit(solution)/shard_map/ppermute | solution.py:81
  945.4 65.6 %collective-permute-start.15 = (bf16[2,256,512]{2,1,0:T(8,128)(2,1)}, bf16[2,256,512]{2,1,0:T(8,128)(2,1)}, u32[]{:S(2)}, u32[]{:S(2)}) collective-permute-start(bf16[2,256,512]{2,1,0:T(8,128)(2,1)} %fusion.112), channel_id=1, source_target_pairs={{0,8},{4,12},{8,0},{12,4},{16,24},{20,28},{24,16},{28,20},{1,9},{5... | collective-permute-start | bytes 1572872 | tf_op jit(solution)/shard_map/ppermute | solution.py:81
  967.0 48.3 %collective-permute-start.18 = (bf16[2,256,512]{1,2,0:T(8,128)(2,1)S(1)}, bf16[2,256,512]{1,2,0:T(8,128)(2,1)S(1)}, u32[]{:S(2)}, u32[]{:S(2)}) collective-permute-start(bf16[2,256,512]{1,2,0:T(8,128)(2,1)S(1)} %bitcast.287), channel_id=1, source_target_pairs={{0,8},{4,12},{8,0},{12,4},{16,24},{20,28},{24,16},{28,20},{1,9},{5... | collective-permute-start | bytes 1572872 | tf_op jit(solution)/shard_map/ppermute | solution.py:81
  989.8 26.5 %collective-permute-start.9 = (bf16[2,256,512]{2,1,0:T(8,128)(2,1)S(1)}, bf16[2,256,512]{2,1,0:T(8,128)(2,1)S(1)}, u32[]{:S(2)}, u32[]{:S(2)}) collective-permute-start(bf16[2,256,512]{2,1,0:T(8,128)(2,1)S(1)} %fusion.110), channel_id=1, source_target_pairs={{0,8},{4,12},{8,0},{12,4},{16,24},{20,28},{24,16},{28,20},{1,9},{5... | collective-permute-start | bytes 1572872 | tf_op jit(solution)/shard_map/ppermute | solution.py:81
  1010.9 22.8 %collective-permute-start.12 = (bf16[2,256,512]{2,1,0:T(8,128)(2,1)S(1)}, bf16[2,256,512]{2,1,0:T(8,128)(2,1)S(1)}, u32[]{:S(2)}, u32[]{:S(2)}) collective-permute-start(bf16[2,256,512]{2,1,0:T(8,128)(2,1)S(1)} %fusion.111), channel_id=1, source_target_pairs={{0,8},{4,12},{8,0},{12,4},{16,24},{20,28},{24,16},{28,20},{1,9},{5... | collective-permute-start | bytes 1572872 | tf_op jit(solution)/shard_map/ppermute | solution.py:81
  1012.4 22.2 %collective-permute-start.16 = (bf16[1,256,512]{2,1,0:T(8,128)(2,1)S(1)}, bf16[1,256,512]{2,1,0:T(8,128)(2,1)S(1)}, u32[]{:S(2)}, u32[]{:S(2)}) collective-permute-start(bf16[1,256,512]{2,1,0:T(8,128)(2,1)S(1)} %dynamic-slice_convert_fusion.11), channel_id=1, source_target_pairs={{0,16},{4,20},{8,24},{12,28},{16,0},{20,4},{24,8},{28,12},{1,17},{... | collective-permute-start | bytes 786440 | tf_op jit(solution)/shard_map/ppermute | solution.py:81
  1016.1 34.5 %collective-permute-start.19 = (bf16[1,256,512]{1,2,0:T(8,128)(2,1)}, bf16[1,256,512]{1,2,0:T(8,128)(2,1)}, u32[]{:S(2)}, u32[]{:S(2)}) collective-permute-start(bf16[1,256,512]{1,2,0:T(8,128)(2,1)} %dynamic-slice_convert_fusion.10), channel_id=1, source_target_pairs={{0,16},{4,20},{8,24},{12,28},{16,0},{20,4},{24,8},{28,12},{1,17},{... | collective-permute-start | bytes 786440 | tf_op jit(solution)/shard_map/ppermute | solution.py:81
  1017.2 39.1 %collective-permute-start.10 = (bf16[1,256,512]{2,1,0:T(8,128)(2,1)}, bf16[1,256,512]{2,1,0:T(8,128)(2,1)}, u32[]{:S(2)}, u32[]{:S(2)}) collective-permute-start(bf16[1,256,512]{2,1,0:T(8,128)(2,1)} %dynamic-slice_convert_fusion.13), channel_id=1, source_target_pairs={{0,16},{4,20},{8,24},{12,28},{16,0},{20,4},{24,8},{28,12},{1,17},{... | collective-permute-start | bytes 786440 | tf_op jit(solution)/shard_map/ppermute | solution.py:81
  1034.5 25.9 %collective-permute-start.13 = (bf16[1,256,512]{2,1,0:T(8,128)(2,1)}, bf16[1,256,512]{2,1,0:T(8,128)(2,1)}, u32[]{:S(2)}, u32[]{:S(2)}) collective-permute-start(bf16[1,256,512]{2,1,0:T(8,128)(2,1)} %dynamic-slice_convert_fusion.12), channel_id=1, source_target_pairs={{0,16},{4,20},{8,24},{12,28},{16,0},{20,4},{24,8},{28,12},{1,17},{... | collective-permute-start | bytes 786440 | tf_op jit(solution)/shard_map/ppermute | solution.py:81
  1037.8 14.8 %collective-permute-start.3 = (f32[4,256]{1,0:T(4,128)S(1)}, f32[4,256]{1,0:T(4,128)S(1)}, u32[]{:S(2)}, u32[]{:S(2)}) collective-permute-start(f32[4,256]{1,0:T(4,128)S(1)} %bitcast.293), channel_id=1, source_target_pairs={{0,4},{4,0},{8,12},{12,8},{16,20},{20,16},{24,28},{28,24},{1,5},{5... | collective-permute-start | bytes 12296 | tf_op jit(solution)/shard_map/ppermute | solution.py:81
  1052.7 5.4 collective-permute-start.4
  1058.2 4.5 collective-permute-start.5
  1062.7 1.2 collective-permute-start.6
  1063.9 6.6 collective-permute-start.7
  (83 other events, 861.3 us)
Sparse Core Ops, SparseCore 0:
  12.6 43.1 all-gather.4
  133.6 51.3 reduce-scatter.4
  188.8 40.3 all-gather.6
  231.2 40.3 all-gather.8
  316.4 51.3 reduce-scatter.8
  374.3 40.4 all-gather.10
  582.7 51.3 reduce-scatter.10
  654.0 51.1 reduce-scatter.6

commit v2 on v0

v2 whole, which is shorter than its diff:
```python
import functools

import jax
import jax.numpy as jnp
from jax import lax
from jax.experimental import pallas as pl
from jax.experimental.pallas import tpu as pltpu
from jax.sharding import PartitionSpec as P

HEAD_DIM = 128
ROWS = 1280
DOCS = 3
GROUPS = 8
QTILE = 256

epsilon = 1e-05
masked_score = -1e30
rope_base = 10000.0
NT = (((1,), (1,)), ((), ()))
TN = (((0,), (0,)), ((), ()))
NN = (((1,), (0,)), ((), ()))


def mm(left, right, dims=NN):
    return lax.dot_general(left, right, dims, preferred_element_type=jnp.float32)


def whole(shape):
    return pl.BlockSpec(shape, lambda *_: (0,) * len(shape))


def turn(values, cosine, sine):
    return values * cosine + pltpu.roll(values, HEAD_DIM // 2, 1) * sine


def qkv_body(first, rank_ref, xa_ref, xb_ref, cos_ref, sin_ref, wq_ref, wk_ref, wv_ref, q_ref, k_ref, v_ref):
    rows = xa_ref.shape[0]
    for half, x_ref in enumerate((xa_ref, xb_ref)):
        span = pl.ds(half * rows, rows)
        x = x_ref[...]
        place = pl.ds(pl.multiple_of((rank_ref[0] ^ (first + half)) * rows, rows), rows)
        cosine, sine = cos_ref[place, :], sin_ref[place, :]
        for w_ref, out_ref in ((wq_ref, q_ref), (wk_ref, k_ref)):
            full = mm(x, w_ref[...])
            for head in range(full.shape[1] // HEAD_DIM):
                lanes = slice(head * HEAD_DIM, (head + 1) * HEAD_DIM)
                out_ref[span, lanes] = turn(full[:, lanes], cosine, sine).astype(jnp.bfloat16)
        v_ref[span, :] = mm(x, wv_ref[...]).astype(jnp.bfloat16)


def qkv_pair(first, rank, xa, xb, cosine, sine, wq, wk, wv):
    rows, depth = xa.shape
    width = wq.shape[1]
    tile = 256
    wspec = pl.BlockSpec((depth, tile), lambda j, *_: (0, j))
    ospec = pl.BlockSpec((2 * rows, tile), lambda j, *_: (0, j))
    out = jax.ShapeDtypeStruct((2 * rows, width), jnp.bfloat16)
    return pl.pallas_call(
        functools.partial(qkv_body, first),
        grid_spec=pltpu.PrefetchScalarGridSpec(
            num_scalar_prefetch=1,
            grid=(width // tile,),
            in_specs=[whole(xa.shape)] * 2 + [whole(cosine.shape)] * 2 + [wspec] * 3,
            out_specs=[ospec] * 3,
        ),
        out_shape=[out] * 3,
        compiler_params=pltpu.CompilerParams(vmem_limit_bytes=60 << 20),
        cost_estimate=pl.CostEstimate(
            flops=12 * rows * depth * width, bytes_accessed=6 * depth * width + 4 * rows * depth, transcendentals=0
        ),
        name="qkv",
    )(rank, xa, xb, cosine, sine, wq, wk, wv)


def in_order(rank_ref, near_ref, far_ref, out_ref):
    piece = near_ref.shape[0] // 2
    for index in range(4):
        src = (near_ref, far_ref)[index // 2]
        at = pl.multiple_of((rank_ref[0] ^ index) * piece, piece)
        out_ref[pl.ds(at, piece), :] = src[pl.ds((index % 2) * piece, piece), :]


def out_of_order(rank_ref, src_ref, near_ref, far_ref):
    piece = near_ref.shape[0] // 2
    for index in range(4):
        dst = (near_ref, far_ref)[index // 2]
        at = pl.multiple_of((rank_ref[0] ^ index) * piece, piece)
        dst[pl.ds((index % 2) * piece, piece), :] = src_ref[pl.ds(at, piece), :].astype(dst.dtype)


def attend_body(rank_ref, qn, qf, kn, kf, vn, vf, low_ref, high_ref, on, of, lse_ref, q_s, k_s, v_s, o_s):
    in_order(rank_ref, qn, qf, q_s)
    in_order(rank_ref, kn, kf, k_s)
    in_order(rank_ref, vn, vf, v_s)
    scale = HEAD_DIM ** (-0.5)
    v_t = v_s[...].T
    for block in range(q_s.shape[0] // QTILE):
        span = pl.ds(block * QTILE, QTILE)
        end = (block + 1) * QTILE
        scores = mm(k_s[:end, :], q_s[span, :], NT)
        at = lax.broadcasted_iota(jnp.int32, scores.shape, 0)
        allowed = (at >= low_ref[:, span]) & (at <= high_ref[:, span])
        scores = jnp.where(allowed, scores * scale, masked_score)
        top = jnp.max(scores, axis=0, keepdims=True)
        prob = jnp.exp(scores - top)
        total = jnp.sum(prob, axis=0, keepdims=True)
        lse_ref[0, :, span] = top + jnp.log(total)
        out_t = mm(v_t[:, :end], prob.astype(jnp.bfloat16)) * (1.0 / total)
        o_s[span, :] = out_t.T
    out_of_order(rank_ref, o_s, on, of)


def attend(rank, qs, ks, vs, low, high):
    half, width = qs[0].shape
    rows = 2 * half
    heads = width // HEAD_DIM
    hspec = pl.BlockSpec((half, HEAD_DIM), lambda h, *_: (0, h))
    row = whole((1, rows))
    return pl.pallas_call(
        attend_body,
        grid_spec=pltpu.PrefetchScalarGridSpec(
            num_scalar_prefetch=1,
            grid=(heads,),
            in_specs=[hspec] * 6 + [row] * 2,
            out_specs=[hspec] * 2 + [pl.BlockSpec((1, 1, rows), lambda h, *_: (h, 0, 0))],
            scratch_shapes=[pltpu.VMEM((rows, HEAD_DIM), jnp.bfloat16)] * 3 + [pltpu.VMEM((rows, HEAD_DIM), jnp.float32)],
        ),
        out_shape=[jax.ShapeDtypeStruct((half, width), jnp.bfloat16)] * 2
        + [jax.ShapeDtypeStruct((heads, 1, rows), jnp.float32)],
        compiler_params=pltpu.CompilerParams(vmem_limit_bytes=60 << 20),
        cost_estimate=pl.CostEstimate(
            flops=8 * rows * rows * width, bytes_accessed=8 * rows * width, transcendentals=heads * rows * rows // 2
        ),
        name="attend",
    )(rank, *qs, *ks, *vs, low, high)


def attend_back_body(
    rank_ref, qn, qf, kn, kf, vn, vf, gn, gf, low_ref, high_ref, lse_ref, cos_ref, sin_ref,
    dqn, dqf, dkn, dkf, dvn, dvf, q_s, k_s, v_s, g_s, dq_s, dk_s, dv_s,
):
    in_order(rank_ref, qn, qf, q_s)
    in_order(rank_ref, kn, kf, k_s)
    in_order(rank_ref, vn, vf, v_s)
    in_order(rank_ref, gn, gf, g_s)
    scale = HEAD_DIM ** (-0.5)
    k_t = k_s[...].T
    blocks = q_s.shape[0] // QTILE
    for block in reversed(range(blocks)):
        span = pl.ds(block * QTILE, QTILE)
        end = (block + 1) * QTILE
        query, grad = q_s[span, :], g_s[span, :]
        scores = mm(k_s[:end, :], query, NT) * scale
        at = lax.broadcasted_iota(jnp.int32, scores.shape, 0)
        allowed = (at >= low_ref[:, span]) & (at <= high_ref[:, span])
        prob = jnp.exp(jnp.where(allowed, scores, masked_score) - lse_ref[0, :, span])
        d_prob = mm(v_s[:end, :], grad, NT)
        dot = jnp.sum(prob * d_prob, axis=0, keepdims=True)
        d_score = (prob * (d_prob - dot) * scale).astype(jnp.bfloat16)
        dq_s[span, :] = mm(k_t[:, :end], d_score).T
        d_key = mm(d_score, query)
        d_value = mm(prob.astype(jnp.bfloat16), grad)
        if block == blocks - 1:
            dk_s[...] = d_key
            dv_s[...] = d_value
        else:
            dk_s[:end, :] += d_key
            dv_s[:end, :] += d_value
    dq_s[...] = turn(dq_s[...], cos_ref[...], sin_ref[...])
    dk_s[...] = turn(dk_s[...], cos_ref[...], sin_ref[...])
    out_of_order(rank_ref, dq_s, dqn, dqf)
    out_of_order(rank_ref, dk_s, dkn, dkf)
    out_of_order(rank_ref, dv_s, dvn, dvf)


def attend_back(rank, qs, ks, vs, gs, low, high, lse, cosine, back_sine):
    half, width = qs[0].shape
    rows = 2 * half
    heads = width // HEAD_DIM
    hspec = pl.BlockSpec((half, HEAD_DIM), lambda h, *_: (0, h))
    row = whole((1, rows))
    return pl.pallas_call(
        attend_back_body,
        grid_spec=pltpu.PrefetchScalarGridSpec(
            num_scalar_prefetch=1,
            grid=(heads,),
            in_specs=[hspec] * 8
            + [row] * 2
            + [pl.BlockSpec((1, 1, rows), lambda h, *_: (h, 0, 0))]
            + [whole((rows, HEAD_DIM))] * 2,
            out_specs=[hspec] * 6,
            scratch_shapes=[pltpu.VMEM((rows, HEAD_DIM), jnp.bfloat16)] * 4
            + [pltpu.VMEM((rows, HEAD_DIM), jnp.float32)] * 3,
        ),
        out_shape=[jax.ShapeDtypeStruct((half, width), jnp.bfloat16)] * 6,
        compiler_params=pltpu.CompilerParams(vmem_limit_bytes=60 << 20),
        cost_estimate=pl.CostEstimate(
            flops=20 * rows * rows * width, bytes_accessed=16 * rows * width, transcendentals=heads * rows * rows // 2
        ),
        name="attend_back",
    )(rank, *qs, *ks, *vs, *gs, low, high, lse, cosine, back_sine)


def mlp_body(xa_ref, xb_ref, ca_ref, cb_ref, wg_ref, wu_ref, wd_ref, mid_ref, dg_ref, du_ref):
    rows = xa_ref.shape[0]
    for half, (x_ref, c_ref) in enumerate(((xa_ref, ca_ref), (xb_ref, cb_ref))):
        span = pl.ds(half * rows, rows)
        x = x_ref[...]
        gate = mm(x, wg_ref[...])
        up = mm(x, wu_ref[...])
        d_mid = mm(c_ref[...], wd_ref[...], NT)
        sigma = 1.0 / (1.0 + jnp.exp(-gate))
        active = gate * sigma
        mid_ref[span, :] = (active * up).astype(jnp.bfloat16)
        dg_ref[span, :] = (d_mid * up * sigma * (1.0 + gate * (1.0 - sigma))).astype(jnp.bfloat16)
        du_ref[span, :] = (d_mid * active).astype(jnp.bfloat16)


def mlp_pair(xa, xb, ca, cb, wg, wu, wd):
    rows, depth = xa.shape
    width = wg.shape[1]
    tile = 256
    wspec = pl.BlockSpec((depth, tile), lambda j: (0, j))
    ospec = pl.BlockSpec((2 * rows, tile), lambda j: (0, j))
    return pl.pallas_call(
        mlp_body,
        grid=(pl.cdiv(width, tile),),
        in_specs=[whole(xa.shape)] * 4 + [wspec] * 2 + [pl.BlockSpec((tile, depth), lambda j: (j, 0))],
        out_specs=[ospec] * 3,
        out_shape=[jax.ShapeDtypeStruct((2 * rows, width), jnp.bfloat16)] * 3,
        compiler_params=pltpu.CompilerParams(vmem_limit_bytes=60 << 20),
        cost_estimate=pl.CostEstimate(
            flops=12 * rows * depth * width,
            bytes_accessed=6 * depth * width + 8 * rows * depth + 12 * rows * width,
            transcendentals=2 * rows * width,
        ),
        name="mlp",
    )(xa, xb, ca, cb, wg, wu, wd)


def gather_rows(parts, out_ref):
    at = 0
    for part in parts:
        out_ref[at : at + part.shape[0], :] = part[...]
        at += part.shape[0]


def grad_send_body(pieces, halves, _, *refs):
    left, rights = refs[:pieces], refs[pieces : pieces + halves]
    out_ref, left_s, right_s = refs[pieces + halves :]

    @pl.when(pl.program_id(0) == 0)
    def _():
        gather_sides(rights, right_s)

    gather_rows(left, left_s)
    out_ref[...] = mm(left_s[...], right_s[...], TN).astype(out_ref.dtype)


def gather_sides(rights, out_ref):
    at = 0
    for near, far in zip(rights[::2], rights[1::2]):
        rows, width = near.shape
        out_ref[:rows, at : at + width] = near[...]
        out_ref[rows:, at : at + width] = far[...]
        at += width


def grad_keep_body(pieces, halves, send, _, *refs):
    left, rights = refs[:pieces], refs[pieces : pieces + halves]
    got_ref, away_ref, own_ref, left_s, right_s = refs[pieces + halves :]
    step = pl.program_id(0)

    @pl.when(step == 0)
    def _():
        gather_sides(rights, right_s)

    gather_rows(left, left_s)
    total = mm(left_s[...], right_s[...], TN) + got_ref[...].astype(jnp.float32)

    @pl.when(step < send)
    def _():
        away_ref[...] = total.astype(away_ref.dtype)

    @pl.when(step >= send)
    def _():
        own_ref[...] = total


def grad_call(order, pieces, rights, tile, got=None):
    rows, depth = pieces[0].shape[0] * len(pieces), pieces[0].shape[1]
    width = sum(near.shape[1] for near in rights[::2])
    count = order.shape[0]
    lspec = pl.BlockSpec((pieces[0].shape[0], tile), lambda j, s: (0, s[j]))
    in_specs = [lspec] * len(pieces) + [whole(r.shape) for r in rights]
    args = [order, *pieces, *rights]
    if got is None:
        body = functools.partial(grad_send_body, len(pieces), len(rights))
        out_specs = pl.BlockSpec((tile, width), lambda j, *_: (j, 0))
        out_shape = jax.ShapeDtypeStruct((count * tile, width), jnp.bfloat16)
    else:
        send = count // 2
        body = functools.partial(grad_keep_body, len(pieces), len(rights), send)
        in_specs.append(pl.BlockSpec((tile, width), lambda j, s: (s[j] // 2, 0)))
        args.append(got)
        out_specs = [
            pl.BlockSpec((tile, width), lambda j, *_: (jnp.minimum(j, send - 1), 0)),
            pl.BlockSpec((tile, width), lambda j, *_: (jnp.maximum(j - send, 0), 0)),
        ]
        out_shape = [
            jax.ShapeDtypeStruct((send * tile, width), jnp.bfloat16),
            jax.ShapeDtypeStruct(((count - send) * tile, width), jnp.float32),
        ]
    return pl.pallas_call(
        body,
        grid_spec=pltpu.PrefetchScalarGridSpec(
            num_scalar_prefetch=1,
            grid=(count,),
            in_specs=in_specs,
            out_specs=out_specs,
            scratch_shapes=[pltpu.VMEM((rows, tile), jnp.bfloat16), pltpu.VMEM((rows, width), jnp.bfloat16)],
        ),
        out_shape=out_shape,
        compiler_params=pltpu.CompilerParams(vmem_limit_bytes=60 << 20),
        cost_estimate=pl.CostEstimate(
            flops=2 * rows * tile * count * width,
            bytes_accessed=2 * rows * (tile * count + width) + 3 * tile * count * width,
            transcendentals=0,
        ),
        name="weight_grad",
    )(*args)


def row_tables(length_row, group_row, mask_row):
    starts = jnp.cumsum(length_row) - length_row
    token = jnp.arange(ROWS, dtype=jnp.int32)
    doc_index = jnp.sum((token[:, None] >= starts[None, 1:]).astype(jnp.int32), axis=1)
    onehot = doc_index[:, None] == jnp.arange(DOCS, dtype=jnp.int32)[None, :]
    first = jnp.sum(jnp.where(onehot, starts[None, :], 0), axis=1)
    group_tok = jnp.sum(jnp.where(onehot, group_row[None, :], 0), axis=1)
    real = jnp.sum(jnp.where(onehot, mask_row[:, None], 0), axis=0)
    last_real = first + jnp.sum(jnp.where(onehot, real[None, :], 0), axis=1) - 1
    return (token - first, first, jnp.minimum(token, last_real), group_tok)


def rope_tables(inside):
    freq = rope_base ** (-jnp.arange(0, HEAD_DIM // 2, dtype=jnp.float32) * 2.0 / HEAD_DIM)
    angle = inside.astype(jnp.float32)[:, None] * freq[None, :]
    cosine, sine = jnp.cos(angle), jnp.sin(angle)
    return (
        jnp.concatenate([cosine, cosine], axis=-1),
        jnp.concatenate([-sine, sine], axis=-1),
        jnp.concatenate([sine, -sine], axis=-1),
    )


def rows_dot(left, right):
    return jnp.dot(left, right, preferred_element_type=jnp.float32)


def rows_dot_t(left, right):
    return lax.dot_general(left, right, NT, preferred_element_type=jnp.float32)


def exchange(values, axis, bit):
    size = lax.axis_size(axis)
    return lax.ppermute(values, axis, [(rank, rank ^ bit) for rank in range(size)])


def butterfly_sum(values, axis):
    size = lax.axis_size(axis)
    bit = 1
    while bit < size:
        values = values + exchange(values, axis, bit)
        bit *= 2
    return values


def after(values, *others):
    return lax.optimization_barrier((values, *others))[0]


def scatter_rest(kept, away, axis, bit):
    size = lax.axis_size(axis)
    rank = lax.axis_index(axis)
    while True:
        got = exchange(away.astype(jnp.bfloat16), axis, bit)
        bit *= 2
        if bit == size:
            return kept.astype(jnp.float32) + got.astype(jnp.float32)
        total = kept.astype(jnp.float32) + got.astype(jnp.float32)
        pairs = total.reshape((total.shape[0] // 2, 2) + total.shape[1:])
        side = (rank // bit) % 2
        kept = lax.dynamic_index_in_dim(pairs, side, axis=1, keepdims=False)
        away = lax.dynamic_index_in_dim(pairs, 1 - side, axis=1, keepdims=False)


def scatter_small(values, axis):
    size = lax.axis_size(axis)
    rank = lax.axis_index(axis)
    kept = values
    bit = 1
    while bit < size:
        pairs = kept.reshape((kept.shape[0], kept.shape[1] // 2, 2) + kept.shape[2:])
        side = (rank // bit) % 2
        own = lax.dynamic_index_in_dim(pairs, side, axis=2, keepdims=False)
        away = lax.dynamic_index_in_dim(pairs, 1 - side, axis=2, keepdims=False)
        kept = own + exchange(away, axis, bit)
        bit *= 2
    return kept[:, 0]


class WeightGrad:
    def __init__(self, pieces, rights):
        self.pieces, self.rights = pieces, rights
        self.size = lax.axis_size("dp")
        self.rank = lax.axis_index("dp")
        self.tile = pieces[0].shape[1] // self.size
        self.blocks = self.tile % 128 == 0 and self.size >= 4

    def send(self):
        if self.blocks:
            order = 2 * jnp.arange(self.size // 2, dtype=jnp.int32) + (1 - self.rank % 2)
            return grad_call(order, self.pieces, self.rights, self.tile)
        left = jnp.concatenate(self.pieces, axis=0)
        right = jnp.concatenate([jnp.concatenate(self.rights[::2], axis=1), jnp.concatenate(self.rights[1::2], axis=1)], axis=0)
        full = lax.dot_general(left, right, TN, preferred_element_type=jnp.float32)
        pairs = full.reshape(self.size // 2, 2, self.tile, -1)
        self.own = lax.dynamic_index_in_dim(pairs, self.rank % 2, axis=1, keepdims=False)
        away = lax.dynamic_index_in_dim(pairs, 1 - self.rank % 2, axis=1, keepdims=False)
        return away.reshape(self.size // 2 * self.tile, -1).astype(jnp.bfloat16)

    def finish(self, got):
        width = got.shape[1]
        if self.blocks:
            place = jnp.arange(self.size // 4, dtype=jnp.int32)
            side = (self.rank // 2) % 2
            blocks = jnp.concatenate([2 * place + 1 - side, 2 * place + side])
            away, kept = grad_call(2 * blocks + self.rank % 2, self.pieces, self.rights, self.tile, got)
            away, kept = (a.reshape(-1, self.tile, width) for a in (away, kept))
        else:
            total = self.own + got.reshape(self.own.shape).astype(jnp.float32)
            pairs = total.reshape(self.size // 4, 2, self.tile, width)
            side = (self.rank // 2) % 2
            kept = lax.dynamic_index_in_dim(pairs, side, axis=1, keepdims=False)
            away = lax.dynamic_index_in_dim(pairs, 1 - side, axis=1, keepdims=False)
        return scatter_rest(kept, away, "dp", 2)[0]


def cut(values):
    half = values.shape[0] // 2
    return values[:half], values[half:]


def send_far(far):
    mine, others = cut(far)
    return (mine.astype(jnp.float32) + exchange(others, "tensor", 1).astype(jnp.float32)).astype(jnp.bfloat16)


def sum_near(near, got):
    mine, others = cut(near)
    return (
        mine.astype(jnp.float32)
        + exchange(others, "tensor", 1).astype(jnp.float32)
        + got.astype(jnp.float32)
    )


def shards(
    hidden_in,
    cotangent,
    gain_attn,
    w_query,
    w_key,
    w_value,
    w_out,
    gain_mlp,
    w_gate,
    w_up,
    w_down,
    doc_lengths,
    doc_groups,
    pad_mask,
):
    rows_local = hidden_in.shape[0]
    rank = lax.axis_index("tensor").astype(jnp.int32)
    rank_ref = rank[None]

    def to_far(values):
        return exchange(values, "tensor", 2)

    def to_mate(values):
        return exchange(values, "tensor", 1)

    x_f = hidden_in.astype(jnp.float32)
    inv_a = lax.rsqrt(jnp.mean(x_f * x_f, axis=-1, keepdims=True) + epsilon)
    a0 = (x_f * inv_a * gain_attn).astype(jnp.bfloat16)
    a2 = to_far(a0)
    a1 = to_mate(a0)
    a3 = to_mate(a2)

    inside, low, high, group_tok = row_tables(doc_lengths[0], doc_groups[0], pad_mask[0])
    low, high = low[None], high[None]
    real_tok = pad_mask[0].astype(jnp.float32)
    onehot_g = group_tok[:, None] == jnp.arange(GROUPS, dtype=jnp.int32)[None, :]
    counts = butterfly_sum(jnp.sum(jnp.where(onehot_g, real_tok[:, None], 0.0), axis=0), "dp")
    live = jnp.sum(counts)
    group_scale = jnp.sqrt(live / (GROUPS * jnp.maximum(counts, 1.0)))
    token_weight = real_tok * jnp.sum(jnp.where(onehot_g, group_scale[None, :], 0.0), axis=-1)
    weight_local = lax.dynamic_slice_in_dim(token_weight, rank * rows_local, rows_local)
    c0 = (cotangent.astype(jnp.float32) * weight_local[:, None]).astype(jnp.bfloat16)
    cosine, sine, back_sine = rope_tables(inside)

    near = qkv_pair(0, rank_ref, a0, a1, cosine, sine, w_query, w_key, w_value)
    c0 = after(c0, a2)
    c2 = to_far(c0)
    c1 = to_mate(c0)
    c3 = to_mate(c2)
    far = qkv_pair(2, rank_ref, a2, a3, cosine, sine, w_query, w_key, w_value)
    qs, ks, vs = zip(near, far)
    heads_near, heads_far, lse = attend(rank_ref, qs, ks, vs, low, high)

    got = to_far(send_far(rows_dot(heads_far, w_out).astype(jnp.bfloat16)))
    mid_h = x_f + sum_near(rows_dot(heads_near, w_out).astype(jnp.bfloat16), got)
    inv_b = lax.rsqrt(jnp.mean(mid_h * mid_h, axis=-1, keepdims=True) + epsilon)
    b0 = (mid_h * inv_b * gain_mlp).astype(jnp.bfloat16)
    b2 = to_far(b0)
    b1 = to_mate(b0)
    b3 = to_mate(b2)
    mid_near, dg_near, du_near = mlp_pair(b0, b1, c0, c1, w_gate, w_up, w_down)
    mid_far, dg_far, du_far = mlp_pair(b2, b3, c2, c3, w_gate, w_up, w_down)

    grad_down = WeightGrad((c0, c1, c2, c3), (mid_near, mid_far))
    grad_gate = WeightGrad((b0, b1, b2, b3), (dg_near, dg_far))
    grad_up = WeightGrad((b0, b1, b2, b3), (du_near, du_far))
    send_down = grad_down.send()
    dg_far, du_far, send_down = lax.optimization_barrier((dg_far, du_far, send_down))
    x_down = exchange(send_down, "dp", 1)
    far_b = (rows_dot_t(dg_far, w_gate) + rows_dot_t(du_far, w_up)).astype(jnp.bfloat16)
    near_b = (rows_dot_t(dg_near, w_gate) + rows_dot_t(du_near, w_up)).astype(jnp.bfloat16)
    got = to_far(send_far(far_b))
    d_b = sum_near(near_b, got)
    send_gate = grad_gate.send()
    send_up = grad_up.send()
    d_b, send_gate, send_up = lax.optimization_barrier((d_b, send_gate, send_up))
    n_b = mid_h * inv_b
    gain_mlp_part = jnp.sum(d_b * n_b, axis=0)
    e_b = d_b * gain_mlp
    weighted = cotangent.astype(jnp.float32) * weight_local[:, None]
    d_h = weighted + inv_b * (e_b - n_b * jnp.mean(e_b * n_b, axis=-1, keepdims=True))
    t0 = d_h.astype(jnp.bfloat16)
    t2 = to_far(t0)
    t1 = to_mate(t0)
    t3 = to_mate(t2)
    gs_near = rows_dot_t(jnp.concatenate([t0, t1], axis=0), w_out).astype(jnp.bfloat16)
    out_far = rows_dot(mid_far, w_down).astype(jnp.bfloat16)
    out_near = rows_dot(mid_near, w_down).astype(jnp.bfloat16)
    gs_far = rows_dot_t(jnp.concatenate([t2, t3], axis=0), w_out).astype(jnp.bfloat16)
    gs_near, gs_far, x_down = lax.optimization_barrier((gs_near, gs_far, x_down))
    x_gate = exchange(after(send_gate, x_down), "dp", 1)
    got = to_far(send_far(after(out_far, t2)))
    output = (mid_h + sum_near(out_near, got)).astype(jnp.bfloat16)
    sum_down = grad_down.finish(x_down)

    dqn, dqf, dkn, dkf, dvn, dvf = attend_back(
        rank_ref, qs, ks, vs, (gs_near, gs_far), low, high, lse, cosine, back_sine
    )
    grad_out = WeightGrad((t0, t1, t2, t3), (heads_near, heads_far))
    grad_qkv = [
        WeightGrad((a0, a1, a2, a3), pair) for pair in ((dqn, dqf), (dkn, dkf), (dvn, dvf))
    ]
    send_out = grad_out.send()
    send_qkv = [grad.send() for grad in grad_qkv]

    def to_input(q_part, k_part, v_part):
        total = rows_dot_t(q_part, w_query)
        total = total + rows_dot_t(k_part, w_key)
        return (total + rows_dot_t(v_part, w_value)).astype(jnp.bfloat16)

    got = to_far(send_far(to_input(dqf, dkf, dvf)))
    d_a = sum_near(to_input(dqn, dkn, dvn), got)
    n_a = x_f * inv_a
    gain_attn_part = jnp.sum(d_a * n_a, axis=0)
    e_a = d_a * gain_attn
    grad_input = d_h + inv_a * (e_a - n_a * jnp.mean(e_a * n_a, axis=-1, keepdims=True))
    gains = jnp.stack([gain_attn_part, gain_mlp_part])
    gains = butterfly_sum(scatter_small(gains.reshape(2, lax.axis_size("dp"), -1), "dp"), "tensor")

    x_up = exchange(after(send_up, x_gate), "dp", 1)
    sum_gate = grad_gate.finish(x_gate)
    x_out = exchange(after(send_out, x_up), "dp", 1)
    sum_up = grad_up.finish(x_up)
    last = x_out
    sum_out = grad_out.finish(x_out)
    sums = []
    for grad, send in zip(grad_qkv, send_qkv):
        last = exchange(after(send, last), "dp", 1)
        sums.append(grad.finish(last))
    return (
        output,
        grad_input,
        gains[0],
        sums[0],
        sums[1],
        sums[2],
        sum_out.T,
        gains[1],
        sum_gate,
        sum_up,
        sum_down.T,
    )


def solution(mesh):
    rows, columns, split = P(("dp", "tensor"), None), P(None, "tensor"), P("tensor", None)
    in_specs = (
        rows,
        rows,
        P(),
        columns,
        columns,
        columns,
        split,
        P(),
        columns,
        columns,
        split,
        P("dp", None),
        P("dp", None),
        P("dp", None),
    )
    grads = P("dp", "tensor")
    grads_t = P("tensor", "dp")
    out_specs = (rows, rows, P("dp"), grads, grads, grads, grads_t, P("dp"), grads, grads, grads_t)
    return jax.shard_map(shards, mesh=mesh, in_specs=in_specs, out_specs=out_specs, check_vma=False)
```

time: 1560 us -> 758 us (0.49)
  waiting for transfers between devices: 1030 us -> 337 us
  matrix products: 343 us -> 69.4 us
  Pallas kernels: 0 us -> 205 us
  blocking collectives: 67.1 us -> 0 us
  starting transfers between devices: 0.98 us -> 50.3 us
    reduce_scatter x11 -> x0, waiting for transfers between devices: 930 us -> none  [the longest x1 196 us: shards(): lax.psum_scatter(grad_gate, 'dp', scatter_dimension=0, tiled=True)]
    ppermute x0 -> x53, waiting for transfers between devices: none -> 337 us  [exchange(): lax.ppermute(values, axis, [(rank, rank ^ bit) for rank in range(size)])]
    dot_general x26 -> x12, matrix products: 283 us -> 49.6 us  [rows_dot_t(): return lax.dot_general(left, right, NT, preferred_element_type=jnp.float32)]
    pallas_call x0 -> x20, Pallas kernels: none -> 205 us  [the longest x14 113 us: grad_call(): pl.pallas_call(body, grid_spec=pltpu.PrefetchScalarGridSpec(num_scalar_pr...]
    all_gather x4 -> x0, waiting for transfers between devices: 96.4 us -> none  [the longest x1 37.6 us: shards(): gathered_a = lax.all_gather(normed_a, 'tensor', axis=0, tiled=True)]
    ppermute x0 -> x53, starting transfers between devices: none -> 50.3 us  [exchange(): lax.ppermute(values, axis, [(rank, rank ^ bit) for rank in range(size)])]
    dot_general x7 -> x4, matrix products: 60.7 us -> 19.8 us  [rows_dot(): return jnp.dot(left, right, preferred_element_type=jnp.float32)]
    unnamed x1 -> x0, blocking collectives: 39.1 us -> none
  transfers between devices with their start and end apart: 15 -> 53, of which waited for: 14 -> 25; matrix products, arithmetic and copies ran while one was open for 19% -> 16% of each run, Pallas kernels for 0% -> 20%
where the time goes in v2:
time: 758 us; the launch traced here: 752 us
  waiting for transfers between devices  337 us (44%)
  Pallas kernels  205 us (27%)
  matrix products  69.4 us (9%)
  other arithmetic  60.7 us (8%)
  starting transfers between devices  50.3 us (7%)
  local copies, waits for them, and re-layouts  28.4 us (4%)
    ppermute x53, waiting for transfers between devices, exchange(): lax.ppermute(values, axis, [(rank, rank ^ bit) for rank in range(size)])  337 us
    pallas_call x14, Pallas kernels, grad_call(): pl.pallas_call(body, grid_spec=pltpu.PrefetchScalarGridSpec(num_scalar_pr...  113 us
    ppermute x53, starting transfers between devices, exchange(): lax.ppermute(values, axis, [(rank, rank ^ bit) for rank in range(size)])  50.3 us
    dot_general x12, matrix products, rows_dot_t(): return lax.dot_general(left, right, NT, preferred_element_type=jnp.float32)  49.6 us
    pallas_call x2, Pallas kernels, mlp_pair(): pl.pallas_call(mlp_body, grid=(pl.cdiv(width, tile),), in_specs=[whole(xa...  37.2 us
    pallas_call x1, Pallas kernels, attend_back(): pl.pallas_call(attend_back_body, grid_spec=pltpu.PrefetchScalarGridSpec(n...  21.9 us
    dot_general x4, matrix products, rows_dot(): return jnp.dot(left, right, preferred_element_type=jnp.float32)  19.8 us
    pallas_call x2, Pallas kernels, qkv_pair(): pl.pallas_call(functools.partial(qkv_body, first), grid_spec=pltpu.Prefet...  18 us
  transfers between devices with their start and end apart: 53, of which 25 were waited for; matrix products, arithmetic and copies ran while one was open for 16% of the time, Pallas kernels for 20%

profile of v2, /device:TPU:0, one launch (start us, length us, event | category | flops | bytes accessed | tf_op | source)
XLA Modules:
  0.0 752.1 jit_solution(2018985572413916583)
XLA Ops:
  9.1 27.0 %collective-permute-done.1.xa_ref.refs_2_ = bf16[320,2048]{1,0:T(8,128)(2,1)} collective-permute-done((bf16[320,2048]{1,0:T(8,128)(2,1)S(1)}, bf16[320,2048]{1,0:T(8,128)(2,1)}, u32[]{:S(2)}, u32[]{:S(2)}) %collective-permute-start.1) | collective-permute-done | bytes 1310752 | tf_op jit(solution)/shard_map/ppermute | solution.py:367
  40.4 9.1 %qkv.2 = (bf16[640,512]{1,0:T(8,128)(2,1)}, bf16[640,512]{1,0:T(8,128)(2,1)}, bf16[640,512]{1,0:T(8,128)(2,1)}) custom-call(s32[1]{0:T(128)} %bitcast.rank_ref, bf16[320,2048]{1,0:T(8,128)(2,1)} %copy-done.5, bf16[320,2048]{1,0:T(8,128)(2,1)} %collective-permute-done.xb_ref.refs_1_, f32[1280,128]{1,0:T(8,128)} %get-tuple-element.137.cos_ref, ...), custom_call_target="tpu_custom_call" | custom-call | flops 4026531840 | bytes 8912896 | tf_op jit(solution)/shard_map/qkv/pallas_call | solution.py:58
  49.5 8.9 %qkv.3 = (bf16[640,512]{1,0:T(8,128)(2,1)}, bf16[640,512]{1,0:T(8,128)(2,1)}, bf16[640,512]{1,0:T(8,128)(2,1)}) custom-call(s32[1]{0:T(128)} %bitcast.rank_ref, bf16[320,2048]{1,0:T(8,128)(2,1)} %collective-permute-done.1.xa_ref.refs_2_, bf16[320,2048]{1,0:T(8,128)(2,1)} %collective-permute-done.2.xb_ref.refs_3_, f32[1280,128]{1,0:T(8,128)} %get-tuple-element.137.cos_ref, ...), custom_call_target="tpu_custom_call" | custom-call | flops 4026531840 | bytes 8912896 | tf_op jit(solution)/shard_map/qkv/pallas_call | solution.py:58
  58.4 14.6 %attend.1 = (bf16[640,512]{1,0:T(8,128)(2,1)}, bf16[640,512]{1,0:T(8,128)(2,1)}, f32[4,1,1280]{2,1,0:T(1,128)}) custom-call(s32[1]{0:T(128)} %bitcast.rank_ref, bf16[640,512]{1,0:T(8,128)(2,1)} %get-tuple-element.63.qn, bf16[640,512]{1,0:T(8,128)(2,1)} %get-tuple-element.64.qf, bf16[640,512]{1,0:T(8,128)(2,1)} %get-tuple-element.65.kn, ...), custom_call_target="tpu_custom_call" | custom-call | flops 6710886400 | bytes 5242880 | tf_op jit(solution)/shard_map/attend/pallas_call | solution.py:119
  99.5 14.0 %collective-permute-done.5 = bf16[320,2048]{1,0:T(8,128)(2,1)} collective-permute-done((bf16[320,2048]{1,0:T(8,128)(2,1)}, bf16[320,2048]{1,0:T(8,128)(2,1)}, u32[]{:S(2)}, u32[]{:S(2)}) %collective-permute-start.5) | collective-permute-done | bytes 1310752 | tf_op jit(solution)/shard_map/ppermute | solution.py:367
  120.2 21.4 %collective-permute-done.14.ca_ref.refs_2_ = bf16[320,2048]{1,0:T(8,128)(2,1)} collective-permute-done((bf16[320,2048]{1,0:T(8,128)(2,1)}, bf16[320,2048]{1,0:T(8,128)(2,1)}, u32[]{:S(2)}, u32[]{:S(2)}) %collective-permute-start.14) | collective-permute-done | bytes 1310752 | tf_op jit(solution)/shard_map/ppermute | solution.py:367
  141.6 27.1 %collective-permute-done.12.xa_ref.refs_2_ = bf16[320,2048]{1,0:T(8,128)(2,1)} collective-permute-done((bf16[320,2048]{1,0:T(8,128)(2,1)S(1)}, bf16[320,2048]{1,0:T(8,128)(2,1)}, u32[]{:S(2)}, u32[]{:S(2)}) %collective-permute-start.12) | collective-permute-done | bytes 1310752 | tf_op jit(solution)/shard_map/ppermute | solution.py:367
  169.2 18.7 %mlp.2 = (bf16[640,1408]{1,0:T(8,128)(2,1)}, bf16[640,1408]{1,0:T(8,128)(2,1)}, bf16[640,1408]{1,0:T(8,128)(2,1)}) custom-call(bf16[320,2048]{1,0:T(8,128)(2,1)} %copy-done.38, bf16[320,2048]{1,0:T(8,128)(2,1)} %collective-permute-done.6.xb_ref.refs_1_, bf16[320,2048]{1,0:T(8,128)(2,1)} %fusion.19.ca_ref.refs_0_, ...), custom_call_target="tpu_custom_call" | custom-call | flops 11072962560 | bytes 27951104 | tf_op jit(solution)/shard_map/mlp/pallas_call | solution.py:225
  188.0 18.5 %mlp.3 = (bf16[640,1408]{1,0:T(8,128)(2,1)}, bf16[640,1408]{1,0:T(8,128)(2,1)}, bf16[640,1408]{1,0:T(8,128)(2,1)}) custom-call(bf16[320,2048]{1,0:T(8,128)(2,1)} %collective-permute-done.12.xa_ref.refs_2_, bf16[320,2048]{1,0:T(8,128)(2,1)} %collective-permute-done.13.xb_ref.refs_3_, bf16[320,2048]{1,0:T(8,128)(2,1)} %collective-permute-done.14.ca_ref.refs_2_, ...), custom_call_target="tpu_custom_call" | custom-call | flops 11072962560 | bytes 27951104 | tf_op jit(solution)/shard_map/mlp/pallas_call | solution.py:225
  206.4 9.4 %weight_grad.14 = bf16[1024,1408]{1,0:T(8,128)(2,1)} custom-call(s32[4]{0:T(128)} %multiply_add_fusion.1._, bf16[320,2048]{1,0:T(8,128)(2,1)} %fusion.19.ca_ref.refs_0_, bf16[320,2048]{1,0:T(8,128)(2,1)} %collective-permute-done.10.cb_ref.refs_1_, bf16[320,2048]{1,0:T(8,128)(2,1)} %collective-permute-done.14.ca_ref.refs_2_, ...), custom_call_target="tpu_custom_call" | custom-call | flops 3690987520 | bytes 10551296 | tf_op jit(solution)/shard_map/weight_grad/pallas_call | solution.py:314
  215.9 9.9 %fusion.38 = f32[640,2048]{1,0:T(8,128)} fusion(bf16[640,1408]{1,0:T(8,128)(2,1)} %get-tuple-element.79.refs_5_, bf16[2048,1408]{1,0:T(8,128)(2,1)} %wu_ref.3), kind=kOutput, calls=%fused_computation.122 | convolution fusion | flops 3690987520 | bytes 12812288 | tf_op jit(solution)/shard_map/dot_general | solution.py:362
  225.7 8.2 %add_convert_fusion.2 = bf16[640,2048]{1,0:T(8,128)(2,1)S(1)} fusion(f32[640,2048]{1,0:T(8,128)} %fusion.38, bf16[640,1408]{1,0:T(8,128)(2,1)S(1)} %copy-done.55, bf16[2048,1408]{1,0:T(8,128)(2,1)} %wg_ref.3), kind=kOutput, calls=%fused_computation.2 | convolution fusion | flops 3693608960 | bytes 15433728 | tf_op jit(solution)/shard_map/dot_general | solution.py:362
  235.4 6.0 fusion.37
  241.4 7.2 add_convert_fusion.3
  252.7 9.4 %weight_grad.16 = bf16[1024,1408]{1,0:T(8,128)(2,1)} custom-call(s32[4]{0:T(128)} %multiply_add_fusion.1._, bf16[320,2048]{1,0:T(8,128)(2,1)} %copy-done.38, bf16[320,2048]{1,0:T(8,128)(2,1)} %collective-permute-done.6.xb_ref.refs_1_, bf16[320,2048]{1,0:T(8,128)(2,1)} %collective-permute-done.12.xa_ref.refs_2_, ...), custom_call_target="tpu_custom_call" | custom-call | flops 3690987520 | bytes 10551296 | tf_op jit(solution)/shard_map/weight_grad/pallas_call | solution.py:314
  262.1 9.4 %weight_grad.15 = bf16[1024,1408]{1,0:T(8,128)(2,1)} custom-call(s32[4]{0:T(128)} %multiply_add_fusion.1._, bf16[320,2048]{1,0:T(8,128)(2,1)} %copy-done.38, bf16[320,2048]{1,0:T(8,128)(2,1)} %collective-permute-done.6.xb_ref.refs_1_, bf16[320,2048]{1,0:T(8,128)(2,1)} %collective-permute-done.12.xa_ref.refs_2_, ...), custom_call_target="tpu_custom_call" | custom-call | flops 3690987520 | bytes 10551296 | tf_op jit(solution)/shard_map/weight_grad/pallas_call | solution.py:314
  271.6 10.5 %collective-permute-done.18 = bf16[320,2048]{1,0:T(8,128)(2,1)} collective-permute-done((bf16[320,2048]{1,0:T(8,128)(2,1)}, bf16[320,2048]{1,0:T(8,128)(2,1)}, u32[]{:S(2)}, u32[]{:S(2)}) %collective-permute-start.18) | collective-permute-done | bytes 1310752 | tf_op jit(solution)/shard_map/ppermute | solution.py:367
  292.4 7.4 convolution_convert_fusion.1
  301.5 17.1 %collective-permute-done.19.refs_2_ = bf16[320,2048]{1,0:T(8,128)(2,1)} collective-permute-done((bf16[320,2048]{1,0:T(8,128)(2,1)S(1)}, bf16[320,2048]{1,0:T(8,128)(2,1)}, u32[]{:S(2)}, u32[]{:S(2)}) %collective-permute-start.19) | collective-permute-done | bytes 1310752 | tf_op jit(solution)/shard_map/ppermute | solution.py:367
  318.6 8.3 %convolution_convert_fusion = bf16[640,2048]{1,0:T(8,128)(2,1)} fusion(bf16[640,1408]{1,0:T(8,128)(2,1)S(1)} %copy-done.56, bf16[1408,2048]{1,0:T(8,128)(2,1)} %wd_ref.3), kind=kOutput, calls=%fused_computation.11 | convolution fusion | flops 3692298240 | bytes 10190848 | tf_op jit(solution)/shard_map/dot_general | solution.py:358
  329.9 3.7 fusion.23.gn
  333.6 4.1 fusion.20.gf
  337.7 16.2 %collective-permute-done.24.refs_6_ = bf16[1024,1408]{1,0:T(8,128)(2,1)} collective-permute-done((bf16[1024,1408]{1,0:T(8,128)(2,1)}, bf16[1024,1408]{1,0:T(8,128)(2,1)}, u32[]{:S(2)}, u32[]{:S(2)}) %collective-permute-start.24) | collective-permute-done | bytes 2883616 | tf_op jit(solution)/shard_map/ppermute | solution.py:367
  354.0 10.8 %weight_grad.27 = (bf16[512,1408]{1,0:T(8,128)(2,1)}, f32[512,1408]{1,0:T(8,128)}) custom-call(s32[4]{0:T(128)} %fusion.29._, bf16[320,2048]{1,0:T(8,128)(2,1)} %fusion.19.ca_ref.refs_0_, bf16[320,2048]{1,0:T(8,128)(2,1)} %collective-permute-done.10.cb_ref.refs_1_, bf16[320,2048]{1,0:T(8,128)(2,1)} %collective-permute-done.14.ca_ref.refs_2_, ...), custom_call_target="tpu_custom_call" | custom-call | flops 3690987520 | bytes 10551296 | tf_op jit(solution)/shard_map/weight_grad/pallas_call | solution.py:314
  370.4 21.9 %attend_back.1 = (bf16[640,512]{1,0:T(8,128)(2,1)}, bf16[640,512]{1,0:T(8,128)(2,1)}, bf16[640,512]{1,0:T(8,128)(2,1)}, bf16[640,512]{1,0:T(8,128)(2,1)}, bf16[6...) custom-call(s32[1]{0:T(128)} %bitcast.rank_ref, bf16[640,512]{1,0:T(8,128)(2,1)} %get-tuple-element.63.qn, ...), custom_call_target="tpu_custom_call" | custom-call | flops 16777216000 | bytes 10485760 | tf_op jit(solution)/shard_map/attend_back/pallas_call | solution.py:182
  404.8 6.3 weight_grad.18
  411.1 6.1 weight_grad.22
  417.2 6.1 weight_grad.20
  427.8 6.5 weight_grad.17
  446.1 22.2 %collective-permute-done.27 = bf16[320,2048]{1,0:T(8,128)(2,1)S(1)} collective-permute-done((bf16[320,2048]{1,0:T(8,128)(2,1)S(1)}, bf16[320,2048]{1,0:T(8,128)(2,1)S(1)}, u32[]{:S(2)}, u32[]{:S(2)}) %collective-permute-start.27) | collective-permute-done | bytes 1310752 | tf_op jit(solution)/shard_map/ppermute | solution.py:367
  471.8 24.1 %collective-permute-done.21 = bf16[320,2048]{1,0:T(8,128)(2,1)} collective-permute-done((bf16[320,2048]{1,0:T(8,128)(2,1)}, bf16[320,2048]{1,0:T(8,128)(2,1)}, u32[]{:S(2)}, u32[]{:S(2)}) %collective-permute-start.21) | collective-permute-done | bytes 1310752 | tf_op jit(solution)/shard_map/ppermute | solution.py:367
  496.0 4.0 add_convert_fusion.5
  500.0 33.6 %collective-permute-done.28 = f32[2,4,256]{2,1,0:T(4,128)S(1)} collective-permute-done((f32[2,4,256]{2,1,0:T(4,128)S(1)}, f32[2,4,256]{2,1,0:T(4,128)S(1)}, u32[]{:S(2)}, u32[]{:S(2)}) %collective-permute-start.28) | collective-permute-done | bytes 8224 | tf_op jit(solution)/shard_map/ppermute | solution.py:367
  542.0 10.8 %weight_grad.25 = (bf16[512,1408]{1,0:T(8,128)(2,1)}, f32[512,1408]{1,0:T(8,128)}) custom-call(s32[4]{0:T(128)} %fusion.29._, bf16[320,2048]{1,0:T(8,128)(2,1)} %copy-done.38, bf16[320,2048]{1,0:T(8,128)(2,1)} %collective-permute-done.6.xb_ref.refs_1_, bf16[320,2048]{1,0:T(8,128)(2,1)} %collective-permute-done.12.xa_ref.refs_2_, ...), custom_call_target="tpu_custom_call" | custom-call | flops 3690987520 | bytes 10551296 | tf_op jit(solution)/shard_map/weight_grad/pallas_call | solution.py:314
  554.6 10.9 %weight_grad.26 = (bf16[512,1408]{1,0:T(8,128)(2,1)}, f32[512,1408]{1,0:T(8,128)}) custom-call(s32[4]{0:T(128)} %fusion.29._, bf16[320,2048]{1,0:T(8,128)(2,1)} %copy-done.38, bf16[320,2048]{1,0:T(8,128)(2,1)} %collective-permute-done.6.xb_ref.refs_1_, bf16[320,2048]{1,0:T(8,128)(2,1)} %collective-permute-done.12.xa_ref.refs_2_, ...), custom_call_target="tpu_custom_call" | custom-call | flops 3690987520 | bytes 10551296 | tf_op jit(solution)/shard_map/weight_grad/pallas_call | solution.py:314
  566.3 5.5 fusion.8
  573.0 14.5 %collective-permute-done.47 = bf16[2,256,1408]{2,1,0:T(8,128)(2,1)} collective-permute-done((bf16[2,256,1408]{2,1,0:T(8,128)(2,1)}, bf16[2,256,1408]{2,1,0:T(8,128)(2,1)}, u32[]{:S(2)}, u32[]{:S(2)}) %collective-permute-start.47) | collective-permute-done | bytes 1441824 | tf_op jit(solution)/shard_map/ppermute | solution.py:367
  592.7 4.0 collective-permute-done.35.refs_6_
  598.2 7.0 weight_grad.24
  611.0 22.9 %collective-permute-done.49 = bf16[2,256,1408]{2,1,0:T(8,128)(2,1)} collective-permute-done((bf16[2,256,1408]{2,1,0:T(8,128)(2,1)}, bf16[2,256,1408]{2,1,0:T(8,128)(2,1)}, u32[]{:S(2)}, u32[]{:S(2)}) %collective-permute-start.49) | collective-permute-done | bytes 1441824 | tf_op jit(solution)/shard_map/ppermute | solution.py:367
  639.4 11.2 %collective-permute-done.45 = bf16[2,256,512]{1,2,0:T(8,128)(2,1)S(1)} collective-permute-done((bf16[2,256,512]{1,2,0:T(8,128)(2,1)}, bf16[2,256,512]{1,2,0:T(8,128)(2,1)S(1)}, u32[]{:S(2)}, u32[]{:S(2)}) %collective-permute-start.45) | collective-permute-done | bytes 524320 | tf_op jit(solution)/shard_map/ppermute | solution.py:367
  653.2 29.4 %collective-permute-done.46 = bf16[1,256,512]{1,2,0:T(8,128)(2,1)S(1)} collective-permute-done((bf16[1,256,512]{1,2,0:T(8,128)(2,1)S(1)}, bf16[1,256,512]{1,2,0:T(8,128)(2,1)S(1)}, u32[]{:S(2)}, u32[]{:S(2)}) %collective-permute-start.46) | collective-permute-done | bytes 262176 | tf_op jit(solution)/shard_map/ppermute | solution.py:367
  685.0 6.7 weight_grad.19
  694.5 6.9 weight_grad.21
  708.2 6.7 weight_grad.23
  715.4 3.6 collective-permute-start.38
  719.3 18.4 %collective-permute-done.43 = bf16[2,256,512]{2,1,0:T(8,128)(2,1)S(1)} collective-permute-done((bf16[2,256,512]{2,1,0:T(8,128)(2,1)}, bf16[2,256,512]{2,1,0:T(8,128)(2,1)S(1)}, u32[]{:S(2)}, u32[]{:S(2)}) %collective-permute-start.43) | collective-permute-done | bytes 524320 | tf_op jit(solution)/shard_map/ppermute | solution.py:367
  740.3 10.5 %collective-permute-done.44 = bf16[1,256,512]{2,1,0:T(8,128)(2,1)S(1)} collective-permute-done((bf16[1,256,512]{2,1,0:T(8,128)(2,1)S(1)}, bf16[1,256,512]{2,1,0:T(8,128)(2,1)S(1)}, u32[]{:S(2)}, u32[]{:S(2)}) %collective-permute-start.44) | collective-permute-done | bytes 262176 | tf_op jit(solution)/shard_map/ppermute | solution.py:367
  (312 shorter events, 153.2 us)
Async XLA Ops:
  4.2 31.9 %collective-permute-start.1 = (bf16[320,2048]{1,0:T(8,128)(2,1)S(1)}, bf16[320,2048]{1,0:T(8,128)(2,1)}, u32[]{:S(2)}, u32[]{:S(2)}) collective-permute-start(bf16[320,2048]{1,0:T(8,128)(2,1)S(1)} %fusion.4.xa_ref.refs_0_), channel_id=1, source_target_pairs={{0,2},{1,3},{2,0},{3,1},{4,6},{5,7},{6,4},{7,5},{8,10},{9,11},{10,... | collective-permute-start | bytes 3932168 | tf_op jit(solution)/shard_map/ppermute | solution.py:367
  7.3 33.1 %collective-permute-start = (bf16[320,2048]{1,0:T(8,128)(2,1)S(1)}, bf16[320,2048]{1,0:T(8,128)(2,1)}, u32[]{:S(2)}, u32[]{:S(2)}) collective-permute-start(bf16[320,2048]{1,0:T(8,128)(2,1)S(1)} %fusion.4.xa_ref.refs_0_), channel_id=1, source_target_pairs={{0,1},{1,0},{2,3},{3,2},{4,5},{5,4},{6,7},{7,6},{8,9},{9,8},{10,11... | collective-permute-start | bytes 3932168 | tf_op jit(solution)/shard_map/ppermute | solution.py:367
  36.2 13.3 %collective-permute-start.2 = (bf16[320,2048]{1,0:T(8,128)(2,1)}, bf16[320,2048]{1,0:T(8,128)(2,1)}, u32[]{:S(2)}, u32[]{:S(2)}) collective-permute-start(bf16[320,2048]{1,0:T(8,128)(2,1)} %collective-permute-done.1.xa_ref.refs_2_), channel_id=1, source_target_pairs={{0,1},{1,0},{2,3},{3,2},{4,5},{5,4},{6,7},{7,6},{8,9},{9,8},{10,11... | collective-permute-start | bytes 3932168 | tf_op jit(solution)/shard_map/ppermute | solution.py:367
  79.5 20.0 %collective-permute-start.3 = (bf16[320,2048]{1,0:T(8,128)(2,1)}, bf16[320,2048]{1,0:T(8,128)(2,1)}, u32[]{:S(2)}, u32[]{:S(2)}) collective-permute-start(bf16[320,2048]{1,0:T(8,128)(2,1)} %slice.77), channel_id=1, source_target_pairs={{0,1},{1,0},{2,3},{3,2},{4,5},{5,4},{6,7},{7,6},{8,9},{9,8},{10,11... | collective-permute-start | bytes 3932168 | tf_op jit(solution)/shard_map/ppermute | solution.py:367
  81.5 32.0 %collective-permute-start.5 = (bf16[320,2048]{1,0:T(8,128)(2,1)}, bf16[320,2048]{1,0:T(8,128)(2,1)}, u32[]{:S(2)}, u32[]{:S(2)}) collective-permute-start(bf16[320,2048]{1,0:T(8,128)(2,1)} %add_convert_fusion.8), channel_id=1, source_target_pairs={{0,2},{1,3},{2,0},{3,1},{4,6},{5,7},{6,4},{7,5},{8,10},{9,11},{10,... | collective-permute-start | bytes 3932168 | tf_op jit(solution)/shard_map/ppermute | solution.py:367
  99.2 42.4 %collective-permute-start.14 = (bf16[320,2048]{1,0:T(8,128)(2,1)}, bf16[320,2048]{1,0:T(8,128)(2,1)}, u32[]{:S(2)}, u32[]{:S(2)}) collective-permute-start(bf16[320,2048]{1,0:T(8,128)(2,1)} %fusion.19.ca_ref.refs_0_), channel_id=1, source_target_pairs={{0,2},{1,3},{2,0},{3,1},{4,6},{5,7},{6,4},{7,5},{8,10},{9,11},{10,... | collective-permute-start | bytes 3932168 | tf_op jit(solution)/shard_map/ppermute | solution.py:367
  117.9 50.9 %collective-permute-start.12 = (bf16[320,2048]{1,0:T(8,128)(2,1)S(1)}, bf16[320,2048]{1,0:T(8,128)(2,1)}, u32[]{:S(2)}, u32[]{:S(2)}) collective-permute-start(bf16[320,2048]{1,0:T(8,128)(2,1)S(1)} %multiply_convert_fusion.xa_ref.refs_0_), channel_id=1, source_target_pairs={{0,2},{1,3},{2,0},{3,1},{4,6},{5,7},{6,4},{7,5},{8,10},{9,11},{10,... | collective-permute-start | bytes 3932168 | tf_op jit(solution)/shard_map/ppermute | solution.py:367
  119.7 49.6 %collective-permute-start.10 = (bf16[320,2048]{1,0:T(8,128)(2,1)}, bf16[320,2048]{1,0:T(8,128)(2,1)}, u32[]{:S(2)}, u32[]{:S(2)}) collective-permute-start(bf16[320,2048]{1,0:T(8,128)(2,1)} %fusion.19.ca_ref.refs_0_), channel_id=1, source_target_pairs={{0,1},{1,0},{2,3},{3,2},{4,5},{5,4},{6,7},{7,6},{8,9},{9,8},{10,11... | collective-permute-start | bytes 3932168 | tf_op jit(solution)/shard_map/ppermute | solution.py:367
  119.7 49.6 %collective-permute-start.6 = (bf16[320,2048]{1,0:T(8,128)(2,1)S(1)}, bf16[320,2048]{1,0:T(8,128)(2,1)}, u32[]{:S(2)}, u32[]{:S(2)}) collective-permute-start(bf16[320,2048]{1,0:T(8,128)(2,1)S(1)} %multiply_convert_fusion.xa_ref.refs_0_), channel_id=1, source_target_pairs={{0,1},{1,0},{2,3},{3,2},{4,5},{5,4},{6,7},{7,6},{8,9},{9,8},{10,11... | collective-permute-start | bytes 3932168 | tf_op jit(solution)/shard_map/ppermute | solution.py:367
  141.6 46.4 %collective-permute-start.15 = (bf16[320,2048]{1,0:T(8,128)(2,1)}, bf16[320,2048]{1,0:T(8,128)(2,1)}, u32[]{:S(2)}, u32[]{:S(2)}) collective-permute-start(bf16[320,2048]{1,0:T(8,128)(2,1)} %collective-permute-done.14.ca_ref.refs_2_), channel_id=1, source_target_pairs={{0,1},{1,0},{2,3},{3,2},{4,5},{5,4},{6,7},{7,6},{8,9},{9,8},{10,11... | collective-permute-start | bytes 3932168 | tf_op jit(solution)/shard_map/ppermute | solution.py:367
  168.7 19.2 %collective-permute-start.13 = (bf16[320,2048]{1,0:T(8,128)(2,1)}, bf16[320,2048]{1,0:T(8,128)(2,1)}, u32[]{:S(2)}, u32[]{:S(2)}) collective-permute-start(bf16[320,2048]{1,0:T(8,128)(2,1)} %collective-permute-done.12.xa_ref.refs_2_), channel_id=1, source_target_pairs={{0,1},{1,0},{2,3},{3,2},{4,5},{5,4},{6,7},{7,6},{8,9},{9,8},{10,11... | collective-permute-start | bytes 3932168 | tf_op jit(solution)/shard_map/ppermute | solution.py:367
  234.1 15.3 %collective-permute-start.17 = (bf16[320,2048]{1,0:T(8,128)(2,1)S(1)}, bf16[320,2048]{1,0:T(8,128)(2,1)S(1)}, u32[]{:S(2)}, u32[]{:S(2)}) collective-permute-start(bf16[320,2048]{1,0:T(8,128)(2,1)S(1)} %slice.85), channel_id=1, source_target_pairs={{0,1},{1,0},{2,3},{3,2},{4,5},{5,4},{6,7},{7,6},{8,9},{9,8},{10,11... | collective-permute-start | bytes 3932168 | tf_op jit(solution)/shard_map/ppermute | solution.py:367
  248.7 22.8 %collective-permute-start.16 = (bf16[320,2048]{1,0:T(8,128)(2,1)S(1)}, bf16[320,2048]{1,0:T(8,128)(2,1)}, u32[]{:S(2)}, u32[]{:S(2)}) collective-permute-start(bf16[320,2048]{1,0:T(8,128)(2,1)S(1)} %slice.83), channel_id=1, source_target_pairs={{0,1},{1,0},{2,3},{3,2},{4,5},{5,4},{6,7},{7,6},{8,9},{9,8},{10,11... | collective-permute-start | bytes 3932168 | tf_op jit(solution)/shard_map/ppermute | solution.py:367
  251.0 31.1 %collective-permute-start.18 = (bf16[320,2048]{1,0:T(8,128)(2,1)}, bf16[320,2048]{1,0:T(8,128)(2,1)}, u32[]{:S(2)}, u32[]{:S(2)}) collective-permute-start(bf16[320,2048]{1,0:T(8,128)(2,1)} %add_convert_fusion.7), channel_id=1, source_target_pairs={{0,2},{1,3},{2,0},{3,1},{4,6},{5,7},{6,4},{7,5},{8,10},{9,11},{10,... | collective-permute-start | bytes 3932168 | tf_op jit(solution)/shard_map/ppermute | solution.py:367
  288.6 30.0 %collective-permute-start.19 = (bf16[320,2048]{1,0:T(8,128)(2,1)S(1)}, bf16[320,2048]{1,0:T(8,128)(2,1)}, u32[]{:S(2)}, u32[]{:S(2)}) collective-permute-start(bf16[320,2048]{1,0:T(8,128)(2,1)S(1)} %get-tuple-element.122.refs_0_), channel_id=1, source_target_pairs={{0,2},{1,3},{2,0},{3,1},{4,6},{5,7},{6,4},{7,5},{8,10},{9,11},{10,... | collective-permute-start | bytes 3932168 | tf_op jit(solution)/shard_map/ppermute | solution.py:367
  290.3 63.7 %collective-permute-start.24 = (bf16[1024,1408]{1,0:T(8,128)(2,1)}, bf16[1024,1408]{1,0:T(8,128)(2,1)}, u32[]{:S(2)}, u32[]{:S(2)}) collective-permute-start(bf16[1024,1408]{1,0:T(8,128)(2,1)} %weight_grad.14), channel_id=1, source_target_pairs={{0,4},{4,0},{8,12},{12,8},{16,20},{20,16},{24,28},{28,24},{1,5},{5... | collective-permute-start | bytes 8650760 | tf_op jit(solution)/shard_map/ppermute | solution.py:367
  292.4 37.5 %collective-permute-start.22 = (bf16[320,2048]{1,0:T(8,128)(2,1)S(1)}, bf16[320,2048]{1,0:T(8,128)(2,1)}, u32[]{:S(2)}, u32[]{:S(2)}) collective-permute-start(bf16[320,2048]{1,0:T(8,128)(2,1)S(1)} %get-tuple-element.122.refs_0_), channel_id=1, source_target_pairs={{0,1},{1,0},{2,3},{3,2},{4,5},{5,4},{6,7},{7,6},{8,9},{9,8},{10,11... | collective-permute-start | bytes 3932168 | tf_op jit(solution)/shard_map/ppermute | solution.py:367
  301.0 170.8 %collective-permute-start.11 = (bf16[320,2048]{1,0:T(8,128)(2,1)}, bf16[320,2048]{1,0:T(8,128)(2,1)}, u32[]{:S(2)}, u32[]{:S(2)}) collective-permute-start(bf16[320,2048]{1,0:T(8,128)(2,1)} %slice.81), channel_id=1, source_target_pairs={{0,1},{1,0},{2,3},{3,2},{4,5},{5,4},{6,7},{7,6},{8,9},{9,8},{10,11... | collective-permute-start | bytes 3932168 | tf_op jit(solution)/shard_map/ppermute | solution.py:367
  318.6 15.0 %collective-permute-start.23 = (bf16[320,2048]{1,0:T(8,128)(2,1)}, bf16[320,2048]{1,0:T(8,128)(2,1)}, u32[]{:S(2)}, u32[]{:S(2)}) collective-permute-start(bf16[320,2048]{1,0:T(8,128)(2,1)} %collective-permute-done.19.refs_2_), channel_id=1, source_target_pairs={{0,1},{1,0},{2,3},{3,2},{4,5},{5,4},{6,7},{7,6},{8,9},{9,8},{10,11... | collective-permute-start | bytes 3932168 | tf_op jit(solution)/shard_map/ppermute | solution.py:367
  329.4 107.2 %collective-permute-start.20 = (bf16[320,2048]{1,0:T(8,128)(2,1)}, bf16[320,2048]{1,0:T(8,128)(2,1)}, u32[]{:S(2)}, u32[]{:S(2)}) collective-permute-start(bf16[320,2048]{1,0:T(8,128)(2,1)} %slice.69), channel_id=1, source_target_pairs={{0,1},{1,0},{2,3},{3,2},{4,5},{5,4},{6,7},{7,6},{8,9},{9,8},{10,11... | collective-permute-start | bytes 3932168 | tf_op jit(solution)/shard_map/ppermute | solution.py:367
  367.3 73.0 %collective-permute-start.51 = (bf16[2,256,1408]{1,2,0:T(8,128)(2,1)}, bf16[2,256,1408]{1,2,0:T(8,128)(2,1)}, u32[]{:S(2)}, u32[]{:S(2)}) collective-permute-start(bf16[2,256,1408]{1,2,0:T(8,128)(2,1)} %copy.31), channel_id=1, source_target_pairs={{0,8},{4,12},{8,0},{12,4},{16,24},{20,28},{24,16},{28,20},{1,9},{5... | collective-permute-start | bytes 4325384 | tf_op jit(solution)/shard_map/ppermute | solution.py:367
  368.9 100.7 %collective-permute-start.33 = (bf16[1024,1408]{1,0:T(8,128)(2,1)}, bf16[1024,1408]{1,0:T(8,128)(2,1)}, u32[]{:S(2)}, u32[]{:S(2)}) collective-permute-start(bf16[1024,1408]{1,0:T(8,128)(2,1)} %weight_grad.15), channel_id=1, source_target_pairs={{0,4},{4,0},{8,12},{12,8},{16,20},{20,16},{24,28},{28,24},{1,5},{5... | collective-permute-start | bytes 8650760 | tf_op jit(solution)/shard_map/ppermute | solution.py:367
  401.3 33.0 %collective-permute-start.26 = (bf16[320,2048]{1,0:T(8,128)(2,1)}, bf16[320,2048]{1,0:T(8,128)(2,1)}, u32[]{:S(2)}, u32[]{:S(2)}) collective-permute-start(bf16[320,2048]{1,0:T(8,128)(2,1)} %slice.89), channel_id=1, source_target_pairs={{0,1},{1,0},{2,3},{3,2},{4,5},{5,4},{6,7},{7,6},{8,9},{9,8},{10,11... | collective-permute-start | bytes 3932168 | tf_op jit(solution)/shard_map/ppermute | solution.py:367
  434.3 9.1 %collective-permute-start.25 = (bf16[320,2048]{1,0:T(8,128)(2,1)}, bf16[320,2048]{1,0:T(8,128)(2,1)S(1)}, u32[]{:S(2)}, u32[]{:S(2)}) collective-permute-start(bf16[320,2048]{1,0:T(8,128)(2,1)} %slice.87), channel_id=1, source_target_pairs={{0,1},{1,0},{2,3},{3,2},{4,5},{5,4},{6,7},{7,6},{8,9},{9,8},{10,11... | collective-permute-start | bytes 3932168 | tf_op jit(solution)/shard_map/ppermute | solution.py:367
  436.6 31.7 %collective-permute-start.27 = (bf16[320,2048]{1,0:T(8,128)(2,1)S(1)}, bf16[320,2048]{1,0:T(8,128)(2,1)S(1)}, u32[]{:S(2)}, u32[]{:S(2)}) collective-permute-start(bf16[320,2048]{1,0:T(8,128)(2,1)S(1)} %add_convert_fusion.4), channel_id=1, source_target_pairs={{0,2},{1,3},{2,0},{3,1},{4,6},{5,7},{6,4},{7,5},{8,10},{9,11},{10,... | collective-permute-start | bytes 3932168 | tf_op jit(solution)/shard_map/ppermute | solution.py:367
  440.3 55.6 %collective-permute-start.21 = (bf16[320,2048]{1,0:T(8,128)(2,1)}, bf16[320,2048]{1,0:T(8,128)(2,1)}, u32[]{:S(2)}, u32[]{:S(2)}) collective-permute-start(bf16[320,2048]{1,0:T(8,128)(2,1)} %add_convert_fusion.6), channel_id=1, source_target_pairs={{0,2},{1,3},{2,0},{3,1},{4,6},{5,7},{6,4},{7,5},{8,10},{9,11},{10,... | collective-permute-start | bytes 3932168 | tf_op jit(solution)/shard_map/ppermute | solution.py:367
  443.5 90.6 %collective-permute-start.52 = (bf16[1,256,1408]{1,2,0:T(8,128)(2,1)S(1)}, bf16[1,256,1408]{1,2,0:T(8,128)(2,1)}, u32[]{:S(2)}, u32[]{:S(2)}) collective-permute-start(bf16[1,256,1408]{1,2,0:T(8,128)(2,1)S(1)} %dynamic-slice_convert_fusion), channel_id=1, source_target_pairs={{0,16},{4,20},{8,24},{12,28},{16,0},{20,4},{24,8},{28,12},{1,17},{... | collective-permute-start | bytes 2162696 | tf_op jit(solution)/shard_map/ppermute | solution.py:367
  469.6 85.0 %collective-permute-start.34 = (bf16[1024,1408]{1,0:T(8,128)(2,1)}, bf16[1024,1408]{1,0:T(8,128)(2,1)}, u32[]{:S(2)}, u32[]{:S(2)}) collective-permute-start(bf16[1024,1408]{1,0:T(8,128)(2,1)} %weight_grad.16), channel_id=1, source_target_pairs={{0,4},{4,0},{8,12},{12,8},{16,20},{20,16},{24,28},{28,24},{1,5},{5... | collective-permute-start | bytes 8650760 | tf_op jit(solution)/shard_map/ppermute | solution.py:367
  470.3 63.4 %collective-permute-start.28 = (f32[2,4,256]{2,1,0:T(4,128)S(1)}, f32[2,4,256]{2,1,0:T(4,128)S(1)}, u32[]{:S(2)}, u32[]{:S(2)}) collective-permute-start(f32[2,4,256]{2,1,0:T(4,128)S(1)} %bitcast.101), channel_id=1, source_target_pairs={{0,4},{4,0},{8,12},{12,8},{16,20},{20,16},{24,28},{28,24},{1,5},{5... | collective-permute-start | bytes 24584 | tf_op jit(solution)/shard_map/ppermute | solution.py:367
  537.4 4.5 collective-permute-start.30
  541.9 12.1 %collective-permute-start.31 = (f32[2,256]{1,0:T(2,128)S(1)}, f32[2,256]{1,0:T(2,128)S(1)}, u32[]{:S(2)}, u32[]{:S(2)}) collective-permute-start(f32[2,256]{1,0:T(2,128)S(1)} %bitcast.103), channel_id=1, source_target_pairs={{0,1},{1,0},{2,3},{3,2},{4,5},{5,4},{6,7},{7,6},{8,9},{9,8},{10,11... | collective-permute-start | bytes 6152 | tf_op jit(solution)/shard_map/ppermute | solution.py:367
  552.8 34.8 %collective-permute-start.47 = (bf16[2,256,1408]{2,1,0:T(8,128)(2,1)}, bf16[2,256,1408]{2,1,0:T(8,128)(2,1)}, u32[]{:S(2)}, u32[]{:S(2)}) collective-permute-start(bf16[2,256,1408]{2,1,0:T(8,128)(2,1)} %bitcast.112), channel_id=1, source_target_pairs={{0,8},{4,12},{8,0},{12,4},{16,24},{20,28},{24,16},{28,20},{1,9},{5... | collective-permute-start | bytes 4325384 | tf_op jit(solution)/shard_map/ppermute | solution.py:367
  554.1 17.8 %collective-permute-start.32 = (f32[2,256]{1,0:T(2,128)S(1)}, f32[2,256]{1,0:T(2,128)S(1)}, u32[]{:S(2)}, u32[]{:S(2)}) collective-permute-start(f32[2,256]{1,0:T(2,128)S(1)} %fusion.34), channel_id=1, source_target_pairs={{0,2},{1,3},{2,0},{3,1},{4,6},{5,7},{6,4},{7,5},{8,10},{9,11},{10,... | collective-permute-start | bytes 6152 | tf_op jit(solution)/shard_map/ppermute | solution.py:367
  565.6 68.3 %collective-permute-start.49 = (bf16[2,256,1408]{2,1,0:T(8,128)(2,1)}, bf16[2,256,1408]{2,1,0:T(8,128)(2,1)}, u32[]{:S(2)}, u32[]{:S(2)}) collective-permute-start(bf16[2,256,1408]{2,1,0:T(8,128)(2,1)} %bitcast.111), channel_id=1, source_target_pairs={{0,8},{4,12},{8,0},{12,4},{16,24},{20,28},{24,16},{28,20},{1,9},{5... | collective-permute-start | bytes 4325384 | tf_op jit(solution)/shard_map/ppermute | solution.py:367
  571.8 24.8 %collective-permute-start.35 = (bf16[1024,512]{1,0:T(8,128)(2,1)S(1)}, bf16[1024,512]{1,0:T(8,128)(2,1)S(1)}, u32[]{:S(2)}, u32[]{:S(2)}) collective-permute-start(bf16[1024,512]{1,0:T(8,128)(2,1)S(1)} %copy-done.43), channel_id=1, source_target_pairs={{0,4},{4,0},{8,12},{12,8},{16,20},{20,16},{24,28},{28,24},{1,5},{5... | collective-permute-start | bytes 3145736 | tf_op jit(solution)/shard_map/ppermute | solution.py:367
  590.2 60.7 %collective-permute-start.48 = (bf16[1,256,1408]{2,1,0:T(8,128)(2,1)}, bf16[1,256,1408]{2,1,0:T(8,128)(2,1)}, u32[]{:S(2)}, u32[]{:S(2)}) collective-permute-start(bf16[1,256,1408]{2,1,0:T(8,128)(2,1)} %dynamic-slice_convert_fusion.2), channel_id=1, source_target_pairs={{0,16},{4,20},{8,24},{12,28},{16,0},{20,4},{24,8},{28,12},{1,17},{... | collective-permute-start | bytes 2162696 | tf_op jit(solution)/shard_map/ppermute | solution.py:367
  597.6 41.2 %collective-permute-start.36 = (bf16[1024,512]{1,0:T(8,128)(2,1)}, bf16[1024,512]{1,0:T(8,128)(2,1)}, u32[]{:S(2)}, u32[]{:S(2)}) collective-permute-start(bf16[1024,512]{1,0:T(8,128)(2,1)} %weight_grad.17), channel_id=1, source_target_pairs={{0,4},{4,0},{8,12},{12,8},{16,20},{20,16},{24,28},{28,24},{1,5},{5... | collective-permute-start | bytes 3145736 | tf_op jit(solution)/shard_map/ppermute | solution.py:367
  607.2 43.4 %collective-permute-start.45 = (bf16[2,256,512]{1,2,0:T(8,128)(2,1)}, bf16[2,256,512]{1,2,0:T(8,128)(2,1)S(1)}, u32[]{:S(2)}, u32[]{:S(2)}) collective-permute-start(bf16[2,256,512]{1,2,0:T(8,128)(2,1)} %copy.29), channel_id=1, source_target_pairs={{0,8},{4,12},{8,0},{12,4},{16,24},{20,28},{24,16},{28,20},{1,9},{5... | collective-permute-start | bytes 1572872 | tf_op jit(solution)/shard_map/ppermute | solution.py:367
  637.6 54.6 %collective-permute-start.50 = (bf16[1,256,1408]{2,1,0:T(8,128)(2,1)}, bf16[1,256,1408]{2,1,0:T(8,128)(2,1)}, u32[]{:S(2)}, u32[]{:S(2)}) collective-permute-start(bf16[1,256,1408]{2,1,0:T(8,128)(2,1)} %dynamic-slice_convert_fusion.1), channel_id=1, source_target_pairs={{0,16},{4,20},{8,24},{12,28},{16,0},{20,4},{24,8},{28,12},{1,17},{... | collective-permute-start | bytes 2162696 | tf_op jit(solution)/shard_map/ppermute | solution.py:367
  638.8 44.6 %collective-permute-start.39 = (bf16[1024,512]{1,0:T(8,128)(2,1)S(1)}, bf16[1024,512]{1,0:T(8,128)(2,1)S(1)}, u32[]{:S(2)}, u32[]{:S(2)}) collective-permute-start(bf16[1024,512]{1,0:T(8,128)(2,1)S(1)} %copy-done.42), channel_id=1, source_target_pairs={{0,4},{4,0},{8,12},{12,8},{16,20},{20,16},{24,28},{28,24},{1,5},{5... | collective-permute-start | bytes 3145736 | tf_op jit(solution)/shard_map/ppermute | solution.py:367
  650.8 31.8 %collective-permute-start.46 = (bf16[1,256,512]{1,2,0:T(8,128)(2,1)S(1)}, bf16[1,256,512]{1,2,0:T(8,128)(2,1)S(1)}, u32[]{:S(2)}, u32[]{:S(2)}) collective-permute-start(bf16[1,256,512]{1,2,0:T(8,128)(2,1)S(1)} %dynamic-slice_convert_fusion.3), channel_id=1, source_target_pairs={{0,16},{4,20},{8,24},{12,28},{16,0},{20,4},{24,8},{28,12},{1,17},{... | collective-permute-start | bytes 786440 | tf_op jit(solution)/shard_map/ppermute | solution.py:367
  684.5 23.7 %collective-permute-start.42 = (bf16[1024,512]{1,0:T(8,128)(2,1)}, bf16[1024,512]{1,0:T(8,128)(2,1)}, u32[]{:S(2)}, u32[]{:S(2)}) collective-permute-start(bf16[1024,512]{1,0:T(8,128)(2,1)} %weight_grad.22), channel_id=1, source_target_pairs={{0,4},{4,0},{8,12},{12,8},{16,20},{20,16},{24,28},{28,24},{1,5},{5... | collective-permute-start | bytes 3145736 | tf_op jit(solution)/shard_map/ppermute | solution.py:367
  691.8 14.1 %collective-permute-start.37 = (bf16[2,256,512]{2,1,0:T(8,128)(2,1)}, bf16[2,256,512]{2,1,0:T(8,128)(2,1)S(1)}, u32[]{:S(2)}, u32[]{:S(2)}) collective-permute-start(bf16[2,256,512]{2,1,0:T(8,128)(2,1)} %bitcast.115), channel_id=1, source_target_pairs={{0,8},{4,12},{8,0},{12,4},{16,24},{20,28},{24,16},{28,20},{1,9},{5... | collective-permute-start | bytes 1572872 | tf_op jit(solution)/shard_map/ppermute | solution.py:367
  701.3 17.6 %collective-permute-start.40 = (bf16[2,256,512]{2,1,0:T(8,128)(2,1)}, bf16[2,256,512]{2,1,0:T(8,128)(2,1)S(1)}, u32[]{:S(2)}, u32[]{:S(2)}) collective-permute-start(bf16[2,256,512]{2,1,0:T(8,128)(2,1)} %bitcast.113), channel_id=1, source_target_pairs={{0,8},{4,12},{8,0},{12,4},{16,24},{20,28},{24,16},{28,20},{1,9},{5... | collective-permute-start | bytes 1572872 | tf_op jit(solution)/shard_map/ppermute | solution.py:367
  715.0 22.7 %collective-permute-start.43 = (bf16[2,256,512]{2,1,0:T(8,128)(2,1)}, bf16[2,256,512]{2,1,0:T(8,128)(2,1)S(1)}, u32[]{:S(2)}, u32[]{:S(2)}) collective-permute-start(bf16[2,256,512]{2,1,0:T(8,128)(2,1)} %bitcast.114), channel_id=1, source_target_pairs={{0,8},{4,12},{8,0},{12,4},{16,24},{20,28},{24,16},{28,20},{1,9},{5... | collective-permute-start | bytes 1572872 | tf_op jit(solution)/shard_map/ppermute | solution.py:367
  715.4 22.6 %collective-permute-start.38 = (bf16[1,256,512]{2,1,0:T(8,128)(2,1)S(1)}, bf16[1,256,512]{2,1,0:T(8,128)(2,1)S(1)}, u32[]{:S(2)}, u32[]{:S(2)}) collective-permute-start(bf16[1,256,512]{2,1,0:T(8,128)(2,1)S(1)} %dynamic-slice_convert_fusion.6), channel_id=1, source_target_pairs={{0,16},{4,20},{8,24},{12,28},{16,0},{20,4},{24,8},{28,12},{1,17},{... | collective-permute-start | bytes 786440 | tf_op jit(solution)/shard_map/ppermute | solution.py:367
  719.2 20.2 %collective-permute-start.41 = (bf16[1,256,512]{2,1,0:T(8,128)(2,1)S(1)}, bf16[1,256,512]{2,1,0:T(8,128)(2,1)S(1)}, u32[]{:S(2)}, u32[]{:S(2)}) collective-permute-start(bf16[1,256,512]{2,1,0:T(8,128)(2,1)S(1)} %dynamic-slice_convert_fusion.5), channel_id=1, source_target_pairs={{0,16},{4,20},{8,24},{12,28},{16,0},{20,4},{24,8},{28,12},{1,17},{... | collective-permute-start | bytes 786440 | tf_op jit(solution)/shard_map/ppermute | solution.py:367
  737.9 12.8 %collective-permute-start.44 = (bf16[1,256,512]{2,1,0:T(8,128)(2,1)S(1)}, bf16[1,256,512]{2,1,0:T(8,128)(2,1)S(1)}, u32[]{:S(2)}, u32[]{:S(2)}) collective-permute-start(bf16[1,256,512]{2,1,0:T(8,128)(2,1)S(1)} %dynamic-slice_convert_fusion.4), channel_id=1, source_target_pairs={{0,16},{4,20},{8,24},{12,28},{16,0},{20,4},{24,8},{28,12},{1,17},{... | collective-permute-start | bytes 786440 | tf_op jit(solution)/shard_map/ppermute | solution.py:367
  (66 other events, 926.3 us)

commit v3 on v2

--- a/solution.py
+++ b/solution.py
@@ -16,6 +16,15 @@
 epsilon = 1e-05
 masked_score = -1e30
 rope_base = 10000.0
+COST = 1000
+
+
+def cost(flops, bytes_accessed, transcendentals):
+    return pl.CostEstimate(
+        flops=flops // COST, bytes_accessed=bytes_accessed // COST, transcendentals=transcendentals // COST
+    )
+
+
 NT = (((1,), (1,)), ((), ()))
 TN = (((0,), (0,)), ((), ()))
 NN = (((1,), (0,)), ((), ()))
@@ -65,7 +74,7 @@
         ),
         out_shape=[out] * 3,
         compiler_params=pltpu.CompilerParams(vmem_limit_bytes=60 << 20),
-        cost_estimate=pl.CostEstimate(
+        cost_estimate=cost(
             flops=12 * rows * depth * width, bytes_accessed=6 * depth * width + 4 * rows * depth, transcendentals=0
         ),
         name="qkv",
@@ -128,7 +137,7 @@
         out_shape=[jax.ShapeDtypeStruct((half, width), jnp.bfloat16)] * 2
         + [jax.ShapeDtypeStruct((heads, 1, rows), jnp.float32)],
         compiler_params=pltpu.CompilerParams(vmem_limit_bytes=60 << 20),
-        cost_estimate=pl.CostEstimate(
+        cost_estimate=cost(
             flops=8 * rows * rows * width, bytes_accessed=8 * rows * width, transcendentals=heads * rows * rows // 2
         ),
         name="attend",
@@ -194,7 +203,7 @@
         ),
         out_shape=[jax.ShapeDtypeStruct((half, width), jnp.bfloat16)] * 6,
         compiler_params=pltpu.CompilerParams(vmem_limit_bytes=60 << 20),
-        cost_estimate=pl.CostEstimate(
+        cost_estimate=cost(
             flops=20 * rows * rows * width, bytes_accessed=16 * rows * width, transcendentals=heads * rows * rows // 2
         ),
         name="attend_back",
@@ -229,7 +238,7 @@
         out_specs=[ospec] * 3,
         out_shape=[jax.ShapeDtypeStruct((2 * rows, width), jnp.bfloat16)] * 3,
         compiler_params=pltpu.CompilerParams(vmem_limit_bytes=60 << 20),
-        cost_estimate=pl.CostEstimate(
+        cost_estimate=cost(
             flops=12 * rows * depth * width,
             bytes_accessed=6 * depth * width + 8 * rows * depth + 12 * rows * width,
             transcendentals=2 * rows * width,
@@ -243,18 +252,6 @@
     for part in parts:
         out_ref[at : at + part.shape[0], :] = part[...]
         at += part.shape[0]
-
-
-def grad_send_body(pieces, halves, _, *refs):
-    left, rights = refs[:pieces], refs[pieces : pieces + halves]
-    out_ref, left_s, right_s = refs[pieces + halves :]
-
-    @pl.when(pl.program_id(0) == 0)
-    def _():
-        gather_sides(rights, right_s)
-
-    gather_rows(left, left_s)
-    out_ref[...] = mm(left_s[...], right_s[...], TN).astype(out_ref.dtype)
 
 
 def gather_sides(rights, out_ref):
@@ -266,9 +263,9 @@
         at += width
 
 
-def grad_keep_body(pieces, halves, send, _, *refs):
+def grad_body(pieces, halves, groups, _, *refs):
     left, rights = refs[:pieces], refs[pieces : pieces + halves]
-    got_ref, away_ref, own_ref, left_s, right_s = refs[pieces + halves :]
+    outs, (left_s, right_s) = refs[pieces + halves : -2], refs[-2:]
     step = pl.program_id(0)
 
     @pl.when(step == 0)
@@ -276,59 +273,100 @@
         gather_sides(rights, right_s)
 
     gather_rows(left, left_s)
-    total = mm(left_s[...], right_s[...], TN) + got_ref[...].astype(jnp.float32)
-
-    @pl.when(step < send)
-    def _():
-        away_ref[...] = total.astype(away_ref.dtype)
-
-    @pl.when(step >= send)
-    def _():
-        own_ref[...] = total
-
-
-def grad_call(order, pieces, rights, tile, got=None):
+    total = mm(left_s[...], right_s[...], TN).astype(jnp.bfloat16)
+    first = 0
+    for out_ref, count in zip(outs, groups):
+
+        @pl.when((step >= first) & (step < first + count))
+        def _():
+            out_ref[0] = total
+
+        first += count
+
+
+def grad_call(order, groups, pieces, rights, tile):
     rows, depth = pieces[0].shape[0] * len(pieces), pieces[0].shape[1]
     width = sum(near.shape[1] for near in rights[::2])
-    count = order.shape[0]
+    count = sum(groups)
     lspec = pl.BlockSpec((pieces[0].shape[0], tile), lambda j, s: (0, s[j]))
-    in_specs = [lspec] * len(pieces) + [whole(r.shape) for r in rights]
-    args = [order, *pieces, *rights]
-    if got is None:
-        body = functools.partial(grad_send_body, len(pieces), len(rights))
-        out_specs = pl.BlockSpec((tile, width), lambda j, *_: (j, 0))
-        out_shape = jax.ShapeDtypeStruct((count * tile, width), jnp.bfloat16)
-    else:
-        send = count // 2
-        body = functools.partial(grad_keep_body, len(pieces), len(rights), send)
-        in_specs.append(pl.BlockSpec((tile, width), lambda j, s: (s[j] // 2, 0)))
-        args.append(got)
-        out_specs = [
-            pl.BlockSpec((tile, width), lambda j, *_: (jnp.minimum(j, send - 1), 0)),
-            pl.BlockSpec((tile, width), lambda j, *_: (jnp.maximum(j - send, 0), 0)),
-        ]
-        out_shape = [
-            jax.ShapeDtypeStruct((send * tile, width), jnp.bfloat16),
-            jax.ShapeDtypeStruct(((count - send) * tile, width), jnp.float32),
-        ]
+    out_specs = []
+    for index, size in enumerate(groups):
+        first = sum(groups[:index])
+        out_specs.append(
+            pl.BlockSpec(
+                (1, tile, width),
+                lambda j, *_, first=first, size=size: (jnp.clip(j - first, 0, size - 1), 0, 0),
+            )
+        )
     return pl.pallas_call(
-        body,
+        functools.partial(grad_body, len(pieces), len(rights), groups),
         grid_spec=pltpu.PrefetchScalarGridSpec(
             num_scalar_prefetch=1,
             grid=(count,),
-            in_specs=in_specs,
+            in_specs=[lspec] * len(pieces) + [whole(r.shape) for r in rights],
             out_specs=out_specs,
             scratch_shapes=[pltpu.VMEM((rows, tile), jnp.bfloat16), pltpu.VMEM((rows, width), jnp.bfloat16)],
         ),
-        out_shape=out_shape,
+        out_shape=[jax.ShapeDtypeStruct((size, tile, width), jnp.bfloat16) for size in groups],
         compiler_params=pltpu.CompilerParams(vmem_limit_bytes=60 << 20),
-        cost_estimate=pl.CostEstimate(
+        cost_estimate=cost(
             flops=2 * rows * tile * count * width,
-            bytes_accessed=2 * rows * (tile * count + width) + 3 * tile * count * width,
+            bytes_accessed=2 * rows * (tile * count + width) + 2 * tile * count * width,
             transcendentals=0,
         ),
         name="weight_grad",
+    )(order, *pieces, *rights)
+
+
+def project_body(terms, split, *refs):
+    at, lefts, weights = 0, [], []
+    for pieces, dims in terms:
+        lefts.append(refs[at : at + pieces])
+        weights.append((refs[at + pieces], dims))
+        at += pieces + 1
+    outs = refs[at:]
+    rows = outs[0].shape[0] // (1 if split else 2)
+    for half in range(2):
+        span = pl.ds(half * rows, rows)
+        total = None
+        for left, (w_ref, dims) in zip(lefts, weights):
+            value = mm(left[half][...] if len(left) == 2 else left[0][span, :], w_ref[...], dims)
+            total = value if total is None else total + value
+        if split:
+            outs[half][...] = total.astype(jnp.bfloat16)
+        else:
+            outs[0][span, :] = total.astype(jnp.bfloat16)
+
+
+def project(terms, split):
+    terms = [(left if isinstance(left, tuple) else (left,), w, NT if flip else NN) for left, w, flip in terms]
+    rows = sum(piece.shape[0] for piece in terms[0][0])
+    width = terms[0][1].shape[0 if terms[0][2] is NT else 1]
+    tile = min(512, width)
+    in_specs, args, flops = [], [], 0
+    for left, w, dims in terms:
+        depth = left[0].shape[1]
+        in_specs += [whole(piece.shape) for piece in left]
+        in_specs.append(
+            pl.BlockSpec((tile, depth), lambda j: (j, 0)) if dims is NT else pl.BlockSpec((depth, tile), lambda j: (0, j))
+        )
+        args += [*left, w]
+        flops += 2 * rows * depth * width
+    count = 2 if split else 1
+    out = jax.ShapeDtypeStruct((rows // count, width), jnp.bfloat16)
+    result = pl.pallas_call(
+        functools.partial(project_body, [(len(left), dims) for left, _, dims in terms], split),
+        grid=(width // tile,),
+        in_specs=in_specs,
+        out_specs=[pl.BlockSpec((rows // count, tile), lambda j: (0, j))] * count,
+        out_shape=[out] * count,
+        compiler_params=pltpu.CompilerParams(vmem_limit_bytes=60 << 20),
+        cost_estimate=cost(
+            flops=flops, bytes_accessed=sum(2 * a.size for a in args) + 2 * rows * width, transcendentals=0
+        ),
+        name="project",
     )(*args)
+    return tuple(result) if split else result[0]
 
 
 def row_tables(length_row, group_row, mask_row):
@@ -376,23 +414,8 @@
     return values
 
 
-def after(values, *others):
-    return lax.optimization_barrier((values, *others))[0]
-
-
-def scatter_rest(kept, away, axis, bit):
-    size = lax.axis_size(axis)
-    rank = lax.axis_index(axis)
-    while True:
-        got = exchange(away.astype(jnp.bfloat16), axis, bit)
-        bit *= 2
-        if bit == size:
-            return kept.astype(jnp.float32) + got.astype(jnp.float32)
-        total = kept.astype(jnp.float32) + got.astype(jnp.float32)
-        pairs = total.reshape((total.shape[0] // 2, 2) + total.shape[1:])
-        side = (rank // bit) % 2
-        kept = lax.dynamic_index_in_dim(pairs, side, axis=1, keepdims=False)
-        away = lax.dynamic_index_in_dim(pairs, 1 - side, axis=1, keepdims=False)
+def tie(*values):
+    return lax.optimization_barrier(values)
 
 
 def scatter_small(values, axis):
@@ -411,54 +434,89 @@
 
 
 class WeightGrad:
-    def __init__(self, pieces, rights):
+    def __init__(self, pieces, rights, start=1):
         self.pieces, self.rights = pieces, rights
-        self.size = lax.axis_size("dp")
-        self.rank = lax.axis_index("dp")
+        self.size, self.rank = lax.axis_size("dp"), lax.axis_index("dp").astype(jnp.int32)
+        self.start = start
         self.tile = pieces[0].shape[1] // self.size
-        self.blocks = self.tile % 128 == 0 and self.size >= 4
-
-    def send(self):
-        if self.blocks:
-            order = 2 * jnp.arange(self.size // 2, dtype=jnp.int32) + (1 - self.rank % 2)
-            return grad_call(order, self.pieces, self.rights, self.tile)
+        self.width = sum(near.shape[1] for near in rights[::2])
+        self.kernel = self.tile % 128 == 0
+
+    def order(self):
+        place = jnp.arange(self.size // 2, dtype=jnp.int32)
+        blocks = place // self.start * (2 * self.start) + place % self.start
+        side = (self.rank // self.start) % 2
+        return blocks + self.start * (1 - side), blocks + self.start * side
+
+    def compute(self, *groups):
+        named = dict(zip(("send", "own"), self.order()))
+        lists = [named[kind][first : first + count] for kind, first, count in groups]
+        if self.kernel:
+            order = jnp.concatenate(lists)
+            return grad_call(order, [count for _, _, count in groups], self.pieces, self.rights, self.tile)
         left = jnp.concatenate(self.pieces, axis=0)
-        right = jnp.concatenate([jnp.concatenate(self.rights[::2], axis=1), jnp.concatenate(self.rights[1::2], axis=1)], axis=0)
-        full = lax.dot_general(left, right, TN, preferred_element_type=jnp.float32)
-        pairs = full.reshape(self.size // 2, 2, self.tile, -1)
-        self.own = lax.dynamic_index_in_dim(pairs, self.rank % 2, axis=1, keepdims=False)
-        away = lax.dynamic_index_in_dim(pairs, 1 - self.rank % 2, axis=1, keepdims=False)
-        return away.reshape(self.size // 2 * self.tile, -1).astype(jnp.bfloat16)
-
-    def finish(self, got):
-        width = got.shape[1]
-        if self.blocks:
-            place = jnp.arange(self.size // 4, dtype=jnp.int32)
-            side = (self.rank // 2) % 2
-            blocks = jnp.concatenate([2 * place + 1 - side, 2 * place + side])
-            away, kept = grad_call(2 * blocks + self.rank % 2, self.pieces, self.rights, self.tile, got)
-            away, kept = (a.reshape(-1, self.tile, width) for a in (away, kept))
-        else:
-            total = self.own + got.reshape(self.own.shape).astype(jnp.float32)
-            pairs = total.reshape(self.size // 4, 2, self.tile, width)
-            side = (self.rank // 2) % 2
-            kept = lax.dynamic_index_in_dim(pairs, side, axis=1, keepdims=False)
-            away = lax.dynamic_index_in_dim(pairs, 1 - side, axis=1, keepdims=False)
-        return scatter_rest(kept, away, "dp", 2)[0]
-
-
-def cut(values):
-    half = values.shape[0] // 2
-    return values[:half], values[half:]
+        sides = [jnp.concatenate(side, axis=1) for side in (self.rights[::2], self.rights[1::2])]
+        full = lax.dot_general(left, jnp.concatenate(sides, axis=0), TN, preferred_element_type=jnp.float32)
+        full = full.astype(jnp.bfloat16).reshape(self.size, self.tile, self.width)
+        return [jnp.take(full, indices, axis=0) for indices in lists]
+
+    def halve(self, blocks, bits, bit):
+        low = 2 ** bits.index(bit)
+        pairs = blocks.reshape((blocks.shape[0] // (2 * low), 2, low) + blocks.shape[1:])
+        side = (self.rank // bit) % 2
+        away, kept = (
+            lax.dynamic_index_in_dim(pairs, at, axis=1, keepdims=False).reshape((-1,) + blocks.shape[1:])
+            for at in (1 - side, side)
+        )
+        return away.astype(jnp.bfloat16), kept
+
+    def bits(self):
+        return [2**i for i in range(self.size.bit_length() - 1)]
+
+    def finish(self, kept, got, bits, todo):
+        while True:
+            kept = kept.astype(jnp.float32) + got.astype(jnp.float32)
+            if not todo:
+                return kept.reshape(self.tile, self.width)
+            away, kept = self.halve(kept, bits, todo[0])
+            got = exchange(away, "dp", todo[0])
+            bits = [b for b in bits if b != todo[0]]
+            todo = todo[1:]
+
+    def after_start(self, own, got):
+        left = [b for b in self.bits() if b != self.start]
+        return self.finish(own, got, left, left)
+
+    def step(self, own, got, bits, bit):
+        total = own.astype(jnp.float32) + got.astype(jnp.float32)
+        away, kept = self.halve(total, bits, bit)
+        return away, kept, [b for b in bits if b != bit]
+
+    def second(self, own, got):
+        total = own.astype(jnp.float32) + got.astype(jnp.float32)
+        return self.halve(total, self.bits()[1:-1], 2)
+
+    def third(self, kept, gots):
+        first, second = (k + g.astype(jnp.float32) for k, g in zip(kept, gots))
+        top = self.rank // (self.size // 2) == 1
+        return jnp.where(top, first, second).astype(jnp.bfloat16), jnp.where(top, second, first)
+
+    def last(self, kept, got):
+        left = self.bits()[2:-1]
+        return self.finish(kept, got, left, left)
+
+
+def hop(values, bit):
+    return exchange(values, "dp", bit)
 
 
 def send_far(far):
-    mine, others = cut(far)
+    mine, others = far
     return (mine.astype(jnp.float32) + exchange(others, "tensor", 1).astype(jnp.float32)).astype(jnp.bfloat16)
 
 
 def sum_near(near, got):
-    mine, others = cut(near)
+    mine, others = near
     return (
         mine.astype(jnp.float32)
         + exchange(others, "tensor", 1).astype(jnp.float32)
@@ -512,37 +570,54 @@
     cosine, sine, back_sine = rope_tables(inside)
 
     near = qkv_pair(0, rank_ref, a0, a1, cosine, sine, w_query, w_key, w_value)
-    c0 = after(c0, a2)
+    a2, c0, *near = tie(a2, c0, *near)
+    a3 = to_mate(a2)
     c2 = to_far(c0)
     c1 = to_mate(c0)
-    c3 = to_mate(c2)
     far = qkv_pair(2, rank_ref, a2, a3, cosine, sine, w_query, w_key, w_value)
     qs, ks, vs = zip(near, far)
     heads_near, heads_far, lse = attend(rank_ref, qs, ks, vs, low, high)
-
-    got = to_far(send_far(rows_dot(heads_far, w_out).astype(jnp.bfloat16)))
-    mid_h = x_f + sum_near(rows_dot(heads_near, w_out).astype(jnp.bfloat16), got)
+    heads_far, c2 = tie(heads_far, c2)
+    c3 = to_mate(c2)
+    got = to_far(send_far(project([(heads_far, w_out, False)], True)))
+    mid_h = x_f + sum_near(project([(heads_near, w_out, False)], True), got)
     inv_b = lax.rsqrt(jnp.mean(mid_h * mid_h, axis=-1, keepdims=True) + epsilon)
     b0 = (mid_h * inv_b * gain_mlp).astype(jnp.bfloat16)
+    b0, c3 = tie(b0, c3)
     b2 = to_far(b0)
     b1 = to_mate(b0)
+    mid_near, dg_near, du_near = mlp_pair(b0, b1, c0, c1, w_gate, w_up, w_down)
+    b2, mid_near, dg_near, du_near = tie(b2, mid_near, dg_near, du_near)
     b3 = to_mate(b2)
-    mid_near, dg_near, du_near = mlp_pair(b0, b1, c0, c1, w_gate, w_up, w_down)
     mid_far, dg_far, du_far = mlp_pair(b2, b3, c2, c3, w_gate, w_up, w_down)
 
-    grad_down = WeightGrad((c0, c1, c2, c3), (mid_near, mid_far))
-    grad_gate = WeightGrad((b0, b1, b2, b3), (dg_near, dg_far))
-    grad_up = WeightGrad((b0, b1, b2, b3), (du_near, du_far))
-    send_down = grad_down.send()
-    dg_far, du_far, send_down = lax.optimization_barrier((dg_far, du_far, send_down))
-    x_down = exchange(send_down, "dp", 1)
-    far_b = (rows_dot_t(dg_far, w_gate) + rows_dot_t(du_far, w_up)).astype(jnp.bfloat16)
-    near_b = (rows_dot_t(dg_near, w_gate) + rows_dot_t(du_near, w_up)).astype(jnp.bfloat16)
-    got = to_far(send_far(far_b))
-    d_b = sum_near(near_b, got)
-    send_gate = grad_gate.send()
-    send_up = grad_up.send()
-    d_b, send_gate, send_up = lax.optimization_barrier((d_b, send_gate, send_up))
+    half = lax.axis_size("dp") // 2
+    part = half // 2
+    b_all, c_all = (b0, b1, b2, b3), (c0, c1, c2, c3)
+    grad_down = WeightGrad(c_all, (mid_near, mid_far))
+    grad_gate = WeightGrad(b_all, (dg_near, dg_far), 2)
+    grad_up = WeightGrad(b_all, (du_near, du_far))
+    sends, owns = ("send", 0, half), ("own", 0, half)
+    both = (("send", 0, part), ("send", part, part), ("own", 0, part), ("own", part, part))
+    (down_send,) = grad_down.compute(sends)
+    (gate_send,) = grad_gate.compute(sends)
+    dg_f, du_f, down_send, gate_send = tie(dg_far, du_far, down_send, gate_send)
+    down_got = hop(down_send, 1)
+    gate_got = hop(gate_send, 2)
+    y5 = send_far(project([(dg_f, w_gate, True), (du_f, w_up, True)], True))
+    got = to_far(y5)
+    dg_n, du_n, y5 = tie(dg_near, du_near, y5)
+    d_b = sum_near(project([(dg_n, w_gate, True), (du_n, w_up, True)], True), got)
+    (down_own,) = grad_down.compute(owns)
+    (gate_own,) = grad_gate.compute(owns)
+    d_b, down_got, gate_got, down_own, gate_own = tie(d_b, down_got, gate_got, down_own, gate_own)
+
+    away, down_own, down_bits = grad_down.step(down_own, down_got, grad_down.bits()[1:], 2)
+    down_got = hop(away, 2)
+    away, gate_own, gate_bits = grad_gate.step(
+        gate_own, gate_got, [b for b in grad_gate.bits() if b != 2], 1
+    )
+    gate_got = hop(away, 1)
     n_b = mid_h * inv_b
     gain_mlp_part = jnp.sum(d_b * n_b, axis=0)
     e_b = d_b * gain_mlp
@@ -551,51 +626,66 @@
     t0 = d_h.astype(jnp.bfloat16)
     t2 = to_far(t0)
     t1 = to_mate(t0)
+    gs_near = project([((t0, t1), w_out, True)], False)
+    up0, up1, own_u0, own_u1 = grad_up.compute(*both)
+    t2, down_got, gate_got, gs_near, up0, up1 = tie(t2, down_got, gate_got, gs_near, up0, up1)
+
+    up0_got = hop(up0, 1)
+    away, gate_own, gate_bits = grad_gate.step(gate_own, gate_got, gate_bits, 4)
+    gate_got = hop(away, 4)
     t3 = to_mate(t2)
-    gs_near = rows_dot_t(jnp.concatenate([t0, t1], axis=0), w_out).astype(jnp.bfloat16)
-    out_far = rows_dot(mid_far, w_down).astype(jnp.bfloat16)
-    out_near = rows_dot(mid_near, w_down).astype(jnp.bfloat16)
-    gs_far = rows_dot_t(jnp.concatenate([t2, t3], axis=0), w_out).astype(jnp.bfloat16)
-    gs_near, gs_far, x_down = lax.optimization_barrier((gs_near, gs_far, x_down))
-    x_gate = exchange(after(send_gate, x_down), "dp", 1)
-    got = to_far(send_far(after(out_far, t2)))
-    output = (mid_h + sum_near(out_near, got)).astype(jnp.bfloat16)
-    sum_down = grad_down.finish(x_down)
-
+    gs_far = project([((t2, t3), w_out, True)], False)
+    y8 = send_far(project([(mid_far, w_down, False)], True))
+    gs_far, y8 = tie(gs_far, y8)
+    got8 = to_far(y8)
     dqn, dqf, dkn, dkf, dvn, dvf = attend_back(
         rank_ref, qs, ks, vs, (gs_near, gs_far), low, high, lse, cosine, back_sine
     )
+    dqf, dkf, dvf, up0_got, gate_got, got8 = tie(dqf, dkf, dvf, up0_got, gate_got, got8)
+
+    up1_got = hop(up1, 1)
+    away, down_own, down_bits = grad_down.step(down_own, down_got, down_bits, 4)
+    down_got = hop(away, 4)
+    away, kept_u0 = grad_up.second(own_u0, up0_got)
+    z_up0 = hop(away, 2)
+    y7 = send_far(project([(dqf, w_query, True), (dkf, w_key, True), (dvf, w_value, True)], True))
+    got = to_far(y7)
+    dqn, dkn, dvn, y7 = tie(dqn, dkn, dvn, y7)
+    d_a = sum_near(project([(dqn, w_query, True), (dkn, w_key, True), (dvn, w_value, True)], True), got)
+    a_all = (a0, a1, a2, a3)
     grad_out = WeightGrad((t0, t1, t2, t3), (heads_near, heads_far))
-    grad_qkv = [
-        WeightGrad((a0, a1, a2, a3), pair) for pair in ((dqn, dqf), (dkn, dkf), (dvn, dvf))
-    ]
-    send_out = grad_out.send()
-    send_qkv = [grad.send() for grad in grad_qkv]
-
-    def to_input(q_part, k_part, v_part):
-        total = rows_dot_t(q_part, w_query)
-        total = total + rows_dot_t(k_part, w_key)
-        return (total + rows_dot_t(v_part, w_value)).astype(jnp.bfloat16)
-
-    got = to_far(send_far(to_input(dqf, dkf, dvf)))
-    d_a = sum_near(to_input(dqn, dkn, dvn), got)
+    grad_v = WeightGrad(a_all, (dvn, dvf), 2)
+    grad_q, grad_k = (WeightGrad(a_all, rights) for rights in ((dqn, dqf), (dkn, dkf)))
+    v_send, v_own = grad_v.compute(sends, owns)
+    q_send, q_own = grad_q.compute(sends, owns)
+    k_send, k_own = grad_k.compute(sends, owns)
+    d_a, up1_got, down_got, z_up0, v_send, q_send, k_send = tie(
+        d_a, up1_got, down_got, z_up0, v_send, q_send, k_send
+    )
+
+    q_got = hop(q_send, 1)
+    v_got = hop(v_send, 2)
+    away, kept_u1 = grad_up.second(own_u1, up1_got)
+    z_up1 = hop(away, 2)
+    out_send, out_own = grad_out.compute(sends, owns)
+    output = (mid_h + sum_near(project([(mid_near, w_down, False)], True), got8)).astype(jnp.bfloat16)
     n_a = x_f * inv_a
     gain_attn_part = jnp.sum(d_a * n_a, axis=0)
     e_a = d_a * gain_attn
     grad_input = d_h + inv_a * (e_a - n_a * jnp.mean(e_a * n_a, axis=-1, keepdims=True))
     gains = jnp.stack([gain_attn_part, gain_mlp_part])
     gains = butterfly_sum(scatter_small(gains.reshape(2, lax.axis_size("dp"), -1), "dp"), "tensor")
-
-    x_up = exchange(after(send_up, x_gate), "dp", 1)
-    sum_gate = grad_gate.finish(x_gate)
-    x_out = exchange(after(send_out, x_up), "dp", 1)
-    sum_up = grad_up.finish(x_up)
-    last = x_out
-    sum_out = grad_out.finish(x_out)
-    sums = []
-    for grad, send in zip(grad_qkv, send_qkv):
-        last = exchange(after(send, last), "dp", 1)
-        sums.append(grad.finish(last))
+    sum_down = grad_down.finish(down_own, down_got, down_bits, down_bits)
+    sum_gate = grad_gate.finish(gate_own, gate_got, gate_bits, gate_bits)
+    u_away, u_kept = grad_up.third((kept_u0, kept_u1), (z_up0, z_up1))
+    sum_up = grad_up.last(u_kept, hop(u_away, half))
+    k_got = hop(tie(k_send, q_got)[0], 1)
+    out_got = hop(tie(out_send, k_got)[0], 1)
+    sum_out = grad_out.after_start(out_own, out_got)
+    sums = [
+        grad.after_start(own, got)
+        for grad, own, got in ((grad_q, q_own, q_got), (grad_k, k_own, k_got), (grad_v, v_own, v_got))
+    ]
     return (
         output,
         grad_input,

time: 758 us -> 620 us (0.82)
  waiting for transfers between devices: 337 us -> 167 us
  matrix products: 69.4 us -> 0 us
  Pallas kernels: 205 us -> 263 us
  other arithmetic: 60.7 us -> 80.9 us
  starting transfers between devices: 50.3 us -> 63.9 us
  local copies, waits for them, and re-layouts: 28.4 us -> 37 us
    ppermute x53 -> x55, waiting for transfers between devices: 337 us -> 167 us  [exchange(): lax.ppermute(values, axis, [(rank, rank ^ bit) for rank in range(size)])]
    dot_general x16 -> x0, matrix products: 69.4 us -> none  [the longest x12 49.6 us: rows_dot_t(): return lax.dot_general(left, right, NT, preferred_element_type=jnp.float32)]
    pallas_call x14 -> x19, Pallas kernels: 113 us -> 172 us  [the longest x9 95.4 us: grad_call(): pl.pallas_call(functools.partial(grad_body, len(pieces), len(rights), gro...]
    add x9 -> x18, other arithmetic: 8.82 us -> 23.6 us  [the longest x4 9.76 us: step(): total = own.astype(jnp.float32) + got.astype(jnp.float32)]
    ppermute x53 -> x55, starting transfers between devices: 50.3 us -> 63.9 us  [exchange(): lax.ppermute(values, axis, [(rank, rank ^ bit) for rank in range(size)])]
    reshape x4 -> x0, local copies, waits for them, and re-layouts: 10.5 us -> none  [finish(): away, kept = (a.reshape(-1, self.tile, width) for a in (away, kept))]
    unnamed x126 -> x94, local copies, waits for them, and re-layouts: 6.76 us -> 16.6 us
    dynamic_slice x0 -> x6, local copies, waits for them, and re-layouts: none -> 9.45 us  [halve(): lax.dynamic_index_in_dim(pairs, at, axis=1, keepdims=False)]
  transfers between devices with their start and end apart: 53 -> 55, of which waited for: 25 -> 20; matrix products, arithmetic and copies ran while one was open for 16% -> 16% of each run, Pallas kernels for 20% -> 34%
where the time goes in v3:
time: 620 us; the launch traced here: 614 us
  Pallas kernels  263 us (42%)
  waiting for transfers between devices  167 us (27%)
  other arithmetic  80.9 us (13%)
  starting transfers between devices  63.9 us (10%)
  local copies, waits for them, and re-layouts  37 us (6%)
    ppermute x55, waiting for transfers between devices, exchange(): lax.ppermute(values, axis, [(rank, rank ^ bit) for rank in range(size)])  167 us
    pallas_call x9, Pallas kernels, grad_call(): pl.pallas_call(functools.partial(grad_body, len(pieces), len(rights), gro...  95.4 us
    pallas_call x10, Pallas kernels, project(): pl.pallas_call(functools.partial(project_body, [(len(left), dims) for lef...  76.4 us
    ppermute x55, starting transfers between devices, exchange(): lax.ppermute(values, axis, [(rank, rank ^ bit) for rank in range(size)])  63.9 us
    pallas_call x2, Pallas kernels, mlp_pair(): pl.pallas_call(mlp_body, grid=(pl.cdiv(width, tile),), in_specs=[whole(xa...  37.2 us
    pallas_call x1, Pallas kernels, attend_back(): pl.pallas_call(attend_back_body, grid_spec=pltpu.PrefetchScalarGridSpec(n...  21.8 us
    pallas_call x2, Pallas kernels, qkv_pair(): pl.pallas_call(functools.partial(qkv_body, first), grid_spec=pltpu.Prefet...  17.9 us
    unnamed x94, local copies, waits for them, and re-layouts  16.6 us
  transfers between devices with their start and end apart: 55, of which 20 were waited for; matrix products, arithmetic and copies ran while one was open for 16% of the time, Pallas kernels for 34%

profile of v3, /device:TPU:0, one launch (start us, length us, event | category | flops | bytes accessed | tf_op | source)
XLA Modules:
  0.0 613.8 jit_solution(10569066586061804199)
XLA Ops:
  25.9 9.1 %qkv.2 = (bf16[640,512]{1,0:T(8,128)(2,1)}, bf16[640,512]{1,0:T(8,128)(2,1)}, bf16[640,512]{1,0:T(8,128)(2,1)}) custom-call(s32[1]{0:T(128)} %bitcast.rank_ref, bf16[320,2048]{1,0:T(8,128)(2,1)} %copy-done.3, bf16[320,2048]{1,0:T(8,128)(2,1)} %copy-done.6, f32[1280,128]{1,0:T(8,128)} %pad_maximum_fusion.cos_ref, f32[1280,128]{1,0:T(8,128)} %get-tuple-element.221.sin_ref, ...), custom_call_target="tpu_custom_call" | custom-call | flops 4026531 | bytes 8912 | tf_op jit(solution)/shard_map/qkv/pallas_call | solution.py:67
  40.5 8.9 %qkv.3 = (bf16[640,512]{1,0:T(8,128)(2,1)}, bf16[640,512]{1,0:T(8,128)(2,1)}, bf16[640,512]{1,0:T(8,128)(2,1)}) custom-call(s32[1]{0:T(128)} %bitcast.rank_ref, bf16[320,2048]{1,0:T(8,128)(2,1)} %collective-permute-done.xa_ref.refs_2_, bf16[320,2048]{1,0:T(8,128)(2,1)} %copy-done.7, f32[1280,128]{1,0:T(8,128)} %pad_maximum_fusion.cos_ref, ...), custom_call_target="tpu_custom_call" | custom-call | flops 4026531 | bytes 8912 | tf_op jit(solution)/shard_map/qkv/pallas_call | solution.py:67
  49.3 14.6 %attend.1 = (bf16[640,512]{1,0:T(8,128)(2,1)}, bf16[640,512]{1,0:T(8,128)(2,1)}, f32[4,1,1280]{2,1,0:T(1,128)}) custom-call(s32[1]{0:T(128)} %bitcast.rank_ref, bf16[640,512]{1,0:T(8,128)(2,1)} %get-tuple-element.113.qn, bf16[640,512]{1,0:T(8,128)(2,1)} %get-tuple-element.115.qf, bf16[640,512]{1,0:T(8,128)(2,1)} %get-tuple-element.116.kn, ...), custom_call_target="tpu_custom_call" | custom-call | flops 6710886 | bytes 5242 | tf_op jit(solution)/shard_map/attend/pallas_call | solution.py:128
  63.9 3.8 collective-permute-done.7.ca_ref.refs_2_
  67.7 4.8 project.11
  72.5 4.9 project.10
  80.7 28.5 %collective-permute-done.9 = bf16[320,2048]{1,0:T(8,128)(2,1)S(1)} collective-permute-done((bf16[320,2048]{1,0:T(8,128)(2,1)S(1)}, bf16[320,2048]{1,0:T(8,128)(2,1)S(1)}, u32[]{:S(2)}, u32[]{:S(2)}) %collective-permute-start.9) | collective-permute-done | bytes 1310752 | tf_op jit(solution)/shard_map/ppermute | solution.py:405
  114.9 18.5 %mlp.2 = (bf16[640,1408]{1,0:T(8,128)(2,1)}, bf16[640,1408]{1,0:T(8,128)(2,1)}, bf16[640,1408]{1,0:T(8,128)(2,1)}) custom-call(bf16[320,2048]{1,0:T(8,128)(2,1)} %multiply_convert_fusion.xa_ref.refs_0_, bf16[320,2048]{1,0:T(8,128)(2,1)} %collective-permute-done.12.xb_ref.refs_1_, bf16[320,2048]{1,0:T(8,128)(2,1)} %fusion.11.ca_ref.refs_0_, ...), custom_call_target="tpu_custom_call" | custom-call | flops 11072962 | bytes 27951 | tf_op jit(solution)/shard_map/mlp/pallas_call | solution.py:234
  133.3 9.7 %collective-permute-done.11.xa_ref.refs_2_ = bf16[320,2048]{1,0:T(8,128)(2,1)} collective-permute-done((bf16[320,2048]{1,0:T(8,128)(2,1)}, bf16[320,2048]{1,0:T(8,128)(2,1)}, u32[]{:S(2)}, u32[]{:S(2)}) %collective-permute-start.11) | collective-permute-done | bytes 1310752 | tf_op jit(solution)/shard_map/ppermute | solution.py:405
  146.4 18.8 %mlp.3 = (bf16[640,1408]{1,0:T(8,128)(2,1)}, bf16[640,1408]{1,0:T(8,128)(2,1)}, bf16[640,1408]{1,0:T(8,128)(2,1)}) custom-call(bf16[320,2048]{1,0:T(8,128)(2,1)} %collective-permute-done.11.xa_ref.refs_2_, bf16[320,2048]{1,0:T(8,128)(2,1)} %collective-permute-done.15.xb_ref.refs_3_, bf16[320,2048]{1,0:T(8,128)(2,1)} %collective-permute-done.7.ca_ref.refs_2_, ...), custom_call_target="tpu_custom_call" | custom-call | flops 11072962 | bytes 27951 | tf_op jit(solution)/shard_map/mlp/pallas_call | solution.py:234
  165.2 9.6 %weight_grad.10 = bf16[4,256,1408]{2,1,0:T(8,128)(2,1)} custom-call(s32[4]{0:T(128)} %broadcast_add_fusion.1._, bf16[320,2048]{1,0:T(8,128)(2,1)} %multiply_convert_fusion.xa_ref.refs_0_, bf16[320,2048]{1,0:T(8,128)(2,1)} %collective-permute-done.12.xb_ref.refs_1_, bf16[320,2048]{1,0:T(8,128)(2,1)} %collective-permute-done.11.xa_ref.refs_2_, ...), custom_call_target="tpu_custom_call" | custom-call | flops 3690987 | bytes 9109 | tf_op jit(solution)/shard_map/weight_grad/pallas_call | solution.py:301
  174.8 9.6 %weight_grad.9 = bf16[4,256,1408]{2,1,0:T(8,128)(2,1)} custom-call(s32[4]{0:T(128)} %fusion.23._, bf16[320,2048]{1,0:T(8,128)(2,1)} %fusion.11.ca_ref.refs_0_, bf16[320,2048]{1,0:T(8,128)(2,1)} %collective-permute-done.13.cb_ref.refs_1_, bf16[320,2048]{1,0:T(8,128)(2,1)} %collective-permute-done.7.ca_ref.refs_2_, ...), custom_call_target="tpu_custom_call" | custom-call | flops 3690987 | bytes 9109 | tf_op jit(solution)/shard_map/weight_grad/pallas_call | solution.py:301
  184.4 12.6 %project.13 = (bf16[320,2048]{1,0:T(8,128)(2,1)}, bf16[320,2048]{1,0:T(8,128)(2,1)}) custom-call(bf16[640,1408]{1,0:T(8,128)(2,1)} %get-tuple-element.143.refs_5_.refs_0_, bf16[2048,1408]{1,0:T(8,128)(2,1)} %refs_1_.12, bf16[640,1408]{1,0:T(8,128)(2,1)} %get-tuple-element.144.refs_2_.refs_5_, bf16[2048,1408]{1,0:T(8,128)(2,1)} %refs_3_.5), custom_call_target="tpu_custom_call" | custom-call | flops 7381975 | bytes 17760 | tf_op jit(solution)/shard_map/project/pallas_call | solution.py:357
  200.5 2.9 add_convert_fusion.3
  203.4 12.6 %project.14 = (bf16[320,2048]{1,0:T(8,128)(2,1)}, bf16[320,2048]{1,0:T(8,128)(2,1)}) custom-call(bf16[640,1408]{1,0:T(8,128)(2,1)} %get-tuple-element.147.refs_4_.refs_0_, bf16[2048,1408]{1,0:T(8,128)(2,1)} %refs_1_.12, bf16[640,1408]{1,0:T(8,128)(2,1)} %get-tuple-element.148.refs_2_.refs_4_, bf16[2048,1408]{1,0:T(8,128)(2,1)} %refs_3_.5), custom_call_target="tpu_custom_call" | custom-call | flops 7381975 | bytes 17760 | tf_op jit(solution)/shard_map/project/pallas_call | solution.py:357
  218.7 9.7 %weight_grad.12 = bf16[4,256,1408]{2,1,0:T(8,128)(2,1)} custom-call(s32[4]{0:T(128)} %broadcast_add_fusion._, bf16[320,2048]{1,0:T(8,128)(2,1)} %multiply_convert_fusion.xa_ref.refs_0_, bf16[320,2048]{1,0:T(8,128)(2,1)} %collective-permute-done.12.xb_ref.refs_1_, bf16[320,2048]{1,0:T(8,128)(2,1)} %collective-permute-done.11.xa_ref.refs_2_, ...), custom_call_target="tpu_custom_call" | custom-call | flops 3690987 | bytes 9109 | tf_op jit(solution)/shard_map/weight_grad/pallas_call | solution.py:301
  228.4 9.8 %weight_grad.11 = bf16[4,256,1408]{2,1,0:T(8,128)(2,1)} custom-call(s32[4]{0:T(128)} %fusion.22._, bf16[320,2048]{1,0:T(8,128)(2,1)} %fusion.11.ca_ref.refs_0_, bf16[320,2048]{1,0:T(8,128)(2,1)} %collective-permute-done.13.cb_ref.refs_1_, bf16[320,2048]{1,0:T(8,128)(2,1)} %collective-permute-done.7.ca_ref.refs_2_, ...), custom_call_target="tpu_custom_call" | custom-call | flops 3690987 | bytes 9109 | tf_op jit(solution)/shard_map/weight_grad/pallas_call | solution.py:301
  238.2 9.3 %collective-permute-done.18 = bf16[320,2048]{1,0:T(8,128)(2,1)} collective-permute-done((bf16[320,2048]{1,0:T(8,128)(2,1)}, bf16[320,2048]{1,0:T(8,128)(2,1)}, u32[]{:S(2)}, u32[]{:S(2)}) %collective-permute-start.18) | collective-permute-done | bytes 1310752 | tf_op jit(solution)/shard_map/ppermute | solution.py:405
  247.5 2.8 convert_add_fusion.6
  250.3 12.0 %collective-permute-done.19 = bf16[4,256,1408]{2,1,0:T(8,128)(2,1)} collective-permute-done((bf16[4,256,1408]{2,1,0:T(8,128)(2,1)}, bf16[4,256,1408]{2,1,0:T(8,128)(2,1)}, u32[]{:S(2)}, u32[]{:S(2)}) %collective-permute-start.19) | collective-permute-done | bytes 2883616 | tf_op jit(solution)/shard_map/ppermute | solution.py:405
  281.2 4.9 fusion.25
  287.8 7.8 %project.17 = (bf16[320,2048]{1,0:T(8,128)(2,1)}, bf16[320,2048]{1,0:T(8,128)(2,1)}) custom-call(bf16[640,1408]{1,0:T(8,128)(2,1)} %get-tuple-element.142.refs_5_.refs_0_, bf16[1408,2048]{1,0:T(8,128)(2,1)} %refs_1_.13), custom_call_target="tpu_custom_call" | custom-call | flops 3690987 | bytes 10190 | tf_op jit(solution)/shard_map/project/pallas_call | solution.py:357
  296.3 16.4 %weight_grad.13 = (bf16[2,256,1408]{2,1,0:T(8,128)(2,1)}, bf16[2,256,1408]{2,1,0:T(8,128)(2,1)}, bf16[2,256,1408]{2,1,0:T(8,128)(2,1)}, bf16[2,256,1408]{2,1,0:T(8,128)(2,1)}) custom-call(s32[8]{0:T(128)} %pad_add_fusion._, bf16[320,2048]{1,0:T(8,128)(2,1)} %multiply_convert_fusion.xa_ref.refs_0_, bf16[320,2048]{1,0:T(8,128)(2,1)} %collective-permute-done.12.xb_ref.refs_1_, ...), custom_call_target="tpu_custom_call" | custom-call | flops 7381975 | bytes 14614 | tf_op jit(solution)/shard_map/weight_grad/pallas_call | solution.py:301
  312.7 4.8 project.15.gn
  317.9 3.3 add_convert_fusion.2
  321.8 4.8 project.16.gf
  335.4 7.8 %project.12 = (bf16[320,2048]{1,0:T(8,128)(2,1)}, bf16[320,2048]{1,0:T(8,128)(2,1)}) custom-call(bf16[640,1408]{1,0:T(8,128)(2,1)} %get-tuple-element.133.refs_0_.refs_4_, bf16[1408,2048]{1,0:T(8,128)(2,1)} %refs_1_.13), custom_call_target="tpu_custom_call" | custom-call | flops 3690987 | bytes 10190 | tf_op jit(solution)/shard_map/project/pallas_call | solution.py:357
  343.2 3.6 constant_dynamic-slice_fusion.8
  346.8 3.4 copy.35
  350.2 21.8 %attend_back.1 = (bf16[640,512]{1,0:T(8,128)(2,1)}, bf16[640,512]{1,0:T(8,128)(2,1)}, bf16[640,512]{1,0:T(8,128)(2,1)}, bf16[640,512]{1,0:T(8,128)(2,1)}, bf16[6...) custom-call(s32[1]{0:T(128)} %bitcast.rank_ref, bf16[640,512]{1,0:T(8,128)(2,1)} %get-tuple-element.113.qn, ...), custom_call_target="tpu_custom_call" | custom-call | flops 16777216 | bytes 10485 | tf_op jit(solution)/shard_map/attend_back/pallas_call | solution.py:191
  372.0 8.1 %project.18 = (bf16[320,2048]{1,0:T(8,128)(2,1)}, bf16[320,2048]{1,0:T(8,128)(2,1)}) custom-call(bf16[640,512]{1,0:T(8,128)(2,1)} %get-tuple-element.176.refs_0_.refs_5_, bf16[2048,512]{1,0:T(8,128)(2,1)} %refs_1_.15, bf16[640,512]{1,0:T(8,128)(2,1)} %get-tuple-element.177.refs_2_.refs_5_, bf16[2048,512]{1,0:T(8,128)(2,1)} %refs_3_.7, ...), custom_call_target="tpu_custom_call" | custom-call | flops 4026531 | bytes 10878 | tf_op jit(solution)/shard_map/project/pallas_call | solution.py:357
  387.5 10.0 %weight_grad.17 = (bf16[4,256,512]{2,1,0:T(8,128)(2,1)}, bf16[4,256,512]{2,1,0:T(8,128)(2,1)}) custom-call(s32[8]{0:T(128)} %pad_add_fusion._, bf16[320,2048]{1,0:T(8,128)(2,1)} %get-tuple-element.216.refs_0_, bf16[320,2048]{1,0:T(8,128)(2,1)} %collective-permute-done.24.refs_1_, bf16[320,2048]{1,0:T(8,128)(2,1)} %collective-permute-done.21.refs_0_.refs_2_, ...), custom_call_target="tpu_custom_call" | custom-call | flops 2684354 | bytes 8650 | tf_op jit(solution)/shard_map/weight_grad/pallas_call | solution.py:301
  397.5 3.8 convert_add_fusion.4
  401.3 2.9 add_convert_fusion
  404.8 8.1 %project.19 = (bf16[320,2048]{1,0:T(8,128)(2,1)}, bf16[320,2048]{1,0:T(8,128)(2,1)}) custom-call(bf16[640,512]{1,0:T(8,128)(2,1)} %get-tuple-element.181.refs_0_.refs_4_, bf16[2048,512]{1,0:T(8,128)(2,1)} %refs_1_.15, bf16[640,512]{1,0:T(8,128)(2,1)} %get-tuple-element.182.refs_2_.refs_4_, bf16[2048,512]{1,0:T(8,128)(2,1)} %refs_3_.7, ...), custom_call_target="tpu_custom_call" | custom-call | flops 4026531 | bytes 10878 | tf_op jit(solution)/shard_map/project/pallas_call | solution.py:357
  415.8 3.8 add_convert_fusion.1
  421.9 10.0 %weight_grad.16 = (bf16[4,256,512]{2,1,0:T(8,128)(2,1)}, bf16[4,256,512]{2,1,0:T(8,128)(2,1)}) custom-call(s32[8]{0:T(128)} %pad_add_fusion._, bf16[320,2048]{1,0:T(8,128)(2,1)} %copy-done.3, bf16[320,2048]{1,0:T(8,128)(2,1)} %copy-done.6, bf16[320,2048]{1,0:T(8,128)(2,1)} %collective-permute-done.xa_ref.refs_2_, bf16[320,2048]{1,0:T(8,128)(2,1)} %copy-done.7, ...), custom_call_target="tpu_custom_call" | custom-call | flops 2684354 | bytes 8650 | tf_op jit(solution)/shard_map/weight_grad/pallas_call | solution.py:301
  431.9 10.0 %weight_grad.15 = (bf16[4,256,512]{2,1,0:T(8,128)(2,1)}, bf16[4,256,512]{2,1,0:T(8,128)(2,1)}) custom-call(s32[8]{0:T(128)} %pad_add_fusion._, bf16[320,2048]{1,0:T(8,128)(2,1)} %copy-done.3, bf16[320,2048]{1,0:T(8,128)(2,1)} %copy-done.6, bf16[320,2048]{1,0:T(8,128)(2,1)} %collective-permute-done.xa_ref.refs_2_, bf16[320,2048]{1,0:T(8,128)(2,1)} %copy-done.7, ...), custom_call_target="tpu_custom_call" | custom-call | flops 2684354 | bytes 8650 | tf_op jit(solution)/shard_map/weight_grad/pallas_call | solution.py:301
  441.9 10.4 %weight_grad.14 = (bf16[4,256,512]{2,1,0:T(8,128)(2,1)}, bf16[4,256,512]{2,1,0:T(8,128)(2,1)}) custom-call(s32[8]{0:T(128)} %pad_add_fusion.1._, bf16[320,2048]{1,0:T(8,128)(2,1)} %copy-done.3, bf16[320,2048]{1,0:T(8,128)(2,1)} %copy-done.6, bf16[320,2048]{1,0:T(8,128)(2,1)} %collective-permute-done.xa_ref.refs_2_, bf16[320,2048]{1,0:T(8,128)(2,1)} %copy-done.7, ...), custom_call_target="tpu_custom_call" | custom-call | flops 2684354 | bytes 8650 | tf_op jit(solution)/shard_map/weight_grad/pallas_call | solution.py:301
  457.8 3.7 convert_add_fusion.3
  470.9 32.0 %collective-permute-done.38 = f32[2,1,256]{2,1,0:T(1,128)S(1)} collective-permute-done((f32[2,1,256]{2,1,0:T(1,128)S(1)}, f32[2,1,256]{2,1,0:T(1,128)S(1)}, u32[]{:S(2)}, u32[]{:S(2)}) %collective-permute-start.38) | collective-permute-done | bytes 2080 | tf_op jit(solution)/shard_map/ppermute | solution.py:405
  503.0 4.9 fusion.8
  512.6 3.4 collective-permute-start.54
  521.1 26.8 %collective-permute-done.54 = bf16[1,256,1408]{2,1,0:T(8,128)(2,1)S(1)} collective-permute-done((bf16[1,256,1408]{2,1,0:T(8,128)(2,1)S(1)}, bf16[1,256,1408]{2,1,0:T(8,128)(2,1)S(1)}, u32[]{:S(2)}, u32[]{:S(2)}) %collective-permute-start.54) | collective-permute-done | bytes 720928 | tf_op jit(solution)/shard_map/ppermute | solution.py:405
  561.3 13.3 %collective-permute-done.50 = bf16[4,256,512]{2,1,0:T(8,128)(2,1)S(1)} collective-permute-done((bf16[4,256,512]{2,1,0:T(8,128)(2,1)S(1)}, bf16[4,256,512]{2,1,0:T(8,128)(2,1)S(1)}, u32[]{:S(2)}, u32[]{:S(2)}) %collective-permute-start.50) | collective-permute-done | bytes 1048608 | tf_op jit(solution)/shard_map/ppermute | solution.py:405
  584.4 3.7 collective-permute-start.46
  588.5 9.2 %collective-permute-done.51 = bf16[2,256,512]{1,2,0:T(8,128)(2,1)} collective-permute-done((bf16[2,256,512]{1,2,0:T(8,128)(2,1)}, bf16[2,256,512]{1,2,0:T(8,128)(2,1)}, u32[]{:S(2)}, u32[]{:S(2)}) %collective-permute-start.51) | collective-permute-done | bytes 524320 | tf_op jit(solution)/shard_map/ppermute | solution.py:405
  603.0 9.5 %collective-permute-done.52 = bf16[1,256,512]{1,2,0:T(8,128)(2,1)S(1)} collective-permute-done((bf16[1,256,512]{1,2,0:T(8,128)(2,1)S(1)}, bf16[1,256,512]{1,2,0:T(8,128)(2,1)S(1)}, u32[]{:S(2)}, u32[]{:S(2)}) %collective-permute-start.52) | collective-permute-done | bytes 262176 | tf_op jit(solution)/shard_map/ppermute | solution.py:405
  (283 shorter events, 147.8 us)
Async XLA Ops:
  3.5 21.2 %collective-permute-start.4 = (bf16[320,2048]{1,0:T(8,128)(2,1)S(1)}, bf16[320,2048]{1,0:T(8,128)(2,1)S(1)}, u32[]{:S(2)}, u32[]{:S(2)}) collective-permute-start(bf16[320,2048]{1,0:T(8,128)(2,1)S(1)} %fusion.4.xa_ref.refs_0_), channel_id=1, source_target_pairs={{0,1},{1,0},{2,3},{3,2},{4,5},{5,4},{6,7},{7,6},{8,9},{9,8},{10,11... | collective-permute-start | bytes 3932168 | tf_op jit(solution)/shard_map/ppermute | solution.py:405
  4.1 32.1 %collective-permute-start = (bf16[320,2048]{1,0:T(8,128)(2,1)S(1)}, bf16[320,2048]{1,0:T(8,128)(2,1)}, u32[]{:S(2)}, u32[]{:S(2)}) collective-permute-start(bf16[320,2048]{1,0:T(8,128)(2,1)S(1)} %fusion.4.xa_ref.refs_0_), channel_id=1, source_target_pairs={{0,2},{1,3},{2,0},{3,1},{4,6},{5,7},{6,4},{7,5},{8,10},{9,11},{10,... | collective-permute-start | bytes 3932168 | tf_op jit(solution)/shard_map/ppermute | solution.py:405
  7.5 6.5 %collective-permute-start.1 = (f32[8]{0:T(128)S(1)}, f32[8]{0:T(128)S(1)}, u32[]{:S(2)}, u32[]{:S(2)}) collective-permute-start(f32[8]{0:T(128)S(1)} %select_reduce_fusion.1), channel_id=1, source_target_pairs={{0,4},{4,0},{8,12},{12,8},{16,20},{20,16},{24,28},{28,24},{1,5},{5... | collective-permute-start | bytes 104 | tf_op jit(solution)/shard_map/ppermute | solution.py:405
  17.5 4.5 collective-permute-start.3
  36.2 31.5 %collective-permute-start.7 = (bf16[320,2048]{1,0:T(8,128)(2,1)}, bf16[320,2048]{1,0:T(8,128)(2,1)}, u32[]{:S(2)}, u32[]{:S(2)}) collective-permute-start(bf16[320,2048]{1,0:T(8,128)(2,1)} %fusion.11.ca_ref.refs_0_), channel_id=1, source_target_pairs={{0,2},{1,3},{2,0},{3,1},{4,6},{5,7},{6,4},{7,5},{8,10},{9,11},{10,... | collective-permute-start | bytes 3932168 | tf_op jit(solution)/shard_map/ppermute | solution.py:405
  72.5 5.3 collective-permute-start.8
  78.3 30.9 %collective-permute-start.9 = (bf16[320,2048]{1,0:T(8,128)(2,1)S(1)}, bf16[320,2048]{1,0:T(8,128)(2,1)S(1)}, u32[]{:S(2)}, u32[]{:S(2)}) collective-permute-start(bf16[320,2048]{1,0:T(8,128)(2,1)S(1)} %add_convert_fusion.4), channel_id=1, source_target_pairs={{0,2},{1,3},{2,0},{3,1},{4,6},{5,7},{6,4},{7,5},{8,10},{9,11},{10,... | collective-permute-start | bytes 3932168 | tf_op jit(solution)/shard_map/ppermute | solution.py:405
  80.1 31.4 %collective-permute-start.10 = (bf16[320,2048]{1,0:T(8,128)(2,1)}, bf16[320,2048]{1,0:T(8,128)(2,1)}, u32[]{:S(2)}, u32[]{:S(2)}) collective-permute-start(bf16[320,2048]{1,0:T(8,128)(2,1)} %collective-permute-done.7.ca_ref.refs_2_), channel_id=1, source_target_pairs={{0,1},{1,0},{2,3},{3,2},{4,5},{5,4},{6,7},{7,6},{8,9},{9,8},{10,11... | collective-permute-start | bytes 3932168 | tf_op jit(solution)/shard_map/ppermute | solution.py:405
  80.1 33.1 %collective-permute-start.13 = (bf16[320,2048]{1,0:T(8,128)(2,1)}, bf16[320,2048]{1,0:T(8,128)(2,1)}, u32[]{:S(2)}, u32[]{:S(2)}) collective-permute-start(bf16[320,2048]{1,0:T(8,128)(2,1)} %fusion.11.ca_ref.refs_0_), channel_id=1, source_target_pairs={{0,1},{1,0},{2,3},{3,2},{4,5},{5,4},{6,7},{7,6},{8,9},{9,8},{10,11... | collective-permute-start | bytes 3932168 | tf_op jit(solution)/shard_map/ppermute | solution.py:405
  111.5 31.5 %collective-permute-start.11 = (bf16[320,2048]{1,0:T(8,128)(2,1)}, bf16[320,2048]{1,0:T(8,128)(2,1)}, u32[]{:S(2)}, u32[]{:S(2)}) collective-permute-start(bf16[320,2048]{1,0:T(8,128)(2,1)} %multiply_convert_fusion.xa_ref.refs_0_), channel_id=1, source_target_pairs={{0,2},{1,3},{2,0},{3,1},{4,6},{5,7},{6,4},{7,5},{8,10},{9,11},{10,... | collective-permute-start | bytes 3932168 | tf_op jit(solution)/shard_map/ppermute | solution.py:405
  197.2 65.1 %collective-permute-start.19 = (bf16[4,256,1408]{2,1,0:T(8,128)(2,1)}, bf16[4,256,1408]{2,1,0:T(8,128)(2,1)}, u32[]{:S(2)}, u32[]{:S(2)}) collective-permute-start(bf16[4,256,1408]{2,1,0:T(8,128)(2,1)} %weight_grad.9), channel_id=1, source_target_pairs={{0,4},{4,0},{8,12},{12,8},{16,20},{20,16},{24,28},{28,24},{1,5},{5... | collective-permute-start | bytes 8650760 | tf_op jit(solution)/shard_map/ppermute | solution.py:405
  198.9 64.8 %collective-permute-start.20 = (bf16[4,256,1408]{2,1,0:T(8,128)(2,1)}, bf16[4,256,1408]{2,1,0:T(8,128)(2,1)}, u32[]{:S(2)}, u32[]{:S(2)}) collective-permute-start(bf16[4,256,1408]{2,1,0:T(8,128)(2,1)} %weight_grad.10), channel_id=1, source_target_pairs={{0,8},{4,12},{8,0},{12,4},{16,24},{20,28},{24,16},{28,20},{1,9},{5... | collective-permute-start | bytes 8650760 | tf_op jit(solution)/shard_map/ppermute | solution.py:405
  216.0 22.2 %collective-permute-start.17 = (bf16[320,2048]{1,0:T(8,128)(2,1)}, bf16[320,2048]{1,0:T(8,128)(2,1)}, u32[]{:S(2)}, u32[]{:S(2)}) collective-permute-start(bf16[320,2048]{1,0:T(8,128)(2,1)} %get-tuple-element.150), channel_id=1, source_target_pairs={{0,1},{1,0},{2,3},{3,2},{4,5},{5,4},{6,7},{7,6},{8,9},{9,8},{10,11... | collective-permute-start | bytes 3932168 | tf_op jit(solution)/shard_map/ppermute | solution.py:405
  216.0 31.5 %collective-permute-start.18 = (bf16[320,2048]{1,0:T(8,128)(2,1)}, bf16[320,2048]{1,0:T(8,128)(2,1)}, u32[]{:S(2)}, u32[]{:S(2)}) collective-permute-start(bf16[320,2048]{1,0:T(8,128)(2,1)} %add_convert_fusion.3), channel_id=1, source_target_pairs={{0,2},{1,3},{2,0},{3,1},{4,6},{5,7},{6,4},{7,5},{8,10},{9,11},{10,... | collective-permute-start | bytes 3932168 | tf_op jit(solution)/shard_map/ppermute | solution.py:405
  268.3 49.4 %collective-permute-start.23 = (bf16[2,256,1408]{2,1,0:T(8,128)(2,1)}, bf16[2,256,1408]{2,1,0:T(8,128)(2,1)}, u32[]{:S(2)}, u32[]{:S(2)}) collective-permute-start(bf16[2,256,1408]{2,1,0:T(8,128)(2,1)} %fusion.12), channel_id=1, source_target_pairs={{0,4},{4,0},{8,12},{12,8},{16,20},{20,16},{24,28},{28,24},{1,5},{5... | collective-permute-start | bytes 4325384 | tf_op jit(solution)/shard_map/ppermute | solution.py:405
  279.7 38.0 %collective-permute-start.22 = (bf16[2,256,1408]{1,2,0:T(8,128)(2,1)}, bf16[2,256,1408]{1,2,0:T(8,128)(2,1)}, u32[]{:S(2)}, u32[]{:S(2)}) collective-permute-start(bf16[2,256,1408]{1,2,0:T(8,128)(2,1)} %bitcast.108), channel_id=1, source_target_pairs={{0,8},{4,12},{8,0},{12,4},{16,24},{20,28},{24,16},{28,20},{1,9},{5... | collective-permute-start | bytes 4325384 | tf_op jit(solution)/shard_map/ppermute | solution.py:405
  286.2 26.6 %collective-permute-start.24 = (bf16[320,2048]{1,0:T(8,128)(2,1)}, bf16[320,2048]{1,0:T(8,128)(2,1)}, u32[]{:S(2)}, u32[]{:S(2)}) collective-permute-start(bf16[320,2048]{1,0:T(8,128)(2,1)} %get-tuple-element.216.refs_0_), channel_id=1, source_target_pairs={{0,1},{1,0},{2,3},{3,2},{4,5},{5,4},{6,7},{7,6},{8,9},{9,8},{10,11... | collective-permute-start | bytes 3932168 | tf_op jit(solution)/shard_map/ppermute | solution.py:405
  286.2 31.5 %collective-permute-start.21 = (bf16[320,2048]{1,0:T(8,128)(2,1)}, bf16[320,2048]{1,0:T(8,128)(2,1)}, u32[]{:S(2)}, u32[]{:S(2)}) collective-permute-start(bf16[320,2048]{1,0:T(8,128)(2,1)} %get-tuple-element.216.refs_0_), channel_id=1, source_target_pairs={{0,2},{1,3},{2,0},{3,1},{4,6},{5,7},{6,4},{7,5},{8,10},{9,11},{10,... | collective-permute-start | bytes 3932168 | tf_op jit(solution)/shard_map/ppermute | solution.py:405
  295.6 22.3 %collective-permute-start.26 = (bf16[320,2048]{1,0:T(8,128)(2,1)}, bf16[320,2048]{1,0:T(8,128)(2,1)}, u32[]{:S(2)}, u32[]{:S(2)}) collective-permute-start(bf16[320,2048]{1,0:T(8,128)(2,1)} %get-tuple-element.163), channel_id=1, source_target_pairs={{0,1},{1,0},{2,3},{3,2},{4,5},{5,4},{6,7},{7,6},{8,9},{9,8},{10,11... | collective-permute-start | bytes 3932168 | tf_op jit(solution)/shard_map/ppermute | solution.py:405
  317.7 4.1 collective-permute-start.25
  321.2 50.8 %collective-permute-start.27 = (bf16[2,256,1408]{2,1,0:T(8,128)(2,1)}, bf16[2,256,1408]{2,1,0:T(8,128)(2,1)}, u32[]{:S(2)}, u32[]{:S(2)}) collective-permute-start(bf16[2,256,1408]{2,1,0:T(8,128)(2,1)} %get-tuple-element.169), channel_id=1, source_target_pairs={{0,4},{4,0},{8,12},{12,8},{16,20},{20,16},{24,28},{28,24},{1,5},{5... | collective-permute-start | bytes 4325384 | tf_op jit(solution)/shard_map/ppermute | solution.py:405
  326.6 45.4 %collective-permute-start.29 = (bf16[320,2048]{1,0:T(8,128)(2,1)}, bf16[320,2048]{1,0:T(8,128)(2,1)}, u32[]{:S(2)}, u32[]{:S(2)}) collective-permute-start(bf16[320,2048]{1,0:T(8,128)(2,1)} %add_convert_fusion.2), channel_id=1, source_target_pairs={{0,2},{1,3},{2,0},{3,1},{4,6},{5,7},{6,4},{7,5},{8,10},{9,11},{10,... | collective-permute-start | bytes 3932168 | tf_op jit(solution)/shard_map/ppermute | solution.py:405
  332.1 39.9 %collective-permute-start.28 = (bf16[1,256,1408]{2,1,0:T(8,128)(2,1)S(1)}, bf16[1,256,1408]{2,1,0:T(8,128)(2,1)}, u32[]{:S(2)}, u32[]{:S(2)}) collective-permute-start(bf16[1,256,1408]{2,1,0:T(8,128)(2,1)S(1)} %dynamic-slice_convert_fusion.3), channel_id=1, source_target_pairs={{0,16},{4,20},{8,24},{12,28},{16,0},{20,4},{24,8},{28,12},{1,17},{... | collective-permute-start | bytes 2162696 | tf_op jit(solution)/shard_map/ppermute | solution.py:405
  343.2 72.1 %collective-permute-start.14 = (bf16[320,2048]{1,0:T(8,128)(2,1)}, bf16[320,2048]{1,0:T(8,128)(2,1)}, u32[]{:S(2)}, u32[]{:S(2)}) collective-permute-start(bf16[320,2048]{1,0:T(8,128)(2,1)} %get-tuple-element.135), channel_id=1, source_target_pairs={{0,1},{1,0},{2,3},{3,2},{4,5},{5,4},{6,7},{7,6},{8,9},{9,8},{10,11... | collective-permute-start | bytes 3932168 | tf_op jit(solution)/shard_map/ppermute | solution.py:405
  380.1 21.2 %collective-permute-start.30 = (bf16[320,2048]{1,0:T(8,128)(2,1)}, bf16[320,2048]{1,0:T(8,128)(2,1)}, u32[]{:S(2)}, u32[]{:S(2)}) collective-permute-start(bf16[320,2048]{1,0:T(8,128)(2,1)} %get-tuple-element.180), channel_id=1, source_target_pairs={{0,1},{1,0},{2,3},{3,2},{4,5},{5,4},{6,7},{7,6},{8,9},{9,8},{10,11... | collective-permute-start | bytes 3932168 | tf_op jit(solution)/shard_map/ppermute | solution.py:405
  385.7 69.1 %collective-permute-start.34 = (bf16[1,256,1408]{1,2,0:T(8,128)(2,1)}, bf16[1,256,1408]{1,2,0:T(8,128)(2,1)}, u32[]{:S(2)}, u32[]{:S(2)}) collective-permute-start(bf16[1,256,1408]{1,2,0:T(8,128)(2,1)} %dynamic-slice_convert_fusion.2), channel_id=1, source_target_pairs={{0,16},{4,20},{8,24},{12,28},{16,0},{20,4},{24,8},{28,12},{1,17},{... | collective-permute-start | bytes 2162696 | tf_op jit(solution)/shard_map/ppermute | solution.py:405
  386.0 68.8 %collective-permute-start.33 = (bf16[2,256,1408]{2,1,0:T(8,128)(2,1)}, bf16[2,256,1408]{2,1,0:T(8,128)(2,1)}, u32[]{:S(2)}, u32[]{:S(2)}) collective-permute-start(bf16[2,256,1408]{2,1,0:T(8,128)(2,1)} %get-tuple-element.186), channel_id=1, source_target_pairs={{0,4},{4,0},{8,12},{12,8},{16,20},{20,16},{24,28},{28,24},{1,5},{5... | collective-permute-start | bytes 4325384 | tf_op jit(solution)/shard_map/ppermute | solution.py:405
  404.1 48.1 %collective-permute-start.32 = (bf16[320,2048]{1,0:T(8,128)(2,1)}, bf16[320,2048]{1,0:T(8,128)(2,1)}, u32[]{:S(2)}, u32[]{:S(2)}) collective-permute-start(bf16[320,2048]{1,0:T(8,128)(2,1)} %add_convert_fusion), channel_id=1, source_target_pairs={{0,2},{1,3},{2,0},{3,1},{4,6},{5,7},{6,4},{7,5},{8,10},{9,11},{10,... | collective-permute-start | bytes 3932168 | tf_op jit(solution)/shard_map/ppermute | solution.py:405
  412.9 39.4 %collective-permute-start.31 = (bf16[320,2048]{1,0:T(8,128)(2,1)}, bf16[320,2048]{1,0:T(8,128)(2,1)}, u32[]{:S(2)}, u32[]{:S(2)}) collective-permute-start(bf16[320,2048]{1,0:T(8,128)(2,1)} %get-tuple-element.185), channel_id=1, source_target_pairs={{0,1},{1,0},{2,3},{3,2},{4,5},{5,4},{6,7},{7,6},{8,9},{9,8},{10,11... | collective-permute-start | bytes 3932168 | tf_op jit(solution)/shard_map/ppermute | solution.py:405
  415.4 39.4 %collective-permute-start.35 = (bf16[1,256,1408]{2,1,0:T(8,128)(2,1)}, bf16[1,256,1408]{2,1,0:T(8,128)(2,1)S(1)}, u32[]{:S(2)}, u32[]{:S(2)}) collective-permute-start(bf16[1,256,1408]{2,1,0:T(8,128)(2,1)} %dynamic-slice_convert_fusion.1), channel_id=1, source_target_pairs={{0,8},{4,12},{8,0},{12,4},{16,24},{20,28},{24,16},{28,20},{1,9},{5... | collective-permute-start | bytes 2162696 | tf_op jit(solution)/shard_map/ppermute | solution.py:405
  457.2 4.3 collective-permute-start.36
  461.5 6.7 %collective-permute-start.37 = (f32[2,2,256]{2,1,0:T(2,128)S(1)}, f32[2,2,256]{2,1,0:T(2,128)S(1)}, u32[]{:S(2)}, u32[]{:S(2)}) collective-permute-start(f32[2,2,256]{2,1,0:T(2,128)S(1)} %bitcast.111), channel_id=1, source_target_pairs={{0,8},{4,12},{8,0},{12,4},{16,24},{20,28},{24,16},{28,20},{1,9},{5... | collective-permute-start | bytes 12296 | tf_op jit(solution)/shard_map/ppermute | solution.py:405
  464.6 47.6 %collective-permute-start.53 = (bf16[1,256,1408]{2,1,0:T(8,128)(2,1)S(1)}, bf16[1,256,1408]{2,1,0:T(8,128)(2,1)S(1)}, u32[]{:S(2)}, u32[]{:S(2)}) collective-permute-start(bf16[1,256,1408]{2,1,0:T(8,128)(2,1)S(1)} %dynamic-slice_convert_fusion), channel_id=1, source_target_pairs={{0,8},{4,12},{8,0},{12,4},{16,24},{20,28},{24,16},{28,20},{1,9},{5... | collective-permute-start | bytes 2162696 | tf_op jit(solution)/shard_map/ppermute | solution.py:405
  465.1 50.8 %collective-permute-start.41 = (bf16[4,256,512]{2,1,0:T(8,128)(2,1)}, bf16[4,256,512]{2,1,0:T(8,128)(2,1)S(1)}, u32[]{:S(2)}, u32[]{:S(2)}) collective-permute-start(bf16[4,256,512]{2,1,0:T(8,128)(2,1)} %get-tuple-element.195), channel_id=1, source_target_pairs={{0,4},{4,0},{8,12},{12,8},{16,20},{20,16},{24,28},{28,24},{1,5},{5... | collective-permute-start | bytes 3145736 | tf_op jit(solution)/shard_map/ppermute | solution.py:405
  466.6 50.8 %collective-permute-start.47 = (bf16[4,256,512]{2,1,0:T(8,128)(2,1)}, bf16[4,256,512]{2,1,0:T(8,128)(2,1)S(1)}, u32[]{:S(2)}, u32[]{:S(2)}) collective-permute-start(bf16[4,256,512]{2,1,0:T(8,128)(2,1)} %get-tuple-element.200), channel_id=1, source_target_pairs={{0,8},{4,12},{8,0},{12,4},{16,24},{20,28},{24,16},{28,20},{1,9},{5... | collective-permute-start | bytes 3145736 | tf_op jit(solution)/shard_map/ppermute | solution.py:405
  468.2 34.6 %collective-permute-start.38 = (f32[2,1,256]{2,1,0:T(1,128)S(1)}, f32[2,1,256]{2,1,0:T(1,128)S(1)}, u32[]{:S(2)}, u32[]{:S(2)}) collective-permute-start(f32[2,1,256]{2,1,0:T(1,128)S(1)} %constant_dynamic-slice_fusion.2), channel_id=1, source_target_pairs={{0,16},{4,20},{8,24},{12,28},{16,0},{20,4},{24,8},{28,12},{1,17},{... | collective-permute-start | bytes 6152 | tf_op jit(solution)/shard_map/ppermute | solution.py:405
  502.9 5.0 collective-permute-start.39
  512.6 35.3 %collective-permute-start.54 = (bf16[1,256,1408]{2,1,0:T(8,128)(2,1)S(1)}, bf16[1,256,1408]{2,1,0:T(8,128)(2,1)S(1)}, u32[]{:S(2)}, u32[]{:S(2)}) collective-permute-start(bf16[1,256,1408]{2,1,0:T(8,128)(2,1)S(1)} %select_convert_fusion), channel_id=1, source_target_pairs={{0,16},{4,20},{8,24},{12,28},{16,0},{20,4},{24,8},{28,12},{1,17},{... | collective-permute-start | bytes 2162696 | tf_op jit(solution)/shard_map/ppermute | solution.py:405
  516.0 33.5 %collective-permute-start.44 = (bf16[4,256,512]{2,1,0:T(8,128)(2,1)S(1)}, bf16[4,256,512]{2,1,0:T(8,128)(2,1)S(1)}, u32[]{:S(2)}, u32[]{:S(2)}) collective-permute-start(bf16[4,256,512]{2,1,0:T(8,128)(2,1)S(1)} %copy-done.42), channel_id=1, source_target_pairs={{0,4},{4,0},{8,12},{12,8},{16,20},{20,16},{24,28},{28,24},{1,5},{5... | collective-permute-start | bytes 3145736 | tf_op jit(solution)/shard_map/ppermute | solution.py:405
  517.9 34.9 %collective-permute-start.48 = (bf16[2,256,512]{2,1,0:T(8,128)(2,1)S(1)}, bf16[2,256,512]{2,1,0:T(8,128)(2,1)S(1)}, u32[]{:S(2)}, u32[]{:S(2)}) collective-permute-start(bf16[2,256,512]{2,1,0:T(8,128)(2,1)S(1)} %fusion.15), channel_id=1, source_target_pairs={{0,4},{4,0},{8,12},{12,8},{16,20},{20,16},{24,28},{28,24},{1,5},{5... | collective-permute-start | bytes 1572872 | tf_op jit(solution)/shard_map/ppermute | solution.py:405
  519.1 35.9 %collective-permute-start.42 = (bf16[2,256,512]{2,1,0:T(8,128)(2,1)S(1)}, bf16[2,256,512]{2,1,0:T(8,128)(2,1)S(1)}, u32[]{:S(2)}, u32[]{:S(2)}) collective-permute-start(bf16[2,256,512]{2,1,0:T(8,128)(2,1)S(1)} %fusion.13), channel_id=1, source_target_pairs={{0,8},{4,12},{8,0},{12,4},{16,24},{20,28},{24,16},{28,20},{1,9},{5... | collective-permute-start | bytes 1572872 | tf_op jit(solution)/shard_map/ppermute | solution.py:405
  549.4 25.2 %collective-permute-start.50 = (bf16[4,256,512]{2,1,0:T(8,128)(2,1)S(1)}, bf16[4,256,512]{2,1,0:T(8,128)(2,1)S(1)}, u32[]{:S(2)}, u32[]{:S(2)}) collective-permute-start(bf16[4,256,512]{2,1,0:T(8,128)(2,1)S(1)} %copy-done.41), channel_id=1, source_target_pairs={{0,4},{4,0},{8,12},{12,8},{16,20},{20,16},{24,28},{28,24},{1,5},{5... | collective-permute-start | bytes 3145736 | tf_op jit(solution)/shard_map/ppermute | solution.py:405
  553.7 26.5 %collective-permute-start.49 = (bf16[1,256,512]{2,1,0:T(8,128)(2,1)}, bf16[1,256,512]{2,1,0:T(8,128)(2,1)}, u32[]{:S(2)}, u32[]{:S(2)}) collective-permute-start(bf16[1,256,512]{2,1,0:T(8,128)(2,1)} %dynamic-slice_convert_fusion.5), channel_id=1, source_target_pairs={{0,16},{4,20},{8,24},{12,28},{16,0},{20,4},{24,8},{28,12},{1,17},{... | collective-permute-start | bytes 786440 | tf_op jit(solution)/shard_map/ppermute | solution.py:405
  556.0 44.3 %collective-permute-start.43 = (bf16[1,256,512]{2,1,0:T(8,128)(2,1)}, bf16[1,256,512]{2,1,0:T(8,128)(2,1)S(1)}, u32[]{:S(2)}, u32[]{:S(2)}) collective-permute-start(bf16[1,256,512]{2,1,0:T(8,128)(2,1)} %dynamic-slice_convert_fusion.7), channel_id=1, source_target_pairs={{0,16},{4,20},{8,24},{12,28},{16,0},{20,4},{24,8},{28,12},{1,17},{... | collective-permute-start | bytes 786440 | tf_op jit(solution)/shard_map/ppermute | solution.py:405
  558.8 23.2 %collective-permute-start.45 = (bf16[2,256,512]{2,1,0:T(8,128)(2,1)}, bf16[2,256,512]{2,1,0:T(8,128)(2,1)}, u32[]{:S(2)}, u32[]{:S(2)}) collective-permute-start(bf16[2,256,512]{2,1,0:T(8,128)(2,1)} %fusion.14), channel_id=1, source_target_pairs={{0,8},{4,12},{8,0},{12,4},{16,24},{20,28},{24,16},{28,20},{1,9},{5... | collective-permute-start | bytes 1572872 | tf_op jit(solution)/shard_map/ppermute | solution.py:405
  577.9 19.8 %collective-permute-start.51 = (bf16[2,256,512]{1,2,0:T(8,128)(2,1)}, bf16[2,256,512]{1,2,0:T(8,128)(2,1)}, u32[]{:S(2)}, u32[]{:S(2)}) collective-permute-start(bf16[2,256,512]{1,2,0:T(8,128)(2,1)} %bitcast.109), channel_id=1, source_target_pairs={{0,8},{4,12},{8,0},{12,4},{16,24},{20,28},{24,16},{28,20},{1,9},{5... | collective-permute-start | bytes 1572872 | tf_op jit(solution)/shard_map/ppermute | solution.py:405
  584.4 16.8 %collective-permute-start.46 = (bf16[1,256,512]{2,1,0:T(8,128)(2,1)}, bf16[1,256,512]{2,1,0:T(8,128)(2,1)}, u32[]{:S(2)}, u32[]{:S(2)}) collective-permute-start(bf16[1,256,512]{2,1,0:T(8,128)(2,1)} %dynamic-slice_convert_fusion.6), channel_id=1, source_target_pairs={{0,16},{4,20},{8,24},{12,28},{16,0},{20,4},{24,8},{28,12},{1,17},{... | collective-permute-start | bytes 786440 | tf_op jit(solution)/shard_map/ppermute | solution.py:405
  598.9 13.6 %collective-permute-start.52 = (bf16[1,256,512]{1,2,0:T(8,128)(2,1)S(1)}, bf16[1,256,512]{1,2,0:T(8,128)(2,1)S(1)}, u32[]{:S(2)}, u32[]{:S(2)}) collective-permute-start(bf16[1,256,512]{1,2,0:T(8,128)(2,1)S(1)} %dynamic-slice_convert_fusion.4), channel_id=1, source_target_pairs={{0,16},{4,20},{8,24},{12,28},{16,0},{20,4},{24,8},{28,12},{1,17},{... | collective-permute-start | bytes 786440 | tf_op jit(solution)/shard_map/ppermute | solution.py:405
  (51 other events, 379.5 us)

commit v4 on v3

--- a/solution.py
+++ b/solution.py
@@ -210,14 +210,14 @@
     )(rank, *qs, *ks, *vs, *gs, low, high, lse, cosine, back_sine)
 
 
-def mlp_body(xa_ref, xb_ref, ca_ref, cb_ref, wg_ref, wu_ref, wd_ref, mid_ref, dg_ref, du_ref):
+def mlp_body(xa_ref, xb_ref, dm_ref, wg_ref, wu_ref, mid_ref, dg_ref, du_ref):
     rows = xa_ref.shape[0]
-    for half, (x_ref, c_ref) in enumerate(((xa_ref, ca_ref), (xb_ref, cb_ref))):
+    for half, x_ref in enumerate((xa_ref, xb_ref)):
         span = pl.ds(half * rows, rows)
         x = x_ref[...]
         gate = mm(x, wg_ref[...])
         up = mm(x, wu_ref[...])
-        d_mid = mm(c_ref[...], wd_ref[...], NT)
+        d_mid = dm_ref[span, :]
         sigma = 1.0 / (1.0 + jnp.exp(-gate))
         active = gate * sigma
         mid_ref[span, :] = (active * up).astype(jnp.bfloat16)
@@ -225,7 +225,7 @@
         du_ref[span, :] = (d_mid * active).astype(jnp.bfloat16)
 
 
-def mlp_pair(xa, xb, ca, cb, wg, wu, wd):
+def mlp_pair(xa, xb, d_mid, wg, wu):
     rows, depth = xa.shape
     width = wg.shape[1]
     tile = 256
@@ -234,17 +234,17 @@
     return pl.pallas_call(
         mlp_body,
         grid=(pl.cdiv(width, tile),),
-        in_specs=[whole(xa.shape)] * 4 + [wspec] * 2 + [pl.BlockSpec((tile, depth), lambda j: (j, 0))],
+        in_specs=[whole(xa.shape)] * 2 + [ospec] + [wspec] * 2,
         out_specs=[ospec] * 3,
         out_shape=[jax.ShapeDtypeStruct((2 * rows, width), jnp.bfloat16)] * 3,
         compiler_params=pltpu.CompilerParams(vmem_limit_bytes=60 << 20),
         cost_estimate=cost(
-            flops=12 * rows * depth * width,
-            bytes_accessed=6 * depth * width + 8 * rows * depth + 12 * rows * width,
+            flops=8 * rows * depth * width,
+            bytes_accessed=4 * depth * width + 4 * rows * depth + 20 * rows * width,
             transcendentals=2 * rows * width,
         ),
         name="mlp",
-    )(xa, xb, ca, cb, wg, wu, wd)
+    )(xa, xb, d_mid, wg, wu)
 
 
 def gather_rows(parts, out_ref):
@@ -263,9 +263,19 @@
         at += width
 
 
-def grad_body(pieces, halves, groups, _, *refs):
-    left, rights = refs[:pieces], refs[pieces : pieces + halves]
-    outs, (left_s, right_s) = refs[pieces + halves : -2], refs[-2:]
+def block_at(place, low, side):
+    return place // low * (2 * low) + place % low + low * side
+
+
+def filled(step, low, side):
+    group, half = step // (2 * low), step // low % 2
+    here = jnp.where(half == side, step % low, jnp.where(half > side, low - 1, -1))
+    return jnp.maximum(group * low + here, 0)
+
+
+def grad_body(pieces, widths, low, sides, rank_ref, *refs):
+    left, rights = refs[:pieces], refs[pieces : pieces + 2 * len(widths)]
+    outs, (left_s, right_s) = refs[pieces + 2 * len(widths) : -2], refs[-2:]
     step = pl.program_id(0)
 
     @pl.when(step == 0)
@@ -274,32 +284,45 @@
 
     gather_rows(left, left_s)
     total = mm(left_s[...], right_s[...], TN).astype(jnp.bfloat16)
-    first = 0
-    for out_ref, count in zip(outs, groups):
-
-        @pl.when((step >= first) & (step < first + count))
-        def _():
-            out_ref[0] = total
-
-        first += count
-
-
-def grad_call(order, groups, pieces, rights, tile):
+
+    def store(refs):
+        at = 0
+        for ref, width in zip(refs, widths):
+            ref[0] = total[:, at : at + width]
+            at += width
+
+    if len(sides) == 1:
+        store(outs)
+    else:
+        sent = step // low % 2 != rank_ref[0] // low % 2
+        pl.when(sent)(lambda: store(outs[: len(widths)]))
+        pl.when(jnp.logical_not(sent))(lambda: store(outs[len(widths) :]))
+
+
+def grad_call(rank, pieces, mats, low, sides, tile):
     rows, depth = pieces[0].shape[0] * len(pieces), pieces[0].shape[1]
-    width = sum(near.shape[1] for near in rights[::2])
-    count = sum(groups)
-    lspec = pl.BlockSpec((pieces[0].shape[0], tile), lambda j, s: (0, s[j]))
+    widths = [near.shape[1] for near, _ in mats]
+    width, half = sum(widths), depth // tile // 2
+    count = half * len(sides)
+
+    def own(s, side):
+        bit = s[0] // low % 2
+        return 1 - bit if side else bit
+
+    if len(sides) == 1:
+        lspec = pl.BlockSpec((pieces[0].shape[0], tile), lambda j, s: (0, block_at(j, low, own(s, sides[0]))))
+    else:
+        lspec = pl.BlockSpec((pieces[0].shape[0], tile), lambda j, s: (0, j))
     out_specs = []
-    for index, size in enumerate(groups):
-        first = sum(groups[:index])
-        out_specs.append(
-            pl.BlockSpec(
-                (1, tile, width),
-                lambda j, *_, first=first, size=size: (jnp.clip(j - first, 0, size - 1), 0, 0),
-            )
-        )
+    for side in sides:
+        for w in widths:
+            if len(sides) == 1:
+                out_specs.append(pl.BlockSpec((1, tile, w), lambda j, s: (j, 0, 0)))
+            else:
+                out_specs.append(pl.BlockSpec((1, tile, w), lambda j, s, side=side: (filled(j, low, own(s, side)), 0, 0)))
+    rights = [part for mat in mats for part in mat]
     return pl.pallas_call(
-        functools.partial(grad_body, len(pieces), len(rights), groups),
+        functools.partial(grad_body, len(pieces), widths, low, sides),
         grid_spec=pltpu.PrefetchScalarGridSpec(
             num_scalar_prefetch=1,
             grid=(count,),
@@ -307,7 +330,7 @@
             out_specs=out_specs,
             scratch_shapes=[pltpu.VMEM((rows, tile), jnp.bfloat16), pltpu.VMEM((rows, width), jnp.bfloat16)],
         ),
-        out_shape=[jax.ShapeDtypeStruct((size, tile, width), jnp.bfloat16) for size in groups],
+        out_shape=[jax.ShapeDtypeStruct((half, tile, w), jnp.bfloat16) for _ in sides for w in widths],
         compiler_params=pltpu.CompilerParams(vmem_limit_bytes=60 << 20),
         cost_estimate=cost(
             flops=2 * rows * tile * count * width,
@@ -315,35 +338,63 @@
             transcendentals=0,
         ),
         name="weight_grad",
-    )(order, *pieces, *rights)
-
-
-def project_body(terms, split, *refs):
+    )(rank, *pieces, *rights)
+
+
+def merge_body(_, own_away, got_away, own_kept, got_kept, away_ref, kept_ref):
+    away_ref[...] = (own_away[...].astype(jnp.float32) + got_away[...].astype(jnp.float32)).astype(jnp.bfloat16)
+    kept_ref[...] = (own_kept[...].astype(jnp.float32) + got_kept[...].astype(jnp.float32)).astype(jnp.bfloat16)
+
+
+def merge_call(rank, own, got, low, bit):
+    count, tile, width = own.shape
+    away, kept = (
+        pl.BlockSpec((1, tile, width), lambda j, s, flip=flip: (block_at(j, low, (s[0] // bit + flip) % 2), 0, 0))
+        for flip in (1, 0)
+    )
+    ospec = pl.BlockSpec((1, tile, width), lambda j, s: (j, 0, 0))
+    return pl.pallas_call(
+        merge_body,
+        grid_spec=pltpu.PrefetchScalarGridSpec(
+            num_scalar_prefetch=1,
+            grid=(count // 2,),
+            in_specs=[away, away, kept, kept],
+            out_specs=[ospec] * 2,
+        ),
+        out_shape=[jax.ShapeDtypeStruct((count // 2, tile, width), jnp.bfloat16)] * 2,
+        compiler_params=pltpu.CompilerParams(vmem_limit_bytes=40 << 20),
+        cost_estimate=cost(flops=count * tile * width, bytes_accessed=6 * count * tile * width, transcendentals=0),
+        name="merge",
+    )(rank, own, got, own, got)
+
+
+def product(lefts, weights, half, rows):
+    total = None
+    for left, (w_ref, dims) in zip(lefts, weights):
+        value = mm(left[half][...] if len(left) == 2 else left[0][pl.ds(half * rows, rows), :], w_ref[...], dims)
+        total = value if total is None else total + value
+    return total
+
+
+def project_body(terms, *refs):
     at, lefts, weights = 0, [], []
     for pieces, dims in terms:
         lefts.append(refs[at : at + pieces])
         weights.append((refs[at + pieces], dims))
         at += pieces + 1
-    outs = refs[at:]
-    rows = outs[0].shape[0] // (1 if split else 2)
+    out_ref = refs[at]
+    rows = out_ref.shape[0] // 2
     for half in range(2):
         span = pl.ds(half * rows, rows)
-        total = None
-        for left, (w_ref, dims) in zip(lefts, weights):
-            value = mm(left[half][...] if len(left) == 2 else left[0][span, :], w_ref[...], dims)
-            total = value if total is None else total + value
-        if split:
-            outs[half][...] = total.astype(jnp.bfloat16)
-        else:
-            outs[0][span, :] = total.astype(jnp.bfloat16)
-
-
-def project(terms, split):
-    terms = [(left if isinstance(left, tuple) else (left,), w, NT if flip else NN) for left, w, flip in terms]
-    rows = sum(piece.shape[0] for piece in terms[0][0])
-    width = terms[0][1].shape[0 if terms[0][2] is NT else 1]
-    tile = min(512, width)
-    in_specs, args, flops = [], [], 0
+        out_ref[span, :] = product(lefts, weights, half, rows).astype(out_ref.dtype)
+
+
+def terms_of(terms):
+    return [(left if isinstance(left, tuple) else (left,), w, NT if flip else NN) for left, w, flip in terms]
+
+
+def term_specs(terms, tile):
+    in_specs, args = [], []
     for left, w, dims in terms:
         depth = left[0].shape[1]
         in_specs += [whole(piece.shape) for piece in left]
@@ -351,22 +402,100 @@
             pl.BlockSpec((tile, depth), lambda j: (j, 0)) if dims is NT else pl.BlockSpec((depth, tile), lambda j: (0, j))
         )
         args += [*left, w]
-        flops += 2 * rows * depth * width
-    count = 2 if split else 1
-    out = jax.ShapeDtypeStruct((rows // count, width), jnp.bfloat16)
-    result = pl.pallas_call(
-        functools.partial(project_body, [(len(left), dims) for left, _, dims in terms], split),
-        grid=(width // tile,),
+    return in_specs, args
+
+
+def project(terms, dtype=jnp.bfloat16):
+    terms = terms_of(terms)
+    rows = sum(piece.shape[0] for piece in terms[0][0])
+    width = terms[0][1].shape[0 if terms[0][2] is NT else 1]
+    tile = min(512, width)
+    in_specs, args = term_specs(terms, tile)
+    return pl.pallas_call(
+        functools.partial(project_body, [(len(left), dims) for left, _, dims in terms]),
+        grid=(pl.cdiv(width, tile),),
         in_specs=in_specs,
-        out_specs=[pl.BlockSpec((rows // count, tile), lambda j: (0, j))] * count,
-        out_shape=[out] * count,
+        out_specs=pl.BlockSpec((rows, tile), lambda j: (0, j)),
+        out_shape=jax.ShapeDtypeStruct((rows, width), dtype),
         compiler_params=pltpu.CompilerParams(vmem_limit_bytes=60 << 20),
         cost_estimate=cost(
-            flops=flops, bytes_accessed=sum(2 * a.size for a in args) + 2 * rows * width, transcendentals=0
+            flops=2 * rows * width * sum(left[0].shape[1] for left, _, _ in terms),
+            bytes_accessed=sum(2 * a.size for a in args) + 2 * rows * width,
+            transcendentals=0,
         ),
         name="project",
     )(*args)
-    return tuple(result) if split else result[0]
+
+
+def pair_body(terms, steps, *refs):
+    at, lefts, weights = 0, [], []
+    for pieces, dims in terms:
+        lefts.append(refs[at : at + pieces])
+        weights.append((refs[at + pieces], dims))
+        at += pieces + 1
+    out_ref, mine_s, away_s, got_s, send_sem, recv_sem = refs[at:]
+    rows = out_ref.shape[0]
+    tile = mine_s.shape[2]
+    step = pl.program_id(0)
+    me = lax.axis_index("tensor")
+    mate = {"tensor": me + 1 - 2 * (me % 2)}
+
+    @pl.when(step == 0)
+    def _():
+        barrier = pltpu.get_barrier_semaphore()
+        pl.semaphore_signal(barrier, inc=1, device_id=mate, device_id_type=pl.DeviceIdType.MESH)
+        pl.semaphore_wait(barrier, 1)
+
+    def copy(index):
+        return pltpu.make_async_remote_copy(
+            src_ref=away_s.at[index],
+            dst_ref=got_s.at[index],
+            send_sem=send_sem.at[index],
+            recv_sem=recv_sem.at[index],
+            device_id=mate,
+            device_id_type=pl.DeviceIdType.MESH,
+        )
+
+    away_s[step] = product(lefts, weights, 1, rows).astype(jnp.bfloat16)
+    copy(step).start()
+    mine_s[step] = product(lefts, weights, 0, rows)
+
+    @pl.when(step == steps - 1)
+    def _():
+        for index in range(steps):
+            copy(index).wait()
+            total = mine_s[index] + got_s[index].astype(jnp.float32)
+            out_ref[:, index * tile : (index + 1) * tile] = total.astype(out_ref.dtype)
+
+
+def pair_sum(terms, ident, dtype):
+    terms = terms_of(terms)
+    rows = sum(piece.shape[0] for piece in terms[0][0]) // 2
+    width = terms[0][1].shape[0 if terms[0][2] is NT else 1]
+    tile = min(512, width)
+    steps = width // tile
+    in_specs, args = term_specs(terms, tile)
+    return pl.pallas_call(
+        functools.partial(pair_body, [(len(left), dims) for left, _, dims in terms], steps),
+        grid=(steps,),
+        in_specs=in_specs,
+        out_specs=whole((rows, width)),
+        out_shape=jax.ShapeDtypeStruct((rows, width), dtype),
+        scratch_shapes=[
+            pltpu.VMEM((steps, rows, tile), jnp.float32),
+            pltpu.VMEM((steps, rows, tile), jnp.bfloat16),
+            pltpu.VMEM((steps, rows, tile), jnp.bfloat16),
+            pltpu.SemaphoreType.DMA((steps,)),
+            pltpu.SemaphoreType.DMA((steps,)),
+        ],
+        compiler_params=pltpu.CompilerParams(vmem_limit_bytes=60 << 20, collective_id=ident),
+        cost_estimate=cost(
+            flops=4 * rows * width * sum(left[0].shape[1] for left, _, _ in terms),
+            bytes_accessed=sum(2 * a.size for a in args) + 4 * rows * width,
+            transcendentals=0,
+        ),
+        name="pair_sum",
+    )(*args)
 
 
 def row_tables(length_row, group_row, mask_row):
@@ -434,94 +563,61 @@
 
 
 class WeightGrad:
-    def __init__(self, pieces, rights, start=1):
-        self.pieces, self.rights = pieces, rights
-        self.size, self.rank = lax.axis_size("dp"), lax.axis_index("dp").astype(jnp.int32)
-        self.start = start
+    def __init__(self, rank, pieces, mats, start=1):
+        self.rank, self.pieces, self.mats, self.start = rank, pieces, mats, start
+        self.size = lax.axis_size("dp")
         self.tile = pieces[0].shape[1] // self.size
-        self.width = sum(near.shape[1] for near in rights[::2])
         self.kernel = self.tile % 128 == 0
-
-    def order(self):
-        place = jnp.arange(self.size // 2, dtype=jnp.int32)
-        blocks = place // self.start * (2 * self.start) + place % self.start
-        side = (self.rank // self.start) % 2
-        return blocks + self.start * (1 - side), blocks + self.start * side
-
-    def compute(self, *groups):
-        named = dict(zip(("send", "own"), self.order()))
-        lists = [named[kind][first : first + count] for kind, first, count in groups]
-        if self.kernel:
-            order = jnp.concatenate(lists)
-            return grad_call(order, [count for _, _, count in groups], self.pieces, self.rights, self.tile)
-        left = jnp.concatenate(self.pieces, axis=0)
-        sides = [jnp.concatenate(side, axis=1) for side in (self.rights[::2], self.rights[1::2])]
-        full = lax.dot_general(left, jnp.concatenate(sides, axis=0), TN, preferred_element_type=jnp.float32)
-        full = full.astype(jnp.bfloat16).reshape(self.size, self.tile, self.width)
-        return [jnp.take(full, indices, axis=0) for indices in lists]
-
-    def halve(self, blocks, bits, bit):
-        low = 2 ** bits.index(bit)
-        pairs = blocks.reshape((blocks.shape[0] // (2 * low), 2, low) + blocks.shape[1:])
-        side = (self.rank // bit) % 2
-        away, kept = (
-            lax.dynamic_index_in_dim(pairs, at, axis=1, keepdims=False).reshape((-1,) + blocks.shape[1:])
-            for at in (1 - side, side)
-        )
-        return away.astype(jnp.bfloat16), kept
 
     def bits(self):
         return [2**i for i in range(self.size.bit_length() - 1)]
 
-    def finish(self, kept, got, bits, todo):
-        while True:
-            kept = kept.astype(jnp.float32) + got.astype(jnp.float32)
-            if not todo:
-                return kept.reshape(self.tile, self.width)
-            away, kept = self.halve(kept, bits, todo[0])
-            got = exchange(away, "dp", todo[0])
-            bits = [b for b in bits if b != todo[0]]
-            todo = todo[1:]
-
-    def after_start(self, own, got):
-        left = [b for b in self.bits() if b != self.start]
-        return self.finish(own, got, left, left)
-
-    def step(self, own, got, bits, bit):
-        total = own.astype(jnp.float32) + got.astype(jnp.float32)
-        away, kept = self.halve(total, bits, bit)
-        return away, kept, [b for b in bits if b != bit]
-
-    def second(self, own, got):
-        total = own.astype(jnp.float32) + got.astype(jnp.float32)
-        return self.halve(total, self.bits()[1:-1], 2)
-
-    def third(self, kept, gots):
-        first, second = (k + g.astype(jnp.float32) for k, g in zip(kept, gots))
-        top = self.rank // (self.size // 2) == 1
-        return jnp.where(top, first, second).astype(jnp.bfloat16), jnp.where(top, second, first)
-
-    def last(self, kept, got):
-        left = self.bits()[2:-1]
-        return self.finish(kept, got, left, left)
+    def compute(self, *sides):
+        if self.kernel:
+            outs = grad_call(self.rank, self.pieces, self.mats, self.start, sides, self.tile)
+        else:
+            left = jnp.concatenate(self.pieces, axis=0)
+            place = jnp.arange(self.size // 2, dtype=jnp.int32)
+            bit = self.rank[0] // self.start % 2
+            fulls = [
+                lax.dot_general(left, jnp.concatenate(mat, axis=0), TN, preferred_element_type=jnp.float32)
+                .astype(jnp.bfloat16)
+                .reshape(self.size, self.tile, -1)
+                for mat in self.mats
+            ]
+            outs = [
+                jnp.take(full, block_at(place, self.start, (bit + side) % 2), axis=0) for side in sides for full in fulls
+            ]
+        return tuple(outs)
+
+
+class Halving:
+    def __init__(self, rank, own, start=1):
+        self.rank, self.kept = rank, own
+        self.size = lax.axis_size("dp")
+        self.left = [2**i for i in range(self.size.bit_length() - 1) if 2**i != start]
+
+    def merge(self, got, bit):
+        low = 2 ** self.left.index(bit)
+        self.left.remove(bit)
+        if got.shape[1] % 128 == 0:
+            away, self.kept = merge_call(self.rank, self.kept, got, low, bit)
+            return away
+        total = self.kept.astype(jnp.float32) + got.astype(jnp.float32)
+        place = jnp.arange(total.shape[0] // 2, dtype=jnp.int32)
+        side = self.rank[0] // bit % 2
+        self.kept = jnp.take(total, block_at(place, low, side), axis=0)
+        return jnp.take(total, block_at(place, low, 1 - side), axis=0).astype(jnp.bfloat16)
+
+    def finish(self, got):
+        while self.left:
+            bit = self.left[0]
+            got = exchange(self.merge(got, bit), "dp", bit)
+        return (self.kept.astype(jnp.float32) + got.astype(jnp.float32))[0]
 
 
 def hop(values, bit):
     return exchange(values, "dp", bit)
-
-
-def send_far(far):
-    mine, others = far
-    return (mine.astype(jnp.float32) + exchange(others, "tensor", 1).astype(jnp.float32)).astype(jnp.bfloat16)
-
-
-def sum_near(near, got):
-    mine, others = near
-    return (
-        mine.astype(jnp.float32)
-        + exchange(others, "tensor", 1).astype(jnp.float32)
-        + got.astype(jnp.float32)
-    )
 
 
 def shards(
@@ -543,6 +639,7 @@
     rows_local = hidden_in.shape[0]
     rank = lax.axis_index("tensor").astype(jnp.int32)
     rank_ref = rank[None]
+    dp_rank = lax.axis_index("dp").astype(jnp.int32)[None]
 
     def to_far(values):
         return exchange(values, "tensor", 2)
@@ -577,115 +674,100 @@
     far = qkv_pair(2, rank_ref, a2, a3, cosine, sine, w_query, w_key, w_value)
     qs, ks, vs = zip(near, far)
     heads_near, heads_far, lse = attend(rank_ref, qs, ks, vs, low, high)
-    heads_far, c2 = tie(heads_far, c2)
+    y1 = pair_sum([(heads_far, w_out, False)], 0, jnp.bfloat16)
+    heads_n, c1, c2, y1 = tie(heads_near, c1, c2, y1)
+    got = to_far(y1)
     c3 = to_mate(c2)
-    got = to_far(send_far(project([(heads_far, w_out, False)], True)))
-    mid_h = x_f + sum_near(project([(heads_near, w_out, False)], True), got)
+    mine = pair_sum([(heads_n, w_out, False)], 1, jnp.float32)
+    dm_near = project([((c0, c1), w_down, True)], jnp.float32)
+    dm_far = project([((c2, c3), w_down, True)], jnp.float32)
+    mid_h = x_f + mine + got.astype(jnp.float32)
     inv_b = lax.rsqrt(jnp.mean(mid_h * mid_h, axis=-1, keepdims=True) + epsilon)
     b0 = (mid_h * inv_b * gain_mlp).astype(jnp.bfloat16)
-    b0, c3 = tie(b0, c3)
+    b0, dm_near, dm_far = tie(b0, dm_near, dm_far)
     b2 = to_far(b0)
     b1 = to_mate(b0)
-    mid_near, dg_near, du_near = mlp_pair(b0, b1, c0, c1, w_gate, w_up, w_down)
+    mid_near, dg_near, du_near = mlp_pair(b0, b1, dm_near, w_gate, w_up)
     b2, mid_near, dg_near, du_near = tie(b2, mid_near, dg_near, du_near)
     b3 = to_mate(b2)
-    mid_far, dg_far, du_far = mlp_pair(b2, b3, c2, c3, w_gate, w_up, w_down)
+    mid_far, dg_far, du_far = mlp_pair(b2, b3, dm_far, w_gate, w_up)
 
     half = lax.axis_size("dp") // 2
-    part = half // 2
     b_all, c_all = (b0, b1, b2, b3), (c0, c1, c2, c3)
-    grad_down = WeightGrad(c_all, (mid_near, mid_far))
-    grad_gate = WeightGrad(b_all, (dg_near, dg_far), 2)
-    grad_up = WeightGrad(b_all, (du_near, du_far))
-    sends, owns = ("send", 0, half), ("own", 0, half)
-    both = (("send", 0, part), ("send", part, part), ("own", 0, part), ("own", part, part))
-    (down_send,) = grad_down.compute(sends)
-    (gate_send,) = grad_gate.compute(sends)
-    dg_f, du_f, down_send, gate_send = tie(dg_far, du_far, down_send, gate_send)
+    grad_down = WeightGrad(dp_rank, c_all, [(mid_near, mid_far)])
+    grad_gate = WeightGrad(dp_rank, b_all, [(dg_near, dg_far)], 2)
+    (down_send,) = grad_down.compute(1)
+    dg_f, du_f, down_send = tie(dg_far, du_far, down_send)
     down_got = hop(down_send, 1)
+    (gate_send,) = grad_gate.compute(1)
+    y5 = pair_sum([(dg_f, w_gate, True), (du_f, w_up, True)], 2, jnp.bfloat16)
+    dg_n, du_n, y5 = tie(dg_near, du_near, y5)
     gate_got = hop(gate_send, 2)
-    y5 = send_far(project([(dg_f, w_gate, True), (du_f, w_up, True)], True))
     got = to_far(y5)
-    dg_n, du_n, y5 = tie(dg_near, du_near, y5)
-    d_b = sum_near(project([(dg_n, w_gate, True), (du_n, w_up, True)], True), got)
-    (down_own,) = grad_down.compute(owns)
-    (gate_own,) = grad_gate.compute(owns)
-    d_b, down_got, gate_got, down_own, gate_own = tie(d_b, down_got, gate_got, down_own, gate_own)
-
-    away, down_own, down_bits = grad_down.step(down_own, down_got, grad_down.bits()[1:], 2)
-    down_got = hop(away, 2)
-    away, gate_own, gate_bits = grad_gate.step(
-        gate_own, gate_got, [b for b in grad_gate.bits() if b != 2], 1
-    )
-    gate_got = hop(away, 1)
+    d_b = pair_sum([(dg_n, w_gate, True), (du_n, w_up, True)], 3, jnp.float32) + got.astype(jnp.float32)
+    (up_send,) = WeightGrad(dp_rank, b_all, [(du_n, du_far)]).compute(1)
+    d_b, up_send = tie(d_b, up_send)
+
     n_b = mid_h * inv_b
     gain_mlp_part = jnp.sum(d_b * n_b, axis=0)
     e_b = d_b * gain_mlp
     weighted = cotangent.astype(jnp.float32) * weight_local[:, None]
     d_h = weighted + inv_b * (e_b - n_b * jnp.mean(e_b * n_b, axis=-1, keepdims=True))
     t0 = d_h.astype(jnp.bfloat16)
+    t0, mid_f, dg_n, du_n = tie(t0, mid_far, dg_near, du_near)
     t2 = to_far(t0)
     t1 = to_mate(t0)
-    gs_near = project([((t0, t1), w_out, True)], False)
-    up0, up1, own_u0, own_u1 = grad_up.compute(*both)
-    t2, down_got, gate_got, gs_near, up0, up1 = tie(t2, down_got, gate_got, gs_near, up0, up1)
-
-    up0_got = hop(up0, 1)
-    away, gate_own, gate_bits = grad_gate.step(gate_own, gate_got, gate_bits, 4)
-    gate_got = hop(away, 4)
+    gs_near = project([((t0, t1), w_out, True)])
+    y8 = pair_sum([(mid_f, w_down, False)], 4, jnp.bfloat16)
+    (down_own,) = WeightGrad(dp_rank, c_all, [(mid_near, mid_f)]).compute(0)
+    (gate_own,) = WeightGrad(dp_rank, b_all, [(dg_n, dg_far)], 2).compute(0)
+    t2, down_got, gate_got, gs_near, y8, down_own, gate_own = tie(t2, down_got, gate_got, gs_near, y8, down_own, gate_own)
+
+    up_got = hop(up_send, 1)
+    got8 = to_far(y8)
+    down, gate = Halving(dp_rank, down_own), Halving(dp_rank, gate_own, 2)
+    down_got = hop(down.merge(down_got, 2), 2)
     t3 = to_mate(t2)
-    gs_far = project([((t2, t3), w_out, True)], False)
-    y8 = send_far(project([(mid_far, w_down, False)], True))
-    gs_far, y8 = tie(gs_far, y8)
-    got8 = to_far(y8)
+    gs_far = project([((t2, t3), w_out, True)])
+    gate_away = gate.merge(gate_got, 1)
+    out_send, out_own = WeightGrad(dp_rank, (t0, t1, t2, t3), [(heads_near, heads_far)]).compute(1, 0)
     dqn, dqf, dkn, dkf, dvn, dvf = attend_back(
         rank_ref, qs, ks, vs, (gs_near, gs_far), low, high, lse, cosine, back_sine
     )
-    dqf, dkf, dvf, up0_got, gate_got, got8 = tie(dqf, dkf, dvf, up0_got, gate_got, got8)
-
-    up1_got = hop(up1, 1)
-    away, down_own, down_bits = grad_down.step(down_own, down_got, down_bits, 4)
-    down_got = hop(away, 4)
-    away, kept_u0 = grad_up.second(own_u0, up0_got)
-    z_up0 = hop(away, 2)
-    y7 = send_far(project([(dqf, w_query, True), (dkf, w_key, True), (dvf, w_value, True)], True))
+    dqf, dkf, dvf, down_got, got8, out_send, gate_away = tie(dqf, dkf, dvf, down_got, got8, out_send, gate_away)
+
+    out_got = hop(out_send, 1)
+    y7 = pair_sum([(dqf, w_query, True), (dkf, w_key, True), (dvf, w_value, True)], 6, jnp.bfloat16)
+    dqn, dkn, dvn, dun, y7 = tie(dqn, dkn, dvn, du_near, y7)
     got = to_far(y7)
-    dqn, dkn, dvn, y7 = tie(dqn, dkn, dvn, y7)
-    d_a = sum_near(project([(dqn, w_query, True), (dkn, w_key, True), (dvn, w_value, True)], True), got)
-    a_all = (a0, a1, a2, a3)
-    grad_out = WeightGrad((t0, t1, t2, t3), (heads_near, heads_far))
-    grad_v = WeightGrad(a_all, (dvn, dvf), 2)
-    grad_q, grad_k = (WeightGrad(a_all, rights) for rights in ((dqn, dqf), (dkn, dkf)))
-    v_send, v_own = grad_v.compute(sends, owns)
-    q_send, q_own = grad_q.compute(sends, owns)
-    k_send, k_own = grad_k.compute(sends, owns)
-    d_a, up1_got, down_got, z_up0, v_send, q_send, k_send = tie(
-        d_a, up1_got, down_got, z_up0, v_send, q_send, k_send
+    grad_qkv = WeightGrad(dp_rank, (a0, a1, a2, a3), [(dqn, dqf), (dkn, dkf), (dvn, dvf)])
+    *sends, q_own, k_own, v_own = grad_qkv.compute(1, 0)
+    down_got = hop(down.merge(down_got, half), half)
+    d_a = pair_sum([(dqn, w_query, True), (dkn, w_key, True), (dvn, w_value, True)], 7, jnp.float32) + got.astype(jnp.float32)
+    (up_own,) = WeightGrad(dp_rank, b_all, [(dun, du_far)]).compute(0)
+    d_a, up_own, up_got, out_got, gate_away, down_got, *sends = tie(
+        d_a, up_own, up_got, out_got, gate_away, down_got, *sends
     )
 
-    q_got = hop(q_send, 1)
-    v_got = hop(v_send, 2)
-    away, kept_u1 = grad_up.second(own_u1, up1_got)
-    z_up1 = hop(away, 2)
-    out_send, out_own = grad_out.compute(sends, owns)
-    output = (mid_h + sum_near(project([(mid_near, w_down, False)], True), got8)).astype(jnp.bfloat16)
+    gate_got = hop(gate_away, 1)
+    up = Halving(dp_rank, up_own)
+    up_got = hop(up.merge(up_got, 2), 2)
+    output = (mid_h + pair_sum([(mid_near, w_down, False)], 5, jnp.float32) + got8.astype(jnp.float32)).astype(jnp.bfloat16)
     n_a = x_f * inv_a
     gain_attn_part = jnp.sum(d_a * n_a, axis=0)
     e_a = d_a * gain_attn
     grad_input = d_h + inv_a * (e_a - n_a * jnp.mean(e_a * n_a, axis=-1, keepdims=True))
     gains = jnp.stack([gain_attn_part, gain_mlp_part])
     gains = butterfly_sum(scatter_small(gains.reshape(2, lax.axis_size("dp"), -1), "dp"), "tensor")
-    sum_down = grad_down.finish(down_own, down_got, down_bits, down_bits)
-    sum_gate = grad_gate.finish(gate_own, gate_got, gate_bits, gate_bits)
-    u_away, u_kept = grad_up.third((kept_u0, kept_u1), (z_up0, z_up1))
-    sum_up = grad_up.last(u_kept, hop(u_away, half))
-    k_got = hop(tie(k_send, q_got)[0], 1)
-    out_got = hop(tie(out_send, k_got)[0], 1)
-    sum_out = grad_out.after_start(out_own, out_got)
-    sums = [
-        grad.after_start(own, got)
-        for grad, own, got in ((grad_q, q_own, q_got), (grad_k, k_own, k_got), (grad_v, v_own, v_got))
-    ]
+    sum_down = down.finish(down_got)
+    sum_gate = gate.finish(gate_got)
+    sum_up = up.finish(up_got)
+    sum_out = Halving(dp_rank, out_own).finish(out_got)
+    sums, last = [], gate_got
+    for send, own in zip(sends, (q_own, k_own, v_own)):
+        send, last = tie(send, last)
+        last = hop(send, 1)
+        sums.append(Halving(dp_rank, own).finish(last))
     return (
         output,
         grad_input,

time: 620 us -> 605 us (0.976)
  other arithmetic: 80.9 us -> 46.4 us
  waiting for transfers between devices: 167 us -> 199 us
  Pallas kernels: 263 us -> 289 us
  local copies, waits for them, and re-layouts: 37 us -> 15.8 us
  starting transfers between devices: 63.9 us -> 47.2 us
    pallas_call x9 -> x30, Pallas kernels: 95.4 us -> 178 us  [the longest x8 83.8 us: pair_sum(): pl.pallas_call(functools.partial(pair_body, [(len(left), dims) for left,...]
    pallas_call x10 -> x4, Pallas kernels: 76.4 us -> 26.5 us  [project(): pl.pallas_call(functools.partial(project_body, [(len(left), dims) for lef...]
    ppermute x55 -> x45, waiting for transfers between devices: 167 us -> 199 us  [exchange(): lax.ppermute(values, axis, [(rank, rank ^ bit) for rank in range(size)])]
    add x20 -> x2, other arithmetic: 28.8 us -> 6.51 us  [the longest x1 4.08 us: shards(): pair_sum([(dqn, w_query, True), (dkn, w_key, True), (dvn, w_value, True)]...]
    ppermute x55 -> x45, starting transfers between devices: 63.9 us -> 47.2 us  [exchange(): lax.ppermute(values, axis, [(rank, rank ^ bit) for rank in range(size)])]
    convert_element_type x12 -> x0, local copies, waits for them, and re-layouts: 9.68 us -> none  [halve(): return (away.astype(jnp.bfloat16), kept)]
    dynamic_slice x6 -> x0, local copies, waits for them, and re-layouts: 9.45 us -> none  [halve(): lax.dynamic_index_in_dim(pairs, at, axis=1, keepdims=False)]
    convert_element_type x6 -> x1, other arithmetic: 13.6 us -> 4.66 us  [shards(): (mid_h + pair_sum([(mid_near, w_down, False)], 5, jnp.float32) + got8.ast...]
  transfers between devices with their start and end apart: 55 -> 45, of which waited for: 20 -> 16; matrix products, arithmetic and copies ran while one was open for 16% -> 8% of each run, Pallas kernels for 34% -> 40%
where the time goes in v4:
time: 605 us; the launch traced here: 599 us
  Pallas kernels  289 us (48%)
  waiting for transfers between devices  199 us (33%)
  starting transfers between devices  47.2 us (8%)
  other arithmetic  46.4 us (8%)
  local copies, waits for them, and re-layouts  15.8 us (3%)
    ppermute x45, waiting for transfers between devices, exchange(): lax.ppermute(values, axis, [(rank, rank ^ bit) for rank in range(size)])  199 us
    pallas_call x8, Pallas kernels, pair_sum(): pl.pallas_call(functools.partial(pair_body, [(len(left), dims) for left,...  83.8 us
    pallas_call x8, Pallas kernels, grad_call(): pl.pallas_call(functools.partial(grad_body, len(pieces), widths, low, sid...  77 us
    ppermute x45, starting transfers between devices, exchange(): lax.ppermute(values, axis, [(rank, rank ^ bit) for rank in range(size)])  47.2 us
    pallas_call x2, Pallas kernels, mlp_pair(): pl.pallas_call(mlp_body, grid=(pl.cdiv(width, tile),), in_specs=[whole(xa...  29.4 us
    pallas_call x4, Pallas kernels, project(): pl.pallas_call(functools.partial(project_body, [(len(left), dims) for lef...  26.5 us
    pallas_call x1, Pallas kernels, attend_back(): pl.pallas_call(attend_back_body, grid_spec=pltpu.PrefetchScalarGridSpec(n...  22 us
    pallas_call x2, Pallas kernels, qkv_pair(): pl.pallas_call(functools.partial(qkv_body, first), grid_spec=pltpu.Prefet...  18.3 us
  transfers between devices with their start and end apart: 45, of which 16 were waited for; matrix products, arithmetic and copies ran while one was open for 8% of the time, Pallas kernels for 40%

profile of v4, /device:TPU:0, one launch (start us, length us, event | category | flops | bytes accessed | tf_op | source)
XLA Modules:
  0.0 599.4 jit_solution(4968014952640841454)
XLA Ops:
  25.4 9.4 %qkv.2 = (bf16[640,512]{1,0:T(8,128)(2,1)}, bf16[640,512]{1,0:T(8,128)(2,1)}, bf16[640,512]{1,0:T(8,128)(2,1)}) custom-call(s32[1]{0:T(128)} %bitcast.rank_ref, bf16[320,2048]{1,0:T(8,128)(2,1)} %copy-done.28, bf16[320,2048]{1,0:T(8,128)(2,1)} %copy-done.30, f32[1280,128]{1,0:T(8,128)} %pad_maximum_fusion.cos_ref, f32[1280,128]{1,0:T(8,128)} %get-tuple-element.275.sin_ref, ...), custom_call_target="tpu_custom_call" | custom-call | flops 4026531 | bytes 8912 | tf_op jit(solution)/shard_map/qkv/pallas_call | solution.py:67
  41.2 8.9 %qkv.3 = (bf16[640,512]{1,0:T(8,128)(2,1)}, bf16[640,512]{1,0:T(8,128)(2,1)}, bf16[640,512]{1,0:T(8,128)(2,1)}) custom-call(s32[1]{0:T(128)} %bitcast.rank_ref, bf16[320,2048]{1,0:T(8,128)(2,1)} %collective-permute-done.xa_ref.refs_2_, bf16[320,2048]{1,0:T(8,128)(2,1)} %copy-done.31, f32[1280,128]{1,0:T(8,128)} %pad_maximum_fusion.cos_ref, ...), custom_call_target="tpu_custom_call" | custom-call | flops 4026531 | bytes 8912 | tf_op jit(solution)/shard_map/qkv/pallas_call | solution.py:67
  50.1 14.6 %attend.1 = (bf16[640,512]{1,0:T(8,128)(2,1)}, bf16[640,512]{1,0:T(8,128)(2,1)}, f32[4,1,1280]{2,1,0:T(1,128)}) custom-call(s32[1]{0:T(128)} %bitcast.rank_ref, bf16[640,512]{1,0:T(8,128)(2,1)} %get-tuple-element.129.qn, bf16[640,512]{1,0:T(8,128)(2,1)} %get-tuple-element.131.qf, bf16[640,512]{1,0:T(8,128)(2,1)} %get-tuple-element.132.kn, ...), custom_call_target="tpu_custom_call" | custom-call | flops 6710886 | bytes 5242 | tf_op jit(solution)/shard_map/attend/pallas_call | solution.py:128
  64.6 6.9 %pair_sum.8 = bf16[320,2048]{1,0:T(8,128)(2,1)} custom-call(bf16[640,512]{1,0:T(8,128)(2,1)} %get-tuple-element.138.refs_0_.refs_5_, bf16[512,2048]{1,0:T(8,128)(2,1)} %refs_2_.7), custom_call_target="tpu_custom_call" | custom-call | flops 1342177 | bytes 5373 | tf_op jit(solution)/shard_map/pair_sum/pallas_call | solution.py:478
  73.2 7.4 %pair_sum.9 = f32[320,2048]{1,0:T(8,128)} custom-call(bf16[640,512]{1,0:T(8,128)(2,1)} %get-tuple-element.139.refs_0_.refs_4_, bf16[512,2048]{1,0:T(8,128)(2,1)} %refs_2_.7), custom_call_target="tpu_custom_call" | custom-call | flops 1342177 | bytes 5373 | tf_op jit(solution)/shard_map/pair_sum/pallas_call | solution.py:478
  80.6 8.3 %project.4.dm_ref = f32[640,1408]{1,0:T(8,128)} custom-call(bf16[320,2048]{1,0:T(8,128)(2,1)} %copy-done.26, bf16[320,2048]{1,0:T(8,128)(2,1)} %copy-done.27, bf16[1408,2048]{1,0:T(8,128)(2,1)} %refs_1_.13), custom_call_target="tpu_custom_call" | custom-call | flops 3690987 | bytes 10190 | tf_op jit(solution)/shard_map/project/pallas_call | solution.py:414
  88.9 13.9 %collective-permute-done.8 = bf16[320,2048]{1,0:T(8,128)(2,1)} collective-permute-done((bf16[320,2048]{1,0:T(8,128)(2,1)}, bf16[320,2048]{1,0:T(8,128)(2,1)}, u32[]{:S(2)}, u32[]{:S(2)}) %collective-permute-start.8) | collective-permute-done | bytes 1310752 | tf_op jit(solution)/shard_map/ppermute | solution.py:534
  102.8 3.1 multiply_reduce_fusion.2
  107.5 8.4 %project.5.dm_ref = f32[640,1408]{1,0:T(8,128)} custom-call(bf16[320,2048]{1,0:T(8,128)(2,1)} %collective-permute-done.7.refs_0_.refs_2_, bf16[320,2048]{1,0:T(8,128)(2,1)} %collective-permute-done.9.refs_1_.refs_3_, bf16[1408,2048]{1,0:T(8,128)(2,1)} %refs_1_.13), custom_call_target="tpu_custom_call" | custom-call | flops 3690987 | bytes 10190 | tf_op jit(solution)/shard_map/project/pallas_call | solution.py:414
  119.3 14.8 %mlp.2 = (bf16[640,1408]{1,0:T(8,128)(2,1)}, bf16[640,1408]{1,0:T(8,128)(2,1)}, bf16[640,1408]{1,0:T(8,128)(2,1)}) custom-call(bf16[320,2048]{1,0:T(8,128)(2,1)} %multiply_convert_fusion.xa_ref.refs_0_, bf16[320,2048]{1,0:T(8,128)(2,1)} %collective-permute-done.11.xb_ref.refs_1_, f32[640,1408]{1,0:T(8,128)} %project.4.dm_ref, bf16[2048,1408]{1,0:T(8,128)(2,1)} %refs_1_.12, ...), custom_call_target="tpu_custom_call" | custom-call | flops 7381975 | bytes 23166 | tf_op jit(solution)/shard_map/mlp/pallas_call | solution.py:234
  134.1 13.3 %collective-permute-done.10.xa_ref.refs_2_ = bf16[320,2048]{1,0:T(8,128)(2,1)} collective-permute-done((bf16[320,2048]{1,0:T(8,128)(2,1)}, bf16[320,2048]{1,0:T(8,128)(2,1)}, u32[]{:S(2)}, u32[]{:S(2)}) %collective-permute-start.10) | collective-permute-done | bytes 1310752 | tf_op jit(solution)/shard_map/ppermute | solution.py:534
  147.4 3.4 collective-permute-done.12.xb_ref.refs_3_
  150.8 14.6 %mlp.3 = (bf16[640,1408]{1,0:T(8,128)(2,1)}, bf16[640,1408]{1,0:T(8,128)(2,1)}, bf16[640,1408]{1,0:T(8,128)(2,1)}) custom-call(bf16[320,2048]{1,0:T(8,128)(2,1)} %collective-permute-done.10.xa_ref.refs_2_, bf16[320,2048]{1,0:T(8,128)(2,1)} %collective-permute-done.12.xb_ref.refs_3_, f32[640,1408]{1,0:T(8,128)} %project.5.dm_ref, ...), custom_call_target="tpu_custom_call" | custom-call | flops 7381975 | bytes 23166 | tf_op jit(solution)/shard_map/mlp/pallas_call | solution.py:234
  165.4 8.8 %weight_grad.8 = bf16[4,256,1408]{2,1,0:T(8,128)(2,1)} custom-call(s32[1]{0:T(128)} %bitcast.7.rank_ref._, bf16[320,2048]{1,0:T(8,128)(2,1)} %copy-done.26, bf16[320,2048]{1,0:T(8,128)(2,1)} %copy-done.27, bf16[320,2048]{1,0:T(8,128)(2,1)} %collective-permute-done.7.refs_0_.refs_2_, bf16[320,2048]{1,0:T(8,128)(2,1)} %collective-permute-done.9.refs_1_.refs_3_, ...), custom_call_target="tpu_custom_call" | custom-call | flops 3690987 | bytes 9109 | tf_op jit(solution)/shard_map/weight_grad/pallas_call | solution.py:324
  174.2 14.3 %pair_sum.11 = bf16[320,2048]{1,0:T(8,128)(2,1)} custom-call(bf16[640,1408]{1,0:T(8,128)(2,1)} %get-tuple-element.156.refs_0_.refs_5_, bf16[2048,1408]{1,0:T(8,128)(2,1)} %refs_1_.12, bf16[640,1408]{1,0:T(8,128)(2,1)} %get-tuple-element.157.refs_2_.refs_5_, bf16[2048,1408]{1,0:T(8,128)(2,1)} %refs_3_.5), custom_call_target="tpu_custom_call" | custom-call | flops 7381975 | bytes 17760 | tf_op jit(solution)/shard_map/pair_sum/pallas_call | solution.py:478
  190.1 8.7 %weight_grad.10 = bf16[4,256,1408]{2,1,0:T(8,128)(2,1)} custom-call(s32[1]{0:T(128)} %bitcast.7.rank_ref._, bf16[320,2048]{1,0:T(8,128)(2,1)} %multiply_convert_fusion.xa_ref.refs_0_, bf16[320,2048]{1,0:T(8,128)(2,1)} %collective-permute-done.11.xb_ref.refs_1_, bf16[320,2048]{1,0:T(8,128)(2,1)} %collective-permute-done.10.xa_ref.refs_2_, ...), custom_call_target="tpu_custom_call" | custom-call | flops 3690987 | bytes 9109 | tf_op jit(solution)/shard_map/weight_grad/pallas_call | solution.py:324
  201.8 8.7 %weight_grad.9 = bf16[4,256,1408]{2,1,0:T(8,128)(2,1)} custom-call(s32[1]{0:T(128)} %bitcast.7.rank_ref._, bf16[320,2048]{1,0:T(8,128)(2,1)} %multiply_convert_fusion.xa_ref.refs_0_, bf16[320,2048]{1,0:T(8,128)(2,1)} %collective-permute-done.11.xb_ref.refs_1_, bf16[320,2048]{1,0:T(8,128)(2,1)} %collective-permute-done.10.xa_ref.refs_2_, ...), custom_call_target="tpu_custom_call" | custom-call | flops 3690987 | bytes 9109 | tf_op jit(solution)/shard_map/weight_grad/pallas_call | solution.py:324
  210.5 14.9 %pair_sum.12 = f32[320,2048]{1,0:T(8,128)} custom-call(bf16[640,1408]{1,0:T(8,128)(2,1)} %get-tuple-element.165.refs_0_.refs_4_, bf16[2048,1408]{1,0:T(8,128)(2,1)} %refs_1_.12, bf16[640,1408]{1,0:T(8,128)(2,1)} %get-tuple-element.191.refs_2_.refs_4_, bf16[2048,1408]{1,0:T(8,128)(2,1)} %refs_3_.5), custom_call_target="tpu_custom_call" | custom-call | flops 7381975 | bytes 17760 | tf_op jit(solution)/shard_map/pair_sum/pallas_call | solution.py:478
  229.2 2.9 fusion.17
  232.8 9.6 %pair_sum.13 = bf16[320,2048]{1,0:T(8,128)(2,1)} custom-call(bf16[640,1408]{1,0:T(8,128)(2,1)} %get-tuple-element.164.refs_5_.refs_0_, bf16[1408,2048]{1,0:T(8,128)(2,1)} %refs_1_.13), custom_call_target="tpu_custom_call" | custom-call | flops 3690987 | bytes 10190 | tf_op jit(solution)/shard_map/pair_sum/pallas_call | solution.py:478
  242.4 8.7 %weight_grad.11.own_away.own_kept = bf16[4,256,1408]{2,1,0:T(8,128)(2,1)} custom-call(s32[1]{0:T(128)} %bitcast.7.rank_ref._, bf16[320,2048]{1,0:T(8,128)(2,1)} %copy-done.26, bf16[320,2048]{1,0:T(8,128)(2,1)} %copy-done.27, bf16[320,2048]{1,0:T(8,128)(2,1)} %collective-permute-done.7.refs_0_.refs_2_, ...), custom_call_target="tpu_custom_call" | custom-call | flops 3690987 | bytes 9109 | tf_op jit(solution)/shard_map/weight_grad/pallas_call | solution.py:324
  251.1 8.8 %weight_grad.12.own_away.own_kept = bf16[4,256,1408]{2,1,0:T(8,128)(2,1)} custom-call(s32[1]{0:T(128)} %bitcast.7.rank_ref._, bf16[320,2048]{1,0:T(8,128)(2,1)} %multiply_convert_fusion.xa_ref.refs_0_, bf16[320,2048]{1,0:T(8,128)(2,1)} %collective-permute-done.11.xb_ref.refs_1_, bf16[320,2048]{1,0:T(8,128)(2,1)} %collective-permute-done.10.xa_ref.refs_2_, ...), custom_call_target="tpu_custom_call" | custom-call | flops 3690987 | bytes 9109 | tf_op jit(solution)/shard_map/weight_grad/pallas_call | solution.py:324
  259.9 4.9 project.6.gn
  264.9 3.0 merge.14
  271.5 2.8 merge.15
  275.4 4.8 project.7.gf
  280.2 9.3 %weight_grad.13 = (bf16[4,256,512]{2,1,0:T(8,128)(2,1)}, bf16[4,256,512]{2,1,0:T(8,128)(2,1)}) custom-call(s32[1]{0:T(128)} %bitcast.7.rank_ref._, bf16[320,2048]{1,0:T(8,128)(2,1)} %get-tuple-element.162.refs_0_, bf16[320,2048]{1,0:T(8,128)(2,1)} %collective-permute-done.17.refs_1_, bf16[320,2048]{1,0:T(8,128)(2,1)} %collective-permute-done.14.refs_0_.refs_2_, ...), custom_call_target="tpu_custom_call" | custom-call | flops 2684354 | bytes 8650 | tf_op jit(solution)/shard_map/weight_grad/pallas_call | solution.py:324
  289.5 22.0 %attend_back.1 = (bf16[640,512]{1,0:T(8,128)(2,1)}, bf16[640,512]{1,0:T(8,128)(2,1)}, bf16[640,512]{1,0:T(8,128)(2,1)}, bf16[640,512]{1,0:T(8,128)(2,1)}, bf16[6...) custom-call(s32[1]{0:T(128)} %bitcast.rank_ref, bf16[640,512]{1,0:T(8,128)(2,1)} %get-tuple-element.129.qn, ...), custom_call_target="tpu_custom_call" | custom-call | flops 16777216 | bytes 10485 | tf_op jit(solution)/shard_map/attend_back/pallas_call | solution.py:191
  311.5 10.1 %pair_sum.14 = bf16[320,2048]{1,0:T(8,128)(2,1)} custom-call(bf16[640,512]{1,0:T(8,128)(2,1)} %get-tuple-element.184.refs_0_.refs_5_, bf16[2048,512]{1,0:T(8,128)(2,1)} %refs_1_.15, bf16[640,512]{1,0:T(8,128)(2,1)} %get-tuple-element.185.refs_2_.refs_7_, bf16[2048,512]{1,0:T(8,128)(2,1)} %refs_3_.7, bf16[640,512]{1,0:T(8,128)(2,1)} %get-tuple-element.186.refs_4_.refs_9_, ...), custom_call_target="tpu_custom_call" | custom-call | flops 4026531 | bytes 10878 | tf_op jit(solution)/shard_map/pair_sum/pallas_call | solution.py:478
  328.3 2.6 collective-permute-start.24
  330.8 8.7 %weight_grad.14.own_away.own_kept = bf16[4,256,1408]{2,1,0:T(8,128)(2,1)} custom-call(s32[1]{0:T(128)} %bitcast.7.rank_ref._, bf16[320,2048]{1,0:T(8,128)(2,1)} %multiply_convert_fusion.xa_ref.refs_0_, bf16[320,2048]{1,0:T(8,128)(2,1)} %collective-permute-done.11.xb_ref.refs_1_, bf16[320,2048]{1,0:T(8,128)(2,1)} %collective-permute-done.10.xa_ref.refs_2_, ...), custom_call_target="tpu_custom_call" | custom-call | flops 3690987 | bytes 9109 | tf_op jit(solution)/shard_map/weight_grad/pallas_call | solution.py:324
  339.5 10.5 %pair_sum.15 = f32[320,2048]{1,0:T(8,128)} custom-call(bf16[640,512]{1,0:T(8,128)(2,1)} %get-tuple-element.187.refs_0_.refs_4_, bf16[2048,512]{1,0:T(8,128)(2,1)} %refs_1_.15, bf16[640,512]{1,0:T(8,128)(2,1)} %get-tuple-element.188.refs_2_.refs_6_, bf16[2048,512]{1,0:T(8,128)(2,1)} %refs_3_.7, bf16[640,512]{1,0:T(8,128)(2,1)} %get-tuple-element.189.refs_4_.refs_8_, ...), custom_call_target="tpu_custom_call" | custom-call | flops 4026531 | bytes 10878 | tf_op jit(solution)/shard_map/pair_sum/pallas_call | solution.py:478
  350.0 15.3 %weight_grad.15 = (bf16[4,256,512]{2,1,0:T(8,128)(2,1)}, bf16[4,256,512]{2,1,0:T(8,128)(2,1)}, bf16[4,256,512]{2,1,0:T(8,128)(2,1)}, bf16[4,256,512]{2,1,0:T(8,1...) custom-call(s32[1]{0:T(128)} %bitcast.7.rank_ref._, bf16[320,2048]{1,0:T(8,128)(2,1)} %copy-done.28, ...), custom_call_target="tpu_custom_call" | custom-call | flops 8053063 | bytes 15466 | tf_op jit(solution)/shard_map/weight_grad/pallas_call | solution.py:324
  365.4 4.1 convert_add_fusion.1
  370.8 2.9 fusion.9
  374.6 10.1 %pair_sum.10 = f32[320,2048]{1,0:T(8,128)} custom-call(bf16[640,1408]{1,0:T(8,128)(2,1)} %get-tuple-element.148.refs_0_.refs_4_, bf16[1408,2048]{1,0:T(8,128)(2,1)} %refs_1_.13), custom_call_target="tpu_custom_call" | custom-call | flops 3690987 | bytes 10190 | tf_op jit(solution)/shard_map/pair_sum/pallas_call | solution.py:478
  384.7 18.8 %collective-permute-done.25 = f32[2,4,256]{2,1,0:T(4,128)S(1)} collective-permute-done((f32[2,4,256]{2,1,0:T(4,128)S(1)}, f32[2,4,256]{2,1,0:T(4,128)S(1)}, u32[]{:S(2)}, u32[]{:S(2)}) %collective-permute-start.25) | collective-permute-done | bytes 8224 | tf_op jit(solution)/shard_map/ppermute | solution.py:534
  406.5 4.7 add_convert_fusion
  416.0 13.7 %collective-permute-done.31.got_away.got_kept = bf16[4,256,512]{2,1,0:T(8,128)(2,1)S(1)} collective-permute-done((bf16[4,256,512]{2,1,0:T(8,128)(2,1)}, bf16[4,256,512]{2,1,0:T(8,128)(2,1)S(1)}, u32[]{:S(2)}, u32[]{:S(2)}) %collective-permute-start.31) | collective-permute-done | bytes 1048608 | tf_op jit(solution)/shard_map/ppermute | solution.py:534
  430.9 22.7 %collective-permute-done.27 = f32[2,1,256]{2,1,0:T(1,128)S(1)} collective-permute-done((f32[2,1,256]{2,1,0:T(1,128)S(1)}, f32[2,1,256]{2,1,0:T(1,128)S(1)}, u32[]{:S(2)}, u32[]{:S(2)}) %collective-permute-start.27) | collective-permute-done | bytes 2080 | tf_op jit(solution)/shard_map/ppermute | solution.py:534
  457.9 3.4 collective-permute-start.41
  472.4 2.9 collective-permute-start.42
  475.3 30.0 %collective-permute-done.41 = bf16[1,256,512]{2,1,0:T(8,128)(2,1)} collective-permute-done((bf16[1,256,512]{2,1,0:T(8,128)(2,1)}, bf16[1,256,512]{2,1,0:T(8,128)(2,1)}, u32[]{:S(2)}, u32[]{:S(2)}) %collective-permute-start.41) | collective-permute-done | bytes 262176 | tf_op jit(solution)/shard_map/ppermute | solution.py:534
  512.0 8.8 %collective-permute-done.44 = bf16[1,256,1408]{2,1,0:T(8,128)(2,1)} collective-permute-done((bf16[1,256,1408]{2,1,0:T(8,128)(2,1)}, bf16[1,256,1408]{2,1,0:T(8,128)(2,1)}, u32[]{:S(2)}, u32[]{:S(2)}) %collective-permute-start.44) | collective-permute-done | bytes 720928 | tf_op jit(solution)/shard_map/ppermute | solution.py:534
  523.1 23.7 %collective-permute-done.32.got_away.got_kept = bf16[2,256,512]{2,1,0:T(8,128)(2,1)S(1)} collective-permute-done((bf16[2,256,512]{2,1,0:T(8,128)(2,1)S(1)}, bf16[2,256,512]{2,1,0:T(8,128)(2,1)S(1)}, u32[]{:S(2)}, u32[]{:S(2)}) %collective-permute-start.32) | collective-permute-done | bytes 524320 | tf_op jit(solution)/shard_map/ppermute | solution.py:534
  547.1 16.6 %collective-permute-done.35.got_away.got_kept = bf16[2,256,512]{2,1,0:T(8,128)(2,1)S(1)} collective-permute-done((bf16[2,256,512]{2,1,0:T(8,128)(2,1)S(1)}, bf16[2,256,512]{2,1,0:T(8,128)(2,1)S(1)}, u32[]{:S(2)}, u32[]{:S(2)}) %collective-permute-start.35) | collective-permute-done | bytes 524320 | tf_op jit(solution)/shard_map/ppermute | solution.py:534
  569.3 15.5 %collective-permute-done.38.got_away.got_kept = bf16[2,256,512]{2,1,0:T(8,128)(2,1)S(1)} collective-permute-done((bf16[2,256,512]{2,1,0:T(8,128)(2,1)S(1)}, bf16[2,256,512]{2,1,0:T(8,128)(2,1)S(1)}, u32[]{:S(2)}, u32[]{:S(2)}) %collective-permute-start.38) | collective-permute-done | bytes 524320 | tf_op jit(solution)/shard_map/ppermute | solution.py:534
  586.9 11.4 %collective-permute-done.39 = bf16[1,256,512]{2,1,0:T(8,128)(2,1)S(1)} collective-permute-done((bf16[1,256,512]{2,1,0:T(8,128)(2,1)S(1)}, bf16[1,256,512]{2,1,0:T(8,128)(2,1)S(1)}, u32[]{:S(2)}, u32[]{:S(2)}) %collective-permute-start.39) | collective-permute-done | bytes 262176 | tf_op jit(solution)/shard_map/ppermute | solution.py:534
  (227 shorter events, 102.4 us)
Async XLA Ops:
  4.1 20.3 %collective-permute-start.4 = (bf16[320,2048]{1,0:T(8,128)(2,1)S(1)}, bf16[320,2048]{1,0:T(8,128)(2,1)S(1)}, u32[]{:S(2)}, u32[]{:S(2)}) collective-permute-start(bf16[320,2048]{1,0:T(8,128)(2,1)S(1)} %fusion.4.xa_ref.refs_0_), channel_id=1, source_target_pairs={{0,1},{1,0},{2,3},{3,2},{4,5},{5,4},{6,7},{7,6},{8,9},{9,8},{10,11... | collective-permute-start | bytes 3932168 | tf_op jit(solution)/shard_map/ppermute | solution.py:534
  4.6 32.1 %collective-permute-start = (bf16[320,2048]{1,0:T(8,128)(2,1)S(1)}, bf16[320,2048]{1,0:T(8,128)(2,1)}, u32[]{:S(2)}, u32[]{:S(2)}) collective-permute-start(bf16[320,2048]{1,0:T(8,128)(2,1)S(1)} %fusion.4.xa_ref.refs_0_), channel_id=1, source_target_pairs={{0,2},{1,3},{2,0},{3,1},{4,6},{5,7},{6,4},{7,5},{8,10},{9,11},{10,... | collective-permute-start | bytes 3932168 | tf_op jit(solution)/shard_map/ppermute | solution.py:534
  8.0 6.5 %collective-permute-start.1 = (f32[8]{0:T(128)S(1)}, f32[8]{0:T(128)S(1)}, u32[]{:S(2)}, u32[]{:S(2)}) collective-permute-start(f32[8]{0:T(128)S(1)} %select_reduce_fusion.1), channel_id=1, source_target_pairs={{0,4},{4,0},{8,12},{12,8},{16,20},{20,16},{24,28},{28,24},{1,5},{5... | collective-permute-start | bytes 104 | tf_op jit(solution)/shard_map/ppermute | solution.py:534
  14.5 3.6 collective-permute-start.2
  18.1 4.5 collective-permute-start.3
  36.7 3.5 collective-permute-start.5
  36.7 34.9 %collective-permute-start.6 = (bf16[320,2048]{1,0:T(8,128)(2,1)S(1)}, bf16[320,2048]{1,0:T(8,128)(2,1)S(1)}, u32[]{:S(2)}, u32[]{:S(2)}) collective-permute-start(bf16[320,2048]{1,0:T(8,128)(2,1)S(1)} %fusion.12.refs_0_), channel_id=1, source_target_pairs={{0,1},{1,0},{2,3},{3,2},{4,5},{5,4},{6,7},{7,6},{8,9},{9,8},{10,11... | collective-permute-start | bytes 3932168 | tf_op jit(solution)/shard_map/ppermute | solution.py:534
  37.2 34.4 %collective-permute-start.7 = (bf16[320,2048]{1,0:T(8,128)(2,1)S(1)}, bf16[320,2048]{1,0:T(8,128)(2,1)}, u32[]{:S(2)}, u32[]{:S(2)}) collective-permute-start(bf16[320,2048]{1,0:T(8,128)(2,1)S(1)} %fusion.12.refs_0_), channel_id=1, source_target_pairs={{0,2},{1,3},{2,0},{3,1},{4,6},{5,7},{6,4},{7,5},{8,10},{9,11},{10,... | collective-permute-start | bytes 3932168 | tf_op jit(solution)/shard_map/ppermute | solution.py:534
  71.6 31.2 %collective-permute-start.8 = (bf16[320,2048]{1,0:T(8,128)(2,1)}, bf16[320,2048]{1,0:T(8,128)(2,1)}, u32[]{:S(2)}, u32[]{:S(2)}) collective-permute-start(bf16[320,2048]{1,0:T(8,128)(2,1)} %pair_sum.8), channel_id=1, source_target_pairs={{0,2},{1,3},{2,0},{3,1},{4,6},{5,7},{6,4},{7,5},{8,10},{9,11},{10,... | collective-permute-start | bytes 3932168 | tf_op jit(solution)/shard_map/ppermute | solution.py:534
  73.2 34.3 %collective-permute-start.9 = (bf16[320,2048]{1,0:T(8,128)(2,1)}, bf16[320,2048]{1,0:T(8,128)(2,1)}, u32[]{:S(2)}, u32[]{:S(2)}) collective-permute-start(bf16[320,2048]{1,0:T(8,128)(2,1)} %collective-permute-done.7.refs_0_.refs_2_), channel_id=1, source_target_pairs={{0,1},{1,0},{2,3},{3,2},{4,5},{5,4},{6,7},{7,6},{8,9},{9,8},{10,11... | collective-permute-start | bytes 3932168 | tf_op jit(solution)/shard_map/ppermute | solution.py:534
  105.9 122.8 %copy-start.23 = (f32[320,2048]{1,0:T(8,128)}, f32[320,2048]{1,0:T(8,128)S(1)}, u32[]{:S(2)}) copy-start(f32[320,2048]{1,0:T(8,128)S(1)} %get-tuple-element.273) | copy-start | bytes 7864324
  115.9 3.4 collective-permute-start.11
  115.9 31.5 %collective-permute-start.10 = (bf16[320,2048]{1,0:T(8,128)(2,1)}, bf16[320,2048]{1,0:T(8,128)(2,1)}, u32[]{:S(2)}, u32[]{:S(2)}) collective-permute-start(bf16[320,2048]{1,0:T(8,128)(2,1)} %multiply_convert_fusion.xa_ref.refs_0_), channel_id=1, source_target_pairs={{0,2},{1,3},{2,0},{3,1},{4,6},{5,7},{6,4},{7,5},{8,10},{9,11},{10,... | collective-permute-start | bytes 3932168 | tf_op jit(solution)/shard_map/ppermute | solution.py:534
  147.4 3.4 collective-permute-start.12
  188.5 36.9 %collective-permute-start.13 = (bf16[320,2048]{1,0:T(8,128)(2,1)}, bf16[320,2048]{1,0:T(8,128)(2,1)}, u32[]{:S(2)}, u32[]{:S(2)}) collective-permute-start(bf16[320,2048]{1,0:T(8,128)(2,1)} %pair_sum.11), channel_id=1, source_target_pairs={{0,2},{1,3},{2,0},{3,1},{4,6},{5,7},{6,4},{7,5},{8,10},{9,11},{10,... | collective-permute-start | bytes 3932168 | tf_op jit(solution)/shard_map/ppermute | solution.py:534
  198.7 66.1 %collective-permute-start.16 = (bf16[4,256,1408]{2,1,0:T(8,128)(2,1)}, bf16[4,256,1408]{2,1,0:T(8,128)(2,1)}, u32[]{:S(2)}, u32[]{:S(2)}) collective-permute-start(bf16[4,256,1408]{2,1,0:T(8,128)(2,1)} %weight_grad.10), channel_id=1, source_target_pairs={{0,8},{4,12},{8,0},{12,4},{16,24},{20,28},{24,16},{28,20},{1,9},{5... | collective-permute-start | bytes 8650760 | tf_op jit(solution)/shard_map/ppermute | solution.py:534
  200.3 64.5 %collective-permute-start.15 = (bf16[4,256,1408]{2,1,0:T(8,128)(2,1)}, bf16[4,256,1408]{2,1,0:T(8,128)(2,1)}, u32[]{:S(2)}, u32[]{:S(2)}) collective-permute-start(bf16[4,256,1408]{2,1,0:T(8,128)(2,1)} %weight_grad.8), channel_id=1, source_target_pairs={{0,4},{4,0},{8,12},{12,8},{16,20},{20,16},{24,28},{28,24},{1,5},{5... | collective-permute-start | bytes 8650760 | tf_op jit(solution)/shard_map/ppermute | solution.py:534
  232.1 27.8 %collective-permute-start.17 = (bf16[320,2048]{1,0:T(8,128)(2,1)}, bf16[320,2048]{1,0:T(8,128)(2,1)}, u32[]{:S(2)}, u32[]{:S(2)}) collective-permute-start(bf16[320,2048]{1,0:T(8,128)(2,1)} %get-tuple-element.162.refs_0_), channel_id=1, source_target_pairs={{0,1},{1,0},{2,3},{3,2},{4,5},{5,4},{6,7},{7,6},{8,9},{9,8},{10,11... | collective-permute-start | bytes 3932168 | tf_op jit(solution)/shard_map/ppermute | solution.py:534
  232.3 32.5 %collective-permute-start.14 = (bf16[320,2048]{1,0:T(8,128)(2,1)}, bf16[320,2048]{1,0:T(8,128)(2,1)}, u32[]{:S(2)}, u32[]{:S(2)}) collective-permute-start(bf16[320,2048]{1,0:T(8,128)(2,1)} %get-tuple-element.162.refs_0_), channel_id=1, source_target_pairs={{0,2},{1,3},{2,0},{3,1},{4,6},{5,7},{6,4},{7,5},{8,10},{9,11},{10,... | collective-permute-start | bytes 3932168 | tf_op jit(solution)/shard_map/ppermute | solution.py:534
  269.0 42.6 %collective-permute-start.19 = (bf16[2,256,1408]{2,1,0:T(8,128)(2,1)}, bf16[2,256,1408]{2,1,0:T(8,128)(2,1)}, u32[]{:S(2)}, u32[]{:S(2)}) collective-permute-start(bf16[2,256,1408]{2,1,0:T(8,128)(2,1)} %get-tuple-element.174), channel_id=1, source_target_pairs={{0,8},{4,12},{8,0},{12,4},{16,24},{20,28},{24,16},{28,20},{1,9},{5... | collective-permute-start | bytes 4325384 | tf_op jit(solution)/shard_map/ppermute | solution.py:534
  269.4 6.0 collective-permute-start.18
  269.4 42.1 %collective-permute-start.20 = (bf16[320,2048]{1,0:T(8,128)(2,1)}, bf16[320,2048]{1,0:T(8,128)(2,1)}, u32[]{:S(2)}, u32[]{:S(2)}) collective-permute-start(bf16[320,2048]{1,0:T(8,128)(2,1)} %pair_sum.13), channel_id=1, source_target_pairs={{0,2},{1,3},{2,0},{3,1},{4,6},{5,7},{6,4},{7,5},{8,10},{9,11},{10,... | collective-permute-start | bytes 3932168 | tf_op jit(solution)/shard_map/ppermute | solution.py:534
  270.9 98.5 %collective-permute-start.22 = (bf16[4,256,1408]{2,1,0:T(8,128)(2,1)}, bf16[4,256,1408]{2,1,0:T(8,128)(2,1)S(1)}, u32[]{:S(2)}, u32[]{:S(2)}) collective-permute-start(bf16[4,256,1408]{2,1,0:T(8,128)(2,1)} %weight_grad.9), channel_id=1, source_target_pairs={{0,4},{4,0},{8,12},{12,8},{16,20},{20,16},{24,28},{28,24},{1,5},{5... | collective-permute-start | bytes 8650760 | tf_op jit(solution)/shard_map/ppermute | solution.py:534
  321.7 43.7 %collective-permute-start.21 = (bf16[320,2048]{1,0:T(8,128)(2,1)}, bf16[320,2048]{1,0:T(8,128)(2,1)}, u32[]{:S(2)}, u32[]{:S(2)}) collective-permute-start(bf16[320,2048]{1,0:T(8,128)(2,1)} %pair_sum.14), channel_id=1, source_target_pairs={{0,2},{1,3},{2,0},{3,1},{4,6},{5,7},{6,4},{7,5},{8,10},{9,11},{10,... | collective-permute-start | bytes 3932168 | tf_op jit(solution)/shard_map/ppermute | solution.py:534
  322.9 46.6 %collective-permute-start.23 = (bf16[4,256,512]{2,1,0:T(8,128)(2,1)}, bf16[4,256,512]{2,1,0:T(8,128)(2,1)}, u32[]{:S(2)}, u32[]{:S(2)}) collective-permute-start(bf16[4,256,512]{2,1,0:T(8,128)(2,1)} %get-tuple-element.193), channel_id=1, source_target_pairs={{0,4},{4,0},{8,12},{12,8},{16,20},{20,16},{24,28},{28,24},{1,5},{5... | collective-permute-start | bytes 3145736 | tf_op jit(solution)/shard_map/ppermute | solution.py:534
  328.3 41.2 %collective-permute-start.24 = (bf16[1,256,1408]{2,1,0:T(8,128)(2,1)}, bf16[1,256,1408]{2,1,0:T(8,128)(2,1)}, u32[]{:S(2)}, u32[]{:S(2)}) collective-permute-start(bf16[1,256,1408]{2,1,0:T(8,128)(2,1)} %get-tuple-element.197), channel_id=1, source_target_pairs={{0,16},{4,20},{8,24},{12,28},{16,0},{20,4},{24,8},{28,12},{1,17},{... | collective-permute-start | bytes 2162696 | tf_op jit(solution)/shard_map/ppermute | solution.py:534
  369.5 35.8 %collective-permute-start.30 = (bf16[2,256,1408]{2,1,0:T(8,128)(2,1)}, bf16[2,256,1408]{2,1,0:T(8,128)(2,1)}, u32[]{:S(2)}, u32[]{:S(2)}) collective-permute-start(bf16[2,256,1408]{2,1,0:T(8,128)(2,1)} %get-tuple-element.204), channel_id=1, source_target_pairs={{0,4},{4,0},{8,12},{12,8},{16,20},{20,16},{24,28},{28,24},{1,5},{5... | collective-permute-start | bytes 4325384 | tf_op jit(solution)/shard_map/ppermute | solution.py:534
  373.7 29.8 %collective-permute-start.25 = (f32[2,4,256]{2,1,0:T(4,128)S(1)}, f32[2,4,256]{2,1,0:T(4,128)S(1)}, u32[]{:S(2)}, u32[]{:S(2)}) collective-permute-start(f32[2,4,256]{2,1,0:T(4,128)S(1)} %bitcast.49), channel_id=1, source_target_pairs={{0,4},{4,0},{8,12},{12,8},{16,20},{20,16},{24,28},{28,24},{1,5},{5... | collective-permute-start | bytes 24584 | tf_op jit(solution)/shard_map/ppermute | solution.py:534
  403.6 12.0 %collective-permute-start.26 = (f32[2,2,256]{2,1,0:T(2,128)S(1)}, f32[2,2,256]{2,1,0:T(2,128)S(1)}, u32[]{:S(2)}, u32[]{:S(2)}) collective-permute-start(f32[2,2,256]{2,1,0:T(2,128)S(1)} %bitcast.50), channel_id=1, source_target_pairs={{0,8},{4,12},{8,0},{12,4},{16,24},{20,28},{24,16},{28,20},{1,9},{5... | collective-permute-start | bytes 12296 | tf_op jit(solution)/shard_map/ppermute | solution.py:534
  405.3 24.4 %collective-permute-start.31 = (bf16[4,256,512]{2,1,0:T(8,128)(2,1)}, bf16[4,256,512]{2,1,0:T(8,128)(2,1)S(1)}, u32[]{:S(2)}, u32[]{:S(2)}) collective-permute-start(bf16[4,256,512]{2,1,0:T(8,128)(2,1)} %get-tuple-element.205), channel_id=1, source_target_pairs={{0,4},{4,0},{8,12},{12,8},{16,20},{20,16},{24,28},{28,24},{1,5},{5... | collective-permute-start | bytes 3145736 | tf_op jit(solution)/shard_map/ppermute | solution.py:534
  411.2 42.5 %copy-start.29 = (f32[320,2048]{1,0:T(8,128)S(1)}, f32[320,2048]{1,0:T(8,128)}, u32[]{:S(2)}) copy-start(f32[320,2048]{1,0:T(8,128)} %get-tuple-element.271) | copy-start | bytes 7864324
  411.9 41.7 %copy-start.24 = (bf16[320,2048]{1,0:T(8,128)(2,1)S(1)}, bf16[320,2048]{1,0:T(8,128)(2,1)}, u32[]{:S(2)}) copy-start(bf16[320,2048]{1,0:T(8,128)(2,1)} %param.14) | copy-start | bytes 3932164
  411.9 49.3 %collective-permute-start.43 = (bf16[2,256,1408]{2,1,0:T(8,128)(2,1)S(1)}, bf16[2,256,1408]{2,1,0:T(8,128)(2,1)S(1)}, u32[]{:S(2)}, u32[]{:S(2)}) collective-permute-start(bf16[2,256,1408]{2,1,0:T(8,128)(2,1)S(1)} %get-tuple-element.236), channel_id=1, source_target_pairs={{0,8},{4,12},{8,0},{12,4},{16,24},{20,28},{24,16},{28,20},{1,9},{5... | collective-permute-start | bytes 4325384 | tf_op jit(solution)/shard_map/ppermute | solution.py:534
  414.4 42.7 %collective-permute-start.40 = (bf16[2,256,512]{2,1,0:T(8,128)(2,1)S(1)}, bf16[2,256,512]{2,1,0:T(8,128)(2,1)S(1)}, u32[]{:S(2)}, u32[]{:S(2)}) collective-permute-start(bf16[2,256,512]{2,1,0:T(8,128)(2,1)S(1)} %get-tuple-element.227), channel_id=1, source_target_pairs={{0,8},{4,12},{8,0},{12,4},{16,24},{20,28},{24,16},{28,20},{1,9},{5... | collective-permute-start | bytes 1572872 | tf_op jit(solution)/shard_map/ppermute | solution.py:534
  415.6 37.9 %collective-permute-start.27 = (f32[2,1,256]{2,1,0:T(1,128)S(1)}, f32[2,1,256]{2,1,0:T(1,128)S(1)}, u32[]{:S(2)}, u32[]{:S(2)}) collective-permute-start(f32[2,1,256]{2,1,0:T(1,128)S(1)} %constant_dynamic-slice_fusion), channel_id=1, source_target_pairs={{0,16},{4,20},{8,24},{12,28},{16,0},{20,4},{24,8},{28,12},{1,17},{... | collective-permute-start | bytes 6152 | tf_op jit(solution)/shard_map/ppermute | solution.py:534
  429.7 33.6 %collective-permute-start.34 = (bf16[4,256,512]{2,1,0:T(8,128)(2,1)S(1)}, bf16[4,256,512]{2,1,0:T(8,128)(2,1)S(1)}, u32[]{:S(2)}, u32[]{:S(2)}) collective-permute-start(bf16[4,256,512]{2,1,0:T(8,128)(2,1)S(1)} %copy-done.38), channel_id=1, source_target_pairs={{0,4},{4,0},{8,12},{12,8},{16,20},{20,16},{24,28},{28,24},{1,5},{5... | collective-permute-start | bytes 3145736 | tf_op jit(solution)/shard_map/ppermute | solution.py:534
  453.6 2.3 collective-permute-start.28
  455.9 12.5 %collective-permute-start.29 = (f32[2,256]{1,0:T(2,128)S(1)}, f32[2,256]{1,0:T(2,128)S(1)}, u32[]{:S(2)}, u32[]{:S(2)}) collective-permute-start(f32[2,256]{1,0:T(2,128)S(1)} %fusion.16), channel_id=1, source_target_pairs={{0,2},{1,3},{2,0},{3,1},{4,6},{5,7},{6,4},{7,5},{8,10},{9,11},{10,... | collective-permute-start | bytes 6152 | tf_op jit(solution)/shard_map/ppermute | solution.py:534
  457.9 47.4 %collective-permute-start.41 = (bf16[1,256,512]{2,1,0:T(8,128)(2,1)}, bf16[1,256,512]{2,1,0:T(8,128)(2,1)}, u32[]{:S(2)}, u32[]{:S(2)}) collective-permute-start(bf16[1,256,512]{2,1,0:T(8,128)(2,1)} %get-tuple-element.229), channel_id=1, source_target_pairs={{0,16},{4,20},{8,24},{12,28},{16,0},{20,4},{24,8},{28,12},{1,17},{... | collective-permute-start | bytes 786440 | tf_op jit(solution)/shard_map/ppermute | solution.py:534
  463.2 57.6 %collective-permute-start.44 = (bf16[1,256,1408]{2,1,0:T(8,128)(2,1)}, bf16[1,256,1408]{2,1,0:T(8,128)(2,1)}, u32[]{:S(2)}, u32[]{:S(2)}) collective-permute-start(bf16[1,256,1408]{2,1,0:T(8,128)(2,1)} %get-tuple-element.238), channel_id=1, source_target_pairs={{0,16},{4,20},{8,24},{12,28},{16,0},{20,4},{24,8},{28,12},{1,17},{... | collective-permute-start | bytes 2162696 | tf_op jit(solution)/shard_map/ppermute | solution.py:534
  464.3 99.6 %collective-permute-start.37 = (bf16[4,256,512]{2,1,0:T(8,128)(2,1)}, bf16[4,256,512]{2,1,0:T(8,128)(2,1)}, u32[]{:S(2)}, u32[]{:S(2)}) collective-permute-start(bf16[4,256,512]{2,1,0:T(8,128)(2,1)} %get-tuple-element.219), channel_id=1, source_target_pairs={{0,4},{4,0},{8,12},{12,8},{16,20},{20,16},{24,28},{28,24},{1,5},{5... | collective-permute-start | bytes 3145736 | tf_op jit(solution)/shard_map/ppermute | solution.py:534
  472.4 94.6 %collective-permute-start.42 = (bf16[1,256,1408]{2,1,0:T(8,128)(2,1)}, bf16[1,256,1408]{2,1,0:T(8,128)(2,1)}, u32[]{:S(2)}, u32[]{:S(2)}) collective-permute-start(bf16[1,256,1408]{2,1,0:T(8,128)(2,1)} %get-tuple-element.232), channel_id=1, source_target_pairs={{0,16},{4,20},{8,24},{12,28},{16,0},{20,4},{24,8},{28,12},{1,17},{... | collective-permute-start | bytes 2162696 | tf_op jit(solution)/shard_map/ppermute | solution.py:534
  509.5 37.3 %collective-permute-start.32 = (bf16[2,256,512]{2,1,0:T(8,128)(2,1)S(1)}, bf16[2,256,512]{2,1,0:T(8,128)(2,1)S(1)}, u32[]{:S(2)}, u32[]{:S(2)}) collective-permute-start(bf16[2,256,512]{2,1,0:T(8,128)(2,1)S(1)} %get-tuple-element.207), channel_id=1, source_target_pairs={{0,8},{4,12},{8,0},{12,4},{16,24},{20,28},{24,16},{28,20},{1,9},{5... | collective-permute-start | bytes 1572872 | tf_op jit(solution)/shard_map/ppermute | solution.py:534
  510.7 52.9 %collective-permute-start.35 = (bf16[2,256,512]{2,1,0:T(8,128)(2,1)S(1)}, bf16[2,256,512]{2,1,0:T(8,128)(2,1)S(1)}, u32[]{:S(2)}, u32[]{:S(2)}) collective-permute-start(bf16[2,256,512]{2,1,0:T(8,128)(2,1)S(1)} %get-tuple-element.214), channel_id=1, source_target_pairs={{0,8},{4,12},{8,0},{12,4},{16,24},{20,28},{24,16},{28,20},{1,9},{5... | collective-permute-start | bytes 1572872 | tf_op jit(solution)/shard_map/ppermute | solution.py:534
  547.0 38.2 %collective-permute-start.33 = (bf16[1,256,512]{2,1,0:T(8,128)(2,1)S(1)}, bf16[1,256,512]{2,1,0:T(8,128)(2,1)S(1)}, u32[]{:S(2)}, u32[]{:S(2)}) collective-permute-start(bf16[1,256,512]{2,1,0:T(8,128)(2,1)S(1)} %get-tuple-element.209), channel_id=1, source_target_pairs={{0,16},{4,20},{8,24},{12,28},{16,0},{20,4},{24,8},{28,12},{1,17},{... | collective-permute-start | bytes 786440 | tf_op jit(solution)/shard_map/ppermute | solution.py:534
  563.8 22.3 %collective-permute-start.36 = (bf16[1,256,512]{2,1,0:T(8,128)(2,1)S(1)}, bf16[1,256,512]{2,1,0:T(8,128)(2,1)S(1)}, u32[]{:S(2)}, u32[]{:S(2)}) collective-permute-start(bf16[1,256,512]{2,1,0:T(8,128)(2,1)S(1)} %get-tuple-element.216), channel_id=1, source_target_pairs={{0,16},{4,20},{8,24},{12,28},{16,0},{20,4},{24,8},{28,12},{1,17},{... | collective-permute-start | bytes 786440 | tf_op jit(solution)/shard_map/ppermute | solution.py:534
  565.3 19.5 %collective-permute-start.38 = (bf16[2,256,512]{2,1,0:T(8,128)(2,1)S(1)}, bf16[2,256,512]{2,1,0:T(8,128)(2,1)S(1)}, u32[]{:S(2)}, u32[]{:S(2)}) collective-permute-start(bf16[2,256,512]{2,1,0:T(8,128)(2,1)S(1)} %get-tuple-element.221), channel_id=1, source_target_pairs={{0,8},{4,12},{8,0},{12,4},{16,24},{20,28},{24,16},{28,20},{1,9},{5... | collective-permute-start | bytes 1572872 | tf_op jit(solution)/shard_map/ppermute | solution.py:534
  584.9 13.4 %collective-permute-start.39 = (bf16[1,256,512]{2,1,0:T(8,128)(2,1)S(1)}, bf16[1,256,512]{2,1,0:T(8,128)(2,1)S(1)}, u32[]{:S(2)}, u32[]{:S(2)}) collective-permute-start(bf16[1,256,512]{2,1,0:T(8,128)(2,1)S(1)} %get-tuple-element.223), channel_id=1, source_target_pairs={{0,16},{4,20},{8,24},{12,28},{16,0},{20,4},{24,8},{28,12},{1,17},{... | collective-permute-start | bytes 786440 | tf_op jit(solution)/shard_map/ppermute | solution.py:534
  (37 other events, 395.2 us)

commit v5 on v4

--- a/solution.py
+++ b/solution.py
@@ -498,6 +498,178 @@
     )(*args)
 
 
+def partner(axis, bit):
+    rank = lax.axis_index(axis)
+    return {axis: rank + bit - 2 * bit * (rank // bit % 2)}
+
+
+def last_body(two, three, *refs):
+    mats = len(two) + three
+    away, kept, refs = refs[:mats], refs[mats : 2 * mats], refs[2 * mats :]
+    gains_ref, outs, sums_ref, refs = refs[0], refs[1 : 1 + mats], refs[1 + mats], refs[2 + mats :]
+    own, first, refs = refs[:mats], refs[mats : 2 * mats], refs[2 * mats :]
+    held, to_z, from_z, refs = refs[:three], refs[three : 2 * three], refs[2 * three : 3 * three], refs[3 * three :]
+    to_last, from_last, refs = refs[:mats], refs[mats : 2 * mats], refs[2 * mats :]
+    gain_in, gain_out, load_sem, send_sem, recv_sem = refs
+    rank = lax.axis_index("dp")
+    z1, z2 = rank // 2 % 2, rank // 4 % 2
+    hops = [("tensor", 1), ("tensor", 2), ("dp", 1), ("dp", 2), ("dp", 4)]
+    copies = []
+
+    barrier = pltpu.get_barrier_semaphore()
+    for axis, bit in hops:
+        pl.semaphore_signal(barrier, inc=1, device_id=partner(axis, bit), device_id_type=pl.DeviceIdType.MESH)
+    pl.semaphore_wait(barrier, len(hops))
+
+    def send(src, dst, axis, bit):
+        index = len(copies)
+        copy = pltpu.make_async_remote_copy(
+            src_ref=src,
+            dst_ref=dst,
+            send_sem=send_sem.at[index],
+            recv_sem=recv_sem.at[index],
+            device_id=partner(axis, bit),
+            device_id_type=pl.DeviceIdType.MESH,
+        )
+        copy.start()
+        copies.append(copy)
+        return copy
+
+    def side(bit, flip):
+        return 1 - bit if flip else bit
+
+    loads = [pltpu.make_async_copy(kept[m], own[m], load_sem.at[m]) for m in range(mats)]
+    for load in loads:
+        load.start()
+    stage = {}
+    for m in (2, 1, 0):
+        for flip in (1, 0):
+            stage[m, flip] = send(away[m].at[side(z2, flip)], first[m].at[flip], "dp", two[m])
+
+    gain_out[0] = gains_ref[...]
+    stage["gains"] = send(gain_out.at[0], gain_in.at[0], *hops[0])
+
+    def gain_hop(index):
+        stage["gains"].wait_recv()
+        total = gain_out[index] + gain_in[index]
+        if index + 1 < len(hops):
+            gain_out[index + 1] = total
+            stage["gains"] = send(gain_out.at[index + 1], gain_in.at[index + 1], *hops[index + 1])
+        else:
+            sums_ref[...] = total
+
+    gain_hop(0)
+    gain_hop(1)
+    for m in range(len(two), mats):
+        for a in (1, 0):
+            for c in (1, 0):
+                stage[m, a, c] = send(away[m].at[side(z1, a) + 2 * side(z2, c)], first[m].at[2 * a + c], "dp", 1)
+    for load in loads:
+        load.wait()
+
+    def wide(value):
+        return value.astype(jnp.float32)
+
+    def near_last(m, flip):
+        stage[m, flip].wait_recv()
+        total = wide(own[m][side(z2, flip)]) + wide(first[m][flip])
+        if flip:
+            to_last[m][...] = total.astype(jnp.bfloat16)
+            stage[m, "last"] = send(to_last[m], from_last[m], "dp", 4)
+        else:
+            outs[m][...] = total
+
+    def from_x(m, a, c):
+        stage[m, a, c].wait_recv()
+        total = wide(own[m][side(z1, a) + 2 * side(z2, c)]) + wide(first[m][2 * a + c])
+        i = m - len(two)
+        if a:
+            to_z[i][c] = total.astype(jnp.bfloat16)
+            stage[m, "z", c] = send(to_z[i].at[c], from_z[i].at[c], "dp", 2)
+        else:
+            held[i][c] = total
+
+    def from_near(m, c):
+        stage[m, "z", c].wait_recv()
+        i = m - len(two)
+        total = held[i][c] + wide(from_z[i][c])
+        if c:
+            to_last[m][...] = total.astype(jnp.bfloat16)
+            stage[m, "last"] = send(to_last[m], from_last[m], "dp", 4)
+        else:
+            outs[m][...] = total
+
+    def finish(m):
+        stage[m, "last"].wait_recv()
+        outs[m][...] += wide(from_last[m][...])
+
+    gate, up, out, q, k, v = range(6)
+    near_last(out, 1)
+    near_last(out, 0)
+    near_last(gate, 1)
+    near_last(up, 1)
+    near_last(gate, 0)
+    gain_hop(2)
+    from_x(q, 1, 1)
+    from_x(q, 1, 0)
+    near_last(up, 0)
+    gain_hop(3)
+    from_x(q, 0, 1)
+    from_x(q, 0, 0)
+    from_near(q, 1)
+    from_x(k, 1, 1)
+    from_near(q, 0)
+    from_x(k, 1, 0)
+    from_x(k, 0, 1)
+    from_x(k, 0, 0)
+    finish(out)
+    from_near(k, 1)
+    from_x(v, 1, 1)
+    from_near(k, 0)
+    from_x(v, 1, 0)
+    from_x(v, 0, 1)
+    from_x(v, 0, 0)
+    from_near(v, 1)
+    finish(gate)
+    from_near(v, 0)
+    gain_hop(4)
+    for m in (up, q, k, v):
+        finish(m)
+    for copy in copies:
+        copy.wait_send()
+
+
+def last_stages(two, three, gains):
+    mats = [t[:2] for t in two] + list(three)
+    away, kept = [m[0] for m in mats], [m[1] for m in mats]
+    shapes = [a.shape for a in away]
+    low = jnp.bfloat16
+    late = shapes[len(two) :]
+    any_space = pl.BlockSpec(memory_space=pl.ANY)
+    inside = pl.BlockSpec(memory_space=pltpu.VMEM)
+    count = 3 * len(two) + 7 * len(three) + 5
+    result = pl.pallas_call(
+        functools.partial(last_body, [t[2] for t in two], len(three)),
+        in_specs=[any_space] * (2 * len(mats)) + [inside],
+        out_specs=[inside] * (len(mats) + 1),
+        out_shape=[jax.ShapeDtypeStruct(shape[1:], jnp.float32) for shape in shapes]
+        + [jax.ShapeDtypeStruct(gains.shape, jnp.float32)],
+        scratch_shapes=[pltpu.VMEM(shape, low) for shape in shapes]
+        + [pltpu.VMEM(shape, low) for shape in shapes]
+        + [pltpu.VMEM((2,) + shape[1:], jnp.float32) for shape in late]
+        + [pltpu.VMEM((2,) + shape[1:], low) for shape in late]
+        + [pltpu.VMEM((2,) + shape[1:], low) for shape in late]
+        + [pltpu.VMEM(shape[1:], low) for shape in shapes]
+        + [pltpu.VMEM(shape[1:], low) for shape in shapes]
+        + [pltpu.VMEM((5,) + gains.shape, jnp.float32)] * 2
+        + [pltpu.SemaphoreType.DMA((len(mats),)), pltpu.SemaphoreType.DMA((count,)), pltpu.SemaphoreType.DMA((count,))],
+        compiler_params=pltpu.CompilerParams(vmem_limit_bytes=62 << 20, collective_id=8),
+        cost_estimate=cost(flops=1 << 24, bytes_accessed=1 << 25, transcendentals=0),
+        name="last_stages",
+    )(*away, *kept, gains)
+    return result[:-1], result[-1]
+
+
 def row_tables(length_row, group_row, mask_row):
     starts = jnp.cumsum(length_row) - length_row
     token = jnp.arange(ROWS, dtype=jnp.int32)
@@ -688,7 +860,8 @@
     b2 = to_far(b0)
     b1 = to_mate(b0)
     mid_near, dg_near, du_near = mlp_pair(b0, b1, dm_near, w_gate, w_up)
-    b2, mid_near, dg_near, du_near = tie(b2, mid_near, dg_near, du_near)
+    mine8 = pair_sum([(mid_near, w_down, False)], 5, jnp.float32)
+    b2, mid_near, dg_near, du_near, mine8 = tie(b2, mid_near, dg_near, du_near, mine8)
     b3 = to_mate(b2)
     mid_far, dg_far, du_far = mlp_pair(b2, b3, dm_far, w_gate, w_up)
 
@@ -749,25 +922,28 @@
         d_a, up_own, up_got, out_got, gate_away, down_got, *sends
     )
 
-    gate_got = hop(gate_away, 1)
-    up = Halving(dp_rank, up_own)
-    up_got = hop(up.merge(up_got, 2), 2)
-    output = (mid_h + pair_sum([(mid_near, w_down, False)], 5, jnp.float32) + got8.astype(jnp.float32)).astype(jnp.bfloat16)
+    up, out = Halving(dp_rank, up_own), Halving(dp_rank, out_own)
+    up_away, out_away = up.merge(up_got, 2), out.merge(out_got, 2)
+    output = (mid_h + mine8 + got8.astype(jnp.float32)).astype(jnp.bfloat16)
     n_a = x_f * inv_a
     gain_attn_part = jnp.sum(d_a * n_a, axis=0)
     e_a = d_a * gain_attn
     grad_input = d_h + inv_a * (e_a - n_a * jnp.mean(e_a * n_a, axis=-1, keepdims=True))
     gains = jnp.stack([gain_attn_part, gain_mlp_part])
-    gains = butterfly_sum(scatter_small(gains.reshape(2, lax.axis_size("dp"), -1), "dp"), "tensor")
     sum_down = down.finish(down_got)
-    sum_gate = gate.finish(gate_got)
-    sum_up = up.finish(up_got)
-    sum_out = Halving(dp_rank, out_own).finish(out_got)
-    sums, last = [], gate_got
-    for send, own in zip(sends, (q_own, k_own, v_own)):
-        send, last = tie(send, last)
-        last = hop(send, 1)
-        sums.append(Halving(dp_rank, own).finish(last))
+    if grad_qkv.kernel and half == 4:
+        (sum_gate, sum_up, sum_out, *sums), gains = last_stages(
+            [(gate_away, gate.kept, 1), (up_away, up.kept, 2), (out_away, out.kept, 2)],
+            list(zip(sends, (q_own, k_own, v_own))),
+            gains,
+        )
+        gains = lax.dynamic_slice_in_dim(gains, dp_rank[0] * grad_qkv.tile, grad_qkv.tile, 1)
+    else:
+        gains = butterfly_sum(scatter_small(gains.reshape(2, lax.axis_size("dp"), -1), "dp"), "tensor")
+        sum_gate = gate.finish(hop(gate_away, 1))
+        sum_up = up.finish(hop(up_away, 2))
+        sum_out = out.finish(hop(out_away, 2))
+        sums = [Halving(dp_rank, own).finish(hop(send, 1)) for send, own in zip(sends, (q_own, k_own, v_own))]
     return (
         output,
         grad_input,

time: 605 us -> 543 us (0.90)
  waiting for transfers between devices: 199 us -> 28.9 us
  Pallas kernels: 289 us -> 421 us
  starting transfers between devices: 47.2 us -> 27.2 us
  other arithmetic: 46.4 us -> 36.5 us
  local copies, waits for them, and re-layouts: 15.8 us -> 22.7 us
    ppermute x45 -> x25, waiting for transfers between devices: 199 us -> 28.9 us  [exchange(): lax.ppermute(values, axis, [(rank, rank ^ bit) for rank in range(size)])]
    pallas_call x0 -> x1, Pallas kernels: none -> 139 us  [last_stages(): pl.pallas_call(functools.partial(last_body, [t[2] for t in two], len(thre...]
    ppermute x45 -> x25, starting transfers between devices: 47.2 us -> 27.2 us  [exchange(): lax.ppermute(values, axis, [(rank, rank ^ bit) for rank in range(size)])]
    pallas_call x14 -> x5, Pallas kernels: 17.6 us -> 10 us  [merge_call(): pl.pallas_call(merge_body, grid_spec=pltpu.PrefetchScalarGridSpec(num_sca...]
    squeeze x5 -> x0, other arithmetic: 7.31 us -> none  [finish(): return (self.kept.astype(jnp.float32) + got.astype(jnp.float32))[0]]
    unnamed x86 -> x77, local copies, waits for them, and re-layouts: 14.5 us -> 20.6 us
  transfers between devices with their start and end apart: 45 -> 25, of which waited for: 16 -> 8; matrix products, arithmetic and copies ran while one was open for 8% -> 5% of each run, Pallas kernels for 40% -> 43%
where the time goes in v5:
time: 543 us; the launch traced here: 537 us
  Pallas kernels  421 us (78%)
  other arithmetic  36.5 us (7%)
  waiting for transfers between devices  28.9 us (5%)
  starting transfers between devices  27.2 us (5%)
  local copies, waits for them, and re-layouts  22.7 us (4%)
    pallas_call x1, Pallas kernels, last_stages(): pl.pallas_call(functools.partial(last_body, [t[2] for t in two], len(thre...  139 us
    pallas_call x8, Pallas kernels, pair_sum(): pl.pallas_call(functools.partial(pair_body, [(len(left), dims) for left,...  83.6 us
    pallas_call x8, Pallas kernels, grad_call(): pl.pallas_call(functools.partial(grad_body, len(pieces), widths, low, sid...  77 us
    pallas_call x2, Pallas kernels, mlp_pair(): pl.pallas_call(mlp_body, grid=(pl.cdiv(width, tile),), in_specs=[whole(xa...  29.4 us
    ppermute x25, waiting for transfers between devices, exchange(): lax.ppermute(values, axis, [(rank, rank ^ bit) for rank in range(size)])  28.9 us
    ppermute x25, starting transfers between devices, exchange(): lax.ppermute(values, axis, [(rank, rank ^ bit) for rank in range(size)])  27.2 us
    pallas_call x4, Pallas kernels, project(): pl.pallas_call(functools.partial(project_body, [(len(left), dims) for lef...  26.4 us
    pallas_call x1, Pallas kernels, attend_back(): pl.pallas_call(attend_back_body, grid_spec=pltpu.PrefetchScalarGridSpec(n...  22 us
  transfers between devices with their start and end apart: 25, of which 8 were waited for; matrix products, arithmetic and copies ran while one was open for 5% of the time, Pallas kernels for 43%

profile of v5, /device:TPU:0, one launch (start us, length us, event | category | flops | bytes accessed | tf_op | source)
XLA Modules:
  0.0 537.4 jit_solution(5401137757110793470)
XLA Ops:
  4.6 2.6 collective-permute-start
  9.6 2.4 fusion.13
  16.1 2.0 collective-permute-done.2
  18.1 2.6 collective-permute-start.3
  24.4 9.4 %qkv.2 = (bf16[640,512]{1,0:T(8,128)(2,1)}, bf16[640,512]{1,0:T(8,128)(2,1)}, bf16[640,512]{1,0:T(8,128)(2,1)}) custom-call(s32[1]{0:T(128)} %bitcast.rank_ref, bf16[320,2048]{1,0:T(8,128)(2,1)} %copy-done.21, bf16[320,2048]{1,0:T(8,128)(2,1)} %collective-permute-done.4.xb_ref.refs_1_, f32[1280,128]{1,0:T(8,128)} %pad_maximum_fusion.cos_ref, ...), custom_call_target="tpu_custom_call" | custom-call | flops 4026531 | bytes 8912 | tf_op jit(solution)/shard_map/qkv/pallas_call | solution.py:67
  33.8 2.9 collective-permute-done.xa_ref.refs_2_
  40.1 8.9 %qkv.3 = (bf16[640,512]{1,0:T(8,128)(2,1)}, bf16[640,512]{1,0:T(8,128)(2,1)}, bf16[640,512]{1,0:T(8,128)(2,1)}) custom-call(s32[1]{0:T(128)} %bitcast.rank_ref, bf16[320,2048]{1,0:T(8,128)(2,1)} %collective-permute-done.xa_ref.refs_2_, bf16[320,2048]{1,0:T(8,128)(2,1)} %collective-permute-done.5.xb_ref.refs_3_, f32[1280,128]{1,0:T(8,128)} %pad_maximum_fusion.cos_ref, ...), custom_call_target="tpu_custom_call" | custom-call | flops 4026531 | bytes 8912 | tf_op jit(solution)/shard_map/qkv/pallas_call | solution.py:67
  48.9 14.6 %attend.1 = (bf16[640,512]{1,0:T(8,128)(2,1)}, bf16[640,512]{1,0:T(8,128)(2,1)}, f32[4,1,1280]{2,1,0:T(1,128)}) custom-call(s32[1]{0:T(128)} %bitcast.rank_ref, bf16[640,512]{1,0:T(8,128)(2,1)} %get-tuple-element.116.qn, bf16[640,512]{1,0:T(8,128)(2,1)} %get-tuple-element.118.qf, bf16[640,512]{1,0:T(8,128)(2,1)} %get-tuple-element.119.kn, ...), custom_call_target="tpu_custom_call" | custom-call | flops 6710886 | bytes 5242 | tf_op jit(solution)/shard_map/attend/pallas_call | solution.py:128
  63.5 6.9 %pair_sum.8 = bf16[320,2048]{1,0:T(8,128)(2,1)} custom-call(bf16[640,512]{1,0:T(8,128)(2,1)} %get-tuple-element.125.refs_0_.refs_5_, bf16[512,2048]{1,0:T(8,128)(2,1)} %refs_2_.7), custom_call_target="tpu_custom_call" | custom-call | flops 1342177 | bytes 5373 | tf_op jit(solution)/shard_map/pair_sum/pallas_call | solution.py:478
  72.3 7.4 %pair_sum.9 = f32[320,2048]{1,0:T(8,128)} custom-call(bf16[640,512]{1,0:T(8,128)(2,1)} %get-tuple-element.126.refs_0_.refs_4_, bf16[512,2048]{1,0:T(8,128)(2,1)} %refs_2_.7), custom_call_target="tpu_custom_call" | custom-call | flops 1342177 | bytes 5373 | tf_op jit(solution)/shard_map/pair_sum/pallas_call | solution.py:478
  79.7 8.4 %project.4.dm_ref = f32[640,1408]{1,0:T(8,128)} custom-call(bf16[320,2048]{1,0:T(8,128)(2,1)} %copy-done.19, bf16[320,2048]{1,0:T(8,128)(2,1)} %copy-done.20, bf16[1408,2048]{1,0:T(8,128)(2,1)} %refs_1_.13), custom_call_target="tpu_custom_call" | custom-call | flops 3690987 | bytes 10190 | tf_op jit(solution)/shard_map/project/pallas_call | solution.py:414
  88.1 13.6 %collective-permute-done.8 = bf16[320,2048]{1,0:T(8,128)(2,1)} collective-permute-done((bf16[320,2048]{1,0:T(8,128)(2,1)}, bf16[320,2048]{1,0:T(8,128)(2,1)}, u32[]{:S(2)}, u32[]{:S(2)}) %collective-permute-start.8) | collective-permute-done | bytes 1310752 | tf_op jit(solution)/shard_map/ppermute | solution.py:706
  101.7 3.1 multiply_reduce_fusion.2
  106.4 8.4 %project.5.dm_ref = f32[640,1408]{1,0:T(8,128)} custom-call(bf16[320,2048]{1,0:T(8,128)(2,1)} %collective-permute-done.7.refs_0_.refs_2_, bf16[320,2048]{1,0:T(8,128)(2,1)} %collective-permute-done.9.refs_1_.refs_3_, bf16[1408,2048]{1,0:T(8,128)(2,1)} %refs_1_.13), custom_call_target="tpu_custom_call" | custom-call | flops 3690987 | bytes 10190 | tf_op jit(solution)/shard_map/project/pallas_call | solution.py:414
  118.2 14.8 %mlp.2 = (bf16[640,1408]{1,0:T(8,128)(2,1)}, bf16[640,1408]{1,0:T(8,128)(2,1)}, bf16[640,1408]{1,0:T(8,128)(2,1)}) custom-call(bf16[320,2048]{1,0:T(8,128)(2,1)} %multiply_convert_fusion.xa_ref.refs_0_, bf16[320,2048]{1,0:T(8,128)(2,1)} %collective-permute-done.11.xb_ref.refs_1_, f32[640,1408]{1,0:T(8,128)} %project.4.dm_ref, bf16[2048,1408]{1,0:T(8,128)(2,1)} %refs_1_.12, ...), custom_call_target="tpu_custom_call" | custom-call | flops 7381975 | bytes 23166 | tf_op jit(solution)/shard_map/mlp/pallas_call | solution.py:234
  132.9 10.0 %pair_sum.10 = f32[320,2048]{1,0:T(8,128)} custom-call(bf16[640,1408]{1,0:T(8,128)(2,1)} %get-tuple-element.142.refs_0_.refs_4_, bf16[1408,2048]{1,0:T(8,128)(2,1)} %refs_1_.13), custom_call_target="tpu_custom_call" | custom-call | flops 3690987 | bytes 10190 | tf_op jit(solution)/shard_map/pair_sum/pallas_call | solution.py:478
  143.0 3.3 collective-permute-done.10.xa_ref.refs_2_
  146.3 3.4 collective-permute-done.12.xb_ref.refs_3_
  149.7 14.6 %mlp.3 = (bf16[640,1408]{1,0:T(8,128)(2,1)}, bf16[640,1408]{1,0:T(8,128)(2,1)}, bf16[640,1408]{1,0:T(8,128)(2,1)}) custom-call(bf16[320,2048]{1,0:T(8,128)(2,1)} %collective-permute-done.10.xa_ref.refs_2_, bf16[320,2048]{1,0:T(8,128)(2,1)} %collective-permute-done.12.xb_ref.refs_3_, f32[640,1408]{1,0:T(8,128)} %project.5.dm_ref, ...), custom_call_target="tpu_custom_call" | custom-call | flops 7381975 | bytes 23166 | tf_op jit(solution)/shard_map/mlp/pallas_call | solution.py:234
  164.3 8.8 %weight_grad.8 = bf16[4,256,1408]{2,1,0:T(8,128)(2,1)} custom-call(s32[1]{0:T(128)} %bitcast.7.rank_ref._, bf16[320,2048]{1,0:T(8,128)(2,1)} %copy-done.19, bf16[320,2048]{1,0:T(8,128)(2,1)} %copy-done.20, bf16[320,2048]{1,0:T(8,128)(2,1)} %collective-permute-done.7.refs_0_.refs_2_, bf16[320,2048]{1,0:T(8,128)(2,1)} %collective-permute-done.9.refs_1_.refs_3_, ...), custom_call_target="tpu_custom_call" | custom-call | flops 3690987 | bytes 9109 | tf_op jit(solution)/shard_map/weight_grad/pallas_call | solution.py:324
  173.0 14.3 %pair_sum.11 = bf16[320,2048]{1,0:T(8,128)(2,1)} custom-call(bf16[640,1408]{1,0:T(8,128)(2,1)} %get-tuple-element.144.refs_0_.refs_5_, bf16[2048,1408]{1,0:T(8,128)(2,1)} %refs_1_.12, bf16[640,1408]{1,0:T(8,128)(2,1)} %get-tuple-element.145.refs_2_.refs_5_, bf16[2048,1408]{1,0:T(8,128)(2,1)} %refs_3_.5), custom_call_target="tpu_custom_call" | custom-call | flops 7381975 | bytes 17760 | tf_op jit(solution)/shard_map/pair_sum/pallas_call | solution.py:478
  189.1 8.7 %weight_grad.10 = bf16[4,256,1408]{2,1,0:T(8,128)(2,1)} custom-call(s32[1]{0:T(128)} %bitcast.7.rank_ref._, bf16[320,2048]{1,0:T(8,128)(2,1)} %multiply_convert_fusion.xa_ref.refs_0_, bf16[320,2048]{1,0:T(8,128)(2,1)} %collective-permute-done.11.xb_ref.refs_1_, bf16[320,2048]{1,0:T(8,128)(2,1)} %collective-permute-done.10.xa_ref.refs_2_, ...), custom_call_target="tpu_custom_call" | custom-call | flops 3690987 | bytes 9109 | tf_op jit(solution)/shard_map/weight_grad/pallas_call | solution.py:324
  200.9 8.7 %weight_grad.9 = bf16[4,256,1408]{2,1,0:T(8,128)(2,1)} custom-call(s32[1]{0:T(128)} %bitcast.7.rank_ref._, bf16[320,2048]{1,0:T(8,128)(2,1)} %multiply_convert_fusion.xa_ref.refs_0_, bf16[320,2048]{1,0:T(8,128)(2,1)} %collective-permute-done.11.xb_ref.refs_1_, bf16[320,2048]{1,0:T(8,128)(2,1)} %collective-permute-done.10.xa_ref.refs_2_, ...), custom_call_target="tpu_custom_call" | custom-call | flops 3690987 | bytes 9109 | tf_op jit(solution)/shard_map/weight_grad/pallas_call | solution.py:324
  209.6 14.9 %pair_sum.12 = f32[320,2048]{1,0:T(8,128)} custom-call(bf16[640,1408]{1,0:T(8,128)(2,1)} %get-tuple-element.153.refs_0_.refs_4_, bf16[2048,1408]{1,0:T(8,128)(2,1)} %refs_1_.12, bf16[640,1408]{1,0:T(8,128)(2,1)} %get-tuple-element.179.refs_2_.refs_4_, bf16[2048,1408]{1,0:T(8,128)(2,1)} %refs_3_.5), custom_call_target="tpu_custom_call" | custom-call | flops 7381975 | bytes 17760 | tf_op jit(solution)/shard_map/pair_sum/pallas_call | solution.py:478
  224.5 2.4 convert_add_fusion.2
  228.2 2.9 fusion.16
  231.9 9.5 %pair_sum.13 = bf16[320,2048]{1,0:T(8,128)(2,1)} custom-call(bf16[640,1408]{1,0:T(8,128)(2,1)} %get-tuple-element.152.refs_5_.refs_0_, bf16[1408,2048]{1,0:T(8,128)(2,1)} %refs_1_.13), custom_call_target="tpu_custom_call" | custom-call | flops 3690987 | bytes 10190 | tf_op jit(solution)/shard_map/pair_sum/pallas_call | solution.py:478
  241.5 8.7 %weight_grad.11.own_away.own_kept = bf16[4,256,1408]{2,1,0:T(8,128)(2,1)} custom-call(s32[1]{0:T(128)} %bitcast.7.rank_ref._, bf16[320,2048]{1,0:T(8,128)(2,1)} %copy-done.19, bf16[320,2048]{1,0:T(8,128)(2,1)} %copy-done.20, bf16[320,2048]{1,0:T(8,128)(2,1)} %collective-permute-done.7.refs_0_.refs_2_, ...), custom_call_target="tpu_custom_call" | custom-call | flops 3690987 | bytes 9109 | tf_op jit(solution)/shard_map/weight_grad/pallas_call | solution.py:324
  250.2 8.8 %weight_grad.12.own_away.own_kept = bf16[4,256,1408]{2,1,0:T(8,128)(2,1)} custom-call(s32[1]{0:T(128)} %bitcast.7.rank_ref._, bf16[320,2048]{1,0:T(8,128)(2,1)} %multiply_convert_fusion.xa_ref.refs_0_, bf16[320,2048]{1,0:T(8,128)(2,1)} %collective-permute-done.11.xb_ref.refs_1_, bf16[320,2048]{1,0:T(8,128)(2,1)} %collective-permute-done.10.xa_ref.refs_2_, ...), custom_call_target="tpu_custom_call" | custom-call | flops 3690987 | bytes 9109 | tf_op jit(solution)/shard_map/weight_grad/pallas_call | solution.py:324
  259.0 4.9 project.6.gn
  263.9 3.0 merge.5
  270.5 2.1 merge.6
  274.9 4.8 project.7.gf
  279.7 9.3 %weight_grad.13 = (bf16[4,256,512]{2,1,0:T(8,128)(2,1)}, bf16[4,256,512]{2,1,0:T(8,128)(2,1)}) custom-call(s32[1]{0:T(128)} %bitcast.7.rank_ref._, bf16[320,2048]{1,0:T(8,128)(2,1)} %get-tuple-element.150.refs_0_, bf16[320,2048]{1,0:T(8,128)(2,1)} %collective-permute-done.17.refs_1_, bf16[320,2048]{1,0:T(8,128)(2,1)} %collective-permute-done.14.refs_0_.refs_2_, ...), custom_call_target="tpu_custom_call" | custom-call | flops 2684354 | bytes 8650 | tf_op jit(solution)/shard_map/weight_grad/pallas_call | solution.py:324
  288.9 22.0 %attend_back.1 = (bf16[640,512]{1,0:T(8,128)(2,1)}, bf16[640,512]{1,0:T(8,128)(2,1)}, bf16[640,512]{1,0:T(8,128)(2,1)}, bf16[640,512]{1,0:T(8,128)(2,1)}, bf16[6...) custom-call(s32[1]{0:T(128)} %bitcast.rank_ref, bf16[640,512]{1,0:T(8,128)(2,1)} %get-tuple-element.116.qn, ...), custom_call_target="tpu_custom_call" | custom-call | flops 16777216 | bytes 10485 | tf_op jit(solution)/shard_map/attend_back/pallas_call | solution.py:191
  311.0 10.1 %pair_sum.14 = bf16[320,2048]{1,0:T(8,128)(2,1)} custom-call(bf16[640,512]{1,0:T(8,128)(2,1)} %get-tuple-element.172.refs_0_.refs_5_, bf16[2048,512]{1,0:T(8,128)(2,1)} %refs_1_.15, bf16[640,512]{1,0:T(8,128)(2,1)} %get-tuple-element.173.refs_2_.refs_7_, bf16[2048,512]{1,0:T(8,128)(2,1)} %refs_3_.7, bf16[640,512]{1,0:T(8,128)(2,1)} %get-tuple-element.174.refs_4_.refs_9_, ...), custom_call_target="tpu_custom_call" | custom-call | flops 4026531 | bytes 10878 | tf_op jit(solution)/shard_map/pair_sum/pallas_call | solution.py:478
  323.7 2.5 merge.7
  327.1 2.6 collective-permute-start.24
  330.5 3.1 add_convert_fusion
  333.5 8.7 %weight_grad.14.own_away.own_kept = bf16[4,256,1408]{2,1,0:T(8,128)(2,1)} custom-call(s32[1]{0:T(128)} %bitcast.7.rank_ref._, bf16[320,2048]{1,0:T(8,128)(2,1)} %multiply_convert_fusion.xa_ref.refs_0_, bf16[320,2048]{1,0:T(8,128)(2,1)} %collective-permute-done.11.xb_ref.refs_1_, bf16[320,2048]{1,0:T(8,128)(2,1)} %collective-permute-done.10.xa_ref.refs_2_, ...), custom_call_target="tpu_custom_call" | custom-call | flops 3690987 | bytes 9109 | tf_op jit(solution)/shard_map/weight_grad/pallas_call | solution.py:324
  342.2 10.5 %pair_sum.15 = f32[320,2048]{1,0:T(8,128)} custom-call(bf16[640,512]{1,0:T(8,128)(2,1)} %get-tuple-element.175.refs_0_.refs_4_, bf16[2048,512]{1,0:T(8,128)(2,1)} %refs_1_.15, bf16[640,512]{1,0:T(8,128)(2,1)} %get-tuple-element.176.refs_2_.refs_6_, bf16[2048,512]{1,0:T(8,128)(2,1)} %refs_3_.7, bf16[640,512]{1,0:T(8,128)(2,1)} %get-tuple-element.177.refs_4_.refs_8_, ...), custom_call_target="tpu_custom_call" | custom-call | flops 4026531 | bytes 10878 | tf_op jit(solution)/shard_map/pair_sum/pallas_call | solution.py:478
  352.7 15.4 %weight_grad.15 = (bf16[4,256,512]{2,1,0:T(8,128)(2,1)}, bf16[4,256,512]{2,1,0:T(8,128)(2,1)}, bf16[4,256,512]{2,1,0:T(8,128)(2,1)}, bf16[4,256,512]{2,1,0:T(8,1...) custom-call(s32[1]{0:T(128)} %bitcast.7.rank_ref._, bf16[320,2048]{1,0:T(8,128)(2,1)} %copy-done.21, ...), custom_call_target="tpu_custom_call" | custom-call | flops 8053063 | bytes 15466 | tf_op jit(solution)/shard_map/weight_grad/pallas_call | solution.py:324
  368.2 2.5 convert_add_fusion.1
  379.5 139.4 %last_stages.1 = (f32[256,1408]{1,0:T(8,128)}, f32[256,1408]{1,0:T(8,128)}, f32[256,512]{1,0:T(8,128)}, f32[256,512]{1,0:T(8,128)}, f32[256,512]{1,0:T(8,128)}, /*index=5*/f32[256,512]{1,0:T(8,128)}, f32[2,2048]{1,0:T(2,128)}) custom-call(bf16[2,256,1408]{2,1,0:T(8,128)(2,1)} %copy-done.6, bf16[2,256,1408]{2,1,0:T(8,128)(2,1)} %copy-done.8, ...), custom_call_target="tpu_custom_call" | custom-call | flops 16777 | bytes 33554 | tf_op jit(solution)/shard_map/last_stages/pallas_call | solution.py:651
  519.0 2.0 copy.27
  521.0 2.5 add_bitcast_fusion
  523.5 2.9 copy.28
  526.4 4.9 fusion.8
  (153 shorter events, 56.1 us)
Async XLA Ops:
  0.6 6.6 %copy-start.34 = (s32[1,3]{1,0:T(1,128)S(1)}, s32[1,3]{1,0:T(1,128)}, u32[]{:S(2)}) copy-start(s32[1,3]{1,0:T(1,128)} %param.25) | copy-start | bytes 40
  0.7 6.9 %copy-start.32 = (s32[1,1280]{1,0:T(1,128)S(1)}, s32[1,1280]{1,0:T(1,128)}, u32[]{:S(2)}) copy-start(s32[1,1280]{1,0:T(1,128)} %param.27) | copy-start | bytes 15364
  0.7 7.1 %copy-start.33 = (s32[1,3]{1,0:T(1,128)S(1)}, s32[1,3]{1,0:T(1,128)}, u32[]{:S(2)}) copy-start(s32[1,3]{1,0:T(1,128)} %param.26) | copy-start | bytes 40
  4.1 10.4 %copy-start.21 = (bf16[320,2048]{1,0:T(8,128)(2,1)}, bf16[320,2048]{1,0:T(8,128)(2,1)S(1)}, u32[]{:S(2)}) copy-start(bf16[320,2048]{1,0:T(8,128)(2,1)S(1)} %fusion.4.xa_ref.refs_0_) | copy-start | bytes 3932164
  4.1 20.3 %collective-permute-start.4 = (bf16[320,2048]{1,0:T(8,128)(2,1)S(1)}, bf16[320,2048]{1,0:T(8,128)(2,1)}, u32[]{:S(2)}, u32[]{:S(2)}) collective-permute-start(bf16[320,2048]{1,0:T(8,128)(2,1)S(1)} %fusion.4.xa_ref.refs_0_), channel_id=1, source_target_pairs={{0,1},{1,0},{2,3},{3,2},{4,5},{5,4},{6,7},{7,6},{8,9},{9,8},{10,11... | collective-permute-start | bytes 3932168 | tf_op jit(solution)/shard_map/ppermute | solution.py:706
  4.6 32.1 %collective-permute-start = (bf16[320,2048]{1,0:T(8,128)(2,1)S(1)}, bf16[320,2048]{1,0:T(8,128)(2,1)}, u32[]{:S(2)}, u32[]{:S(2)}) collective-permute-start(bf16[320,2048]{1,0:T(8,128)(2,1)S(1)} %fusion.4.xa_ref.refs_0_), channel_id=1, source_target_pairs={{0,2},{1,3},{2,0},{3,1},{4,6},{5,7},{6,4},{7,5},{8,10},{9,11},{10,... | collective-permute-start | bytes 3932168 | tf_op jit(solution)/shard_map/ppermute | solution.py:706
  8.0 6.5 %collective-permute-start.1 = (f32[8]{0:T(128)S(1)}, f32[8]{0:T(128)S(1)}, u32[]{:S(2)}, u32[]{:S(2)}) collective-permute-start(f32[8]{0:T(128)S(1)} %select_reduce_fusion.1), channel_id=1, source_target_pairs={{0,4},{4,0},{8,12},{12,8},{16,20},{20,16},{24,28},{28,24},{1,5},{5... | collective-permute-start | bytes 104 | tf_op jit(solution)/shard_map/ppermute | solution.py:706
  9.5 14.5 %copy-start.23 = (bf16[320,2048]{1,0:T(8,128)(2,1)S(1)}, bf16[320,2048]{1,0:T(8,128)(2,1)}, u32[]{:S(2)}) copy-start(bf16[320,2048]{1,0:T(8,128)(2,1)} %param.15) | copy-start | bytes 3932164
  14.5 3.6 collective-permute-start.2
  18.1 4.5 collective-permute-start.3
  24.3 14.1 %copy-start.19 = (bf16[320,2048]{1,0:T(8,128)(2,1)}, bf16[320,2048]{1,0:T(8,128)(2,1)S(1)}, u32[]{:S(2)}) copy-start(bf16[320,2048]{1,0:T(8,128)(2,1)S(1)} %fusion.12.refs_0_) | copy-start | bytes 3932164
  36.7 3.4 collective-permute-start.5
  36.7 33.7 %collective-permute-start.7 = (bf16[320,2048]{1,0:T(8,128)(2,1)S(1)}, bf16[320,2048]{1,0:T(8,128)(2,1)}, u32[]{:S(2)}, u32[]{:S(2)}) collective-permute-start(bf16[320,2048]{1,0:T(8,128)(2,1)S(1)} %fusion.12.refs_0_), channel_id=1, source_target_pairs={{0,2},{1,3},{2,0},{3,1},{4,6},{5,7},{6,4},{7,5},{8,10},{9,11},{10,... | collective-permute-start | bytes 3932168 | tf_op jit(solution)/shard_map/ppermute | solution.py:706
  38.4 32.0 %collective-permute-start.6 = (bf16[320,2048]{1,0:T(8,128)(2,1)S(1)}, bf16[320,2048]{1,0:T(8,128)(2,1)S(1)}, u32[]{:S(2)}, u32[]{:S(2)}) collective-permute-start(bf16[320,2048]{1,0:T(8,128)(2,1)S(1)} %fusion.12.refs_0_), channel_id=1, source_target_pairs={{0,1},{1,0},{2,3},{3,2},{4,5},{5,4},{6,7},{7,6},{8,9},{9,8},{10,11... | collective-permute-start | bytes 3932168 | tf_op jit(solution)/shard_map/ppermute | solution.py:706
  70.4 9.3 %copy-start.20 = (bf16[320,2048]{1,0:T(8,128)(2,1)}, bf16[320,2048]{1,0:T(8,128)(2,1)S(1)}, u32[]{:S(2)}) copy-start(bf16[320,2048]{1,0:T(8,128)(2,1)S(1)} %collective-permute-done.6.refs_1_) | copy-start | bytes 3932164
  70.5 31.2 %collective-permute-start.8 = (bf16[320,2048]{1,0:T(8,128)(2,1)}, bf16[320,2048]{1,0:T(8,128)(2,1)}, u32[]{:S(2)}, u32[]{:S(2)}) collective-permute-start(bf16[320,2048]{1,0:T(8,128)(2,1)} %pair_sum.8), channel_id=1, source_target_pairs={{0,2},{1,3},{2,0},{3,1},{4,6},{5,7},{6,4},{7,5},{8,10},{9,11},{10,... | collective-permute-start | bytes 3932168 | tf_op jit(solution)/shard_map/ppermute | solution.py:706
  72.3 34.2 %collective-permute-start.9 = (bf16[320,2048]{1,0:T(8,128)(2,1)}, bf16[320,2048]{1,0:T(8,128)(2,1)}, u32[]{:S(2)}, u32[]{:S(2)}) collective-permute-start(bf16[320,2048]{1,0:T(8,128)(2,1)} %collective-permute-done.7.refs_0_.refs_2_), channel_id=1, source_target_pairs={{0,1},{1,0},{2,3},{3,2},{4,5},{5,4},{6,7},{7,6},{8,9},{9,8},{10,11... | collective-permute-start | bytes 3932168 | tf_op jit(solution)/shard_map/ppermute | solution.py:706
  88.1 16.7 %copy-start.30 = (f32[2048]{0:T(1024)S(1)}, f32[2048]{0:T(1024)}, u32[]{:S(2)}) copy-start(f32[2048]{0:T(1024)} %param.21) | copy-start | bytes 24580
  104.8 122.9 %copy-start.14 = (f32[320,2048]{1,0:T(8,128)}, f32[320,2048]{1,0:T(8,128)S(1)}, u32[]{:S(2)}) copy-start(f32[320,2048]{1,0:T(8,128)S(1)} %get-tuple-element.247) | copy-start | bytes 7864324
  114.8 3.4 collective-permute-start.11
  114.8 31.5 %collective-permute-start.10 = (bf16[320,2048]{1,0:T(8,128)(2,1)}, bf16[320,2048]{1,0:T(8,128)(2,1)}, u32[]{:S(2)}, u32[]{:S(2)}) collective-permute-start(bf16[320,2048]{1,0:T(8,128)(2,1)} %multiply_convert_fusion.xa_ref.refs_0_), channel_id=1, source_target_pairs={{0,2},{1,3},{2,0},{3,1},{4,6},{5,7},{6,4},{7,5},{8,10},{9,11},{10,... | collective-permute-start | bytes 3932168 | tf_op jit(solution)/shard_map/ppermute | solution.py:706
  146.3 3.4 collective-permute-start.12
  187.3 37.1 %collective-permute-start.13 = (bf16[320,2048]{1,0:T(8,128)(2,1)}, bf16[320,2048]{1,0:T(8,128)(2,1)}, u32[]{:S(2)}, u32[]{:S(2)}) collective-permute-start(bf16[320,2048]{1,0:T(8,128)(2,1)} %pair_sum.11), channel_id=1, source_target_pairs={{0,2},{1,3},{2,0},{3,1},{4,6},{5,7},{6,4},{7,5},{8,10},{9,11},{10,... | collective-permute-start | bytes 3932168 | tf_op jit(solution)/shard_map/ppermute | solution.py:706
  197.8 66.1 %collective-permute-start.16 = (bf16[4,256,1408]{2,1,0:T(8,128)(2,1)}, bf16[4,256,1408]{2,1,0:T(8,128)(2,1)}, u32[]{:S(2)}, u32[]{:S(2)}) collective-permute-start(bf16[4,256,1408]{2,1,0:T(8,128)(2,1)} %weight_grad.10), channel_id=1, source_target_pairs={{0,8},{4,12},{8,0},{12,4},{16,24},{20,28},{24,16},{28,20},{1,9},{5... | collective-permute-start | bytes 8650760 | tf_op jit(solution)/shard_map/ppermute | solution.py:706
  199.4 64.5 %collective-permute-start.15 = (bf16[4,256,1408]{2,1,0:T(8,128)(2,1)}, bf16[4,256,1408]{2,1,0:T(8,128)(2,1)}, u32[]{:S(2)}, u32[]{:S(2)}) collective-permute-start(bf16[4,256,1408]{2,1,0:T(8,128)(2,1)} %weight_grad.8), channel_id=1, source_target_pairs={{0,4},{4,0},{8,12},{12,8},{16,20},{20,16},{24,28},{28,24},{1,5},{5... | collective-permute-start | bytes 8650760 | tf_op jit(solution)/shard_map/ppermute | solution.py:706
  231.1 27.8 %collective-permute-start.17 = (bf16[320,2048]{1,0:T(8,128)(2,1)}, bf16[320,2048]{1,0:T(8,128)(2,1)}, u32[]{:S(2)}, u32[]{:S(2)}) collective-permute-start(bf16[320,2048]{1,0:T(8,128)(2,1)} %get-tuple-element.150.refs_0_), channel_id=1, source_target_pairs={{0,1},{1,0},{2,3},{3,2},{4,5},{5,4},{6,7},{7,6},{8,9},{9,8},{10,11... | collective-permute-start | bytes 3932168 | tf_op jit(solution)/shard_map/ppermute | solution.py:706
  231.4 32.5 %collective-permute-start.14 = (bf16[320,2048]{1,0:T(8,128)(2,1)}, bf16[320,2048]{1,0:T(8,128)(2,1)}, u32[]{:S(2)}, u32[]{:S(2)}) collective-permute-start(bf16[320,2048]{1,0:T(8,128)(2,1)} %get-tuple-element.150.refs_0_), channel_id=1, source_target_pairs={{0,2},{1,3},{2,0},{3,1},{4,6},{5,7},{6,4},{7,5},{8,10},{9,11},{10,... | collective-permute-start | bytes 3932168 | tf_op jit(solution)/shard_map/ppermute | solution.py:706
  258.9 5.0 copy-start.2
  263.9 6.6 %copy-start.1 = (bf16[4,256,1408]{2,1,0:T(8,128)(2,1)S(1)}, bf16[4,256,1408]{2,1,0:T(8,128)(2,1)}, u32[]{:S(2)}) copy-start(bf16[4,256,1408]{2,1,0:T(8,128)(2,1)} %weight_grad.12.own_away.own_kept) | copy-start | bytes 8650756
  268.0 43.0 %collective-permute-start.19 = (bf16[2,256,1408]{2,1,0:T(8,128)(2,1)}, bf16[2,256,1408]{2,1,0:T(8,128)(2,1)}, u32[]{:S(2)}, u32[]{:S(2)}) collective-permute-start(bf16[2,256,1408]{2,1,0:T(8,128)(2,1)} %get-tuple-element.162), channel_id=1, source_target_pairs={{0,8},{4,12},{8,0},{12,4},{16,24},{20,28},{24,16},{28,20},{1,9},{5... | collective-permute-start | bytes 4325384 | tf_op jit(solution)/shard_map/ppermute | solution.py:706
  268.5 6.4 %collective-permute-start.18 = (bf16[320,2048]{1,0:T(8,128)(2,1)}, bf16[320,2048]{1,0:T(8,128)(2,1)}, u32[]{:S(2)}, u32[]{:S(2)}) collective-permute-start(bf16[320,2048]{1,0:T(8,128)(2,1)} %collective-permute-done.14.refs_0_.refs_2_), channel_id=1, source_target_pairs={{0,1},{1,0},{2,3},{3,2},{4,5},{5,4},{6,7},{7,6},{8,9},{9,8},{10,11... | collective-permute-start | bytes 3932168 | tf_op jit(solution)/shard_map/ppermute | solution.py:706
  268.5 42.5 %collective-permute-start.20 = (bf16[320,2048]{1,0:T(8,128)(2,1)}, bf16[320,2048]{1,0:T(8,128)(2,1)}, u32[]{:S(2)}, u32[]{:S(2)}) collective-permute-start(bf16[320,2048]{1,0:T(8,128)(2,1)} %pair_sum.13), channel_id=1, source_target_pairs={{0,2},{1,3},{2,0},{3,1},{4,6},{5,7},{6,4},{7,5},{8,10},{9,11},{10,... | collective-permute-start | bytes 3932168 | tf_op jit(solution)/shard_map/ppermute | solution.py:706
  270.0 100.7 %collective-permute-start.22 = (bf16[4,256,1408]{2,1,0:T(8,128)(2,1)}, bf16[4,256,1408]{2,1,0:T(8,128)(2,1)S(1)}, u32[]{:S(2)}, u32[]{:S(2)}) collective-permute-start(bf16[4,256,1408]{2,1,0:T(8,128)(2,1)} %weight_grad.9), channel_id=1, source_target_pairs={{0,4},{4,0},{8,12},{12,8},{16,20},{20,16},{24,28},{28,24},{1,5},{5... | collective-permute-start | bytes 8650760 | tf_op jit(solution)/shard_map/ppermute | solution.py:706
  321.1 47.1 %collective-permute-start.21 = (bf16[320,2048]{1,0:T(8,128)(2,1)}, bf16[320,2048]{1,0:T(8,128)(2,1)}, u32[]{:S(2)}, u32[]{:S(2)}) collective-permute-start(bf16[320,2048]{1,0:T(8,128)(2,1)} %pair_sum.14), channel_id=1, source_target_pairs={{0,2},{1,3},{2,0},{3,1},{4,6},{5,7},{6,4},{7,5},{8,10},{9,11},{10,... | collective-permute-start | bytes 3932168 | tf_op jit(solution)/shard_map/ppermute | solution.py:706
  323.7 6.8 %copy-start.15 = (f32[320,2048]{1,0:T(8,128)S(1)}, f32[320,2048]{1,0:T(8,128)}, u32[]{:S(2)}) copy-start(f32[320,2048]{1,0:T(8,128)} %copy-done.14) | copy-start | bytes 7864324
  323.7 6.8 %copy-start.22 = (f32[320,2048]{1,0:T(8,128)S(1)}, f32[320,2048]{1,0:T(8,128)}, u32[]{:S(2)}) copy-start(f32[320,2048]{1,0:T(8,128)} %pair_sum.10) | copy-start | bytes 7864324
  327.1 43.7 %collective-permute-start.24 = (bf16[1,256,1408]{2,1,0:T(8,128)(2,1)}, bf16[1,256,1408]{2,1,0:T(8,128)(2,1)}, u32[]{:S(2)}, u32[]{:S(2)}) collective-permute-start(bf16[1,256,1408]{2,1,0:T(8,128)(2,1)} %get-tuple-element.185), channel_id=1, source_target_pairs={{0,16},{4,20},{8,24},{12,28},{16,0},{20,4},{24,8},{28,12},{1,17},{... | collective-permute-start | bytes 2162696 | tf_op jit(solution)/shard_map/ppermute | solution.py:706
  329.6 41.1 %collective-permute-start.23 = (bf16[4,256,512]{2,1,0:T(8,128)(2,1)}, bf16[4,256,512]{2,1,0:T(8,128)(2,1)}, u32[]{:S(2)}, u32[]{:S(2)}) collective-permute-start(bf16[4,256,512]{2,1,0:T(8,128)(2,1)} %get-tuple-element.181), channel_id=1, source_target_pairs={{0,4},{4,0},{8,12},{12,8},{16,20},{20,16},{24,28},{28,24},{1,5},{5... | collective-permute-start | bytes 3145736 | tf_op jit(solution)/shard_map/ppermute | solution.py:706
  368.1 2.6 copy-start.16
  368.1 2.6 copy-start.31
  371.6 4.2 copy-start
  379.5 141.5 %copy-start.11 = (bf16[1,256,1408]{2,1,0:T(8,128)(2,1)S(1)}, bf16[1,256,1408]{2,1,0:T(8,128)(2,1)}, u32[]{:S(2)}) copy-start(bf16[1,256,1408]{2,1,0:T(8,128)(2,1)} %copy-done.10) | copy-start | bytes 2162692
  521.0 5.4 copy-start.17
  526.4 6.3 %copy-start.29 = (f32[256,512]{1,0:T(8,128)S(1)}, f32[256,512]{1,0:T(8,128)}, u32[]{:S(2)}) copy-start(f32[256,512]{1,0:T(8,128)} %get-tuple-element.269) | copy-start | bytes 1572868
  526.4 7.1 %copy-start.28 = (f32[256,512]{1,0:T(8,128)S(1)}, f32[256,512]{1,0:T(8,128)}, u32[]{:S(2)}) copy-start(f32[256,512]{1,0:T(8,128)} %get-tuple-element.270) | copy-start | bytes 1572868
  526.4 7.9 %copy-start.27 = (f32[256,512]{1,0:T(8,128)S(1)}, f32[256,512]{1,0:T(8,128)}, u32[]{:S(2)}) copy-start(f32[256,512]{1,0:T(8,128)} %get-tuple-element.271) | copy-start | bytes 1572868
  531.2 3.8 copy-start.26
  533.5 2.7 copy-start.25
  (12 other events, 14.2 us)

commit v6 on v5

--- a/solution.py
+++ b/solution.py
@@ -503,13 +503,15 @@
     return {axis: rank + bit - 2 * bit * (rank // bit % 2)}
 
 
-def last_body(two, three, *refs):
-    mats = len(two) + three
+def last_body(ones, twos, threes, *refs):
+    mats = ones + twos + threes
     away, kept, refs = refs[:mats], refs[mats : 2 * mats], refs[2 * mats :]
-    gains_ref, outs, sums_ref, refs = refs[0], refs[1 : 1 + mats], refs[1 + mats], refs[2 + mats :]
+    ready_ref, got_ref, gains_ref, refs = refs[0], refs[1], refs[2], refs[3:]
+    outs, done_ref, sums_ref, refs = refs[:mats], refs[mats], refs[mats + 1], refs[mats + 2 :]
     own, first, refs = refs[:mats], refs[mats : 2 * mats], refs[2 * mats :]
-    held, to_z, from_z, refs = refs[:three], refs[three : 2 * three], refs[2 * three : 3 * three], refs[3 * three :]
-    to_last, from_last, refs = refs[:mats], refs[mats : 2 * mats], refs[2 * mats :]
+    held, to_z, from_z, refs = refs[:threes], refs[threes : 2 * threes], refs[2 * threes : 3 * threes], refs[3 * threes :]
+    late = twos + threes
+    to_last, from_last, total_s, refs = refs[:late], refs[late : 2 * late], refs[2 * late : 2 * late + twos], refs[2 * late + twos :]
     gain_in, gain_out, load_sem, send_sem, recv_sem = refs
     rank = lax.axis_index("dp")
     z1, z2 = rank // 2 % 2, rank // 4 % 2
@@ -538,14 +540,7 @@
     def side(bit, flip):
         return 1 - bit if flip else bit
 
-    loads = [pltpu.make_async_copy(kept[m], own[m], load_sem.at[m]) for m in range(mats)]
-    for load in loads:
-        load.start()
     stage = {}
-    for m in (2, 1, 0):
-        for flip in (1, 0):
-            stage[m, flip] = send(away[m].at[side(z2, flip)], first[m].at[flip], "dp", two[m])
-
     gain_out[0] = gains_ref[...]
     stage["gains"] = send(gain_out.at[0], gain_in.at[0], *hops[0])
 
@@ -558,31 +553,35 @@
         else:
             sums_ref[...] = total
 
-    gain_hop(0)
-    gain_hop(1)
-    for m in range(len(two), mats):
+    for m in range(ones, ones + twos):
+        for c in (1, 0):
+            stage[m, "z", c] = send(away[m].at[side(z2, c)], first[m].at[c], "dp", 2)
+    for m in range(ones):
+        stage[m, "last"] = send(away[m], first[m], "dp", 4)
+
+    def send_all(m):
         for a in (1, 0):
             for c in (1, 0):
                 stage[m, a, c] = send(away[m].at[side(z1, a) + 2 * side(z2, c)], first[m].at[2 * a + c], "dp", 1)
+
+    loads = [pltpu.make_async_copy(kept[m], own[m], load_sem.at[m]) for m in range(mats)]
+    for load in loads:
+        load.start()
+    send_all(ones + twos)
+    gain_hop(0)
+    gain_hop(1)
+    for m in range(ones + twos + 1, mats):
+        send_all(m)
     for load in loads:
         load.wait()
 
     def wide(value):
         return value.astype(jnp.float32)
-
-    def near_last(m, flip):
-        stage[m, flip].wait_recv()
-        total = wide(own[m][side(z2, flip)]) + wide(first[m][flip])
-        if flip:
-            to_last[m][...] = total.astype(jnp.bfloat16)
-            stage[m, "last"] = send(to_last[m], from_last[m], "dp", 4)
-        else:
-            outs[m][...] = total
 
     def from_x(m, a, c):
         stage[m, a, c].wait_recv()
         total = wide(own[m][side(z1, a) + 2 * side(z2, c)]) + wide(first[m][2 * a + c])
-        i = m - len(two)
+        i = m - ones - twos
         if a:
             to_z[i][c] = total.astype(jnp.bfloat16)
             stage[m, "z", c] = send(to_z[i].at[c], from_z[i].at[c], "dp", 2)
@@ -591,83 +590,94 @@
 
     def from_near(m, c):
         stage[m, "z", c].wait_recv()
-        i = m - len(two)
-        total = held[i][c] + wide(from_z[i][c])
+        if m < ones + twos:
+            total = wide(own[m][side(z2, c)]) + wide(first[m][c])
+            dst = total_s[m - ones]
+        else:
+            total = held[m - ones - twos][c] + wide(from_z[m - ones - twos][c])
+            dst = outs[m]
         if c:
-            to_last[m][...] = total.astype(jnp.bfloat16)
-            stage[m, "last"] = send(to_last[m], from_last[m], "dp", 4)
+            to_last[m - ones][...] = total.astype(jnp.bfloat16)
+            stage[m, "last"] = send(to_last[m - ones], from_last[m - ones], "dp", 4)
         else:
-            outs[m][...] = total
+            dst[...] = total
 
     def finish(m):
         stage[m, "last"].wait_recv()
-        outs[m][...] += wide(from_last[m][...])
+        if m < ones:
+            outs[m][...] = wide(own[m][0]) + wide(first[m][0])
+        elif m < ones + twos:
+            outs[m][...] = (total_s[m - ones][...] + wide(from_last[m - ones][...])).T
+        else:
+            outs[m][...] += wide(from_last[m - ones][...])
 
     gate, up, out, q, k, v = range(6)
-    near_last(out, 1)
-    near_last(out, 0)
-    near_last(gate, 1)
-    near_last(up, 1)
-    near_last(gate, 0)
-    gain_hop(2)
+    from_near(out, 1)
     from_x(q, 1, 1)
     from_x(q, 1, 0)
-    near_last(up, 0)
-    gain_hop(3)
+    from_near(out, 0)
     from_x(q, 0, 1)
     from_x(q, 0, 0)
+    done_ref[...] = (wide(ready_ref[0]) + wide(got_ref[0])).T
+    from_x(k, 1, 1)
     from_near(q, 1)
-    from_x(k, 1, 1)
+    from_x(k, 1, 0)
     from_near(q, 0)
-    from_x(k, 1, 0)
     from_x(k, 0, 1)
+    finish(gate)
     from_x(k, 0, 0)
-    finish(out)
+    gain_hop(2)
+    from_x(v, 1, 1)
     from_near(k, 1)
-    from_x(v, 1, 1)
+    from_x(v, 1, 0)
     from_near(k, 0)
-    from_x(v, 1, 0)
+    gain_hop(3)
+    finish(up)
     from_x(v, 0, 1)
     from_x(v, 0, 0)
+    finish(out)
     from_near(v, 1)
-    finish(gate)
     from_near(v, 0)
     gain_hop(4)
-    for m in (up, q, k, v):
+    for m in (q, k, v):
         finish(m)
     for copy in copies:
         copy.wait_send()
 
 
-def last_stages(two, three, gains):
-    mats = [t[:2] for t in two] + list(three)
+def last_stages(ones, twos, threes, ready, gains):
+    mats = [*ones, *twos, *threes]
     away, kept = [m[0] for m in mats], [m[1] for m in mats]
     shapes = [a.shape for a in away]
-    low = jnp.bfloat16
-    late = shapes[len(two) :]
+    low, wide = jnp.bfloat16, jnp.float32
+    late, last = shapes[len(ones) + len(twos) :], shapes[len(ones) :]
+    flat = [shape[1:] for shape in shapes]
+    for m in range(len(ones), len(ones) + len(twos)):
+        flat[m] = flat[m][::-1]
     any_space = pl.BlockSpec(memory_space=pl.ANY)
     inside = pl.BlockSpec(memory_space=pltpu.VMEM)
-    count = 3 * len(two) + 7 * len(three) + 5
+    count = len(ones) + 3 * len(twos) + 7 * len(threes) + 5
     result = pl.pallas_call(
-        functools.partial(last_body, [t[2] for t in two], len(three)),
-        in_specs=[any_space] * (2 * len(mats)) + [inside],
-        out_specs=[inside] * (len(mats) + 1),
-        out_shape=[jax.ShapeDtypeStruct(shape[1:], jnp.float32) for shape in shapes]
-        + [jax.ShapeDtypeStruct(gains.shape, jnp.float32)],
+        functools.partial(last_body, len(ones), len(twos), len(threes)),
+        in_specs=[any_space] * (2 * len(mats)) + [inside] * 3,
+        out_specs=[inside] * (len(mats) + 2),
+        out_shape=[jax.ShapeDtypeStruct(shape, wide) for shape in flat]
+        + [jax.ShapeDtypeStruct(ready[0].shape[:0:-1], wide), jax.ShapeDtypeStruct(gains.shape, wide)],
         scratch_shapes=[pltpu.VMEM(shape, low) for shape in shapes]
         + [pltpu.VMEM(shape, low) for shape in shapes]
-        + [pltpu.VMEM((2,) + shape[1:], jnp.float32) for shape in late]
+        + [pltpu.VMEM((2,) + shape[1:], wide) for shape in late]
         + [pltpu.VMEM((2,) + shape[1:], low) for shape in late]
         + [pltpu.VMEM((2,) + shape[1:], low) for shape in late]
-        + [pltpu.VMEM(shape[1:], low) for shape in shapes]
-        + [pltpu.VMEM(shape[1:], low) for shape in shapes]
-        + [pltpu.VMEM((5,) + gains.shape, jnp.float32)] * 2
+        + [pltpu.VMEM(shape[1:], low) for shape in last]
+        + [pltpu.VMEM(shape[1:], low) for shape in last]
+        + [pltpu.VMEM(shape[1:], wide) for shape in last[: len(twos)]]
+        + [pltpu.VMEM((5,) + gains.shape, wide)] * 2
         + [pltpu.SemaphoreType.DMA((len(mats),)), pltpu.SemaphoreType.DMA((count,)), pltpu.SemaphoreType.DMA((count,))],
         compiler_params=pltpu.CompilerParams(vmem_limit_bytes=62 << 20, collective_id=8),
         cost_estimate=cost(flops=1 << 24, bytes_accessed=1 << 25, transcendentals=0),
         name="last_stages",
-    )(*away, *kept, gains)
-    return result[:-1], result[-1]
+    )(*away, *kept, *ready, gains)
+    return result[:-2], result[-2], result[-1]
 
 
 def row_tables(length_row, group_row, mask_row):
@@ -853,10 +863,10 @@
     mine = pair_sum([(heads_n, w_out, False)], 1, jnp.float32)
     dm_near = project([((c0, c1), w_down, True)], jnp.float32)
     dm_far = project([((c2, c3), w_down, True)], jnp.float32)
+    got, dm_near, dm_far, mine = tie(got, dm_near, dm_far, mine)
     mid_h = x_f + mine + got.astype(jnp.float32)
     inv_b = lax.rsqrt(jnp.mean(mid_h * mid_h, axis=-1, keepdims=True) + epsilon)
     b0 = (mid_h * inv_b * gain_mlp).astype(jnp.bfloat16)
-    b0, dm_near, dm_far = tie(b0, dm_near, dm_far)
     b2 = to_far(b0)
     b1 = to_mate(b0)
     mid_near, dg_near, du_near = mlp_pair(b0, b1, dm_near, w_gate, w_up)
@@ -874,12 +884,16 @@
     down_got = hop(down_send, 1)
     (gate_send,) = grad_gate.compute(1)
     y5 = pair_sum([(dg_f, w_gate, True), (du_f, w_up, True)], 2, jnp.bfloat16)
-    dg_n, du_n, y5 = tie(dg_near, du_near, y5)
+    dg_n, du_n, mid_n, y5 = tie(dg_near, du_near, mid_near, y5)
     gate_got = hop(gate_send, 2)
     got = to_far(y5)
     d_b = pair_sum([(dg_n, w_gate, True), (du_n, w_up, True)], 3, jnp.float32) + got.astype(jnp.float32)
     (up_send,) = WeightGrad(dp_rank, b_all, [(du_n, du_far)]).compute(1)
-    d_b, up_send = tie(d_b, up_send)
+    (down_own,) = WeightGrad(dp_rank, c_all, [(mid_n, mid_far)]).compute(0)
+    d_b, up_send, down_got, down_own = tie(d_b, up_send, down_got, down_own)
+    up_got = hop(up_send, 1)
+    down = Halving(dp_rank, down_own)
+    down_got = hop(down.merge(down_got, 2), 2)
 
     n_b = mid_h * inv_b
     gain_mlp_part = jnp.sum(d_b * n_b, axis=0)
@@ -892,57 +906,59 @@
     t1 = to_mate(t0)
     gs_near = project([((t0, t1), w_out, True)])
     y8 = pair_sum([(mid_f, w_down, False)], 4, jnp.bfloat16)
-    (down_own,) = WeightGrad(dp_rank, c_all, [(mid_near, mid_f)]).compute(0)
     (gate_own,) = WeightGrad(dp_rank, b_all, [(dg_n, dg_far)], 2).compute(0)
-    t2, down_got, gate_got, gs_near, y8, down_own, gate_own = tie(t2, down_got, gate_got, gs_near, y8, down_own, gate_own)
-
-    up_got = hop(up_send, 1)
+    t2, gate_got, gs_near, y8, gate_own = tie(t2, gate_got, gs_near, y8, gate_own)
+
     got8 = to_far(y8)
-    down, gate = Halving(dp_rank, down_own), Halving(dp_rank, gate_own, 2)
-    down_got = hop(down.merge(down_got, 2), 2)
+    gate = Halving(dp_rank, gate_own, 2)
     t3 = to_mate(t2)
     gs_far = project([((t2, t3), w_out, True)])
     gate_away = gate.merge(gate_got, 1)
+    (up_own,) = WeightGrad(dp_rank, b_all, [(du_n, du_far)]).compute(0)
     out_send, out_own = WeightGrad(dp_rank, (t0, t1, t2, t3), [(heads_near, heads_far)]).compute(1, 0)
     dqn, dqf, dkn, dkf, dvn, dvf = attend_back(
         rank_ref, qs, ks, vs, (gs_near, gs_far), low, high, lse, cosine, back_sine
     )
-    dqf, dkf, dvf, down_got, got8, out_send, gate_away = tie(dqf, dkf, dvf, down_got, got8, out_send, gate_away)
-
-    out_got = hop(out_send, 1)
+    dqf, dkf, dvf, down_got, got8, out_send, gate_away, up_got, up_own = tie(
+        dqf, dkf, dvf, down_got, got8, out_send, gate_away, up_got, up_own
+    )
+
+    out_got, gate_got = hop(out_send, 1), hop(gate_away, 1)
+    up = Halving(dp_rank, up_own)
+    up_got = hop(up.merge(up_got, 2), 2)
     y7 = pair_sum([(dqf, w_query, True), (dkf, w_key, True), (dvf, w_value, True)], 6, jnp.bfloat16)
-    dqn, dkn, dvn, dun, y7 = tie(dqn, dkn, dvn, du_near, y7)
+    dqn, dkn, dvn, y7 = tie(dqn, dkn, dvn, y7)
     got = to_far(y7)
     grad_qkv = WeightGrad(dp_rank, (a0, a1, a2, a3), [(dqn, dqf), (dkn, dkf), (dvn, dvf)])
     *sends, q_own, k_own, v_own = grad_qkv.compute(1, 0)
     down_got = hop(down.merge(down_got, half), half)
     d_a = pair_sum([(dqn, w_query, True), (dkn, w_key, True), (dvn, w_value, True)], 7, jnp.float32) + got.astype(jnp.float32)
-    (up_own,) = WeightGrad(dp_rank, b_all, [(dun, du_far)]).compute(0)
-    d_a, up_own, up_got, out_got, gate_away, down_got, *sends = tie(
-        d_a, up_own, up_got, out_got, gate_away, down_got, *sends
-    )
-
-    up, out = Halving(dp_rank, up_own), Halving(dp_rank, out_own)
-    up_away, out_away = up.merge(up_got, 2), out.merge(out_got, 2)
+    d_a, up_got, out_got, gate_got, down_got, *sends = tie(d_a, up_got, out_got, gate_got, down_got, *sends)
+
+    out = Halving(dp_rank, out_own)
+    out_away = out.merge(out_got, 2)
+    gate_away, up_away = gate.merge(gate_got, half), up.merge(up_got, half)
     output = (mid_h + mine8 + got8.astype(jnp.float32)).astype(jnp.bfloat16)
     n_a = x_f * inv_a
     gain_attn_part = jnp.sum(d_a * n_a, axis=0)
     e_a = d_a * gain_attn
     grad_input = d_h + inv_a * (e_a - n_a * jnp.mean(e_a * n_a, axis=-1, keepdims=True))
     gains = jnp.stack([gain_attn_part, gain_mlp_part])
-    sum_down = down.finish(down_got)
     if grad_qkv.kernel and half == 4:
-        (sum_gate, sum_up, sum_out, *sums), gains = last_stages(
-            [(gate_away, gate.kept, 1), (up_away, up.kept, 2), (out_away, out.kept, 2)],
+        (sum_gate, sum_up, sum_out, *sums), sum_down, gains = last_stages(
+            [(gate_away, gate.kept), (up_away, up.kept)],
+            [(out_away, out.kept)],
             list(zip(sends, (q_own, k_own, v_own))),
+            (down.kept, down_got),
             gains,
         )
         gains = lax.dynamic_slice_in_dim(gains, dp_rank[0] * grad_qkv.tile, grad_qkv.tile, 1)
     else:
         gains = butterfly_sum(scatter_small(gains.reshape(2, lax.axis_size("dp"), -1), "dp"), "tensor")
-        sum_gate = gate.finish(hop(gate_away, 1))
-        sum_up = up.finish(hop(up_away, 2))
-        sum_out = out.finish(hop(out_away, 2))
+        sum_gate = gate.finish(hop(gate_away, half))
+        sum_up = up.finish(hop(up_away, half))
+        sum_out = out.finish(hop(out_away, 2)).T
+        sum_down = down.finish(down_got).T
         sums = [Halving(dp_rank, own).finish(hop(send, 1)) for send, own in zip(sends, (q_own, k_own, v_own))]
     return (
         output,
@@ -951,11 +967,11 @@
         sums[0],
         sums[1],
         sums[2],
-        sum_out.T,
+        sum_out,
         gains[1],
         sum_gate,
         sum_up,
-        sum_down.T,
+        sum_down,
     )
 
 

time: 543 us -> 528 us (0.972)
  Pallas kernels: 421 us -> 399 us
  starting transfers between devices: 27.2 us -> 32.7 us
    pallas_call x1, Pallas kernels: 139 us -> 117 us  [last_stages(): pl.pallas_call(functools.partial(last_body, len(ones), len(twos), len(thr...]
    ppermute x25 -> x27, starting transfers between devices: 27.2 us -> 32.7 us  [exchange(): lax.ppermute(values, axis, [(rank, rank ^ bit) for rank in range(size)])]
    ppermute x25 -> x27, waiting for transfers between devices: 28.9 us -> 32.9 us  [exchange(): lax.ppermute(values, axis, [(rank, rank ^ bit) for rank in range(size)])]
    unnamed x77 -> x107, local copies, waits for them, and re-layouts: 20.6 us -> 22.5 us
  transfers between devices with their start and end apart: 25 -> 27, of which waited for: 8 -> 12; matrix products, arithmetic and copies ran while one was open for 5% -> 4% of each run, Pallas kernels for 43% -> 47%
where the time goes in v6:
time: 528 us; the launch traced here: 522 us
  Pallas kernels  399 us (76%)
  waiting for transfers between devices  32.9 us (6%)
  starting transfers between devices  32.7 us (6%)
  other arithmetic  31.7 us (6%)
  local copies, waits for them, and re-layouts  24.6 us (5%)
    pallas_call x1, Pallas kernels, last_stages(): pl.pallas_call(functools.partial(last_body, len(ones), len(twos), len(thr...  117 us
    pallas_call x8, Pallas kernels, pair_sum(): pl.pallas_call(functools.partial(pair_body, [(len(left), dims) for left,...  83.6 us
    pallas_call x8, Pallas kernels, grad_call(): pl.pallas_call(functools.partial(grad_body, len(pieces), widths, low, sid...  77.2 us
    ppermute x27, waiting for transfers between devices, exchange(): lax.ppermute(values, axis, [(rank, rank ^ bit) for rank in range(size)])  32.9 us
    ppermute x27, starting transfers between devices, exchange(): lax.ppermute(values, axis, [(rank, rank ^ bit) for rank in range(size)])  32.7 us
    pallas_call x2, Pallas kernels, mlp_pair(): pl.pallas_call(mlp_body, grid=(pl.cdiv(width, tile),), in_specs=[whole(xa...  29.4 us
    pallas_call x4, Pallas kernels, project(): pl.pallas_call(functools.partial(project_body, [(len(left), dims) for lef...  26.5 us
    unnamed x107, local copies, waits for them, and re-layouts  22.5 us
  transfers between devices with their start and end apart: 27, of which 12 were waited for; matrix products, arithmetic and copies ran while one was open for 4% of the time, Pallas kernels for 47%

profile of v6, /device:TPU:0, one launch (start us, length us, event | category | flops | bytes accessed | tf_op | source)
XLA Modules:
  0.0 522.1 jit_solution(8675302460961327049)
XLA Ops:
  4.6 2.6 collective-permute-start
  9.6 2.4 fusion.13
  16.1 2.0 collective-permute-done.2
  18.1 2.6 collective-permute-start.3
  20.7 1.9 collective-permute-done.3
  25.4 9.4 %qkv.2 = (bf16[640,512]{1,0:T(8,128)(2,1)}, bf16[640,512]{1,0:T(8,128)(2,1)}, bf16[640,512]{1,0:T(8,128)(2,1)}) custom-call(s32[1]{0:T(128)} %bitcast.rank_ref, bf16[320,2048]{1,0:T(8,128)(2,1)} %copy-done.32, bf16[320,2048]{1,0:T(8,128)(2,1)} %copy-done.35, f32[1280,128]{1,0:T(8,128)} %pad_maximum_fusion.cos_ref, f32[1280,128]{1,0:T(8,128)} %get-tuple-element.243.sin_ref, ...), custom_call_target="tpu_custom_call" | custom-call | flops 4026531 | bytes 8912 | tf_op jit(solution)/shard_map/qkv/pallas_call | solution.py:67
  34.8 1.9 collective-permute-done.xa_ref.refs_2_
  40.1 8.9 %qkv.3 = (bf16[640,512]{1,0:T(8,128)(2,1)}, bf16[640,512]{1,0:T(8,128)(2,1)}, bf16[640,512]{1,0:T(8,128)(2,1)}) custom-call(s32[1]{0:T(128)} %bitcast.rank_ref, bf16[320,2048]{1,0:T(8,128)(2,1)} %collective-permute-done.xa_ref.refs_2_, bf16[320,2048]{1,0:T(8,128)(2,1)} %collective-permute-done.5.xb_ref.refs_3_, f32[1280,128]{1,0:T(8,128)} %pad_maximum_fusion.cos_ref, ...), custom_call_target="tpu_custom_call" | custom-call | flops 4026531 | bytes 8912 | tf_op jit(solution)/shard_map/qkv/pallas_call | solution.py:67
  49.0 14.6 %attend.1 = (bf16[640,512]{1,0:T(8,128)(2,1)}, bf16[640,512]{1,0:T(8,128)(2,1)}, f32[4,1,1280]{2,1,0:T(1,128)}) custom-call(s32[1]{0:T(128)} %bitcast.rank_ref, bf16[640,512]{1,0:T(8,128)(2,1)} %get-tuple-element.124.qn, bf16[640,512]{1,0:T(8,128)(2,1)} %get-tuple-element.126.qf, bf16[640,512]{1,0:T(8,128)(2,1)} %get-tuple-element.127.kn, ...), custom_call_target="tpu_custom_call" | custom-call | flops 6710886 | bytes 5242 | tf_op jit(solution)/shard_map/attend/pallas_call | solution.py:128
  63.6 6.9 %pair_sum.8 = bf16[320,2048]{1,0:T(8,128)(2,1)} custom-call(bf16[640,512]{1,0:T(8,128)(2,1)} %get-tuple-element.133.refs_0_.refs_5_, bf16[512,2048]{1,0:T(8,128)(2,1)} %refs_2_.7), custom_call_target="tpu_custom_call" | custom-call | flops 1342177 | bytes 5373 | tf_op jit(solution)/shard_map/pair_sum/pallas_call | solution.py:478
  72.5 7.4 %pair_sum.9 = f32[320,2048]{1,0:T(8,128)} custom-call(bf16[640,512]{1,0:T(8,128)(2,1)} %get-tuple-element.137.refs_0_.refs_4_, bf16[512,2048]{1,0:T(8,128)(2,1)} %refs_2_.7), custom_call_target="tpu_custom_call" | custom-call | flops 1342177 | bytes 5373 | tf_op jit(solution)/shard_map/pair_sum/pallas_call | solution.py:478
  79.8 8.4 %project.4.dm_ref = f32[640,1408]{1,0:T(8,128)} custom-call(bf16[320,2048]{1,0:T(8,128)(2,1)} %copy-done.29, bf16[320,2048]{1,0:T(8,128)(2,1)} %copy-done.31, bf16[1408,2048]{1,0:T(8,128)(2,1)} %refs_1_.13), custom_call_target="tpu_custom_call" | custom-call | flops 3690987 | bytes 10190 | tf_op jit(solution)/shard_map/project/pallas_call | solution.py:414
  88.2 8.6 %project.5.dm_ref = f32[640,1408]{1,0:T(8,128)} custom-call(bf16[320,2048]{1,0:T(8,128)(2,1)} %copy-done.30, bf16[320,2048]{1,0:T(8,128)(2,1)} %collective-permute-done.9.refs_1_.refs_3_, bf16[1408,2048]{1,0:T(8,128)(2,1)} %refs_1_.13), custom_call_target="tpu_custom_call" | custom-call | flops 3690987 | bytes 10190 | tf_op jit(solution)/shard_map/project/pallas_call | solution.py:414
  96.8 5.3 %collective-permute-done.8 = bf16[320,2048]{1,0:T(8,128)(2,1)} collective-permute-done((bf16[320,2048]{1,0:T(8,128)(2,1)}, bf16[320,2048]{1,0:T(8,128)(2,1)}, u32[]{:S(2)}, u32[]{:S(2)}) %collective-permute-start.8) | collective-permute-done | bytes 1310752 | tf_op jit(solution)/shard_map/ppermute | solution.py:716
  102.1 1.9 multiply_reduce_fusion.2
  110.0 14.8 %mlp.2 = (bf16[640,1408]{1,0:T(8,128)(2,1)}, bf16[640,1408]{1,0:T(8,128)(2,1)}, bf16[640,1408]{1,0:T(8,128)(2,1)}) custom-call(bf16[320,2048]{1,0:T(8,128)(2,1)} %copy-done.21, bf16[320,2048]{1,0:T(8,128)(2,1)} %copy-done.22, f32[640,1408]{1,0:T(8,128)} %project.4.dm_ref, bf16[2048,1408]{1,0:T(8,128)(2,1)} %refs_1_.12, bf16[2048,1408]{1,0:T(8,128)(2,1)} %refs_3_.5), custom_call_target="tpu_custom_call" | custom-call | flops 7381975 | bytes 23166 | tf_op jit(solution)/shard_map/mlp/pallas_call | solution.py:234
  124.8 10.0 %pair_sum.10 = f32[320,2048]{1,0:T(8,128)} custom-call(bf16[640,1408]{1,0:T(8,128)(2,1)} %get-tuple-element.159.refs_0_.refs_4_, bf16[1408,2048]{1,0:T(8,128)(2,1)} %refs_1_.13), custom_call_target="tpu_custom_call" | custom-call | flops 3690987 | bytes 10190 | tf_op jit(solution)/shard_map/pair_sum/pallas_call | solution.py:478
  134.7 2.3 collective-permute-done.10.xa_ref.refs_2_
  137.1 3.0 collective-permute-done.12.xb_ref.refs_3_
  141.2 14.6 %mlp.3 = (bf16[640,1408]{1,0:T(8,128)(2,1)}, bf16[640,1408]{1,0:T(8,128)(2,1)}, bf16[640,1408]{1,0:T(8,128)(2,1)}) custom-call(bf16[320,2048]{1,0:T(8,128)(2,1)} %copy-done.23, bf16[320,2048]{1,0:T(8,128)(2,1)} %copy-done.24, f32[640,1408]{1,0:T(8,128)} %project.5.dm_ref, bf16[2048,1408]{1,0:T(8,128)(2,1)} %refs_1_.12, bf16[2048,1408]{1,0:T(8,128)(2,1)} %refs_3_.5), custom_call_target="tpu_custom_call" | custom-call | flops 7381975 | bytes 23166 | tf_op jit(solution)/shard_map/mlp/pallas_call | solution.py:234
  155.8 8.7 %weight_grad.8 = bf16[4,256,1408]{2,1,0:T(8,128)(2,1)} custom-call(s32[1]{0:T(128)} %bitcast.7.rank_ref._, bf16[320,2048]{1,0:T(8,128)(2,1)} %copy-done.29, bf16[320,2048]{1,0:T(8,128)(2,1)} %copy-done.31, bf16[320,2048]{1,0:T(8,128)(2,1)} %copy-done.30, bf16[320,2048]{1,0:T(8,128)(2,1)} %collective-permute-done.9.refs_1_.refs_3_, ...), custom_call_target="tpu_custom_call" | custom-call | flops 3690987 | bytes 9109 | tf_op jit(solution)/shard_map/weight_grad/pallas_call | solution.py:324
  166.2 14.3 %pair_sum.11 = bf16[320,2048]{1,0:T(8,128)(2,1)} custom-call(bf16[640,1408]{1,0:T(8,128)(2,1)} %get-tuple-element.153.refs_0_.refs_5_, bf16[2048,1408]{1,0:T(8,128)(2,1)} %refs_1_.12, bf16[640,1408]{1,0:T(8,128)(2,1)} %get-tuple-element.154.refs_2_.refs_5_, bf16[2048,1408]{1,0:T(8,128)(2,1)} %refs_3_.5), custom_call_target="tpu_custom_call" | custom-call | flops 7381975 | bytes 17760 | tf_op jit(solution)/shard_map/pair_sum/pallas_call | solution.py:478
  182.1 8.8 %weight_grad.11 = bf16[4,256,1408]{2,1,0:T(8,128)(2,1)} custom-call(s32[1]{0:T(128)} %bitcast.7.rank_ref._, bf16[320,2048]{1,0:T(8,128)(2,1)} %copy-done.21, bf16[320,2048]{1,0:T(8,128)(2,1)} %copy-done.22, bf16[320,2048]{1,0:T(8,128)(2,1)} %copy-done.23, bf16[320,2048]{1,0:T(8,128)(2,1)} %copy-done.24, ...), custom_call_target="tpu_custom_call" | custom-call | flops 3690987 | bytes 9109 | tf_op jit(solution)/shard_map/weight_grad/pallas_call | solution.py:324
  192.4 8.7 %weight_grad.10.own_away.own_kept = bf16[4,256,1408]{2,1,0:T(8,128)(2,1)} custom-call(s32[1]{0:T(128)} %bitcast.7.rank_ref._, bf16[320,2048]{1,0:T(8,128)(2,1)} %copy-done.29, bf16[320,2048]{1,0:T(8,128)(2,1)} %copy-done.31, bf16[320,2048]{1,0:T(8,128)(2,1)} %copy-done.30, bf16[320,2048]{1,0:T(8,128)(2,1)} %collective-permute-done.9.refs_1_.refs_3_, ...), custom_call_target="tpu_custom_call" | custom-call | flops 3690987 | bytes 9109 | tf_op jit(solution)/shard_map/weight_grad/pallas_call | solution.py:324
  201.1 8.7 %weight_grad.9 = bf16[4,256,1408]{2,1,0:T(8,128)(2,1)} custom-call(s32[1]{0:T(128)} %bitcast.7.rank_ref._, bf16[320,2048]{1,0:T(8,128)(2,1)} %copy-done.21, bf16[320,2048]{1,0:T(8,128)(2,1)} %copy-done.22, bf16[320,2048]{1,0:T(8,128)(2,1)} %copy-done.23, bf16[320,2048]{1,0:T(8,128)(2,1)} %copy-done.24, bf16[640,1408]{1,0:T(8,128)(2,1)} %get-tuple-element.179.refs_2_.refs_4_, ...), custom_call_target="tpu_custom_call" | custom-call | flops 3690987 | bytes 9109 | tf_op jit(solution)/shard_map/weight_grad/pallas_call | solution.py:324
  209.8 14.9 %pair_sum.12 = f32[320,2048]{1,0:T(8,128)} custom-call(bf16[640,1408]{1,0:T(8,128)(2,1)} %get-tuple-element.163.refs_0_.refs_4_, bf16[2048,1408]{1,0:T(8,128)(2,1)} %refs_1_.12, bf16[640,1408]{1,0:T(8,128)(2,1)} %get-tuple-element.179.refs_2_.refs_4_, bf16[2048,1408]{1,0:T(8,128)(2,1)} %refs_3_.5), custom_call_target="tpu_custom_call" | custom-call | flops 7381975 | bytes 17760 | tf_op jit(solution)/shard_map/pair_sum/pallas_call | solution.py:478
  224.8 2.6 convert_add_fusion.2
  231.7 2.9 fusion.16
  240.3 9.5 %pair_sum.13 = bf16[320,2048]{1,0:T(8,128)(2,1)} custom-call(bf16[640,1408]{1,0:T(8,128)(2,1)} %get-tuple-element.162.refs_5_.refs_0_, bf16[1408,2048]{1,0:T(8,128)(2,1)} %refs_1_.13), custom_call_target="tpu_custom_call" | custom-call | flops 3690987 | bytes 10190 | tf_op jit(solution)/shard_map/pair_sum/pallas_call | solution.py:478
  249.8 8.8 %weight_grad.12.own_away.own_kept = bf16[4,256,1408]{2,1,0:T(8,128)(2,1)} custom-call(s32[1]{0:T(128)} %bitcast.7.rank_ref._, bf16[320,2048]{1,0:T(8,128)(2,1)} %copy-done.21, bf16[320,2048]{1,0:T(8,128)(2,1)} %copy-done.22, bf16[320,2048]{1,0:T(8,128)(2,1)} %copy-done.23, bf16[320,2048]{1,0:T(8,128)(2,1)} %copy-done.24, ...), custom_call_target="tpu_custom_call" | custom-call | flops 3690987 | bytes 9109 | tf_op jit(solution)/shard_map/weight_grad/pallas_call | solution.py:324
  258.6 4.8 project.6.gn
  263.4 2.7 collective-permute-done.15.refs_0_.refs_2_
  267.7 8.8 %weight_grad.14.own_away.own_kept = bf16[4,256,1408]{2,1,0:T(8,128)(2,1)} custom-call(s32[1]{0:T(128)} %bitcast.7.rank_ref._, bf16[320,2048]{1,0:T(8,128)(2,1)} %copy-done.21, bf16[320,2048]{1,0:T(8,128)(2,1)} %copy-done.22, bf16[320,2048]{1,0:T(8,128)(2,1)} %copy-done.23, bf16[320,2048]{1,0:T(8,128)(2,1)} %copy-done.24, ...), custom_call_target="tpu_custom_call" | custom-call | flops 3690987 | bytes 9109 | tf_op jit(solution)/shard_map/weight_grad/pallas_call | solution.py:324
  276.4 2.1 merge.8
  280.8 4.8 project.7.gf
  285.6 9.3 %weight_grad.13 = (bf16[4,256,512]{2,1,0:T(8,128)(2,1)}, bf16[4,256,512]{2,1,0:T(8,128)(2,1)}) custom-call(s32[1]{0:T(128)} %bitcast.7.rank_ref._, bf16[320,2048]{1,0:T(8,128)(2,1)} %get-tuple-element.161.refs_0_, bf16[320,2048]{1,0:T(8,128)(2,1)} %collective-permute-done.17.refs_1_, bf16[320,2048]{1,0:T(8,128)(2,1)} %collective-permute-done.15.refs_0_.refs_2_, ...), custom_call_target="tpu_custom_call" | custom-call | flops 2684354 | bytes 8650 | tf_op jit(solution)/shard_map/weight_grad/pallas_call | solution.py:324
  294.8 22.0 %attend_back.1 = (bf16[640,512]{1,0:T(8,128)(2,1)}, bf16[640,512]{1,0:T(8,128)(2,1)}, bf16[640,512]{1,0:T(8,128)(2,1)}, bf16[640,512]{1,0:T(8,128)(2,1)}, bf16[6...) custom-call(s32[1]{0:T(128)} %bitcast.rank_ref, bf16[640,512]{1,0:T(8,128)(2,1)} %get-tuple-element.124.qn, ...), custom_call_target="tpu_custom_call" | custom-call | flops 16777216 | bytes 10485 | tf_op jit(solution)/shard_map/attend_back/pallas_call | solution.py:191
  316.9 10.2 %pair_sum.14 = bf16[320,2048]{1,0:T(8,128)(2,1)} custom-call(bf16[640,512]{1,0:T(8,128)(2,1)} %get-tuple-element.184.refs_0_.refs_5_, bf16[2048,512]{1,0:T(8,128)(2,1)} %refs_1_.15, bf16[640,512]{1,0:T(8,128)(2,1)} %get-tuple-element.185.refs_2_.refs_7_, bf16[2048,512]{1,0:T(8,128)(2,1)} %refs_3_.7, bf16[640,512]{1,0:T(8,128)(2,1)} %get-tuple-element.186.refs_4_.refs_9_, ...), custom_call_target="tpu_custom_call" | custom-call | flops 4026531 | bytes 10878 | tf_op jit(solution)/shard_map/pair_sum/pallas_call | solution.py:478
  328.0 2.8 merge.9
  337.7 2.6 collective-permute-start.26
  341.8 3.1 add_convert_fusion
  344.9 10.4 %pair_sum.15 = f32[320,2048]{1,0:T(8,128)} custom-call(bf16[640,512]{1,0:T(8,128)(2,1)} %get-tuple-element.187.refs_0_.refs_4_, bf16[2048,512]{1,0:T(8,128)(2,1)} %refs_1_.15, bf16[640,512]{1,0:T(8,128)(2,1)} %get-tuple-element.188.refs_2_.refs_6_, bf16[2048,512]{1,0:T(8,128)(2,1)} %refs_3_.7, bf16[640,512]{1,0:T(8,128)(2,1)} %get-tuple-element.189.refs_4_.refs_8_, ...), custom_call_target="tpu_custom_call" | custom-call | flops 4026531 | bytes 10878 | tf_op jit(solution)/shard_map/pair_sum/pallas_call | solution.py:478
  355.4 15.4 %weight_grad.15 = (bf16[4,256,512]{2,1,0:T(8,128)(2,1)}, bf16[4,256,512]{2,1,0:T(8,128)(2,1)}, bf16[4,256,512]{2,1,0:T(8,128)(2,1)}, bf16[4,256,512]{2,1,0:T(8,1...) custom-call(s32[1]{0:T(128)} %bitcast.7.rank_ref._, bf16[320,2048]{1,0:T(8,128)(2,1)} %copy-done.32, ...), custom_call_target="tpu_custom_call" | custom-call | flops 8053063 | bytes 15466 | tf_op jit(solution)/shard_map/weight_grad/pallas_call | solution.py:324
  370.8 2.5 convert_add_fusion.1
  373.4 6.7 %collective-permute-done.26.refs_13_ = bf16[1,256,1408]{2,1,0:T(8,128)(2,1)} collective-permute-done((bf16[1,256,1408]{2,1,0:T(8,128)(2,1)S(1)}, bf16[1,256,1408]{2,1,0:T(8,128)(2,1)}, u32[]{:S(2)}, u32[]{:S(2)}) %collective-permute-start.26) | collective-permute-done | bytes 720928 | tf_op jit(solution)/shard_map/ppermute | solution.py:716
  380.0 3.8 collective-permute-done.24.got_away.got_kept
  392.5 116.6 %last_stages.1 = (f32[256,1408]{1,0:T(8,128)}, f32[256,1408]{1,0:T(8,128)}, f32[512,256]{1,0:T(8,128)}, f32[256,512]{1,0:T(8,128)}, f32[256,512]{1,0:T(8,128)}, ...) custom-call(bf16[1,256,1408]{2,1,0:T(8,128)(2,1)} %copy-done.11, bf16[1,256,1408]{2,1,0:T(8,128)(2,1)} %copy-done.13, ...), custom_call_target="tpu_custom_call" | custom-call | flops 16777 | bytes 33554 | tf_op jit(solution)/shard_map/last_stages/pallas_call | solution.py:660
  509.1 4.9 fusion.8
  (188 shorter events, 70.0 us)
Async XLA Ops:
  0.7 6.9 %copy-start.47 = (s32[1,1280]{1,0:T(1,128)S(1)}, s32[1,1280]{1,0:T(1,128)}, u32[]{:S(2)}) copy-start(s32[1,1280]{1,0:T(1,128)} %param.27) | copy-start | bytes 15364
  0.7 7.1 %copy-start.48 = (s32[1,3]{1,0:T(1,128)S(1)}, s32[1,3]{1,0:T(1,128)}, u32[]{:S(2)}) copy-start(s32[1,3]{1,0:T(1,128)} %param.26) | copy-start | bytes 40
  4.1 10.4 %copy-start.32 = (bf16[320,2048]{1,0:T(8,128)(2,1)}, bf16[320,2048]{1,0:T(8,128)(2,1)S(1)}, u32[]{:S(2)}) copy-start(bf16[320,2048]{1,0:T(8,128)(2,1)S(1)} %fusion.4.xa_ref.refs_0_) | copy-start | bytes 3932164
  4.1 20.2 %collective-permute-start.4 = (bf16[320,2048]{1,0:T(8,128)(2,1)S(1)}, bf16[320,2048]{1,0:T(8,128)(2,1)S(1)}, u32[]{:S(2)}, u32[]{:S(2)}) collective-permute-start(bf16[320,2048]{1,0:T(8,128)(2,1)S(1)} %fusion.4.xa_ref.refs_0_), channel_id=1, source_target_pairs={{0,1},{1,0},{2,3},{3,2},{4,5},{5,4},{6,7},{7,6},{8,9},{9,8},{10,11... | collective-permute-start | bytes 3932168 | tf_op jit(solution)/shard_map/ppermute | solution.py:716
  4.6 32.1 %collective-permute-start = (bf16[320,2048]{1,0:T(8,128)(2,1)S(1)}, bf16[320,2048]{1,0:T(8,128)(2,1)}, u32[]{:S(2)}, u32[]{:S(2)}) collective-permute-start(bf16[320,2048]{1,0:T(8,128)(2,1)S(1)} %fusion.4.xa_ref.refs_0_), channel_id=1, source_target_pairs={{0,2},{1,3},{2,0},{3,1},{4,6},{5,7},{6,4},{7,5},{8,10},{9,11},{10,... | collective-permute-start | bytes 3932168 | tf_op jit(solution)/shard_map/ppermute | solution.py:716
  8.0 6.5 %collective-permute-start.1 = (f32[8]{0:T(128)S(1)}, f32[8]{0:T(128)S(1)}, u32[]{:S(2)}, u32[]{:S(2)}) collective-permute-start(f32[8]{0:T(128)S(1)} %select_reduce_fusion.1), channel_id=1, source_target_pairs={{0,4},{4,0},{8,12},{12,8},{16,20},{20,16},{24,28},{28,24},{1,5},{5... | collective-permute-start | bytes 104 | tf_op jit(solution)/shard_map/ppermute | solution.py:716
  9.5 14.5 %copy-start.36 = (bf16[320,2048]{1,0:T(8,128)(2,1)S(1)}, bf16[320,2048]{1,0:T(8,128)(2,1)}, u32[]{:S(2)}) copy-start(bf16[320,2048]{1,0:T(8,128)(2,1)} %param.15) | copy-start | bytes 3932164
  14.5 3.6 collective-permute-start.2
  18.1 4.5 collective-permute-start.3
  24.3 14.1 %copy-start.29 = (bf16[320,2048]{1,0:T(8,128)(2,1)}, bf16[320,2048]{1,0:T(8,128)(2,1)S(1)}, u32[]{:S(2)}) copy-start(bf16[320,2048]{1,0:T(8,128)(2,1)S(1)} %fusion.12.refs_0_) | copy-start | bytes 3932164
  36.7 3.4 collective-permute-start.5
  36.7 33.8 %collective-permute-start.7 = (bf16[320,2048]{1,0:T(8,128)(2,1)S(1)}, bf16[320,2048]{1,0:T(8,128)(2,1)S(1)}, u32[]{:S(2)}, u32[]{:S(2)}) collective-permute-start(bf16[320,2048]{1,0:T(8,128)(2,1)S(1)} %fusion.12.refs_0_), channel_id=1, source_target_pairs={{0,2},{1,3},{2,0},{3,1},{4,6},{5,7},{6,4},{7,5},{8,10},{9,11},{10,... | collective-permute-start | bytes 3932168 | tf_op jit(solution)/shard_map/ppermute | solution.py:716
  38.4 32.1 %collective-permute-start.6 = (bf16[320,2048]{1,0:T(8,128)(2,1)S(1)}, bf16[320,2048]{1,0:T(8,128)(2,1)S(1)}, u32[]{:S(2)}, u32[]{:S(2)}) collective-permute-start(bf16[320,2048]{1,0:T(8,128)(2,1)S(1)} %fusion.12.refs_0_), channel_id=1, source_target_pairs={{0,1},{1,0},{2,3},{3,2},{4,5},{5,4},{6,7},{7,6},{8,9},{9,8},{10,11... | collective-permute-start | bytes 3932168 | tf_op jit(solution)/shard_map/ppermute | solution.py:716
  70.5 9.3 %copy-start.30 = (bf16[320,2048]{1,0:T(8,128)(2,1)}, bf16[320,2048]{1,0:T(8,128)(2,1)S(1)}, u32[]{:S(2)}) copy-start(bf16[320,2048]{1,0:T(8,128)(2,1)S(1)} %collective-permute-done.7.refs_0_.refs_2_) | copy-start | bytes 3932164
  70.5 9.3 %copy-start.31 = (bf16[320,2048]{1,0:T(8,128)(2,1)}, bf16[320,2048]{1,0:T(8,128)(2,1)S(1)}, u32[]{:S(2)}) copy-start(bf16[320,2048]{1,0:T(8,128)(2,1)S(1)} %collective-permute-done.6.refs_1_) | copy-start | bytes 3932164
  70.5 17.7 %collective-permute-start.9 = (bf16[320,2048]{1,0:T(8,128)(2,1)S(1)}, bf16[320,2048]{1,0:T(8,128)(2,1)}, u32[]{:S(2)}, u32[]{:S(2)}) collective-permute-start(bf16[320,2048]{1,0:T(8,128)(2,1)S(1)} %collective-permute-done.7.refs_0_.refs_2_), channel_id=1, source_target_pairs={{0,1},{1,0},{2,3},{3,2},{4,5},{5,4},{6,7},{7,6},{8,9},{9,8},{10,11... | collective-permute-start | bytes 3932168 | tf_op jit(solution)/shard_map/ppermute | solution.py:716
  70.7 31.4 %collective-permute-start.8 = (bf16[320,2048]{1,0:T(8,128)(2,1)}, bf16[320,2048]{1,0:T(8,128)(2,1)}, u32[]{:S(2)}, u32[]{:S(2)}) collective-permute-start(bf16[320,2048]{1,0:T(8,128)(2,1)} %pair_sum.8), channel_id=1, source_target_pairs={{0,2},{1,3},{2,0},{3,1},{4,6},{5,7},{6,4},{7,5},{8,10},{9,11},{10,... | collective-permute-start | bytes 3932168 | tf_op jit(solution)/shard_map/ppermute | solution.py:716
  88.2 13.9 %copy-start.25 = (bf16[320,2048]{1,0:T(8,128)(2,1)S(1)}, bf16[320,2048]{1,0:T(8,128)(2,1)}, u32[]{:S(2)}) copy-start(bf16[320,2048]{1,0:T(8,128)(2,1)} %param.14) | copy-start | bytes 3932164
  88.2 13.9 %copy-start.34 = (f32[320,2048]{1,0:T(8,128)S(1)}, f32[320,2048]{1,0:T(8,128)}, u32[]{:S(2)}) copy-start(f32[320,2048]{1,0:T(8,128)} %pair_sum.9) | copy-start | bytes 7864324
  96.8 8.8 %copy-start.45 = (f32[2048]{0:T(1024)S(1)}, f32[2048]{0:T(1024)}, u32[]{:S(2)}) copy-start(f32[2048]{0:T(1024)} %param.21) | copy-start | bytes 24580
  105.8 3.1 collective-permute-start.11
  105.9 31.2 %collective-permute-start.10 = (bf16[320,2048]{1,0:T(8,128)(2,1)S(1)}, bf16[320,2048]{1,0:T(8,128)(2,1)S(1)}, u32[]{:S(2)}, u32[]{:S(2)}) collective-permute-start(bf16[320,2048]{1,0:T(8,128)(2,1)S(1)} %multiply_convert_fusion.xa_ref.refs_0_), channel_id=1, source_target_pairs={{0,2},{1,3},{2,0},{3,1},{4,6},{5,7},{6,4},{7,5},{8,10},{9,11},{10,... | collective-permute-start | bytes 3932168 | tf_op jit(solution)/shard_map/ppermute | solution.py:716
  137.1 3.0 collective-permute-start.12
  164.5 64.7 %collective-permute-start.14 = (bf16[4,256,1408]{2,1,0:T(8,128)(2,1)}, bf16[4,256,1408]{2,1,0:T(8,128)(2,1)S(1)}, u32[]{:S(2)}, u32[]{:S(2)}) collective-permute-start(bf16[4,256,1408]{2,1,0:T(8,128)(2,1)} %weight_grad.8), channel_id=1, source_target_pairs={{0,4},{4,0},{8,12},{12,8},{16,20},{20,16},{24,28},{28,24},{1,5},{5... | collective-permute-start | bytes 8650760 | tf_op jit(solution)/shard_map/ppermute | solution.py:716
  180.5 44.3 %collective-permute-start.13 = (bf16[320,2048]{1,0:T(8,128)(2,1)}, bf16[320,2048]{1,0:T(8,128)(2,1)}, u32[]{:S(2)}, u32[]{:S(2)}) collective-permute-start(bf16[320,2048]{1,0:T(8,128)(2,1)} %pair_sum.11), channel_id=1, source_target_pairs={{0,2},{1,3},{2,0},{3,1},{4,6},{5,7},{6,4},{7,5},{8,10},{9,11},{10,... | collective-permute-start | bytes 3932168 | tf_op jit(solution)/shard_map/ppermute | solution.py:716
  190.8 72.6 %collective-permute-start.16 = (bf16[4,256,1408]{2,1,0:T(8,128)(2,1)}, bf16[4,256,1408]{2,1,0:T(8,128)(2,1)}, u32[]{:S(2)}, u32[]{:S(2)}) collective-permute-start(bf16[4,256,1408]{2,1,0:T(8,128)(2,1)} %weight_grad.11), channel_id=1, source_target_pairs={{0,8},{4,12},{8,0},{12,4},{16,24},{20,28},{24,16},{28,20},{1,9},{5... | collective-permute-start | bytes 8650760 | tf_op jit(solution)/shard_map/ppermute | solution.py:716
  229.2 87.7 %collective-permute-start.21 = (bf16[4,256,1408]{2,1,0:T(8,128)(2,1)}, bf16[4,256,1408]{2,1,0:T(8,128)(2,1)}, u32[]{:S(2)}, u32[]{:S(2)}) collective-permute-start(bf16[4,256,1408]{2,1,0:T(8,128)(2,1)} %weight_grad.9), channel_id=1, source_target_pairs={{0,4},{4,0},{8,12},{12,8},{16,20},{20,16},{24,28},{28,24},{1,5},{5... | collective-permute-start | bytes 8650760 | tf_op jit(solution)/shard_map/ppermute | solution.py:716
  234.6 24.0 %collective-permute-start.17 = (bf16[320,2048]{1,0:T(8,128)(2,1)}, bf16[320,2048]{1,0:T(8,128)(2,1)}, u32[]{:S(2)}, u32[]{:S(2)}) collective-permute-start(bf16[320,2048]{1,0:T(8,128)(2,1)} %get-tuple-element.161.refs_0_), channel_id=1, source_target_pairs={{0,1},{1,0},{2,3},{3,2},{4,5},{5,4},{6,7},{7,6},{8,9},{9,8},{10,11... | collective-permute-start | bytes 3932168 | tf_op jit(solution)/shard_map/ppermute | solution.py:716
  234.6 31.5 %collective-permute-start.15 = (bf16[320,2048]{1,0:T(8,128)(2,1)}, bf16[320,2048]{1,0:T(8,128)(2,1)}, u32[]{:S(2)}, u32[]{:S(2)}) collective-permute-start(bf16[320,2048]{1,0:T(8,128)(2,1)} %get-tuple-element.161.refs_0_), channel_id=1, source_target_pairs={{0,2},{1,3},{2,0},{3,1},{4,6},{5,7},{6,4},{7,5},{8,10},{9,11},{10,... | collective-permute-start | bytes 3932168 | tf_op jit(solution)/shard_map/ppermute | solution.py:716
  238.7 78.1 %collective-permute-start.19 = (bf16[2,256,1408]{2,1,0:T(8,128)(2,1)}, bf16[2,256,1408]{2,1,0:T(8,128)(2,1)}, u32[]{:S(2)}, u32[]{:S(2)}) collective-permute-start(bf16[2,256,1408]{2,1,0:T(8,128)(2,1)} %get-tuple-element.172), channel_id=1, source_target_pairs={{0,8},{4,12},{8,0},{12,4},{16,24},{20,28},{24,16},{28,20},{1,9},{5... | collective-permute-start | bytes 4325384 | tf_op jit(solution)/shard_map/ppermute | solution.py:716
  263.4 13.0 %copy-start.2 = (bf16[4,256,1408]{2,1,0:T(8,128)(2,1)S(1)}, bf16[4,256,1408]{2,1,0:T(8,128)(2,1)}, u32[]{:S(2)}) copy-start(bf16[4,256,1408]{2,1,0:T(8,128)(2,1)} %weight_grad.12.own_away.own_kept) | copy-start | bytes 8650756
  266.1 14.6 %collective-permute-start.18 = (bf16[320,2048]{1,0:T(8,128)(2,1)}, bf16[320,2048]{1,0:T(8,128)(2,1)}, u32[]{:S(2)}, u32[]{:S(2)}) collective-permute-start(bf16[320,2048]{1,0:T(8,128)(2,1)} %collective-permute-done.15.refs_0_.refs_2_), channel_id=1, source_target_pairs={{0,1},{1,0},{2,3},{3,2},{4,5},{5,4},{6,7},{7,6},{8,9},{9,8},{10,11... | collective-permute-start | bytes 3932168 | tf_op jit(solution)/shard_map/ppermute | solution.py:716
  266.1 50.7 %collective-permute-start.20 = (bf16[320,2048]{1,0:T(8,128)(2,1)}, bf16[320,2048]{1,0:T(8,128)(2,1)}, u32[]{:S(2)}, u32[]{:S(2)}) collective-permute-start(bf16[320,2048]{1,0:T(8,128)(2,1)} %pair_sum.13), channel_id=1, source_target_pairs={{0,2},{1,3},{2,0},{3,1},{4,6},{5,7},{6,4},{7,5},{8,10},{9,11},{10,... | collective-permute-start | bytes 3932168 | tf_op jit(solution)/shard_map/ppermute | solution.py:716
  316.9 11.1 %copy-start = (bf16[4,256,1408]{2,1,0:T(8,128)(2,1)S(1)}, bf16[4,256,1408]{2,1,0:T(8,128)(2,1)}, u32[]{:S(2)}) copy-start(bf16[4,256,1408]{2,1,0:T(8,128)(2,1)} %weight_grad.14.own_away.own_kept) | copy-start | bytes 8650756
  327.1 43.7 %collective-permute-start.22 = (bf16[320,2048]{1,0:T(8,128)(2,1)}, bf16[320,2048]{1,0:T(8,128)(2,1)}, u32[]{:S(2)}, u32[]{:S(2)}) collective-permute-start(bf16[320,2048]{1,0:T(8,128)(2,1)} %pair_sum.14), channel_id=1, source_target_pairs={{0,2},{1,3},{2,0},{3,1},{4,6},{5,7},{6,4},{7,5},{8,10},{9,11},{10,... | collective-permute-start | bytes 3932168 | tf_op jit(solution)/shard_map/ppermute | solution.py:716
  327.7 56.1 %collective-permute-start.25 = (bf16[2,256,1408]{2,1,0:T(8,128)(2,1)}, bf16[2,256,1408]{2,1,0:T(8,128)(2,1)}, u32[]{:S(2)}, u32[]{:S(2)}) collective-permute-start(bf16[2,256,1408]{2,1,0:T(8,128)(2,1)} %copy-done.17), channel_id=1, source_target_pairs={{0,4},{4,0},{8,12},{12,8},{16,20},{20,16},{24,28},{28,24},{1,5},{5... | collective-permute-start | bytes 4325384 | tf_op jit(solution)/shard_map/ppermute | solution.py:716
  331.9 51.9 %collective-permute-start.23 = (bf16[2,256,1408]{2,1,0:T(8,128)(2,1)}, bf16[2,256,1408]{2,1,0:T(8,128)(2,1)S(1)}, u32[]{:S(2)}, u32[]{:S(2)}) collective-permute-start(bf16[2,256,1408]{2,1,0:T(8,128)(2,1)} %get-tuple-element.193), channel_id=1, source_target_pairs={{0,8},{4,12},{8,0},{12,4},{16,24},{20,28},{24,16},{28,20},{1,9},{5... | collective-permute-start | bytes 4325384 | tf_op jit(solution)/shard_map/ppermute | solution.py:716
  335.1 6.8 %copy-start.20 = (f32[320,2048]{1,0:T(8,128)S(1)}, f32[320,2048]{1,0:T(8,128)}, u32[]{:S(2)}) copy-start(f32[320,2048]{1,0:T(8,128)} %copy-done.18) | copy-start | bytes 7864324
  335.1 6.8 %copy-start.33 = (f32[320,2048]{1,0:T(8,128)S(1)}, f32[320,2048]{1,0:T(8,128)}, u32[]{:S(2)}) copy-start(f32[320,2048]{1,0:T(8,128)} %pair_sum.10) | copy-start | bytes 7864324
  337.7 42.3 %collective-permute-start.26 = (bf16[1,256,1408]{2,1,0:T(8,128)(2,1)S(1)}, bf16[1,256,1408]{2,1,0:T(8,128)(2,1)}, u32[]{:S(2)}, u32[]{:S(2)}) collective-permute-start(bf16[1,256,1408]{2,1,0:T(8,128)(2,1)S(1)} %get-tuple-element.198), channel_id=1, source_target_pairs={{0,16},{4,20},{8,24},{12,28},{16,0},{20,4},{24,8},{28,12},{1,17},{... | collective-permute-start | bytes 2162696 | tf_op jit(solution)/shard_map/ppermute | solution.py:716
  340.3 43.5 %collective-permute-start.24 = (bf16[4,256,512]{2,1,0:T(8,128)(2,1)}, bf16[4,256,512]{2,1,0:T(8,128)(2,1)S(1)}, u32[]{:S(2)}, u32[]{:S(2)}) collective-permute-start(bf16[4,256,512]{2,1,0:T(8,128)(2,1)} %get-tuple-element.194), channel_id=1, source_target_pairs={{0,4},{4,0},{8,12},{12,8},{16,20},{20,16},{24,28},{28,24},{1,5},{5... | collective-permute-start | bytes 3145736 | tf_op jit(solution)/shard_map/ppermute | solution.py:716
  370.8 13.1 %copy-start.26 = (bf16[320,2048]{1,0:T(8,128)(2,1)S(1)}, bf16[320,2048]{1,0:T(8,128)(2,1)}, u32[]{:S(2)}) copy-start(bf16[320,2048]{1,0:T(8,128)(2,1)} %param.14) | copy-start | bytes 3932164
  370.8 13.1 %copy-start.46 = (f32[2048]{0:T(1024)S(1)}, f32[2048]{0:T(1024)}, u32[]{:S(2)}) copy-start(f32[2048]{0:T(1024)} %param.16) | copy-start | bytes 24580
  373.3 11.4 %copy-start.28 = (f32[320,2048]{1,0:T(8,128)}, f32[320,2048]{1,0:T(8,128)S(1)}, u32[]{:S(2)}) copy-start(f32[320,2048]{1,0:T(8,128)S(1)} %convert_add_fusion.1) | copy-start | bytes 7864324
  373.3 11.4 %copy-start.4 = (bf16[2,256,1408]{2,1,0:T(8,128)(2,1)S(1)}, bf16[2,256,1408]{2,1,0:T(8,128)(2,1)}, u32[]{:S(2)}) copy-start(bf16[2,256,1408]{2,1,0:T(8,128)(2,1)} %copy-done.3) | copy-start | bytes 4325380
  392.5 116.6 %copy-start.27 = (bf16[320,2048]{1,0:T(8,128)(2,1)S(1)}, bf16[320,2048]{1,0:T(8,128)(2,1)}, u32[]{:S(2)}) copy-start(bf16[320,2048]{1,0:T(8,128)(2,1)} %param.14) | copy-start | bytes 3932164
  509.1 7.1 %copy-start.43 = (f32[256,512]{1,0:T(8,128)S(1)}, f32[256,512]{1,0:T(8,128)}, u32[]{:S(2)}) copy-start(f32[256,512]{1,0:T(8,128)} %get-tuple-element.264) | copy-start | bytes 1572868
  509.1 7.9 %copy-start.42 = (f32[256,512]{1,0:T(8,128)S(1)}, f32[256,512]{1,0:T(8,128)}, u32[]{:S(2)}) copy-start(f32[256,512]{1,0:T(8,128)} %get-tuple-element.265) | copy-start | bytes 1572868
  (29 other events, 68.6 us)

commit v7 on v6

--- a/solution.py
+++ b/solution.py
@@ -611,7 +611,7 @@
         else:
             outs[m][...] += wide(from_last[m - ones][...])
 
-    gate, up, out, q, k, v = range(6)
+    up, out, q, k, v = range(5)
     from_near(out, 1)
     from_x(q, 1, 1)
     from_x(q, 1, 0)
@@ -624,7 +624,6 @@
     from_x(k, 1, 0)
     from_near(q, 0)
     from_x(k, 0, 1)
-    finish(gate)
     from_x(k, 0, 0)
     gain_hop(2)
     from_x(v, 1, 1)
@@ -883,9 +882,9 @@
     dg_f, du_f, down_send = tie(dg_far, du_far, down_send)
     down_got = hop(down_send, 1)
     (gate_send,) = grad_gate.compute(1)
+    gate_got = hop(gate_send, 2)
     y5 = pair_sum([(dg_f, w_gate, True), (du_f, w_up, True)], 2, jnp.bfloat16)
     dg_n, du_n, mid_n, y5 = tie(dg_near, du_near, mid_near, y5)
-    gate_got = hop(gate_send, 2)
     got = to_far(y5)
     d_b = pair_sum([(dg_n, w_gate, True), (du_n, w_up, True)], 3, jnp.float32) + got.astype(jnp.float32)
     (up_send,) = WeightGrad(dp_rank, b_all, [(du_n, du_far)]).compute(1)
@@ -913,40 +912,41 @@
     gate = Halving(dp_rank, gate_own, 2)
     t3 = to_mate(t2)
     gs_far = project([((t2, t3), w_out, True)])
-    gate_away = gate.merge(gate_got, 1)
+    gate_got = hop(gate.merge(gate_got, 1), 1)
     (up_own,) = WeightGrad(dp_rank, b_all, [(du_n, du_far)]).compute(0)
     out_send, out_own = WeightGrad(dp_rank, (t0, t1, t2, t3), [(heads_near, heads_far)]).compute(1, 0)
+    gs_far, up_got, down_got, up_own, out_send = tie(gs_far, up_got, down_got, up_own, out_send)
+    up = Halving(dp_rank, up_own)
+    up_got = hop(up.merge(up_got, 2), 2)
+    down_got = hop(down.merge(down_got, half), half)
     dqn, dqf, dkn, dkf, dvn, dvf = attend_back(
         rank_ref, qs, ks, vs, (gs_near, gs_far), low, high, lse, cosine, back_sine
     )
-    dqf, dkf, dvf, down_got, got8, out_send, gate_away, up_got, up_own = tie(
-        dqf, dkf, dvf, down_got, got8, out_send, gate_away, up_got, up_own
-    )
-
-    out_got, gate_got = hop(out_send, 1), hop(gate_away, 1)
-    up = Halving(dp_rank, up_own)
-    up_got = hop(up.merge(up_got, 2), 2)
+    dqf, dkf, dvf, got8, out_send = tie(dqf, dkf, dvf, got8, out_send)
+
+    out_got = hop(out_send, 1)
     y7 = pair_sum([(dqf, w_query, True), (dkf, w_key, True), (dvf, w_value, True)], 6, jnp.bfloat16)
-    dqn, dkn, dvn, y7 = tie(dqn, dkn, dvn, y7)
     got = to_far(y7)
+    dqn, dkn, dvn, y7, up_got, gate_got, down_got = tie(dqn, dkn, dvn, y7, up_got, gate_got, down_got)
+    gate_got = hop(gate.merge(gate_got, half), half)
+    up_away = up.merge(up_got, half)
     grad_qkv = WeightGrad(dp_rank, (a0, a1, a2, a3), [(dqn, dqf), (dkn, dkf), (dvn, dvf)])
     *sends, q_own, k_own, v_own = grad_qkv.compute(1, 0)
-    down_got = hop(down.merge(down_got, half), half)
     d_a = pair_sum([(dqn, w_query, True), (dkn, w_key, True), (dvn, w_value, True)], 7, jnp.float32) + got.astype(jnp.float32)
-    d_a, up_got, out_got, gate_got, down_got, *sends = tie(d_a, up_got, out_got, gate_got, down_got, *sends)
+    d_a, out_got, gate_got, up_away, *sends = tie(d_a, out_got, gate_got, up_away, *sends)
 
     out = Halving(dp_rank, out_own)
     out_away = out.merge(out_got, 2)
-    gate_away, up_away = gate.merge(gate_got, half), up.merge(up_got, half)
     output = (mid_h + mine8 + got8.astype(jnp.float32)).astype(jnp.bfloat16)
     n_a = x_f * inv_a
     gain_attn_part = jnp.sum(d_a * n_a, axis=0)
     e_a = d_a * gain_attn
     grad_input = d_h + inv_a * (e_a - n_a * jnp.mean(e_a * n_a, axis=-1, keepdims=True))
     gains = jnp.stack([gain_attn_part, gain_mlp_part])
+    sum_gate = gate.finish(gate_got)
     if grad_qkv.kernel and half == 4:
-        (sum_gate, sum_up, sum_out, *sums), sum_down, gains = last_stages(
-            [(gate_away, gate.kept), (up_away, up.kept)],
+        (sum_up, sum_out, *sums), sum_down, gains = last_stages(
+            [(up_away, up.kept)],
             [(out_away, out.kept)],
             list(zip(sends, (q_own, k_own, v_own))),
             (down.kept, down_got),
@@ -955,7 +955,6 @@
         gains = lax.dynamic_slice_in_dim(gains, dp_rank[0] * grad_qkv.tile, grad_qkv.tile, 1)
     else:
         gains = butterfly_sum(scatter_small(gains.reshape(2, lax.axis_size("dp"), -1), "dp"), "tensor")
-        sum_gate = gate.finish(hop(gate_away, half))
         sum_up = up.finish(hop(up_away, half))
         sum_out = out.finish(hop(out_away, 2)).T
         sum_down = down.finish(down_got).T

time: 528 us -> 504 us (0.955)
  Pallas kernels: 399 us -> 377 us
    pallas_call x1, Pallas kernels: 117 us -> 92 us  [last_stages(): pl.pallas_call(functools.partial(last_body, len(ones), len(twos), len(thr...]
    ppermute x27 -> x28, starting transfers between devices: 32.7 us -> 36.3 us  [exchange(): lax.ppermute(values, axis, [(rank, rank ^ bit) for rank in range(size)])]
    ppermute x27 -> x28, waiting for transfers between devices: 32.9 us -> 29.3 us  [exchange(): lax.ppermute(values, axis, [(rank, rank ^ bit) for rank in range(size)])]
    unnamed x107 -> x104, local copies, waits for them, and re-layouts: 22.5 us -> 19.6 us
  transfers between devices with their start and end apart: 27 -> 28, of which waited for: 12 -> 12; matrix products, arithmetic and copies ran while one was open for 4% -> 4% of each run, Pallas kernels for 47% -> 52%
where the time goes in v7:
time: 504 us; the launch traced here: 499 us
  Pallas kernels  377 us (75%)
  starting transfers between devices  36.3 us (7%)
  other arithmetic  32.9 us (7%)
  waiting for transfers between devices  29.3 us (6%)
  local copies, waits for them, and re-layouts  21.6 us (4%)
    pallas_call x1, Pallas kernels, last_stages(): pl.pallas_call(functools.partial(last_body, len(ones), len(twos), len(thr...  92 us
    pallas_call x8, Pallas kernels, pair_sum(): pl.pallas_call(functools.partial(pair_body, [(len(left), dims) for left,...  83.5 us
    pallas_call x8, Pallas kernels, grad_call(): pl.pallas_call(functools.partial(grad_body, len(pieces), widths, low, sid...  77.1 us
    ppermute x28, starting transfers between devices, exchange(): lax.ppermute(values, axis, [(rank, rank ^ bit) for rank in range(size)])  36.3 us
    pallas_call x2, Pallas kernels, mlp_pair(): pl.pallas_call(mlp_body, grid=(pl.cdiv(width, tile),), in_specs=[whole(xa...  29.4 us
    ppermute x28, waiting for transfers between devices, exchange(): lax.ppermute(values, axis, [(rank, rank ^ bit) for rank in range(size)])  29.3 us
    pallas_call x4, Pallas kernels, project(): pl.pallas_call(functools.partial(project_body, [(len(left), dims) for lef...  26.5 us
    pallas_call x1, Pallas kernels, attend_back(): pl.pallas_call(attend_back_body, grid_spec=pltpu.PrefetchScalarGridSpec(n...  21.7 us
  transfers between devices with their start and end apart: 28, of which 12 were waited for; matrix products, arithmetic and copies ran while one was open for 4% of the time, Pallas kernels for 52%

profile of v7, /device:TPU:0, one launch (start us, length us, event | category | flops | bytes accessed | tf_op | source)
XLA Modules:
  0.0 498.9 jit_solution(3541501192561977398)
XLA Ops:
  4.6 2.6 collective-permute-start
  9.6 2.4 fusion.13
  16.1 2.0 collective-permute-done.2
  18.1 2.6 collective-permute-start.3
  25.4 9.4 %qkv.2 = (bf16[640,512]{1,0:T(8,128)(2,1)}, bf16[640,512]{1,0:T(8,128)(2,1)}, bf16[640,512]{1,0:T(8,128)(2,1)}) custom-call(s32[1]{0:T(128)} %bitcast.rank_ref, bf16[320,2048]{1,0:T(8,128)(2,1)} %copy-done.30, bf16[320,2048]{1,0:T(8,128)(2,1)} %copy-done.33, f32[1280,128]{1,0:T(8,128)} %pad_maximum_fusion.cos_ref, f32[1280,128]{1,0:T(8,128)} %get-tuple-element.245.sin_ref, ...), custom_call_target="tpu_custom_call" | custom-call | flops 4026531 | bytes 8912 | tf_op jit(solution)/shard_map/qkv/pallas_call | solution.py:67
  40.1 8.8 %qkv.3 = (bf16[640,512]{1,0:T(8,128)(2,1)}, bf16[640,512]{1,0:T(8,128)(2,1)}, bf16[640,512]{1,0:T(8,128)(2,1)}) custom-call(s32[1]{0:T(128)} %bitcast.rank_ref, bf16[320,2048]{1,0:T(8,128)(2,1)} %collective-permute-done.xa_ref.refs_2_, bf16[320,2048]{1,0:T(8,128)(2,1)} %collective-permute-done.5.xb_ref.refs_3_, f32[1280,128]{1,0:T(8,128)} %pad_maximum_fusion.cos_ref, ...), custom_call_target="tpu_custom_call" | custom-call | flops 4026531 | bytes 8912 | tf_op jit(solution)/shard_map/qkv/pallas_call | solution.py:67
  48.9 14.6 %attend.1 = (bf16[640,512]{1,0:T(8,128)(2,1)}, bf16[640,512]{1,0:T(8,128)(2,1)}, f32[4,1,1280]{2,1,0:T(1,128)}) custom-call(s32[1]{0:T(128)} %bitcast.rank_ref, bf16[640,512]{1,0:T(8,128)(2,1)} %get-tuple-element.125.qn, bf16[640,512]{1,0:T(8,128)(2,1)} %get-tuple-element.127.qf, bf16[640,512]{1,0:T(8,128)(2,1)} %get-tuple-element.128.kn, ...), custom_call_target="tpu_custom_call" | custom-call | flops 6710886 | bytes 5242 | tf_op jit(solution)/shard_map/attend/pallas_call | solution.py:128
  63.5 6.9 %pair_sum.8 = bf16[320,2048]{1,0:T(8,128)(2,1)} custom-call(bf16[640,512]{1,0:T(8,128)(2,1)} %get-tuple-element.134.refs_0_.refs_5_, bf16[512,2048]{1,0:T(8,128)(2,1)} %refs_2_.7), custom_call_target="tpu_custom_call" | custom-call | flops 1342177 | bytes 5373 | tf_op jit(solution)/shard_map/pair_sum/pallas_call | solution.py:478
  72.4 7.4 %pair_sum.9 = f32[320,2048]{1,0:T(8,128)} custom-call(bf16[640,512]{1,0:T(8,128)(2,1)} %get-tuple-element.138.refs_0_.refs_4_, bf16[512,2048]{1,0:T(8,128)(2,1)} %refs_2_.7), custom_call_target="tpu_custom_call" | custom-call | flops 1342177 | bytes 5373 | tf_op jit(solution)/shard_map/pair_sum/pallas_call | solution.py:478
  79.8 8.4 %project.4.dm_ref = f32[640,1408]{1,0:T(8,128)} custom-call(bf16[320,2048]{1,0:T(8,128)(2,1)} %copy-done.27, bf16[320,2048]{1,0:T(8,128)(2,1)} %copy-done.29, bf16[1408,2048]{1,0:T(8,128)(2,1)} %refs_1_.13), custom_call_target="tpu_custom_call" | custom-call | flops 3690987 | bytes 10190 | tf_op jit(solution)/shard_map/project/pallas_call | solution.py:414
  88.1 8.6 %project.5.dm_ref = f32[640,1408]{1,0:T(8,128)} custom-call(bf16[320,2048]{1,0:T(8,128)(2,1)} %copy-done.28, bf16[320,2048]{1,0:T(8,128)(2,1)} %collective-permute-done.9.refs_1_.refs_3_, bf16[1408,2048]{1,0:T(8,128)(2,1)} %refs_1_.13), custom_call_target="tpu_custom_call" | custom-call | flops 3690987 | bytes 10190 | tf_op jit(solution)/shard_map/project/pallas_call | solution.py:414
  96.7 5.3 %collective-permute-done.8 = bf16[320,2048]{1,0:T(8,128)(2,1)} collective-permute-done((bf16[320,2048]{1,0:T(8,128)(2,1)}, bf16[320,2048]{1,0:T(8,128)(2,1)}, u32[]{:S(2)}, u32[]{:S(2)}) %collective-permute-start.8) | collective-permute-done | bytes 1310752 | tf_op jit(solution)/shard_map/ppermute | solution.py:715
  109.9 14.8 %mlp.2 = (bf16[640,1408]{1,0:T(8,128)(2,1)}, bf16[640,1408]{1,0:T(8,128)(2,1)}, bf16[640,1408]{1,0:T(8,128)(2,1)}) custom-call(bf16[320,2048]{1,0:T(8,128)(2,1)} %copy-done.20, bf16[320,2048]{1,0:T(8,128)(2,1)} %copy-done.21, f32[640,1408]{1,0:T(8,128)} %project.4.dm_ref, bf16[2048,1408]{1,0:T(8,128)(2,1)} %refs_1_.12, bf16[2048,1408]{1,0:T(8,128)(2,1)} %refs_3_.5), custom_call_target="tpu_custom_call" | custom-call | flops 7381975 | bytes 23166 | tf_op jit(solution)/shard_map/mlp/pallas_call | solution.py:234
  124.7 10.0 %pair_sum.10 = f32[320,2048]{1,0:T(8,128)} custom-call(bf16[640,1408]{1,0:T(8,128)(2,1)} %get-tuple-element.160.refs_0_.refs_4_, bf16[1408,2048]{1,0:T(8,128)(2,1)} %refs_1_.13), custom_call_target="tpu_custom_call" | custom-call | flops 3690987 | bytes 10190 | tf_op jit(solution)/shard_map/pair_sum/pallas_call | solution.py:478
  134.6 2.3 collective-permute-done.10.xa_ref.refs_2_
  137.0 3.0 collective-permute-done.12.xb_ref.refs_3_
  141.1 14.6 %mlp.3 = (bf16[640,1408]{1,0:T(8,128)(2,1)}, bf16[640,1408]{1,0:T(8,128)(2,1)}, bf16[640,1408]{1,0:T(8,128)(2,1)}) custom-call(bf16[320,2048]{1,0:T(8,128)(2,1)} %copy-done.22, bf16[320,2048]{1,0:T(8,128)(2,1)} %copy-done.23, f32[640,1408]{1,0:T(8,128)} %project.5.dm_ref, bf16[2048,1408]{1,0:T(8,128)(2,1)} %refs_1_.12, bf16[2048,1408]{1,0:T(8,128)(2,1)} %refs_3_.5), custom_call_target="tpu_custom_call" | custom-call | flops 7381975 | bytes 23166 | tf_op jit(solution)/shard_map/mlp/pallas_call | solution.py:234
  155.7 8.7 %weight_grad.8 = bf16[4,256,1408]{2,1,0:T(8,128)(2,1)} custom-call(s32[1]{0:T(128)} %bitcast.7.rank_ref._, bf16[320,2048]{1,0:T(8,128)(2,1)} %copy-done.27, bf16[320,2048]{1,0:T(8,128)(2,1)} %copy-done.29, bf16[320,2048]{1,0:T(8,128)(2,1)} %copy-done.28, bf16[320,2048]{1,0:T(8,128)(2,1)} %collective-permute-done.9.refs_1_.refs_3_, ...), custom_call_target="tpu_custom_call" | custom-call | flops 3690987 | bytes 9109 | tf_op jit(solution)/shard_map/weight_grad/pallas_call | solution.py:324
  166.1 14.3 %pair_sum.11 = bf16[320,2048]{1,0:T(8,128)(2,1)} custom-call(bf16[640,1408]{1,0:T(8,128)(2,1)} %get-tuple-element.154.refs_0_.refs_5_, bf16[2048,1408]{1,0:T(8,128)(2,1)} %refs_1_.12, bf16[640,1408]{1,0:T(8,128)(2,1)} %get-tuple-element.155.refs_2_.refs_5_, bf16[2048,1408]{1,0:T(8,128)(2,1)} %refs_3_.5), custom_call_target="tpu_custom_call" | custom-call | flops 7381975 | bytes 17760 | tf_op jit(solution)/shard_map/pair_sum/pallas_call | solution.py:478
  182.0 8.7 %weight_grad.11 = bf16[4,256,1408]{2,1,0:T(8,128)(2,1)} custom-call(s32[1]{0:T(128)} %bitcast.7.rank_ref._, bf16[320,2048]{1,0:T(8,128)(2,1)} %copy-done.20, bf16[320,2048]{1,0:T(8,128)(2,1)} %copy-done.21, bf16[320,2048]{1,0:T(8,128)(2,1)} %copy-done.22, bf16[320,2048]{1,0:T(8,128)(2,1)} %copy-done.23, ...), custom_call_target="tpu_custom_call" | custom-call | flops 3690987 | bytes 9109 | tf_op jit(solution)/shard_map/weight_grad/pallas_call | solution.py:324
  192.2 8.7 %weight_grad.10.own_away.own_kept = bf16[4,256,1408]{2,1,0:T(8,128)(2,1)} custom-call(s32[1]{0:T(128)} %bitcast.7.rank_ref._, bf16[320,2048]{1,0:T(8,128)(2,1)} %copy-done.27, bf16[320,2048]{1,0:T(8,128)(2,1)} %copy-done.29, bf16[320,2048]{1,0:T(8,128)(2,1)} %copy-done.28, bf16[320,2048]{1,0:T(8,128)(2,1)} %collective-permute-done.9.refs_1_.refs_3_, ...), custom_call_target="tpu_custom_call" | custom-call | flops 3690987 | bytes 9109 | tf_op jit(solution)/shard_map/weight_grad/pallas_call | solution.py:324
  201.0 8.7 %weight_grad.9 = bf16[4,256,1408]{2,1,0:T(8,128)(2,1)} custom-call(s32[1]{0:T(128)} %bitcast.7.rank_ref._, bf16[320,2048]{1,0:T(8,128)(2,1)} %copy-done.20, bf16[320,2048]{1,0:T(8,128)(2,1)} %copy-done.21, bf16[320,2048]{1,0:T(8,128)(2,1)} %copy-done.22, bf16[320,2048]{1,0:T(8,128)(2,1)} %copy-done.23, bf16[640,1408]{1,0:T(8,128)(2,1)} %get-tuple-element.171.refs_2_.refs_4_, ...), custom_call_target="tpu_custom_call" | custom-call | flops 3690987 | bytes 9109 | tf_op jit(solution)/shard_map/weight_grad/pallas_call | solution.py:324
  209.7 14.9 %pair_sum.12 = f32[320,2048]{1,0:T(8,128)} custom-call(bf16[640,1408]{1,0:T(8,128)(2,1)} %get-tuple-element.164.refs_0_.refs_4_, bf16[2048,1408]{1,0:T(8,128)(2,1)} %refs_1_.12, bf16[640,1408]{1,0:T(8,128)(2,1)} %get-tuple-element.171.refs_2_.refs_4_, bf16[2048,1408]{1,0:T(8,128)(2,1)} %refs_3_.5), custom_call_target="tpu_custom_call" | custom-call | flops 7381975 | bytes 17760 | tf_op jit(solution)/shard_map/pair_sum/pallas_call | solution.py:478
  224.6 2.6 convert_add_fusion.2
  227.2 1.9 collective-permute-done.14.got_away.got_kept
  231.7 2.8 fusion.16
  240.1 9.6 %pair_sum.13 = bf16[320,2048]{1,0:T(8,128)(2,1)} custom-call(bf16[640,1408]{1,0:T(8,128)(2,1)} %get-tuple-element.163.refs_5_.refs_0_, bf16[1408,2048]{1,0:T(8,128)(2,1)} %refs_1_.13), custom_call_target="tpu_custom_call" | custom-call | flops 3690987 | bytes 10190 | tf_op jit(solution)/shard_map/pair_sum/pallas_call | solution.py:478
  249.6 8.8 %weight_grad.12.own_away.own_kept = bf16[4,256,1408]{2,1,0:T(8,128)(2,1)} custom-call(s32[1]{0:T(128)} %bitcast.7.rank_ref._, bf16[320,2048]{1,0:T(8,128)(2,1)} %copy-done.20, bf16[320,2048]{1,0:T(8,128)(2,1)} %copy-done.21, bf16[320,2048]{1,0:T(8,128)(2,1)} %copy-done.22, bf16[320,2048]{1,0:T(8,128)(2,1)} %copy-done.23, ...), custom_call_target="tpu_custom_call" | custom-call | flops 3690987 | bytes 9109 | tf_op jit(solution)/shard_map/weight_grad/pallas_call | solution.py:324
  258.4 4.8 project.6.gn
  263.2 2.8 collective-permute-done.15.refs_0_.refs_2_
  267.5 8.7 %weight_grad.13.own_away.own_kept = bf16[4,256,1408]{2,1,0:T(8,128)(2,1)} custom-call(s32[1]{0:T(128)} %bitcast.7.rank_ref._, bf16[320,2048]{1,0:T(8,128)(2,1)} %copy-done.20, bf16[320,2048]{1,0:T(8,128)(2,1)} %copy-done.21, bf16[320,2048]{1,0:T(8,128)(2,1)} %copy-done.22, bf16[320,2048]{1,0:T(8,128)(2,1)} %copy-done.23, ...), custom_call_target="tpu_custom_call" | custom-call | flops 3690987 | bytes 9109 | tf_op jit(solution)/shard_map/weight_grad/pallas_call | solution.py:324
  276.2 2.9 merge.9
  280.7 4.8 project.7.gf
  285.5 9.4 %weight_grad.14 = (bf16[4,256,512]{2,1,0:T(8,128)(2,1)}, bf16[4,256,512]{2,1,0:T(8,128)(2,1)}) custom-call(s32[1]{0:T(128)} %bitcast.7.rank_ref._, bf16[320,2048]{1,0:T(8,128)(2,1)} %get-tuple-element.162.refs_0_, bf16[320,2048]{1,0:T(8,128)(2,1)} %collective-permute-done.17.refs_1_, bf16[320,2048]{1,0:T(8,128)(2,1)} %collective-permute-done.15.refs_0_.refs_2_, ...), custom_call_target="tpu_custom_call" | custom-call | flops 2684354 | bytes 8650 | tf_op jit(solution)/shard_map/weight_grad/pallas_call | solution.py:324
  295.0 3.3 merge.8
  301.0 2.4 merge.10
  304.2 2.6 collective-permute-start.24
  306.8 21.7 %attend_back.1 = (bf16[640,512]{1,0:T(8,128)(2,1)}, bf16[640,512]{1,0:T(8,128)(2,1)}, bf16[640,512]{1,0:T(8,128)(2,1)}, bf16[640,512]{1,0:T(8,128)(2,1)}, bf16[6...) custom-call(s32[1]{0:T(128)} %bitcast.rank_ref, bf16[640,512]{1,0:T(8,128)(2,1)} %get-tuple-element.125.qn, ...), custom_call_target="tpu_custom_call" | custom-call | flops 16777216 | bytes 10485 | tf_op jit(solution)/shard_map/attend_back/pallas_call | solution.py:191
  328.5 10.1 %pair_sum.14 = bf16[320,2048]{1,0:T(8,128)(2,1)} custom-call(bf16[640,512]{1,0:T(8,128)(2,1)} %get-tuple-element.184.refs_0_.refs_5_, bf16[2048,512]{1,0:T(8,128)(2,1)} %refs_1_.15, bf16[640,512]{1,0:T(8,128)(2,1)} %get-tuple-element.185.refs_2_.refs_7_, bf16[2048,512]{1,0:T(8,128)(2,1)} %refs_3_.7, bf16[640,512]{1,0:T(8,128)(2,1)} %get-tuple-element.186.refs_4_.refs_9_, ...), custom_call_target="tpu_custom_call" | custom-call | flops 4026531 | bytes 10878 | tf_op jit(solution)/shard_map/pair_sum/pallas_call | solution.py:478
  341.8 6.0 %collective-permute-done.24.refs_11_ = bf16[1,256,1408]{2,1,0:T(8,128)(2,1)} collective-permute-done((bf16[1,256,1408]{2,1,0:T(8,128)(2,1)}, bf16[1,256,1408]{2,1,0:T(8,128)(2,1)}, u32[]{:S(2)}, u32[]{:S(2)}) %collective-permute-start.24) | collective-permute-done | bytes 720928 | tf_op jit(solution)/shard_map/ppermute | solution.py:715
  348.5 2.5 merge.11
  351.9 2.6 collective-permute-start.27
  354.5 3.1 add_convert_fusion
  359.7 10.4 %pair_sum.15 = f32[320,2048]{1,0:T(8,128)} custom-call(bf16[640,512]{1,0:T(8,128)(2,1)} %get-tuple-element.196.refs_0_.refs_4_, bf16[2048,512]{1,0:T(8,128)(2,1)} %refs_1_.15, bf16[640,512]{1,0:T(8,128)(2,1)} %get-tuple-element.197.refs_2_.refs_6_, bf16[2048,512]{1,0:T(8,128)(2,1)} %refs_3_.7, bf16[640,512]{1,0:T(8,128)(2,1)} %get-tuple-element.198.refs_4_.refs_8_, ...), custom_call_target="tpu_custom_call" | custom-call | flops 4026531 | bytes 10878 | tf_op jit(solution)/shard_map/pair_sum/pallas_call | solution.py:478
  370.1 15.3 %weight_grad.15 = (bf16[4,256,512]{2,1,0:T(8,128)(2,1)}, bf16[4,256,512]{2,1,0:T(8,128)(2,1)}, bf16[4,256,512]{2,1,0:T(8,128)(2,1)}, bf16[4,256,512]{2,1,0:T(8,1...) custom-call(s32[1]{0:T(128)} %bitcast.7.rank_ref._, bf16[320,2048]{1,0:T(8,128)(2,1)} %copy-done.30, ...), custom_call_target="tpu_custom_call" | custom-call | flops 8053063 | bytes 15466 | tf_op jit(solution)/shard_map/weight_grad/pallas_call | solution.py:324
  385.5 2.5 convert_add_fusion.1
  393.8 92.0 %last_stages.1 = (f32[256,1408]{1,0:T(8,128)}, f32[512,256]{1,0:T(8,128)}, f32[256,512]{1,0:T(8,128)}, f32[256,512]{1,0:T(8,128)}, f32[256,512]{1,0:T(8,128)}, /*index=5*/f32[1408,256]{1,0:T(8,128)}, f32[2,2048]{1,0:T(2,128)}) custom-call(bf16[1,256,1408]{2,1,0:T(8,128)(2,1)} %copy-done.13, bf16[2,256,512]{2,1,0:T(8,128)(2,1)} %copy-done.15, ...), custom_call_target="tpu_custom_call" | custom-call | flops 16777 | bytes 33554 | tf_op jit(solution)/shard_map/last_stages/pallas_call | solution.py:659
  485.9 4.8 fusion.8
  (188 shorter events, 71.6 us)
Async XLA Ops:
  0.6 6.6 %copy-start.48 = (s32[1,3]{1,0:T(1,128)S(1)}, s32[1,3]{1,0:T(1,128)}, u32[]{:S(2)}) copy-start(s32[1,3]{1,0:T(1,128)} %param.25) | copy-start | bytes 40
  0.7 6.9 %copy-start.46 = (s32[1,1280]{1,0:T(1,128)S(1)}, s32[1,1280]{1,0:T(1,128)}, u32[]{:S(2)}) copy-start(s32[1,1280]{1,0:T(1,128)} %param.27) | copy-start | bytes 15364
  0.7 7.1 %copy-start.47 = (s32[1,3]{1,0:T(1,128)S(1)}, s32[1,3]{1,0:T(1,128)}, u32[]{:S(2)}) copy-start(s32[1,3]{1,0:T(1,128)} %param.26) | copy-start | bytes 40
  4.1 10.4 %copy-start.30 = (bf16[320,2048]{1,0:T(8,128)(2,1)}, bf16[320,2048]{1,0:T(8,128)(2,1)S(1)}, u32[]{:S(2)}) copy-start(bf16[320,2048]{1,0:T(8,128)(2,1)S(1)} %fusion.4.xa_ref.refs_0_) | copy-start | bytes 3932164
  4.1 20.3 %collective-permute-start.4 = (bf16[320,2048]{1,0:T(8,128)(2,1)S(1)}, bf16[320,2048]{1,0:T(8,128)(2,1)S(1)}, u32[]{:S(2)}, u32[]{:S(2)}) collective-permute-start(bf16[320,2048]{1,0:T(8,128)(2,1)S(1)} %fusion.4.xa_ref.refs_0_), channel_id=1, source_target_pairs={{0,1},{1,0},{2,3},{3,2},{4,5},{5,4},{6,7},{7,6},{8,9},{9,8},{10,11... | collective-permute-start | bytes 3932168 | tf_op jit(solution)/shard_map/ppermute | solution.py:715
  4.6 32.1 %collective-permute-start = (bf16[320,2048]{1,0:T(8,128)(2,1)S(1)}, bf16[320,2048]{1,0:T(8,128)(2,1)}, u32[]{:S(2)}, u32[]{:S(2)}) collective-permute-start(bf16[320,2048]{1,0:T(8,128)(2,1)S(1)} %fusion.4.xa_ref.refs_0_), channel_id=1, source_target_pairs={{0,2},{1,3},{2,0},{3,1},{4,6},{5,7},{6,4},{7,5},{8,10},{9,11},{10,... | collective-permute-start | bytes 3932168 | tf_op jit(solution)/shard_map/ppermute | solution.py:715
  8.0 6.5 %collective-permute-start.1 = (f32[8]{0:T(128)S(1)}, f32[8]{0:T(128)S(1)}, u32[]{:S(2)}, u32[]{:S(2)}) collective-permute-start(f32[8]{0:T(128)S(1)} %select_reduce_fusion.1), channel_id=1, source_target_pairs={{0,4},{4,0},{8,12},{12,8},{16,20},{20,16},{24,28},{28,24},{1,5},{5... | collective-permute-start | bytes 104 | tf_op jit(solution)/shard_map/ppermute | solution.py:715
  9.5 14.5 %copy-start.34 = (bf16[320,2048]{1,0:T(8,128)(2,1)S(1)}, bf16[320,2048]{1,0:T(8,128)(2,1)}, u32[]{:S(2)}) copy-start(bf16[320,2048]{1,0:T(8,128)(2,1)} %param.15) | copy-start | bytes 3932164
  14.5 3.6 collective-permute-start.2
  18.1 4.5 collective-permute-start.3
  24.3 14.1 %copy-start.27 = (bf16[320,2048]{1,0:T(8,128)(2,1)}, bf16[320,2048]{1,0:T(8,128)(2,1)S(1)}, u32[]{:S(2)}) copy-start(bf16[320,2048]{1,0:T(8,128)(2,1)S(1)} %fusion.12.refs_0_) | copy-start | bytes 3932164
  36.7 3.4 collective-permute-start.5
  36.7 33.7 %collective-permute-start.7 = (bf16[320,2048]{1,0:T(8,128)(2,1)S(1)}, bf16[320,2048]{1,0:T(8,128)(2,1)S(1)}, u32[]{:S(2)}, u32[]{:S(2)}) collective-permute-start(bf16[320,2048]{1,0:T(8,128)(2,1)S(1)} %fusion.12.refs_0_), channel_id=1, source_target_pairs={{0,2},{1,3},{2,0},{3,1},{4,6},{5,7},{6,4},{7,5},{8,10},{9,11},{10,... | collective-permute-start | bytes 3932168 | tf_op jit(solution)/shard_map/ppermute | solution.py:715
  38.4 32.0 %collective-permute-start.6 = (bf16[320,2048]{1,0:T(8,128)(2,1)S(1)}, bf16[320,2048]{1,0:T(8,128)(2,1)S(1)}, u32[]{:S(2)}, u32[]{:S(2)}) collective-permute-start(bf16[320,2048]{1,0:T(8,128)(2,1)S(1)} %fusion.12.refs_0_), channel_id=1, source_target_pairs={{0,1},{1,0},{2,3},{3,2},{4,5},{5,4},{6,7},{7,6},{8,9},{9,8},{10,11... | collective-permute-start | bytes 3932168 | tf_op jit(solution)/shard_map/ppermute | solution.py:715
  70.4 9.3 %copy-start.28 = (bf16[320,2048]{1,0:T(8,128)(2,1)}, bf16[320,2048]{1,0:T(8,128)(2,1)S(1)}, u32[]{:S(2)}) copy-start(bf16[320,2048]{1,0:T(8,128)(2,1)S(1)} %collective-permute-done.7.refs_0_.refs_2_) | copy-start | bytes 3932164
  70.4 9.3 %copy-start.29 = (bf16[320,2048]{1,0:T(8,128)(2,1)}, bf16[320,2048]{1,0:T(8,128)(2,1)S(1)}, u32[]{:S(2)}) copy-start(bf16[320,2048]{1,0:T(8,128)(2,1)S(1)} %collective-permute-done.6.refs_1_) | copy-start | bytes 3932164
  70.4 17.7 %collective-permute-start.9 = (bf16[320,2048]{1,0:T(8,128)(2,1)S(1)}, bf16[320,2048]{1,0:T(8,128)(2,1)}, u32[]{:S(2)}, u32[]{:S(2)}) collective-permute-start(bf16[320,2048]{1,0:T(8,128)(2,1)S(1)} %collective-permute-done.7.refs_0_.refs_2_), channel_id=1, source_target_pairs={{0,1},{1,0},{2,3},{3,2},{4,5},{5,4},{6,7},{7,6},{8,9},{9,8},{10,11... | collective-permute-start | bytes 3932168 | tf_op jit(solution)/shard_map/ppermute | solution.py:715
  70.6 31.4 %collective-permute-start.8 = (bf16[320,2048]{1,0:T(8,128)(2,1)}, bf16[320,2048]{1,0:T(8,128)(2,1)}, u32[]{:S(2)}, u32[]{:S(2)}) collective-permute-start(bf16[320,2048]{1,0:T(8,128)(2,1)} %pair_sum.8), channel_id=1, source_target_pairs={{0,2},{1,3},{2,0},{3,1},{4,6},{5,7},{6,4},{7,5},{8,10},{9,11},{10,... | collective-permute-start | bytes 3932168 | tf_op jit(solution)/shard_map/ppermute | solution.py:715
  88.1 13.9 %copy-start.24 = (bf16[320,2048]{1,0:T(8,128)(2,1)S(1)}, bf16[320,2048]{1,0:T(8,128)(2,1)}, u32[]{:S(2)}) copy-start(bf16[320,2048]{1,0:T(8,128)(2,1)} %param.14) | copy-start | bytes 3932164
  88.1 13.9 %copy-start.32 = (f32[320,2048]{1,0:T(8,128)S(1)}, f32[320,2048]{1,0:T(8,128)}, u32[]{:S(2)}) copy-start(f32[320,2048]{1,0:T(8,128)} %pair_sum.9) | copy-start | bytes 7864324
  96.7 8.8 %copy-start.44 = (f32[2048]{0:T(1024)S(1)}, f32[2048]{0:T(1024)}, u32[]{:S(2)}) copy-start(f32[2048]{0:T(1024)} %param.21) | copy-start | bytes 24580
  105.7 3.1 collective-permute-start.11
  105.8 31.2 %collective-permute-start.10 = (bf16[320,2048]{1,0:T(8,128)(2,1)S(1)}, bf16[320,2048]{1,0:T(8,128)(2,1)S(1)}, u32[]{:S(2)}, u32[]{:S(2)}) collective-permute-start(bf16[320,2048]{1,0:T(8,128)(2,1)S(1)} %multiply_convert_fusion.xa_ref.refs_0_), channel_id=1, source_target_pairs={{0,2},{1,3},{2,0},{3,1},{4,6},{5,7},{6,4},{7,5},{8,10},{9,11},{10,... | collective-permute-start | bytes 3932168 | tf_op jit(solution)/shard_map/ppermute | solution.py:715
  137.0 3.0 collective-permute-start.12
  164.4 64.7 %collective-permute-start.14 = (bf16[4,256,1408]{2,1,0:T(8,128)(2,1)}, bf16[4,256,1408]{2,1,0:T(8,128)(2,1)S(1)}, u32[]{:S(2)}, u32[]{:S(2)}) collective-permute-start(bf16[4,256,1408]{2,1,0:T(8,128)(2,1)} %weight_grad.8), channel_id=1, source_target_pairs={{0,4},{4,0},{8,12},{12,8},{16,20},{20,16},{24,28},{28,24},{1,5},{5... | collective-permute-start | bytes 8650760 | tf_op jit(solution)/shard_map/ppermute | solution.py:715
  180.4 44.2 %collective-permute-start.13 = (bf16[320,2048]{1,0:T(8,128)(2,1)}, bf16[320,2048]{1,0:T(8,128)(2,1)}, u32[]{:S(2)}, u32[]{:S(2)}) collective-permute-start(bf16[320,2048]{1,0:T(8,128)(2,1)} %pair_sum.11), channel_id=1, source_target_pairs={{0,2},{1,3},{2,0},{3,1},{4,6},{5,7},{6,4},{7,5},{8,10},{9,11},{10,... | collective-permute-start | bytes 3932168 | tf_op jit(solution)/shard_map/ppermute | solution.py:715
  190.7 72.6 %collective-permute-start.16 = (bf16[4,256,1408]{2,1,0:T(8,128)(2,1)}, bf16[4,256,1408]{2,1,0:T(8,128)(2,1)}, u32[]{:S(2)}, u32[]{:S(2)}) collective-permute-start(bf16[4,256,1408]{2,1,0:T(8,128)(2,1)} %weight_grad.11), channel_id=1, source_target_pairs={{0,8},{4,12},{8,0},{12,4},{16,24},{20,28},{24,16},{28,20},{1,9},{5... | collective-permute-start | bytes 8650760 | tf_op jit(solution)/shard_map/ppermute | solution.py:715
  224.6 6.3 %copy-start.18 = (f32[320,2048]{1,0:T(8,128)S(1)}, f32[320,2048]{1,0:T(8,128)}, u32[]{:S(2)}) copy-start(f32[320,2048]{1,0:T(8,128)} %copy-done.17) | copy-start | bytes 7864324
  229.1 65.8 %collective-permute-start.19 = (bf16[4,256,1408]{2,1,0:T(8,128)(2,1)}, bf16[4,256,1408]{2,1,0:T(8,128)(2,1)}, u32[]{:S(2)}, u32[]{:S(2)}) collective-permute-start(bf16[4,256,1408]{2,1,0:T(8,128)(2,1)} %weight_grad.9), channel_id=1, source_target_pairs={{0,4},{4,0},{8,12},{12,8},{16,20},{20,16},{24,28},{28,24},{1,5},{5... | collective-permute-start | bytes 8650760 | tf_op jit(solution)/shard_map/ppermute | solution.py:715
  234.5 24.0 %collective-permute-start.17 = (bf16[320,2048]{1,0:T(8,128)(2,1)}, bf16[320,2048]{1,0:T(8,128)(2,1)}, u32[]{:S(2)}, u32[]{:S(2)}) collective-permute-start(bf16[320,2048]{1,0:T(8,128)(2,1)} %get-tuple-element.162.refs_0_), channel_id=1, source_target_pairs={{0,1},{1,0},{2,3},{3,2},{4,5},{5,4},{6,7},{7,6},{8,9},{9,8},{10,11... | collective-permute-start | bytes 3932168 | tf_op jit(solution)/shard_map/ppermute | solution.py:715
  234.5 31.5 %collective-permute-start.15 = (bf16[320,2048]{1,0:T(8,128)(2,1)}, bf16[320,2048]{1,0:T(8,128)(2,1)}, u32[]{:S(2)}, u32[]{:S(2)}) collective-permute-start(bf16[320,2048]{1,0:T(8,128)(2,1)} %get-tuple-element.162.refs_0_), channel_id=1, source_target_pairs={{0,2},{1,3},{2,0},{3,1},{4,6},{5,7},{6,4},{7,5},{8,10},{9,11},{10,... | collective-permute-start | bytes 3932168 | tf_op jit(solution)/shard_map/ppermute | solution.py:715
  238.5 56.5 %collective-permute-start.20 = (bf16[2,256,1408]{2,1,0:T(8,128)(2,1)}, bf16[2,256,1408]{2,1,0:T(8,128)(2,1)}, u32[]{:S(2)}, u32[]{:S(2)}) collective-permute-start(bf16[2,256,1408]{2,1,0:T(8,128)(2,1)} %get-tuple-element.170), channel_id=1, source_target_pairs={{0,8},{4,12},{8,0},{12,4},{16,24},{20,28},{24,16},{28,20},{1,9},{5... | collective-permute-start | bytes 4325384 | tf_op jit(solution)/shard_map/ppermute | solution.py:715
  263.2 13.0 %copy-start.2 = (bf16[4,256,1408]{2,1,0:T(8,128)(2,1)S(1)}, bf16[4,256,1408]{2,1,0:T(8,128)(2,1)}, u32[]{:S(2)}) copy-start(bf16[4,256,1408]{2,1,0:T(8,128)(2,1)} %weight_grad.12.own_away.own_kept) | copy-start | bytes 8650756
  266.0 14.7 %collective-permute-start.18 = (bf16[320,2048]{1,0:T(8,128)(2,1)}, bf16[320,2048]{1,0:T(8,128)(2,1)}, u32[]{:S(2)}, u32[]{:S(2)}) collective-permute-start(bf16[320,2048]{1,0:T(8,128)(2,1)} %collective-permute-done.15.refs_0_.refs_2_), channel_id=1, source_target_pairs={{0,1},{1,0},{2,3},{3,2},{4,5},{5,4},{6,7},{7,6},{8,9},{9,8},{10,11... | collective-permute-start | bytes 3932168 | tf_op jit(solution)/shard_map/ppermute | solution.py:715
  266.0 62.6 %collective-permute-start.21 = (bf16[320,2048]{1,0:T(8,128)(2,1)}, bf16[320,2048]{1,0:T(8,128)(2,1)}, u32[]{:S(2)}, u32[]{:S(2)}) collective-permute-start(bf16[320,2048]{1,0:T(8,128)(2,1)} %pair_sum.13), channel_id=1, source_target_pairs={{0,2},{1,3},{2,0},{3,1},{4,6},{5,7},{6,4},{7,5},{8,10},{9,11},{10,... | collective-permute-start | bytes 3932168 | tf_op jit(solution)/shard_map/ppermute | solution.py:715
  280.2 61.6 %collective-permute-start.23 = (bf16[2,256,1408]{2,1,0:T(8,128)(2,1)}, bf16[2,256,1408]{2,1,0:T(8,128)(2,1)}, u32[]{:S(2)}, u32[]{:S(2)}) collective-permute-start(bf16[2,256,1408]{2,1,0:T(8,128)(2,1)} %get-tuple-element.192), channel_id=1, source_target_pairs={{0,4},{4,0},{8,12},{12,8},{16,20},{20,16},{24,28},{28,24},{1,5},{5... | collective-permute-start | bytes 4325384 | tf_op jit(solution)/shard_map/ppermute | solution.py:715
  285.5 9.5 %copy-start.1 = (bf16[4,256,1408]{2,1,0:T(8,128)(2,1)S(1)}, bf16[4,256,1408]{2,1,0:T(8,128)(2,1)}, u32[]{:S(2)}) copy-start(bf16[4,256,1408]{2,1,0:T(8,128)(2,1)} %weight_grad.13.own_away.own_kept) | copy-start | bytes 8650756
  295.0 6.0 %copy-start.8 = (bf16[2,256,1408]{2,1,0:T(8,128)(2,1)S(1)}, bf16[2,256,1408]{2,1,0:T(8,128)(2,1)}, u32[]{:S(2)}) copy-start(bf16[2,256,1408]{2,1,0:T(8,128)(2,1)} %copy-done.7) | copy-start | bytes 4325380
  299.4 49.1 %collective-permute-start.22 = (bf16[2,256,1408]{2,1,0:T(8,128)(2,1)}, bf16[2,256,1408]{2,1,0:T(8,128)(2,1)S(1)}, u32[]{:S(2)}, u32[]{:S(2)}) collective-permute-start(bf16[2,256,1408]{2,1,0:T(8,128)(2,1)} %get-tuple-element.189), channel_id=1, source_target_pairs={{0,8},{4,12},{8,0},{12,4},{16,24},{20,28},{24,16},{28,20},{1,9},{5... | collective-permute-start | bytes 4325384 | tf_op jit(solution)/shard_map/ppermute | solution.py:715
  304.2 43.5 %collective-permute-start.24 = (bf16[1,256,1408]{2,1,0:T(8,128)(2,1)}, bf16[1,256,1408]{2,1,0:T(8,128)(2,1)}, u32[]{:S(2)}, u32[]{:S(2)}) collective-permute-start(bf16[1,256,1408]{2,1,0:T(8,128)(2,1)} %get-tuple-element.195), channel_id=1, source_target_pairs={{0,16},{4,20},{8,24},{12,28},{16,0},{20,4},{24,8},{28,12},{1,17},{... | collective-permute-start | bytes 2162696 | tf_op jit(solution)/shard_map/ppermute | solution.py:715
  328.5 20.0 %copy-start.4 = (bf16[2,256,1408]{2,1,0:T(8,128)(2,1)S(1)}, bf16[2,256,1408]{2,1,0:T(8,128)(2,1)}, u32[]{:S(2)}) copy-start(bf16[2,256,1408]{2,1,0:T(8,128)(2,1)} %copy-done.3) | copy-start | bytes 4325380
  338.7 46.8 %collective-permute-start.25 = (bf16[320,2048]{1,0:T(8,128)(2,1)}, bf16[320,2048]{1,0:T(8,128)(2,1)}, u32[]{:S(2)}, u32[]{:S(2)}) collective-permute-start(bf16[320,2048]{1,0:T(8,128)(2,1)} %pair_sum.14), channel_id=1, source_target_pairs={{0,2},{1,3},{2,0},{3,1},{4,6},{5,7},{6,4},{7,5},{8,10},{9,11},{10,... | collective-permute-start | bytes 3932168 | tf_op jit(solution)/shard_map/ppermute | solution.py:715
  340.3 47.8 %collective-permute-start.26 = (bf16[4,256,512]{2,1,0:T(8,128)(2,1)}, bf16[4,256,512]{2,1,0:T(8,128)(2,1)}, u32[]{:S(2)}, u32[]{:S(2)}) collective-permute-start(bf16[4,256,512]{2,1,0:T(8,128)(2,1)} %get-tuple-element.199), channel_id=1, source_target_pairs={{0,4},{4,0},{8,12},{12,8},{16,20},{20,16},{24,28},{28,24},{1,5},{5... | collective-permute-start | bytes 3145736 | tf_op jit(solution)/shard_map/ppermute | solution.py:715
  348.5 6.0 %copy-start.19 = (f32[320,2048]{1,0:T(8,128)S(1)}, f32[320,2048]{1,0:T(8,128)}, u32[]{:S(2)}) copy-start(f32[320,2048]{1,0:T(8,128)} %copy-done.17) | copy-start | bytes 7864324
  348.5 6.0 %copy-start.31 = (f32[320,2048]{1,0:T(8,128)S(1)}, f32[320,2048]{1,0:T(8,128)}, u32[]{:S(2)}) copy-start(f32[320,2048]{1,0:T(8,128)} %pair_sum.10) | copy-start | bytes 7864324
  351.9 5.7 %copy-start.6 = (bf16[2,256,1408]{2,1,0:T(8,128)(2,1)S(1)}, bf16[2,256,1408]{2,1,0:T(8,128)(2,1)}, u32[]{:S(2)}) copy-start(bf16[2,256,1408]{2,1,0:T(8,128)(2,1)} %copy-done.5) | copy-start | bytes 4325380
  351.9 36.1 %collective-permute-start.27 = (bf16[1,256,1408]{2,1,0:T(8,128)(2,1)}, bf16[1,256,1408]{2,1,0:T(8,128)(2,1)S(1)}, u32[]{:S(2)}, u32[]{:S(2)}) collective-permute-start(bf16[1,256,1408]{2,1,0:T(8,128)(2,1)} %get-tuple-element.202), channel_id=1, source_target_pairs={{0,16},{4,20},{8,24},{12,28},{16,0},{20,4},{24,8},{28,12},{1,17},{... | collective-permute-start | bytes 2162696 | tf_op jit(solution)/shard_map/ppermute | solution.py:715
  490.7 5.0 %copy-start.40 = (f32[512,256]{1,0:T(8,128)S(1)}, f32[512,256]{1,0:T(8,128)}, u32[]{:S(2)}) copy-start(f32[512,256]{1,0:T(8,128)} %get-tuple-element.268) | copy-start | bytes 1572868
  (29 other events, 67.6 us)

commit v8 on v7

--- a/solution.py
+++ b/solution.py
@@ -42,19 +42,20 @@
     return values * cosine + pltpu.roll(values, HEAD_DIM // 2, 1) * sine
 
 
-def qkv_body(first, rank_ref, xa_ref, xb_ref, cos_ref, sin_ref, wq_ref, wk_ref, wv_ref, q_ref, k_ref, v_ref):
+def qkv_body(first, rank_ref, xa_ref, xb_ref, cos_ref, sin_ref, wq_ref, wk_ref, wv_ref, q_ref, k_ref, v_ref, x_s):
     rows = xa_ref.shape[0]
-    for half, x_ref in enumerate((xa_ref, xb_ref)):
-        span = pl.ds(half * rows, rows)
-        x = x_ref[...]
-        place = pl.ds(pl.multiple_of((rank_ref[0] ^ (first + half)) * rows, rows), rows)
-        cosine, sine = cos_ref[place, :], sin_ref[place, :]
-        for w_ref, out_ref in ((wq_ref, q_ref), (wk_ref, k_ref)):
-            full = mm(x, w_ref[...])
+    lay_together((xa_ref, xb_ref), x_s)
+    for w_ref, out_ref in ((wq_ref, q_ref), (wk_ref, k_ref)):
+        full = mm(x_s[...], w_ref[...])
+        for half in range(2):
+            span = pl.ds(half * rows, rows)
+            place = pl.ds(pl.multiple_of((rank_ref[0] ^ (first + half)) * rows, rows), rows)
+            cosine, sine = cos_ref[place, :], sin_ref[place, :]
             for head in range(full.shape[1] // HEAD_DIM):
                 lanes = slice(head * HEAD_DIM, (head + 1) * HEAD_DIM)
-                out_ref[span, lanes] = turn(full[:, lanes], cosine, sine).astype(jnp.bfloat16)
-        v_ref[span, :] = mm(x, wv_ref[...]).astype(jnp.bfloat16)
+                part = full[half * rows : (half + 1) * rows, lanes]
+                out_ref[span, lanes] = turn(part, cosine, sine).astype(jnp.bfloat16)
+    v_ref[...] = mm(x_s[...], wv_ref[...]).astype(jnp.bfloat16)
 
 
 def qkv_pair(first, rank, xa, xb, cosine, sine, wq, wk, wv):
@@ -71,6 +72,7 @@
             grid=(width // tile,),
             in_specs=[whole(xa.shape)] * 2 + [whole(cosine.shape)] * 2 + [wspec] * 3,
             out_specs=[ospec] * 3,
+            scratch_shapes=[pltpu.VMEM((2 * rows, depth), jnp.bfloat16)],
         ),
         out_shape=[out] * 3,
         compiler_params=pltpu.CompilerParams(vmem_limit_bytes=60 << 20),
@@ -210,13 +212,13 @@
     )(rank, *qs, *ks, *vs, *gs, low, high, lse, cosine, back_sine)
 
 
-def mlp_body(xa_ref, xb_ref, dm_ref, wg_ref, wu_ref, mid_ref, dg_ref, du_ref):
+def mlp_body(xa_ref, xb_ref, dm_ref, wg_ref, wu_ref, mid_ref, dg_ref, du_ref, x_s):
     rows = xa_ref.shape[0]
-    for half, x_ref in enumerate((xa_ref, xb_ref)):
+    lay_together((xa_ref, xb_ref), x_s)
+    gates, ups = mm(x_s[...], wg_ref[...]), mm(x_s[...], wu_ref[...])
+    for half in range(2):
         span = pl.ds(half * rows, rows)
-        x = x_ref[...]
-        gate = mm(x, wg_ref[...])
-        up = mm(x, wu_ref[...])
+        gate, up = (both[half * rows : (half + 1) * rows, :] for both in (gates, ups))
         d_mid = dm_ref[span, :]
         sigma = 1.0 / (1.0 + jnp.exp(-gate))
         active = gate * sigma
@@ -237,6 +239,7 @@
         in_specs=[whole(xa.shape)] * 2 + [ospec] + [wspec] * 2,
         out_specs=[ospec] * 3,
         out_shape=[jax.ShapeDtypeStruct((2 * rows, width), jnp.bfloat16)] * 3,
+        scratch_shapes=[pltpu.VMEM((2 * rows, depth), jnp.bfloat16)],
         compiler_params=pltpu.CompilerParams(vmem_limit_bytes=60 << 20),
         cost_estimate=cost(
             flops=8 * rows * depth * width,
@@ -368,12 +371,18 @@
     )(rank, own, got, own, got)
 
 
-def product(lefts, weights, half, rows):
+def product(lefts, weights):
     total = None
     for left, (w_ref, dims) in zip(lefts, weights):
-        value = mm(left[half][...] if len(left) == 2 else left[0][pl.ds(half * rows, rows), :], w_ref[...], dims)
+        value = mm(left[...], w_ref[...], dims)
         total = value if total is None else total + value
     return total
+
+
+def lay_together(parts, out_ref):
+    @pl.when(pl.program_id(0) == 0)
+    def _():
+        gather_rows(parts, out_ref)
 
 
 def project_body(terms, *refs):
@@ -382,11 +391,14 @@
         lefts.append(refs[at : at + pieces])
         weights.append((refs[at + pieces], dims))
         at += pieces + 1
-    out_ref = refs[at]
-    rows = out_ref.shape[0] // 2
-    for half in range(2):
-        span = pl.ds(half * rows, rows)
-        out_ref[span, :] = product(lefts, weights, half, rows).astype(out_ref.dtype)
+    out_ref, scratch = refs[at], list(refs[at + 1 :])
+    for index, left in enumerate(lefts):
+        if len(left) > 1:
+            lay_together(left, scratch[0])
+            lefts[index] = scratch.pop(0)
+        else:
+            lefts[index] = left[0]
+    out_ref[...] = product(lefts, weights).astype(out_ref.dtype)
 
 
 def terms_of(terms):
@@ -417,6 +429,9 @@
         in_specs=in_specs,
         out_specs=pl.BlockSpec((rows, tile), lambda j: (0, j)),
         out_shape=jax.ShapeDtypeStruct((rows, width), dtype),
+        scratch_shapes=[
+            pltpu.VMEM((rows, left[0].shape[1]), jnp.bfloat16) for left, _, _ in terms if len(left) > 1
+        ],
         compiler_params=pltpu.CompilerParams(vmem_limit_bytes=60 << 20),
         cost_estimate=cost(
             flops=2 * rows * width * sum(left[0].shape[1] for left, _, _ in terms),
@@ -430,7 +445,7 @@
 def pair_body(terms, steps, *refs):
     at, lefts, weights = 0, [], []
     for pieces, dims in terms:
-        lefts.append(refs[at : at + pieces])
+        lefts.append(refs[at])
         weights.append((refs[at + pieces], dims))
         at += pieces + 1
     out_ref, mine_s, away_s, got_s, send_sem, recv_sem = refs[at:]
@@ -456,16 +471,17 @@
             device_id_type=pl.DeviceIdType.MESH,
         )
 
-    away_s[step] = product(lefts, weights, 1, rows).astype(jnp.bfloat16)
+    total = product(lefts, weights)
+    away_s[step] = total[rows:, :].astype(jnp.bfloat16)
     copy(step).start()
-    mine_s[step] = product(lefts, weights, 0, rows)
+    mine_s[step] = total[:rows, :]
 
     @pl.when(step == steps - 1)
     def _():
         for index in range(steps):
             copy(index).wait()
-            total = mine_s[index] + got_s[index].astype(jnp.float32)
-            out_ref[:, index * tile : (index + 1) * tile] = total.astype(out_ref.dtype)
+            both = mine_s[index] + got_s[index].astype(jnp.float32)
+            out_ref[:, index * tile : (index + 1) * tile] = both.astype(out_ref.dtype)
 
 
 def pair_sum(terms, ident, dtype):

time: 504 us -> 505 us (level)
  transfers between devices with their start and end apart: 28 -> 28, of which waited for: 12 -> 12; matrix products, arithmetic and copies ran while one was open for 4% -> 4% of each run, Pallas kernels for 52% -> 53%
where the time goes in v8:
time: 505 us; the launch traced here: 499 us
  Pallas kernels  380 us (75%)
  starting transfers between devices  36.4 us (7%)
  other arithmetic  32.9 us (7%)
  waiting for transfers between devices  27 us (5%)
  local copies, waits for them, and re-layouts  21.6 us (4%)
    pallas_call x1, Pallas kernels, last_stages(): pl.pallas_call(functools.partial(last_body, len(ones), len(twos), len(thr...  92 us
    pallas_call x8, Pallas kernels, pair_sum(): pl.pallas_call(functools.partial(pair_body, [(len(left), dims) for left,...  85.2 us
    pallas_call x8, Pallas kernels, grad_call(): pl.pallas_call(functools.partial(grad_body, len(pieces), widths, low, sid...  77.1 us
    ppermute x28, starting transfers between devices, exchange(): lax.ppermute(values, axis, [(rank, rank ^ bit) for rank in range(size)])  36.4 us
    pallas_call x2, Pallas kernels, mlp_pair(): pl.pallas_call(mlp_body, grid=(pl.cdiv(width, tile),), in_specs=[whole(xa...  29.8 us
    ppermute x28, waiting for transfers between devices, exchange(): lax.ppermute(values, axis, [(rank, rank ^ bit) for rank in range(size)])  27 us
    pallas_call x4, Pallas kernels, project(): pl.pallas_call(functools.partial(project_body, [(len(left), dims) for lef...  26.8 us
    pallas_call x1, Pallas kernels, attend_back(): pl.pallas_call(attend_back_body, grid_spec=pltpu.PrefetchScalarGridSpec(n...  21.7 us
  transfers between devices with their start and end apart: 28, of which 12 were waited for; matrix products, arithmetic and copies ran while one was open for 4% of the time, Pallas kernels for 53%

profile of v8, /device:TPU:0, one launch (start us, length us, event | category | flops | bytes accessed | tf_op | source)
XLA Modules:
  0.0 499.3 jit_solution(3129237819818291879)
XLA Ops:
  4.6 2.6 collective-permute-start
  9.6 2.4 fusion.13
  16.1 2.0 collective-permute-done.2
  18.1 2.6 collective-permute-start.3
  20.7 1.9 collective-permute-done.3
  25.4 9.5 %qkv.2 = (bf16[640,512]{1,0:T(8,128)(2,1)}, bf16[640,512]{1,0:T(8,128)(2,1)}, bf16[640,512]{1,0:T(8,128)(2,1)}) custom-call(s32[1]{0:T(128)} %bitcast.rank_ref, bf16[320,2048]{1,0:T(8,128)(2,1)} %copy-done.30, bf16[320,2048]{1,0:T(8,128)(2,1)} %copy-done.33, f32[1280,128]{1,0:T(8,128)} %pad_maximum_fusion.cos_ref, f32[1280,128]{1,0:T(8,128)} %get-tuple-element.245.sin_ref, ...), custom_call_target="tpu_custom_call" | custom-call | flops 4026531 | bytes 8912 | tf_op jit(solution)/shard_map/qkv/pallas_call | solution.py:68
  40.1 8.9 %qkv.3 = (bf16[640,512]{1,0:T(8,128)(2,1)}, bf16[640,512]{1,0:T(8,128)(2,1)}, bf16[640,512]{1,0:T(8,128)(2,1)}) custom-call(s32[1]{0:T(128)} %bitcast.rank_ref, bf16[320,2048]{1,0:T(8,128)(2,1)} %collective-permute-done.xa_ref.refs_2_, bf16[320,2048]{1,0:T(8,128)(2,1)} %collective-permute-done.5.xb_ref.refs_3_, f32[1280,128]{1,0:T(8,128)} %pad_maximum_fusion.cos_ref, ...), custom_call_target="tpu_custom_call" | custom-call | flops 4026531 | bytes 8912 | tf_op jit(solution)/shard_map/qkv/pallas_call | solution.py:68
  49.0 14.6 %attend.1 = (bf16[640,512]{1,0:T(8,128)(2,1)}, bf16[640,512]{1,0:T(8,128)(2,1)}, f32[4,1,1280]{2,1,0:T(1,128)}) custom-call(s32[1]{0:T(128)} %bitcast.rank_ref, bf16[640,512]{1,0:T(8,128)(2,1)} %get-tuple-element.125.qn, bf16[640,512]{1,0:T(8,128)(2,1)} %get-tuple-element.127.qf, bf16[640,512]{1,0:T(8,128)(2,1)} %get-tuple-element.128.kn, ...), custom_call_target="tpu_custom_call" | custom-call | flops 6710886 | bytes 5242 | tf_op jit(solution)/shard_map/attend/pallas_call | solution.py:130
  63.6 6.8 %pair_sum.8 = bf16[320,2048]{1,0:T(8,128)(2,1)} custom-call(bf16[640,512]{1,0:T(8,128)(2,1)} %get-tuple-element.134.refs_0_.refs_5_, bf16[512,2048]{1,0:T(8,128)(2,1)} %refs_2_.7), custom_call_target="tpu_custom_call" | custom-call | flops 1342177 | bytes 5373 | tf_op jit(solution)/shard_map/pair_sum/pallas_call | solution.py:494
  72.4 7.3 %pair_sum.9 = f32[320,2048]{1,0:T(8,128)} custom-call(bf16[640,512]{1,0:T(8,128)(2,1)} %get-tuple-element.138.refs_0_.refs_4_, bf16[512,2048]{1,0:T(8,128)(2,1)} %refs_2_.7), custom_call_target="tpu_custom_call" | custom-call | flops 1342177 | bytes 5373 | tf_op jit(solution)/shard_map/pair_sum/pallas_call | solution.py:494
  79.7 8.5 %project.4.dm_ref = f32[640,1408]{1,0:T(8,128)} custom-call(bf16[320,2048]{1,0:T(8,128)(2,1)} %copy-done.27, bf16[320,2048]{1,0:T(8,128)(2,1)} %copy-done.29, bf16[1408,2048]{1,0:T(8,128)(2,1)} %refs_1_.13), custom_call_target="tpu_custom_call" | custom-call | flops 3690987 | bytes 10190 | tf_op jit(solution)/shard_map/project/pallas_call | solution.py:426
  88.3 8.7 %project.5.dm_ref = f32[640,1408]{1,0:T(8,128)} custom-call(bf16[320,2048]{1,0:T(8,128)(2,1)} %copy-done.28, bf16[320,2048]{1,0:T(8,128)(2,1)} %collective-permute-done.9.refs_1_.refs_3_, bf16[1408,2048]{1,0:T(8,128)(2,1)} %refs_1_.13), custom_call_target="tpu_custom_call" | custom-call | flops 3690987 | bytes 10190 | tf_op jit(solution)/shard_map/project/pallas_call | solution.py:426
  97.0 5.1 %collective-permute-done.8 = bf16[320,2048]{1,0:T(8,128)(2,1)} collective-permute-done((bf16[320,2048]{1,0:T(8,128)(2,1)}, bf16[320,2048]{1,0:T(8,128)(2,1)}, u32[]{:S(2)}, u32[]{:S(2)}) %collective-permute-start.8) | collective-permute-done | bytes 1310752 | tf_op jit(solution)/shard_map/ppermute | solution.py:731
  102.0 1.9 multiply_reduce_fusion.2
  109.9 15.0 %mlp.2 = (bf16[640,1408]{1,0:T(8,128)(2,1)}, bf16[640,1408]{1,0:T(8,128)(2,1)}, bf16[640,1408]{1,0:T(8,128)(2,1)}) custom-call(bf16[320,2048]{1,0:T(8,128)(2,1)} %copy-done.20, bf16[320,2048]{1,0:T(8,128)(2,1)} %copy-done.21, f32[640,1408]{1,0:T(8,128)} %project.4.dm_ref, bf16[2048,1408]{1,0:T(8,128)(2,1)} %refs_1_.12, bf16[2048,1408]{1,0:T(8,128)(2,1)} %refs_3_.5), custom_call_target="tpu_custom_call" | custom-call | flops 7381975 | bytes 23166 | tf_op jit(solution)/shard_map/mlp/pallas_call | solution.py:236
  124.9 10.2 %pair_sum.10 = f32[320,2048]{1,0:T(8,128)} custom-call(bf16[640,1408]{1,0:T(8,128)(2,1)} %get-tuple-element.160.refs_0_.refs_4_, bf16[1408,2048]{1,0:T(8,128)(2,1)} %refs_1_.13), custom_call_target="tpu_custom_call" | custom-call | flops 3690987 | bytes 10190 | tf_op jit(solution)/shard_map/pair_sum/pallas_call | solution.py:494
  137.0 3.0 collective-permute-done.12.xb_ref.refs_3_
  141.1 14.8 %mlp.3 = (bf16[640,1408]{1,0:T(8,128)(2,1)}, bf16[640,1408]{1,0:T(8,128)(2,1)}, bf16[640,1408]{1,0:T(8,128)(2,1)}) custom-call(bf16[320,2048]{1,0:T(8,128)(2,1)} %copy-done.22, bf16[320,2048]{1,0:T(8,128)(2,1)} %copy-done.23, f32[640,1408]{1,0:T(8,128)} %project.5.dm_ref, bf16[2048,1408]{1,0:T(8,128)(2,1)} %refs_1_.12, bf16[2048,1408]{1,0:T(8,128)(2,1)} %refs_3_.5), custom_call_target="tpu_custom_call" | custom-call | flops 7381975 | bytes 23166 | tf_op jit(solution)/shard_map/mlp/pallas_call | solution.py:236
  155.9 8.7 %weight_grad.8 = bf16[4,256,1408]{2,1,0:T(8,128)(2,1)} custom-call(s32[1]{0:T(128)} %bitcast.7.rank_ref._, bf16[320,2048]{1,0:T(8,128)(2,1)} %copy-done.27, bf16[320,2048]{1,0:T(8,128)(2,1)} %copy-done.29, bf16[320,2048]{1,0:T(8,128)(2,1)} %copy-done.28, bf16[320,2048]{1,0:T(8,128)(2,1)} %collective-permute-done.9.refs_1_.refs_3_, ...), custom_call_target="tpu_custom_call" | custom-call | flops 3690987 | bytes 9109 | tf_op jit(solution)/shard_map/weight_grad/pallas_call | solution.py:327
  166.4 14.8 %pair_sum.11 = bf16[320,2048]{1,0:T(8,128)(2,1)} custom-call(bf16[640,1408]{1,0:T(8,128)(2,1)} %get-tuple-element.154.refs_0_.refs_5_, bf16[2048,1408]{1,0:T(8,128)(2,1)} %refs_1_.12, bf16[640,1408]{1,0:T(8,128)(2,1)} %get-tuple-element.155.refs_2_.refs_5_, bf16[2048,1408]{1,0:T(8,128)(2,1)} %refs_3_.5), custom_call_target="tpu_custom_call" | custom-call | flops 7381975 | bytes 17760 | tf_op jit(solution)/shard_map/pair_sum/pallas_call | solution.py:494
  182.8 8.7 %weight_grad.11 = bf16[4,256,1408]{2,1,0:T(8,128)(2,1)} custom-call(s32[1]{0:T(128)} %bitcast.7.rank_ref._, bf16[320,2048]{1,0:T(8,128)(2,1)} %copy-done.20, bf16[320,2048]{1,0:T(8,128)(2,1)} %copy-done.21, bf16[320,2048]{1,0:T(8,128)(2,1)} %copy-done.22, bf16[320,2048]{1,0:T(8,128)(2,1)} %copy-done.23, ...), custom_call_target="tpu_custom_call" | custom-call | flops 3690987 | bytes 9109 | tf_op jit(solution)/shard_map/weight_grad/pallas_call | solution.py:327
  193.1 8.7 %weight_grad.10.own_away.own_kept = bf16[4,256,1408]{2,1,0:T(8,128)(2,1)} custom-call(s32[1]{0:T(128)} %bitcast.7.rank_ref._, bf16[320,2048]{1,0:T(8,128)(2,1)} %copy-done.27, bf16[320,2048]{1,0:T(8,128)(2,1)} %copy-done.29, bf16[320,2048]{1,0:T(8,128)(2,1)} %copy-done.28, bf16[320,2048]{1,0:T(8,128)(2,1)} %collective-permute-done.9.refs_1_.refs_3_, ...), custom_call_target="tpu_custom_call" | custom-call | flops 3690987 | bytes 9109 | tf_op jit(solution)/shard_map/weight_grad/pallas_call | solution.py:327
  201.8 8.7 %weight_grad.9 = bf16[4,256,1408]{2,1,0:T(8,128)(2,1)} custom-call(s32[1]{0:T(128)} %bitcast.7.rank_ref._, bf16[320,2048]{1,0:T(8,128)(2,1)} %copy-done.20, bf16[320,2048]{1,0:T(8,128)(2,1)} %copy-done.21, bf16[320,2048]{1,0:T(8,128)(2,1)} %copy-done.22, bf16[320,2048]{1,0:T(8,128)(2,1)} %copy-done.23, bf16[640,1408]{1,0:T(8,128)(2,1)} %get-tuple-element.171.refs_2_.refs_4_, ...), custom_call_target="tpu_custom_call" | custom-call | flops 3690987 | bytes 9109 | tf_op jit(solution)/shard_map/weight_grad/pallas_call | solution.py:327
  210.5 15.5 %pair_sum.12 = f32[320,2048]{1,0:T(8,128)} custom-call(bf16[640,1408]{1,0:T(8,128)(2,1)} %get-tuple-element.164.refs_0_.refs_4_, bf16[2048,1408]{1,0:T(8,128)(2,1)} %refs_1_.12, bf16[640,1408]{1,0:T(8,128)(2,1)} %get-tuple-element.171.refs_2_.refs_4_, bf16[2048,1408]{1,0:T(8,128)(2,1)} %refs_3_.5), custom_call_target="tpu_custom_call" | custom-call | flops 7381975 | bytes 17760 | tf_op jit(solution)/shard_map/pair_sum/pallas_call | solution.py:494
  226.0 2.6 convert_add_fusion.2
  231.9 2.8 fusion.16
  240.3 9.8 %pair_sum.13 = bf16[320,2048]{1,0:T(8,128)(2,1)} custom-call(bf16[640,1408]{1,0:T(8,128)(2,1)} %get-tuple-element.163.refs_5_.refs_0_, bf16[1408,2048]{1,0:T(8,128)(2,1)} %refs_1_.13), custom_call_target="tpu_custom_call" | custom-call | flops 3690987 | bytes 10190 | tf_op jit(solution)/shard_map/pair_sum/pallas_call | solution.py:494
  250.2 8.8 %weight_grad.12.own_away.own_kept = bf16[4,256,1408]{2,1,0:T(8,128)(2,1)} custom-call(s32[1]{0:T(128)} %bitcast.7.rank_ref._, bf16[320,2048]{1,0:T(8,128)(2,1)} %copy-done.20, bf16[320,2048]{1,0:T(8,128)(2,1)} %copy-done.21, bf16[320,2048]{1,0:T(8,128)(2,1)} %copy-done.22, bf16[320,2048]{1,0:T(8,128)(2,1)} %copy-done.23, ...), custom_call_target="tpu_custom_call" | custom-call | flops 3690987 | bytes 9109 | tf_op jit(solution)/shard_map/weight_grad/pallas_call | solution.py:327
  259.0 4.8 project.6.gn
  263.7 2.5 collective-permute-done.15.refs_0_.refs_2_
  267.8 8.7 %weight_grad.13.own_away.own_kept = bf16[4,256,1408]{2,1,0:T(8,128)(2,1)} custom-call(s32[1]{0:T(128)} %bitcast.7.rank_ref._, bf16[320,2048]{1,0:T(8,128)(2,1)} %copy-done.20, bf16[320,2048]{1,0:T(8,128)(2,1)} %copy-done.21, bf16[320,2048]{1,0:T(8,128)(2,1)} %copy-done.22, bf16[320,2048]{1,0:T(8,128)(2,1)} %copy-done.23, ...), custom_call_target="tpu_custom_call" | custom-call | flops 3690987 | bytes 9109 | tf_op jit(solution)/shard_map/weight_grad/pallas_call | solution.py:327
  276.4 2.9 merge.9
  281.0 4.8 project.7.gf
  285.8 9.4 %weight_grad.14 = (bf16[4,256,512]{2,1,0:T(8,128)(2,1)}, bf16[4,256,512]{2,1,0:T(8,128)(2,1)}) custom-call(s32[1]{0:T(128)} %bitcast.7.rank_ref._, bf16[320,2048]{1,0:T(8,128)(2,1)} %get-tuple-element.162.refs_0_, bf16[320,2048]{1,0:T(8,128)(2,1)} %collective-permute-done.17.refs_1_, bf16[320,2048]{1,0:T(8,128)(2,1)} %collective-permute-done.15.refs_0_.refs_2_, ...), custom_call_target="tpu_custom_call" | custom-call | flops 2684354 | bytes 8650 | tf_op jit(solution)/shard_map/weight_grad/pallas_call | solution.py:327
  295.3 3.3 merge.8
  301.3 2.4 merge.10
  304.5 2.6 collective-permute-start.24
  307.1 21.7 %attend_back.1 = (bf16[640,512]{1,0:T(8,128)(2,1)}, bf16[640,512]{1,0:T(8,128)(2,1)}, bf16[640,512]{1,0:T(8,128)(2,1)}, bf16[640,512]{1,0:T(8,128)(2,1)}, bf16[6...) custom-call(s32[1]{0:T(128)} %bitcast.rank_ref, bf16[640,512]{1,0:T(8,128)(2,1)} %get-tuple-element.125.qn, ...), custom_call_target="tpu_custom_call" | custom-call | flops 16777216 | bytes 10485 | tf_op jit(solution)/shard_map/attend_back/pallas_call | solution.py:193
  328.8 10.2 %pair_sum.14 = bf16[320,2048]{1,0:T(8,128)(2,1)} custom-call(bf16[640,512]{1,0:T(8,128)(2,1)} %get-tuple-element.184.refs_0_.refs_5_, bf16[2048,512]{1,0:T(8,128)(2,1)} %refs_1_.15, bf16[640,512]{1,0:T(8,128)(2,1)} %get-tuple-element.185.refs_2_.refs_7_, bf16[2048,512]{1,0:T(8,128)(2,1)} %refs_3_.7, bf16[640,512]{1,0:T(8,128)(2,1)} %get-tuple-element.186.refs_4_.refs_9_, ...), custom_call_target="tpu_custom_call" | custom-call | flops 4026531 | bytes 10878 | tf_op jit(solution)/shard_map/pair_sum/pallas_call | solution.py:494
  342.1 5.9 %collective-permute-done.24.refs_11_ = bf16[1,256,1408]{2,1,0:T(8,128)(2,1)} collective-permute-done((bf16[1,256,1408]{2,1,0:T(8,128)(2,1)}, bf16[1,256,1408]{2,1,0:T(8,128)(2,1)}, u32[]{:S(2)}, u32[]{:S(2)}) %collective-permute-start.24) | collective-permute-done | bytes 720928 | tf_op jit(solution)/shard_map/ppermute | solution.py:731
  348.8 2.5 merge.11
  352.2 2.6 collective-permute-start.27
  354.8 3.1 add_convert_fusion
  360.0 10.5 %pair_sum.15 = f32[320,2048]{1,0:T(8,128)} custom-call(bf16[640,512]{1,0:T(8,128)(2,1)} %get-tuple-element.196.refs_0_.refs_4_, bf16[2048,512]{1,0:T(8,128)(2,1)} %refs_1_.15, bf16[640,512]{1,0:T(8,128)(2,1)} %get-tuple-element.197.refs_2_.refs_6_, bf16[2048,512]{1,0:T(8,128)(2,1)} %refs_3_.7, bf16[640,512]{1,0:T(8,128)(2,1)} %get-tuple-element.198.refs_4_.refs_8_, ...), custom_call_target="tpu_custom_call" | custom-call | flops 4026531 | bytes 10878 | tf_op jit(solution)/shard_map/pair_sum/pallas_call | solution.py:494
  370.5 15.3 %weight_grad.15 = (bf16[4,256,512]{2,1,0:T(8,128)(2,1)}, bf16[4,256,512]{2,1,0:T(8,128)(2,1)}, bf16[4,256,512]{2,1,0:T(8,128)(2,1)}, bf16[4,256,512]{2,1,0:T(8,1...) custom-call(s32[1]{0:T(128)} %bitcast.7.rank_ref._, bf16[320,2048]{1,0:T(8,128)(2,1)} %copy-done.30, ...), custom_call_target="tpu_custom_call" | custom-call | flops 8053063 | bytes 15466 | tf_op jit(solution)/shard_map/weight_grad/pallas_call | solution.py:327
  385.9 2.5 convert_add_fusion.1
  394.2 92.0 %last_stages.1 = (f32[256,1408]{1,0:T(8,128)}, f32[512,256]{1,0:T(8,128)}, f32[256,512]{1,0:T(8,128)}, f32[256,512]{1,0:T(8,128)}, f32[256,512]{1,0:T(8,128)}, /*index=5*/f32[1408,256]{1,0:T(8,128)}, f32[2,2048]{1,0:T(2,128)}) custom-call(bf16[1,256,1408]{2,1,0:T(8,128)(2,1)} %copy-done.13, bf16[2,256,512]{2,1,0:T(8,128)(2,1)} %copy-done.15, ...), custom_call_target="tpu_custom_call" | custom-call | flops 16777 | bytes 33554 | tf_op jit(solution)/shard_map/last_stages/pallas_call | solution.py:675
  486.2 4.8 fusion.8
  (188 shorter events, 70.3 us)
Async XLA Ops:
  0.6 6.6 %copy-start.48 = (s32[1,3]{1,0:T(1,128)S(1)}, s32[1,3]{1,0:T(1,128)}, u32[]{:S(2)}) copy-start(s32[1,3]{1,0:T(1,128)} %param.25) | copy-start | bytes 40
  0.7 6.9 %copy-start.46 = (s32[1,1280]{1,0:T(1,128)S(1)}, s32[1,1280]{1,0:T(1,128)}, u32[]{:S(2)}) copy-start(s32[1,1280]{1,0:T(1,128)} %param.27) | copy-start | bytes 15364
  0.7 7.1 %copy-start.47 = (s32[1,3]{1,0:T(1,128)S(1)}, s32[1,3]{1,0:T(1,128)}, u32[]{:S(2)}) copy-start(s32[1,3]{1,0:T(1,128)} %param.26) | copy-start | bytes 40
  4.1 10.4 %copy-start.30 = (bf16[320,2048]{1,0:T(8,128)(2,1)}, bf16[320,2048]{1,0:T(8,128)(2,1)S(1)}, u32[]{:S(2)}) copy-start(bf16[320,2048]{1,0:T(8,128)(2,1)S(1)} %fusion.4.xa_ref.refs_0_) | copy-start | bytes 3932164
  4.1 20.3 %collective-permute-start.4 = (bf16[320,2048]{1,0:T(8,128)(2,1)S(1)}, bf16[320,2048]{1,0:T(8,128)(2,1)S(1)}, u32[]{:S(2)}, u32[]{:S(2)}) collective-permute-start(bf16[320,2048]{1,0:T(8,128)(2,1)S(1)} %fusion.4.xa_ref.refs_0_), channel_id=1, source_target_pairs={{0,1},{1,0},{2,3},{3,2},{4,5},{5,4},{6,7},{7,6},{8,9},{9,8},{10,11... | collective-permute-start | bytes 3932168 | tf_op jit(solution)/shard_map/ppermute | solution.py:731
  4.6 32.1 %collective-permute-start = (bf16[320,2048]{1,0:T(8,128)(2,1)S(1)}, bf16[320,2048]{1,0:T(8,128)(2,1)}, u32[]{:S(2)}, u32[]{:S(2)}) collective-permute-start(bf16[320,2048]{1,0:T(8,128)(2,1)S(1)} %fusion.4.xa_ref.refs_0_), channel_id=1, source_target_pairs={{0,2},{1,3},{2,0},{3,1},{4,6},{5,7},{6,4},{7,5},{8,10},{9,11},{10,... | collective-permute-start | bytes 3932168 | tf_op jit(solution)/shard_map/ppermute | solution.py:731
  8.0 6.5 %collective-permute-start.1 = (f32[8]{0:T(128)S(1)}, f32[8]{0:T(128)S(1)}, u32[]{:S(2)}, u32[]{:S(2)}) collective-permute-start(f32[8]{0:T(128)S(1)} %select_reduce_fusion.1), channel_id=1, source_target_pairs={{0,4},{4,0},{8,12},{12,8},{16,20},{20,16},{24,28},{28,24},{1,5},{5... | collective-permute-start | bytes 104 | tf_op jit(solution)/shard_map/ppermute | solution.py:731
  9.5 14.5 %copy-start.34 = (bf16[320,2048]{1,0:T(8,128)(2,1)S(1)}, bf16[320,2048]{1,0:T(8,128)(2,1)}, u32[]{:S(2)}) copy-start(bf16[320,2048]{1,0:T(8,128)(2,1)} %param.15) | copy-start | bytes 3932164
  14.5 3.6 collective-permute-start.2
  18.1 4.5 collective-permute-start.3
  24.3 14.1 %copy-start.27 = (bf16[320,2048]{1,0:T(8,128)(2,1)}, bf16[320,2048]{1,0:T(8,128)(2,1)S(1)}, u32[]{:S(2)}) copy-start(bf16[320,2048]{1,0:T(8,128)(2,1)S(1)} %fusion.12.refs_0_) | copy-start | bytes 3932164
  36.7 3.4 collective-permute-start.5
  36.7 33.7 %collective-permute-start.7 = (bf16[320,2048]{1,0:T(8,128)(2,1)S(1)}, bf16[320,2048]{1,0:T(8,128)(2,1)S(1)}, u32[]{:S(2)}, u32[]{:S(2)}) collective-permute-start(bf16[320,2048]{1,0:T(8,128)(2,1)S(1)} %fusion.12.refs_0_), channel_id=1, source_target_pairs={{0,2},{1,3},{2,0},{3,1},{4,6},{5,7},{6,4},{7,5},{8,10},{9,11},{10,... | collective-permute-start | bytes 3932168 | tf_op jit(solution)/shard_map/ppermute | solution.py:731
  38.4 32.0 %collective-permute-start.6 = (bf16[320,2048]{1,0:T(8,128)(2,1)S(1)}, bf16[320,2048]{1,0:T(8,128)(2,1)S(1)}, u32[]{:S(2)}, u32[]{:S(2)}) collective-permute-start(bf16[320,2048]{1,0:T(8,128)(2,1)S(1)} %fusion.12.refs_0_), channel_id=1, source_target_pairs={{0,1},{1,0},{2,3},{3,2},{4,5},{5,4},{6,7},{7,6},{8,9},{9,8},{10,11... | collective-permute-start | bytes 3932168 | tf_op jit(solution)/shard_map/ppermute | solution.py:731
  70.4 9.3 %copy-start.28 = (bf16[320,2048]{1,0:T(8,128)(2,1)}, bf16[320,2048]{1,0:T(8,128)(2,1)S(1)}, u32[]{:S(2)}) copy-start(bf16[320,2048]{1,0:T(8,128)(2,1)S(1)} %collective-permute-done.7.refs_0_.refs_2_) | copy-start | bytes 3932164
  70.5 9.3 %copy-start.29 = (bf16[320,2048]{1,0:T(8,128)(2,1)}, bf16[320,2048]{1,0:T(8,128)(2,1)S(1)}, u32[]{:S(2)}) copy-start(bf16[320,2048]{1,0:T(8,128)(2,1)S(1)} %collective-permute-done.6.refs_1_) | copy-start | bytes 3932164
  70.5 17.8 %collective-permute-start.9 = (bf16[320,2048]{1,0:T(8,128)(2,1)S(1)}, bf16[320,2048]{1,0:T(8,128)(2,1)}, u32[]{:S(2)}, u32[]{:S(2)}) collective-permute-start(bf16[320,2048]{1,0:T(8,128)(2,1)S(1)} %collective-permute-done.7.refs_0_.refs_2_), channel_id=1, source_target_pairs={{0,1},{1,0},{2,3},{3,2},{4,5},{5,4},{6,7},{7,6},{8,9},{9,8},{10,11... | collective-permute-start | bytes 3932168 | tf_op jit(solution)/shard_map/ppermute | solution.py:731
  70.7 31.4 %collective-permute-start.8 = (bf16[320,2048]{1,0:T(8,128)(2,1)}, bf16[320,2048]{1,0:T(8,128)(2,1)}, u32[]{:S(2)}, u32[]{:S(2)}) collective-permute-start(bf16[320,2048]{1,0:T(8,128)(2,1)} %pair_sum.8), channel_id=1, source_target_pairs={{0,2},{1,3},{2,0},{3,1},{4,6},{5,7},{6,4},{7,5},{8,10},{9,11},{10,... | collective-permute-start | bytes 3932168 | tf_op jit(solution)/shard_map/ppermute | solution.py:731
  88.2 13.8 %copy-start.24 = (bf16[320,2048]{1,0:T(8,128)(2,1)S(1)}, bf16[320,2048]{1,0:T(8,128)(2,1)}, u32[]{:S(2)}) copy-start(bf16[320,2048]{1,0:T(8,128)(2,1)} %param.14) | copy-start | bytes 3932164
  88.3 13.8 %copy-start.32 = (f32[320,2048]{1,0:T(8,128)S(1)}, f32[320,2048]{1,0:T(8,128)}, u32[]{:S(2)}) copy-start(f32[320,2048]{1,0:T(8,128)} %pair_sum.9) | copy-start | bytes 7864324
  97.0 8.5 %copy-start.44 = (f32[2048]{0:T(1024)S(1)}, f32[2048]{0:T(1024)}, u32[]{:S(2)}) copy-start(f32[2048]{0:T(1024)} %param.21) | copy-start | bytes 24580
  105.8 3.1 collective-permute-start.11
  105.8 31.2 %collective-permute-start.10 = (bf16[320,2048]{1,0:T(8,128)(2,1)S(1)}, bf16[320,2048]{1,0:T(8,128)(2,1)S(1)}, u32[]{:S(2)}, u32[]{:S(2)}) collective-permute-start(bf16[320,2048]{1,0:T(8,128)(2,1)S(1)} %multiply_convert_fusion.xa_ref.refs_0_), channel_id=1, source_target_pairs={{0,2},{1,3},{2,0},{3,1},{4,6},{5,7},{6,4},{7,5},{8,10},{9,11},{10,... | collective-permute-start | bytes 3932168 | tf_op jit(solution)/shard_map/ppermute | solution.py:731
  137.0 3.0 collective-permute-start.12
  164.7 64.7 %collective-permute-start.14 = (bf16[4,256,1408]{2,1,0:T(8,128)(2,1)}, bf16[4,256,1408]{2,1,0:T(8,128)(2,1)S(1)}, u32[]{:S(2)}, u32[]{:S(2)}) collective-permute-start(bf16[4,256,1408]{2,1,0:T(8,128)(2,1)} %weight_grad.8), channel_id=1, source_target_pairs={{0,4},{4,0},{8,12},{12,8},{16,20},{20,16},{24,28},{28,24},{1,5},{5... | collective-permute-start | bytes 8650760 | tf_op jit(solution)/shard_map/ppermute | solution.py:731
  181.2 44.8 %collective-permute-start.13 = (bf16[320,2048]{1,0:T(8,128)(2,1)}, bf16[320,2048]{1,0:T(8,128)(2,1)}, u32[]{:S(2)}, u32[]{:S(2)}) collective-permute-start(bf16[320,2048]{1,0:T(8,128)(2,1)} %pair_sum.11), channel_id=1, source_target_pairs={{0,2},{1,3},{2,0},{3,1},{4,6},{5,7},{6,4},{7,5},{8,10},{9,11},{10,... | collective-permute-start | bytes 3932168 | tf_op jit(solution)/shard_map/ppermute | solution.py:731
  191.5 72.3 %collective-permute-start.16 = (bf16[4,256,1408]{2,1,0:T(8,128)(2,1)}, bf16[4,256,1408]{2,1,0:T(8,128)(2,1)}, u32[]{:S(2)}, u32[]{:S(2)}) collective-permute-start(bf16[4,256,1408]{2,1,0:T(8,128)(2,1)} %weight_grad.11), channel_id=1, source_target_pairs={{0,8},{4,12},{8,0},{12,4},{16,24},{20,28},{24,16},{28,20},{1,9},{5... | collective-permute-start | bytes 8650760 | tf_op jit(solution)/shard_map/ppermute | solution.py:731
  226.0 5.1 %copy-start.18 = (f32[320,2048]{1,0:T(8,128)S(1)}, f32[320,2048]{1,0:T(8,128)}, u32[]{:S(2)}) copy-start(f32[320,2048]{1,0:T(8,128)} %copy-done.17) | copy-start | bytes 7864324
  229.4 65.8 %collective-permute-start.19 = (bf16[4,256,1408]{2,1,0:T(8,128)(2,1)}, bf16[4,256,1408]{2,1,0:T(8,128)(2,1)}, u32[]{:S(2)}, u32[]{:S(2)}) collective-permute-start(bf16[4,256,1408]{2,1,0:T(8,128)(2,1)} %weight_grad.9), channel_id=1, source_target_pairs={{0,4},{4,0},{8,12},{12,8},{16,20},{20,16},{24,28},{28,24},{1,5},{5... | collective-permute-start | bytes 8650760 | tf_op jit(solution)/shard_map/ppermute | solution.py:731
  234.7 24.2 %collective-permute-start.17 = (bf16[320,2048]{1,0:T(8,128)(2,1)}, bf16[320,2048]{1,0:T(8,128)(2,1)}, u32[]{:S(2)}, u32[]{:S(2)}) collective-permute-start(bf16[320,2048]{1,0:T(8,128)(2,1)} %get-tuple-element.162.refs_0_), channel_id=1, source_target_pairs={{0,1},{1,0},{2,3},{3,2},{4,5},{5,4},{6,7},{7,6},{8,9},{9,8},{10,11... | collective-permute-start | bytes 3932168 | tf_op jit(solution)/shard_map/ppermute | solution.py:731
  234.7 31.5 %collective-permute-start.15 = (bf16[320,2048]{1,0:T(8,128)(2,1)}, bf16[320,2048]{1,0:T(8,128)(2,1)}, u32[]{:S(2)}, u32[]{:S(2)}) collective-permute-start(bf16[320,2048]{1,0:T(8,128)(2,1)} %get-tuple-element.162.refs_0_), channel_id=1, source_target_pairs={{0,2},{1,3},{2,0},{3,1},{4,6},{5,7},{6,4},{7,5},{8,10},{9,11},{10,... | collective-permute-start | bytes 3932168 | tf_op jit(solution)/shard_map/ppermute | solution.py:731
  238.8 56.5 %collective-permute-start.20 = (bf16[2,256,1408]{2,1,0:T(8,128)(2,1)}, bf16[2,256,1408]{2,1,0:T(8,128)(2,1)}, u32[]{:S(2)}, u32[]{:S(2)}) collective-permute-start(bf16[2,256,1408]{2,1,0:T(8,128)(2,1)} %get-tuple-element.170), channel_id=1, source_target_pairs={{0,8},{4,12},{8,0},{12,4},{16,24},{20,28},{24,16},{28,20},{1,9},{5... | collective-permute-start | bytes 4325384 | tf_op jit(solution)/shard_map/ppermute | solution.py:731
  263.7 12.7 %copy-start.2 = (bf16[4,256,1408]{2,1,0:T(8,128)(2,1)S(1)}, bf16[4,256,1408]{2,1,0:T(8,128)(2,1)}, u32[]{:S(2)}) copy-start(bf16[4,256,1408]{2,1,0:T(8,128)(2,1)} %weight_grad.12.own_away.own_kept) | copy-start | bytes 8650756
  266.2 14.7 %collective-permute-start.18 = (bf16[320,2048]{1,0:T(8,128)(2,1)}, bf16[320,2048]{1,0:T(8,128)(2,1)}, u32[]{:S(2)}, u32[]{:S(2)}) collective-permute-start(bf16[320,2048]{1,0:T(8,128)(2,1)} %collective-permute-done.15.refs_0_.refs_2_), channel_id=1, source_target_pairs={{0,1},{1,0},{2,3},{3,2},{4,5},{5,4},{6,7},{7,6},{8,9},{9,8},{10,11... | collective-permute-start | bytes 3932168 | tf_op jit(solution)/shard_map/ppermute | solution.py:731
  266.2 62.6 %collective-permute-start.21 = (bf16[320,2048]{1,0:T(8,128)(2,1)}, bf16[320,2048]{1,0:T(8,128)(2,1)}, u32[]{:S(2)}, u32[]{:S(2)}) collective-permute-start(bf16[320,2048]{1,0:T(8,128)(2,1)} %pair_sum.13), channel_id=1, source_target_pairs={{0,2},{1,3},{2,0},{3,1},{4,6},{5,7},{6,4},{7,5},{8,10},{9,11},{10,... | collective-permute-start | bytes 3932168 | tf_op jit(solution)/shard_map/ppermute | solution.py:731
  280.4 61.7 %collective-permute-start.23 = (bf16[2,256,1408]{2,1,0:T(8,128)(2,1)}, bf16[2,256,1408]{2,1,0:T(8,128)(2,1)}, u32[]{:S(2)}, u32[]{:S(2)}) collective-permute-start(bf16[2,256,1408]{2,1,0:T(8,128)(2,1)} %get-tuple-element.192), channel_id=1, source_target_pairs={{0,4},{4,0},{8,12},{12,8},{16,20},{20,16},{24,28},{28,24},{1,5},{5... | collective-permute-start | bytes 4325384 | tf_op jit(solution)/shard_map/ppermute | solution.py:731
  285.8 9.5 %copy-start.1 = (bf16[4,256,1408]{2,1,0:T(8,128)(2,1)S(1)}, bf16[4,256,1408]{2,1,0:T(8,128)(2,1)}, u32[]{:S(2)}) copy-start(bf16[4,256,1408]{2,1,0:T(8,128)(2,1)} %weight_grad.13.own_away.own_kept) | copy-start | bytes 8650756
  295.3 6.0 %copy-start.8 = (bf16[2,256,1408]{2,1,0:T(8,128)(2,1)S(1)}, bf16[2,256,1408]{2,1,0:T(8,128)(2,1)}, u32[]{:S(2)}) copy-start(bf16[2,256,1408]{2,1,0:T(8,128)(2,1)} %copy-done.7) | copy-start | bytes 4325380
  299.7 49.1 %collective-permute-start.22 = (bf16[2,256,1408]{2,1,0:T(8,128)(2,1)}, bf16[2,256,1408]{2,1,0:T(8,128)(2,1)S(1)}, u32[]{:S(2)}, u32[]{:S(2)}) collective-permute-start(bf16[2,256,1408]{2,1,0:T(8,128)(2,1)} %get-tuple-element.189), channel_id=1, source_target_pairs={{0,8},{4,12},{8,0},{12,4},{16,24},{20,28},{24,16},{28,20},{1,9},{5... | collective-permute-start | bytes 4325384 | tf_op jit(solution)/shard_map/ppermute | solution.py:731
  304.5 43.5 %collective-permute-start.24 = (bf16[1,256,1408]{2,1,0:T(8,128)(2,1)}, bf16[1,256,1408]{2,1,0:T(8,128)(2,1)}, u32[]{:S(2)}, u32[]{:S(2)}) collective-permute-start(bf16[1,256,1408]{2,1,0:T(8,128)(2,1)} %get-tuple-element.195), channel_id=1, source_target_pairs={{0,16},{4,20},{8,24},{12,28},{16,0},{20,4},{24,8},{28,12},{1,17},{... | collective-permute-start | bytes 2162696 | tf_op jit(solution)/shard_map/ppermute | solution.py:731
  328.8 20.0 %copy-start.4 = (bf16[2,256,1408]{2,1,0:T(8,128)(2,1)S(1)}, bf16[2,256,1408]{2,1,0:T(8,128)(2,1)}, u32[]{:S(2)}) copy-start(bf16[2,256,1408]{2,1,0:T(8,128)(2,1)} %copy-done.3) | copy-start | bytes 4325380
  339.1 46.8 %collective-permute-start.25 = (bf16[320,2048]{1,0:T(8,128)(2,1)}, bf16[320,2048]{1,0:T(8,128)(2,1)}, u32[]{:S(2)}, u32[]{:S(2)}) collective-permute-start(bf16[320,2048]{1,0:T(8,128)(2,1)} %pair_sum.14), channel_id=1, source_target_pairs={{0,2},{1,3},{2,0},{3,1},{4,6},{5,7},{6,4},{7,5},{8,10},{9,11},{10,... | collective-permute-start | bytes 3932168 | tf_op jit(solution)/shard_map/ppermute | solution.py:731
  340.6 47.8 %collective-permute-start.26 = (bf16[4,256,512]{2,1,0:T(8,128)(2,1)}, bf16[4,256,512]{2,1,0:T(8,128)(2,1)}, u32[]{:S(2)}, u32[]{:S(2)}) collective-permute-start(bf16[4,256,512]{2,1,0:T(8,128)(2,1)} %get-tuple-element.199), channel_id=1, source_target_pairs={{0,4},{4,0},{8,12},{12,8},{16,20},{20,16},{24,28},{28,24},{1,5},{5... | collective-permute-start | bytes 3145736 | tf_op jit(solution)/shard_map/ppermute | solution.py:731
  348.8 6.0 %copy-start.19 = (f32[320,2048]{1,0:T(8,128)S(1)}, f32[320,2048]{1,0:T(8,128)}, u32[]{:S(2)}) copy-start(f32[320,2048]{1,0:T(8,128)} %copy-done.17) | copy-start | bytes 7864324
  348.8 6.0 %copy-start.31 = (f32[320,2048]{1,0:T(8,128)S(1)}, f32[320,2048]{1,0:T(8,128)}, u32[]{:S(2)}) copy-start(f32[320,2048]{1,0:T(8,128)} %pair_sum.10) | copy-start | bytes 7864324
  352.2 5.7 %copy-start.6 = (bf16[2,256,1408]{2,1,0:T(8,128)(2,1)S(1)}, bf16[2,256,1408]{2,1,0:T(8,128)(2,1)}, u32[]{:S(2)}) copy-start(bf16[2,256,1408]{2,1,0:T(8,128)(2,1)} %copy-done.5) | copy-start | bytes 4325380
  352.2 36.2 %collective-permute-start.27 = (bf16[1,256,1408]{2,1,0:T(8,128)(2,1)}, bf16[1,256,1408]{2,1,0:T(8,128)(2,1)S(1)}, u32[]{:S(2)}, u32[]{:S(2)}) collective-permute-start(bf16[1,256,1408]{2,1,0:T(8,128)(2,1)} %get-tuple-element.202), channel_id=1, source_target_pairs={{0,16},{4,20},{8,24},{12,28},{16,0},{20,4},{24,8},{28,12},{1,17},{... | collective-permute-start | bytes 2162696 | tf_op jit(solution)/shard_map/ppermute | solution.py:731
  491.1 5.0 %copy-start.40 = (f32[512,256]{1,0:T(8,128)S(1)}, f32[512,256]{1,0:T(8,128)}, u32[]{:S(2)}) copy-start(f32[512,256]{1,0:T(8,128)} %get-tuple-element.268) | copy-start | bytes 1572868
  (29 other events, 66.5 us)

commit v9 on v7

--- a/solution.py
+++ b/solution.py
@@ -503,7 +503,8 @@
     return {axis: rank + bit - 2 * bit * (rank // bit % 2)}
 
 
-def last_body(ones, twos, threes, *refs):
+def last_body(flips, twos, threes, *refs):
+    ones = len(flips)
     mats = ones + twos + threes
     away, kept, refs = refs[:mats], refs[mats : 2 * mats], refs[2 * mats :]
     ready_ref, got_ref, gains_ref, refs = refs[0], refs[1], refs[2], refs[3:]
@@ -511,7 +512,7 @@
     own, first, refs = refs[:mats], refs[mats : 2 * mats], refs[2 * mats :]
     held, to_z, from_z, refs = refs[:threes], refs[threes : 2 * threes], refs[2 * threes : 3 * threes], refs[3 * threes :]
     late = twos + threes
-    to_last, from_last, total_s, refs = refs[:late], refs[late : 2 * late], refs[2 * late : 2 * late + twos], refs[2 * late + twos :]
+    to_last, from_last, refs = refs[:late], refs[late : 2 * late], refs[2 * late :]
     gain_in, gain_out, load_sem, send_sem, recv_sem = refs
     rank = lax.axis_index("dp")
     z1, z2 = rank // 2 % 2, rank // 4 % 2
@@ -556,7 +557,7 @@
     for m in range(ones, ones + twos):
         for c in (1, 0):
             stage[m, "z", c] = send(away[m].at[side(z2, c)], first[m].at[c], "dp", 2)
-    for m in range(ones):
+    for m in reversed(range(ones)):
         stage[m, "last"] = send(away[m], first[m], "dp", 4)
 
     def send_all(m):
@@ -592,54 +593,46 @@
         stage[m, "z", c].wait_recv()
         if m < ones + twos:
             total = wide(own[m][side(z2, c)]) + wide(first[m][c])
-            dst = total_s[m - ones]
         else:
             total = held[m - ones - twos][c] + wide(from_z[m - ones - twos][c])
-            dst = outs[m]
         if c:
             to_last[m - ones][...] = total.astype(jnp.bfloat16)
             stage[m, "last"] = send(to_last[m - ones], from_last[m - ones], "dp", 4)
         else:
-            dst[...] = total
+            outs[m][...] = total
 
     def finish(m):
         stage[m, "last"].wait_recv()
         if m < ones:
-            outs[m][...] = wide(own[m][0]) + wide(first[m][0])
-        elif m < ones + twos:
-            outs[m][...] = (total_s[m - ones][...] + wide(from_last[m - ones][...])).T
+            total = wide(own[m][0]) + wide(first[m][0])
+            outs[m][...] = total.T if flips[m] else total
         else:
             outs[m][...] += wide(from_last[m - ones][...])
 
     up, out, q, k, v = range(5)
-    from_near(out, 1)
-    from_x(q, 1, 1)
-    from_x(q, 1, 0)
-    from_near(out, 0)
-    from_x(q, 0, 1)
-    from_x(q, 0, 0)
     done_ref[...] = (wide(ready_ref[0]) + wide(got_ref[0])).T
+    from_near(q, 1)
     from_x(k, 1, 1)
-    from_near(q, 1)
     from_x(k, 1, 0)
     from_near(q, 0)
     from_x(k, 0, 1)
     from_x(k, 0, 0)
     gain_hop(2)
+    finish(out)
     from_x(v, 1, 1)
     from_near(k, 1)
     from_x(v, 1, 0)
     from_near(k, 0)
-    gain_hop(3)
-    finish(up)
     from_x(v, 0, 1)
     from_x(v, 0, 0)
-    finish(out)
+    finish(up)
+    gain_hop(3)
     from_near(v, 1)
     from_near(v, 0)
+    finish(q)
     gain_hop(4)
-    for m in (q, k, v):
-        finish(m)
+    finish(k)
+    finish(v)
     for copy in copies:
         copy.wait_send()
 
@@ -651,13 +644,12 @@
     low, wide = jnp.bfloat16, jnp.float32
     late, last = shapes[len(ones) + len(twos) :], shapes[len(ones) :]
     flat = [shape[1:] for shape in shapes]
-    for m in range(len(ones), len(ones) + len(twos)):
-        flat[m] = flat[m][::-1]
+    flat = [shape[::-1] if m < len(ones) and ones[m][2] else shape for m, shape in enumerate(flat)]
     any_space = pl.BlockSpec(memory_space=pl.ANY)
     inside = pl.BlockSpec(memory_space=pltpu.VMEM)
     count = len(ones) + 3 * len(twos) + 7 * len(threes) + 5
     result = pl.pallas_call(
-        functools.partial(last_body, len(ones), len(twos), len(threes)),
+        functools.partial(last_body, [m[2] for m in ones], len(twos), len(threes)),
         in_specs=[any_space] * (2 * len(mats)) + [inside] * 3,
         out_specs=[inside] * (len(mats) + 2),
         out_shape=[jax.ShapeDtypeStruct(shape, wide) for shape in flat]
@@ -669,7 +661,6 @@
         + [pltpu.VMEM((2,) + shape[1:], low) for shape in late]
         + [pltpu.VMEM(shape[1:], low) for shape in last]
         + [pltpu.VMEM(shape[1:], low) for shape in last]
-        + [pltpu.VMEM(shape[1:], wide) for shape in last[: len(twos)]]
         + [pltpu.VMEM((5,) + gains.shape, wide)] * 2
         + [pltpu.SemaphoreType.DMA((len(mats),)), pltpu.SemaphoreType.DMA((count,)), pltpu.SemaphoreType.DMA((count,))],
         compiler_params=pltpu.CompilerParams(vmem_limit_bytes=62 << 20, collective_id=8),
@@ -925,18 +916,22 @@
     dqf, dkf, dvf, got8, out_send = tie(dqf, dkf, dvf, got8, out_send)
 
     out_got = hop(out_send, 1)
+    grad_qkv = WeightGrad(dp_rank, (a0, a1, a2, a3), [(dqn, dqf), (dkn, dkf), (dvn, dvf)])
+    *sends, q_own, k_own, v_own = grad_qkv.compute(1, 0)
+    dqf, dkf, dvf, down_got, *sends = tie(dqf, dkf, dvf, down_got, *sends)
+    q_got = hop(sends[0], 1)
     y7 = pair_sum([(dqf, w_query, True), (dkf, w_key, True), (dvf, w_value, True)], 6, jnp.bfloat16)
     got = to_far(y7)
-    dqn, dkn, dvn, y7, up_got, gate_got, down_got = tie(dqn, dkn, dvn, y7, up_got, gate_got, down_got)
+    dqn, dkn, dvn, y7, up_got, gate_got, out_got = tie(dqn, dkn, dvn, y7, up_got, gate_got, out_got)
+    out = Halving(dp_rank, out_own)
+    out_got = hop(out.merge(out_got, 2), 2)
     gate_got = hop(gate.merge(gate_got, half), half)
     up_away = up.merge(up_got, half)
-    grad_qkv = WeightGrad(dp_rank, (a0, a1, a2, a3), [(dqn, dqf), (dkn, dkf), (dvn, dvf)])
-    *sends, q_own, k_own, v_own = grad_qkv.compute(1, 0)
     d_a = pair_sum([(dqn, w_query, True), (dkn, w_key, True), (dvn, w_value, True)], 7, jnp.float32) + got.astype(jnp.float32)
-    d_a, out_got, gate_got, up_away, *sends = tie(d_a, out_got, gate_got, up_away, *sends)
-
-    out = Halving(dp_rank, out_own)
-    out_away = out.merge(out_got, 2)
+    d_a, out_got, gate_got, q_got, up_away = tie(d_a, out_got, gate_got, q_got, up_away)
+
+    q = Halving(dp_rank, q_own)
+    q_away, out_away = q.merge(q_got, 2), out.merge(out_got, half)
     output = (mid_h + mine8 + got8.astype(jnp.float32)).astype(jnp.bfloat16)
     n_a = x_f * inv_a
     gain_attn_part = jnp.sum(d_a * n_a, axis=0)
@@ -946,9 +941,9 @@
     sum_gate = gate.finish(gate_got)
     if grad_qkv.kernel and half == 4:
         (sum_up, sum_out, *sums), sum_down, gains = last_stages(
-            [(up_away, up.kept)],
-            [(out_away, out.kept)],
-            list(zip(sends, (q_own, k_own, v_own))),
+            [(up_away, up.kept, False), (out_away, out.kept, True)],
+            [(q_away, q.kept)],
+            [(sends[1], k_own), (sends[2], v_own)],
             (down.kept, down_got),
             gains,
         )
@@ -956,9 +951,10 @@
     else:
         gains = butterfly_sum(scatter_small(gains.reshape(2, lax.axis_size("dp"), -1), "dp"), "tensor")
         sum_up = up.finish(hop(up_away, half))
-        sum_out = out.finish(hop(out_away, 2)).T
+        sum_out = out.finish(hop(out_away, half)).T
         sum_down = down.finish(down_got).T
-        sums = [Halving(dp_rank, own).finish(hop(send, 1)) for send, own in zip(sends, (q_own, k_own, v_own))]
+        sums = [q.finish(hop(q_away, 2))]
+        sums += [Halving(dp_rank, own).finish(hop(send, 1)) for send, own in zip(sends[1:], (k_own, v_own))]
     return (
         output,
         grad_input,

time: 504 us -> 508 us (level)
  waiting for transfers between devices: 29.3 us -> 37.9 us
  Pallas kernels: 377 us -> 370 us
    ppermute x28 -> x30, waiting for transfers between devices: 29.3 us -> 37.9 us  [exchange(): lax.ppermute(values, axis, [(rank, rank ^ bit) for rank in range(size)])]
    pallas_call x1, Pallas kernels: 92 us -> 83.7 us  [last_stages(): pl.pallas_call(functools.partial(last_body, [m[2] for m in ones], len(two...]
    ppermute x28 -> x30, starting transfers between devices: 36.3 us -> 37.9 us  [exchange(): lax.ppermute(values, axis, [(rank, rank ^ bit) for rank in range(size)])]
    pallas_call x7 -> x9, Pallas kernels: 14.4 us -> 15.1 us  [merge_call(): pl.pallas_call(merge_body, grid_spec=pltpu.PrefetchScalarGridSpec(num_sca...]
    unnamed x104 -> x108, local copies, waits for them, and re-layouts: 19.6 us -> 18.8 us
  transfers between devices with their start and end apart: 28 -> 30, of which waited for: 12 -> 14; matrix products, arithmetic and copies ran while one was open for 4% -> 4% of each run, Pallas kernels for 52% -> 52%
where the time goes in v9:
time: 508 us; the launch traced here: 502 us
  Pallas kernels  370 us (73%)
  starting transfers between devices  37.9 us (7%)
  waiting for transfers between devices  37.9 us (7%)
  other arithmetic  34.1 us (7%)
  local copies, waits for them, and re-layouts  20.9 us (4%)
    pallas_call x8, Pallas kernels, pair_sum(): pl.pallas_call(functools.partial(pair_body, [(len(left), dims) for left,...  83.9 us
    pallas_call x1, Pallas kernels, last_stages(): pl.pallas_call(functools.partial(last_body, [m[2] for m in ones], len(two...  83.7 us
    pallas_call x8, Pallas kernels, grad_call(): pl.pallas_call(functools.partial(grad_body, len(pieces), widths, low, sid...  77 us
    ppermute x30, waiting for transfers between devices, exchange(): lax.ppermute(values, axis, [(rank, rank ^ bit) for rank in range(size)])  37.9 us
    ppermute x30, starting transfers between devices, exchange(): lax.ppermute(values, axis, [(rank, rank ^ bit) for rank in range(size)])  37.9 us
    pallas_call x2, Pallas kernels, mlp_pair(): pl.pallas_call(mlp_body, grid=(pl.cdiv(width, tile),), in_specs=[whole(xa...  29.5 us
    pallas_call x4, Pallas kernels, project(): pl.pallas_call(functools.partial(project_body, [(len(left), dims) for lef...  26.4 us
    pallas_call x1, Pallas kernels, attend_back(): pl.pallas_call(attend_back_body, grid_spec=pltpu.PrefetchScalarGridSpec(n...  21.6 us
  transfers between devices with their start and end apart: 30, of which 14 were waited for; matrix products, arithmetic and copies ran while one was open for 4% of the time, Pallas kernels for 52%

profile of v9, /device:TPU:0, one launch (start us, length us, event | category | flops | bytes accessed | tf_op | source)
XLA Modules:
  0.0 502.2 jit_solution(16028110947975616834)
XLA Ops:
  4.6 2.6 collective-permute-start
  9.6 2.4 fusion.13
  18.1 2.6 collective-permute-start.3
  25.4 9.4 %qkv.2 = (bf16[640,512]{1,0:T(8,128)(2,1)}, bf16[640,512]{1,0:T(8,128)(2,1)}, bf16[640,512]{1,0:T(8,128)(2,1)}) custom-call(s32[1]{0:T(128)} %bitcast.rank_ref, bf16[320,2048]{1,0:T(8,128)(2,1)} %copy-done.33, bf16[320,2048]{1,0:T(8,128)(2,1)} %copy-done.36, f32[1280,128]{1,0:T(8,128)} %pad_maximum_fusion.cos_ref, f32[1280,128]{1,0:T(8,128)} %get-tuple-element.263.sin_ref, ...), custom_call_target="tpu_custom_call" | custom-call | flops 4026531 | bytes 8912 | tf_op jit(solution)/shard_map/qkv/pallas_call | solution.py:67
  40.1 8.8 %qkv.3 = (bf16[640,512]{1,0:T(8,128)(2,1)}, bf16[640,512]{1,0:T(8,128)(2,1)}, bf16[640,512]{1,0:T(8,128)(2,1)}) custom-call(s32[1]{0:T(128)} %bitcast.rank_ref, bf16[320,2048]{1,0:T(8,128)(2,1)} %collective-permute-done.xa_ref.refs_2_, bf16[320,2048]{1,0:T(8,128)(2,1)} %collective-permute-done.5.xb_ref.refs_3_, f32[1280,128]{1,0:T(8,128)} %pad_maximum_fusion.cos_ref, ...), custom_call_target="tpu_custom_call" | custom-call | flops 4026531 | bytes 8912 | tf_op jit(solution)/shard_map/qkv/pallas_call | solution.py:67
  48.9 14.6 %attend.1 = (bf16[640,512]{1,0:T(8,128)(2,1)}, bf16[640,512]{1,0:T(8,128)(2,1)}, f32[4,1,1280]{2,1,0:T(1,128)}) custom-call(s32[1]{0:T(128)} %bitcast.rank_ref, bf16[640,512]{1,0:T(8,128)(2,1)} %get-tuple-element.134.qn, bf16[640,512]{1,0:T(8,128)(2,1)} %get-tuple-element.136.qf, bf16[640,512]{1,0:T(8,128)(2,1)} %get-tuple-element.137.kn, ...), custom_call_target="tpu_custom_call" | custom-call | flops 6710886 | bytes 5242 | tf_op jit(solution)/shard_map/attend/pallas_call | solution.py:128
  63.5 6.9 %pair_sum.8 = bf16[320,2048]{1,0:T(8,128)(2,1)} custom-call(bf16[640,512]{1,0:T(8,128)(2,1)} %get-tuple-element.143.refs_0_.refs_5_, bf16[512,2048]{1,0:T(8,128)(2,1)} %refs_2_.7), custom_call_target="tpu_custom_call" | custom-call | flops 1342177 | bytes 5373 | tf_op jit(solution)/shard_map/pair_sum/pallas_call | solution.py:478
  72.4 7.4 %pair_sum.9 = f32[320,2048]{1,0:T(8,128)} custom-call(bf16[640,512]{1,0:T(8,128)(2,1)} %get-tuple-element.147.refs_0_.refs_4_, bf16[512,2048]{1,0:T(8,128)(2,1)} %refs_2_.7), custom_call_target="tpu_custom_call" | custom-call | flops 1342177 | bytes 5373 | tf_op jit(solution)/shard_map/pair_sum/pallas_call | solution.py:478
  79.8 8.4 %project.4.dm_ref = f32[640,1408]{1,0:T(8,128)} custom-call(bf16[320,2048]{1,0:T(8,128)(2,1)} %copy-done.30, bf16[320,2048]{1,0:T(8,128)(2,1)} %copy-done.32, bf16[1408,2048]{1,0:T(8,128)(2,1)} %refs_1_.13), custom_call_target="tpu_custom_call" | custom-call | flops 3690987 | bytes 10190 | tf_op jit(solution)/shard_map/project/pallas_call | solution.py:414
  88.2 8.5 %project.5.dm_ref = f32[640,1408]{1,0:T(8,128)} custom-call(bf16[320,2048]{1,0:T(8,128)(2,1)} %copy-done.31, bf16[320,2048]{1,0:T(8,128)(2,1)} %collective-permute-done.9.refs_1_.refs_3_, bf16[1408,2048]{1,0:T(8,128)(2,1)} %refs_1_.13), custom_call_target="tpu_custom_call" | custom-call | flops 3690987 | bytes 10190 | tf_op jit(solution)/shard_map/project/pallas_call | solution.py:414
  96.7 5.4 %collective-permute-done.8 = bf16[320,2048]{1,0:T(8,128)(2,1)} collective-permute-done((bf16[320,2048]{1,0:T(8,128)(2,1)}, bf16[320,2048]{1,0:T(8,128)(2,1)}, u32[]{:S(2)}, u32[]{:S(2)}) %collective-permute-start.8) | collective-permute-done | bytes 1310752 | tf_op jit(solution)/shard_map/ppermute | solution.py:706
  109.9 14.8 %mlp.2 = (bf16[640,1408]{1,0:T(8,128)(2,1)}, bf16[640,1408]{1,0:T(8,128)(2,1)}, bf16[640,1408]{1,0:T(8,128)(2,1)}) custom-call(bf16[320,2048]{1,0:T(8,128)(2,1)} %copy-done.23, bf16[320,2048]{1,0:T(8,128)(2,1)} %copy-done.24, f32[640,1408]{1,0:T(8,128)} %project.4.dm_ref, bf16[2048,1408]{1,0:T(8,128)(2,1)} %refs_1_.12, bf16[2048,1408]{1,0:T(8,128)(2,1)} %refs_3_.5), custom_call_target="tpu_custom_call" | custom-call | flops 7381975 | bytes 23166 | tf_op jit(solution)/shard_map/mlp/pallas_call | solution.py:234
  124.7 10.0 %pair_sum.10 = f32[320,2048]{1,0:T(8,128)} custom-call(bf16[640,1408]{1,0:T(8,128)(2,1)} %get-tuple-element.169.refs_0_.refs_4_, bf16[1408,2048]{1,0:T(8,128)(2,1)} %refs_1_.13), custom_call_target="tpu_custom_call" | custom-call | flops 3690987 | bytes 10190 | tf_op jit(solution)/shard_map/pair_sum/pallas_call | solution.py:478
  134.7 2.3 collective-permute-done.10.xa_ref.refs_2_
  137.0 3.0 collective-permute-done.12.xb_ref.refs_3_
  141.1 14.7 %mlp.3 = (bf16[640,1408]{1,0:T(8,128)(2,1)}, bf16[640,1408]{1,0:T(8,128)(2,1)}, bf16[640,1408]{1,0:T(8,128)(2,1)}) custom-call(bf16[320,2048]{1,0:T(8,128)(2,1)} %copy-done.25, bf16[320,2048]{1,0:T(8,128)(2,1)} %copy-done.26, f32[640,1408]{1,0:T(8,128)} %project.5.dm_ref, bf16[2048,1408]{1,0:T(8,128)(2,1)} %refs_1_.12, bf16[2048,1408]{1,0:T(8,128)(2,1)} %refs_3_.5), custom_call_target="tpu_custom_call" | custom-call | flops 7381975 | bytes 23166 | tf_op jit(solution)/shard_map/mlp/pallas_call | solution.py:234
  155.8 8.7 %weight_grad.8 = bf16[4,256,1408]{2,1,0:T(8,128)(2,1)} custom-call(s32[1]{0:T(128)} %bitcast.7.rank_ref._, bf16[320,2048]{1,0:T(8,128)(2,1)} %copy-done.30, bf16[320,2048]{1,0:T(8,128)(2,1)} %copy-done.32, bf16[320,2048]{1,0:T(8,128)(2,1)} %copy-done.31, bf16[320,2048]{1,0:T(8,128)(2,1)} %collective-permute-done.9.refs_1_.refs_3_, ...), custom_call_target="tpu_custom_call" | custom-call | flops 3690987 | bytes 9109 | tf_op jit(solution)/shard_map/weight_grad/pallas_call | solution.py:324
  166.2 14.3 %pair_sum.11 = bf16[320,2048]{1,0:T(8,128)(2,1)} custom-call(bf16[640,1408]{1,0:T(8,128)(2,1)} %get-tuple-element.163.refs_0_.refs_5_, bf16[2048,1408]{1,0:T(8,128)(2,1)} %refs_1_.12, bf16[640,1408]{1,0:T(8,128)(2,1)} %get-tuple-element.164.refs_2_.refs_5_, bf16[2048,1408]{1,0:T(8,128)(2,1)} %refs_3_.5), custom_call_target="tpu_custom_call" | custom-call | flops 7381975 | bytes 17760 | tf_op jit(solution)/shard_map/pair_sum/pallas_call | solution.py:478
  182.0 8.7 %weight_grad.11 = bf16[4,256,1408]{2,1,0:T(8,128)(2,1)} custom-call(s32[1]{0:T(128)} %bitcast.7.rank_ref._, bf16[320,2048]{1,0:T(8,128)(2,1)} %copy-done.23, bf16[320,2048]{1,0:T(8,128)(2,1)} %copy-done.24, bf16[320,2048]{1,0:T(8,128)(2,1)} %copy-done.25, bf16[320,2048]{1,0:T(8,128)(2,1)} %copy-done.26, ...), custom_call_target="tpu_custom_call" | custom-call | flops 3690987 | bytes 9109 | tf_op jit(solution)/shard_map/weight_grad/pallas_call | solution.py:324
  192.3 8.7 %weight_grad.10.own_away.own_kept = bf16[4,256,1408]{2,1,0:T(8,128)(2,1)} custom-call(s32[1]{0:T(128)} %bitcast.7.rank_ref._, bf16[320,2048]{1,0:T(8,128)(2,1)} %copy-done.30, bf16[320,2048]{1,0:T(8,128)(2,1)} %copy-done.32, bf16[320,2048]{1,0:T(8,128)(2,1)} %copy-done.31, bf16[320,2048]{1,0:T(8,128)(2,1)} %collective-permute-done.9.refs_1_.refs_3_, ...), custom_call_target="tpu_custom_call" | custom-call | flops 3690987 | bytes 9109 | tf_op jit(solution)/shard_map/weight_grad/pallas_call | solution.py:324
  201.0 8.7 %weight_grad.9 = bf16[4,256,1408]{2,1,0:T(8,128)(2,1)} custom-call(s32[1]{0:T(128)} %bitcast.7.rank_ref._, bf16[320,2048]{1,0:T(8,128)(2,1)} %copy-done.23, bf16[320,2048]{1,0:T(8,128)(2,1)} %copy-done.24, bf16[320,2048]{1,0:T(8,128)(2,1)} %copy-done.25, bf16[320,2048]{1,0:T(8,128)(2,1)} %copy-done.26, bf16[640,1408]{1,0:T(8,128)(2,1)} %get-tuple-element.180.refs_2_.refs_4_, ...), custom_call_target="tpu_custom_call" | custom-call | flops 3690987 | bytes 9109 | tf_op jit(solution)/shard_map/weight_grad/pallas_call | solution.py:324
  209.8 14.9 %pair_sum.12 = f32[320,2048]{1,0:T(8,128)} custom-call(bf16[640,1408]{1,0:T(8,128)(2,1)} %get-tuple-element.173.refs_0_.refs_4_, bf16[2048,1408]{1,0:T(8,128)(2,1)} %refs_1_.12, bf16[640,1408]{1,0:T(8,128)(2,1)} %get-tuple-element.180.refs_2_.refs_4_, bf16[2048,1408]{1,0:T(8,128)(2,1)} %refs_3_.5), custom_call_target="tpu_custom_call" | custom-call | flops 7381975 | bytes 17760 | tf_op jit(solution)/shard_map/pair_sum/pallas_call | solution.py:478
  224.7 2.6 convert_add_fusion.2
  231.7 2.8 fusion.16
  240.2 9.5 %pair_sum.13 = bf16[320,2048]{1,0:T(8,128)(2,1)} custom-call(bf16[640,1408]{1,0:T(8,128)(2,1)} %get-tuple-element.172.refs_5_.refs_0_, bf16[1408,2048]{1,0:T(8,128)(2,1)} %refs_1_.13), custom_call_target="tpu_custom_call" | custom-call | flops 3690987 | bytes 10190 | tf_op jit(solution)/shard_map/pair_sum/pallas_call | solution.py:478
  249.7 8.8 %weight_grad.12.own_away.own_kept = bf16[4,256,1408]{2,1,0:T(8,128)(2,1)} custom-call(s32[1]{0:T(128)} %bitcast.7.rank_ref._, bf16[320,2048]{1,0:T(8,128)(2,1)} %copy-done.23, bf16[320,2048]{1,0:T(8,128)(2,1)} %copy-done.24, bf16[320,2048]{1,0:T(8,128)(2,1)} %copy-done.25, bf16[320,2048]{1,0:T(8,128)(2,1)} %copy-done.26, ...), custom_call_target="tpu_custom_call" | custom-call | flops 3690987 | bytes 9109 | tf_op jit(solution)/shard_map/weight_grad/pallas_call | solution.py:324
  258.5 4.8 project.6.gn
  263.3 2.8 collective-permute-done.15.refs_0_.refs_2_
  267.6 8.7 %weight_grad.13.own_away.own_kept = bf16[4,256,1408]{2,1,0:T(8,128)(2,1)} custom-call(s32[1]{0:T(128)} %bitcast.7.rank_ref._, bf16[320,2048]{1,0:T(8,128)(2,1)} %copy-done.23, bf16[320,2048]{1,0:T(8,128)(2,1)} %copy-done.24, bf16[320,2048]{1,0:T(8,128)(2,1)} %copy-done.25, bf16[320,2048]{1,0:T(8,128)(2,1)} %copy-done.26, ...), custom_call_target="tpu_custom_call" | custom-call | flops 3690987 | bytes 9109 | tf_op jit(solution)/shard_map/weight_grad/pallas_call | solution.py:324
  276.3 2.8 merge.12
  280.9 4.8 project.7.gf
  285.7 9.4 %weight_grad.14 = (bf16[4,256,512]{2,1,0:T(8,128)(2,1)}, bf16[4,256,512]{2,1,0:T(8,128)(2,1)}) custom-call(s32[1]{0:T(128)} %bitcast.7.rank_ref._, bf16[320,2048]{1,0:T(8,128)(2,1)} %get-tuple-element.171.refs_0_, bf16[320,2048]{1,0:T(8,128)(2,1)} %collective-permute-done.17.refs_1_, bf16[320,2048]{1,0:T(8,128)(2,1)} %collective-permute-done.15.refs_0_.refs_2_, ...), custom_call_target="tpu_custom_call" | custom-call | flops 2684354 | bytes 8650 | tf_op jit(solution)/shard_map/weight_grad/pallas_call | solution.py:324
  295.1 3.3 merge.11
  303.7 2.6 collective-permute-start.22
  306.2 21.6 %attend_back.1 = (bf16[640,512]{1,0:T(8,128)(2,1)}, bf16[640,512]{1,0:T(8,128)(2,1)}, bf16[640,512]{1,0:T(8,128)(2,1)}, bf16[640,512]{1,0:T(8,128)(2,1)}, bf16[6...) custom-call(s32[1]{0:T(128)} %bitcast.rank_ref, bf16[640,512]{1,0:T(8,128)(2,1)} %get-tuple-element.134.qn, ...), custom_call_target="tpu_custom_call" | custom-call | flops 16777216 | bytes 10485 | tf_op jit(solution)/shard_map/attend_back/pallas_call | solution.py:191
  329.4 15.3 %weight_grad.15 = (bf16[4,256,512]{2,1,0:T(8,128)(2,1)}, bf16[4,256,512]{2,1,0:T(8,128)(2,1)}, bf16[4,256,512]{2,1,0:T(8,128)(2,1)}, bf16[4,256,512]{2,1,0:T(8,1...) custom-call(s32[1]{0:T(128)} %bitcast.7.rank_ref._, bf16[320,2048]{1,0:T(8,128)(2,1)} %copy-done.33, ...), custom_call_target="tpu_custom_call" | custom-call | flops 8053063 | bytes 15466 | tf_op jit(solution)/shard_map/weight_grad/pallas_call | solution.py:324
  344.7 3.0 collective-permute-done.22.refs_11_
  348.6 10.1 %pair_sum.14 = bf16[320,2048]{1,0:T(8,128)(2,1)} custom-call(bf16[640,512]{1,0:T(8,128)(2,1)} %get-tuple-element.202.refs_5_.refs_0_, bf16[2048,512]{1,0:T(8,128)(2,1)} %refs_1_.15, bf16[640,512]{1,0:T(8,128)(2,1)} %get-tuple-element.203.refs_7_.refs_2_, bf16[2048,512]{1,0:T(8,128)(2,1)} %refs_3_.7, bf16[640,512]{1,0:T(8,128)(2,1)} %get-tuple-element.204.refs_9_.refs_4_, ...), custom_call_target="tpu_custom_call" | custom-call | flops 4026531 | bytes 10878 | tf_op jit(solution)/shard_map/pair_sum/pallas_call | solution.py:478
  360.8 2.6 merge.14
  364.3 3.4 collective-permute-start.28
  367.6 3.1 add_convert_fusion
  373.7 10.8 %pair_sum.15 = f32[320,2048]{1,0:T(8,128)} custom-call(bf16[640,512]{1,0:T(8,128)(2,1)} %get-tuple-element.212.refs_4_.refs_0_, bf16[2048,512]{1,0:T(8,128)(2,1)} %refs_1_.15, bf16[640,512]{1,0:T(8,128)(2,1)} %get-tuple-element.213.refs_6_.refs_2_, bf16[2048,512]{1,0:T(8,128)(2,1)} %refs_3_.7, bf16[640,512]{1,0:T(8,128)(2,1)} %get-tuple-element.214.refs_8_.refs_4_, ...), custom_call_target="tpu_custom_call" | custom-call | flops 4026531 | bytes 10878 | tf_op jit(solution)/shard_map/pair_sum/pallas_call | solution.py:478
  384.6 5.3 %collective-permute-done.26 = bf16[320,2048]{1,0:T(8,128)(2,1)} collective-permute-done((bf16[320,2048]{1,0:T(8,128)(2,1)}, bf16[320,2048]{1,0:T(8,128)(2,1)}, u32[]{:S(2)}, u32[]{:S(2)}) %collective-permute-start.26) | collective-permute-done | bytes 1310752 | tf_op jit(solution)/shard_map/ppermute | solution.py:706
  389.9 2.5 convert_add_fusion.1
  394.3 5.0 collective-permute-done.28
  404.1 83.7 %last_stages.1 = (f32[256,1408]{1,0:T(8,128)}, f32[512,256]{1,0:T(8,128)}, f32[256,512]{1,0:T(8,128)}, f32[256,512]{1,0:T(8,128)}, f32[256,512]{1,0:T(8,128)}, /*index=5*/f32[1408,256]{1,0:T(8,128)}, f32[2,2048]{1,0:T(2,128)}) custom-call(bf16[1,256,1408]{2,1,0:T(8,128)(2,1)} %copy-done.14, bf16[1,256,512]{2,1,0:T(8,128)(2,1)} %copy-done.18, ...), custom_call_target="tpu_custom_call" | custom-call | flops 16777 | bytes 33554 | tf_op jit(solution)/shard_map/last_stages/pallas_call | solution.py:651
  487.8 4.8 fusion.8
  492.7 2.5 add_bitcast_fusion
  (198 shorter events, 78.4 us)
Async XLA Ops:
  0.7 6.9 %copy-start.48 = (s32[1,1280]{1,0:T(1,128)S(1)}, s32[1,1280]{1,0:T(1,128)}, u32[]{:S(2)}) copy-start(s32[1,1280]{1,0:T(1,128)} %param.27) | copy-start | bytes 15364
  0.7 7.1 %copy-start.49 = (s32[1,3]{1,0:T(1,128)S(1)}, s32[1,3]{1,0:T(1,128)}, u32[]{:S(2)}) copy-start(s32[1,3]{1,0:T(1,128)} %param.26) | copy-start | bytes 40
  4.1 10.4 %copy-start.33 = (bf16[320,2048]{1,0:T(8,128)(2,1)}, bf16[320,2048]{1,0:T(8,128)(2,1)S(1)}, u32[]{:S(2)}) copy-start(bf16[320,2048]{1,0:T(8,128)(2,1)S(1)} %fusion.4.xa_ref.refs_0_) | copy-start | bytes 3932164
  4.1 20.3 %collective-permute-start.4 = (bf16[320,2048]{1,0:T(8,128)(2,1)S(1)}, bf16[320,2048]{1,0:T(8,128)(2,1)S(1)}, u32[]{:S(2)}, u32[]{:S(2)}) collective-permute-start(bf16[320,2048]{1,0:T(8,128)(2,1)S(1)} %fusion.4.xa_ref.refs_0_), channel_id=1, source_target_pairs={{0,1},{1,0},{2,3},{3,2},{4,5},{5,4},{6,7},{7,6},{8,9},{9,8},{10,11... | collective-permute-start | bytes 3932168 | tf_op jit(solution)/shard_map/ppermute | solution.py:706
  4.6 32.1 %collective-permute-start = (bf16[320,2048]{1,0:T(8,128)(2,1)S(1)}, bf16[320,2048]{1,0:T(8,128)(2,1)}, u32[]{:S(2)}, u32[]{:S(2)}) collective-permute-start(bf16[320,2048]{1,0:T(8,128)(2,1)S(1)} %fusion.4.xa_ref.refs_0_), channel_id=1, source_target_pairs={{0,2},{1,3},{2,0},{3,1},{4,6},{5,7},{6,4},{7,5},{8,10},{9,11},{10,... | collective-permute-start | bytes 3932168 | tf_op jit(solution)/shard_map/ppermute | solution.py:706
  8.0 6.5 %collective-permute-start.1 = (f32[8]{0:T(128)S(1)}, f32[8]{0:T(128)S(1)}, u32[]{:S(2)}, u32[]{:S(2)}) collective-permute-start(f32[8]{0:T(128)S(1)} %select_reduce_fusion.1), channel_id=1, source_target_pairs={{0,4},{4,0},{8,12},{12,8},{16,20},{20,16},{24,28},{28,24},{1,5},{5... | collective-permute-start | bytes 104 | tf_op jit(solution)/shard_map/ppermute | solution.py:706
  9.6 14.5 %copy-start.37 = (bf16[320,2048]{1,0:T(8,128)(2,1)S(1)}, bf16[320,2048]{1,0:T(8,128)(2,1)}, u32[]{:S(2)}) copy-start(bf16[320,2048]{1,0:T(8,128)(2,1)} %param.15) | copy-start | bytes 3932164
  14.5 3.6 collective-permute-start.2
  18.1 4.5 collective-permute-start.3
  24.3 14.1 %copy-start.30 = (bf16[320,2048]{1,0:T(8,128)(2,1)}, bf16[320,2048]{1,0:T(8,128)(2,1)S(1)}, u32[]{:S(2)}) copy-start(bf16[320,2048]{1,0:T(8,128)(2,1)S(1)} %fusion.12.refs_0_) | copy-start | bytes 3932164
  36.7 3.4 collective-permute-start.5
  36.7 33.7 %collective-permute-start.7 = (bf16[320,2048]{1,0:T(8,128)(2,1)S(1)}, bf16[320,2048]{1,0:T(8,128)(2,1)S(1)}, u32[]{:S(2)}, u32[]{:S(2)}) collective-permute-start(bf16[320,2048]{1,0:T(8,128)(2,1)S(1)} %fusion.12.refs_0_), channel_id=1, source_target_pairs={{0,2},{1,3},{2,0},{3,1},{4,6},{5,7},{6,4},{7,5},{8,10},{9,11},{10,... | collective-permute-start | bytes 3932168 | tf_op jit(solution)/shard_map/ppermute | solution.py:706
  38.4 32.0 %collective-permute-start.6 = (bf16[320,2048]{1,0:T(8,128)(2,1)S(1)}, bf16[320,2048]{1,0:T(8,128)(2,1)S(1)}, u32[]{:S(2)}, u32[]{:S(2)}) collective-permute-start(bf16[320,2048]{1,0:T(8,128)(2,1)S(1)} %fusion.12.refs_0_), channel_id=1, source_target_pairs={{0,1},{1,0},{2,3},{3,2},{4,5},{5,4},{6,7},{7,6},{8,9},{9,8},{10,11... | collective-permute-start | bytes 3932168 | tf_op jit(solution)/shard_map/ppermute | solution.py:706
  70.4 9.4 %copy-start.31 = (bf16[320,2048]{1,0:T(8,128)(2,1)}, bf16[320,2048]{1,0:T(8,128)(2,1)S(1)}, u32[]{:S(2)}) copy-start(bf16[320,2048]{1,0:T(8,128)(2,1)S(1)} %collective-permute-done.7.refs_0_.refs_2_) | copy-start | bytes 3932164
  70.4 9.3 %copy-start.32 = (bf16[320,2048]{1,0:T(8,128)(2,1)}, bf16[320,2048]{1,0:T(8,128)(2,1)S(1)}, u32[]{:S(2)}) copy-start(bf16[320,2048]{1,0:T(8,128)(2,1)S(1)} %collective-permute-done.6.refs_1_) | copy-start | bytes 3932164
  70.4 17.7 %collective-permute-start.9 = (bf16[320,2048]{1,0:T(8,128)(2,1)S(1)}, bf16[320,2048]{1,0:T(8,128)(2,1)}, u32[]{:S(2)}, u32[]{:S(2)}) collective-permute-start(bf16[320,2048]{1,0:T(8,128)(2,1)S(1)} %collective-permute-done.7.refs_0_.refs_2_), channel_id=1, source_target_pairs={{0,1},{1,0},{2,3},{3,2},{4,5},{5,4},{6,7},{7,6},{8,9},{9,8},{10,11... | collective-permute-start | bytes 3932168 | tf_op jit(solution)/shard_map/ppermute | solution.py:706
  70.6 31.4 %collective-permute-start.8 = (bf16[320,2048]{1,0:T(8,128)(2,1)}, bf16[320,2048]{1,0:T(8,128)(2,1)}, u32[]{:S(2)}, u32[]{:S(2)}) collective-permute-start(bf16[320,2048]{1,0:T(8,128)(2,1)} %pair_sum.8), channel_id=1, source_target_pairs={{0,2},{1,3},{2,0},{3,1},{4,6},{5,7},{6,4},{7,5},{8,10},{9,11},{10,... | collective-permute-start | bytes 3932168 | tf_op jit(solution)/shard_map/ppermute | solution.py:706
  88.2 13.8 %copy-start.27 = (bf16[320,2048]{1,0:T(8,128)(2,1)S(1)}, bf16[320,2048]{1,0:T(8,128)(2,1)}, u32[]{:S(2)}) copy-start(bf16[320,2048]{1,0:T(8,128)(2,1)} %param.14) | copy-start | bytes 3932164
  88.2 13.8 %copy-start.35 = (f32[320,2048]{1,0:T(8,128)S(1)}, f32[320,2048]{1,0:T(8,128)}, u32[]{:S(2)}) copy-start(f32[320,2048]{1,0:T(8,128)} %pair_sum.9) | copy-start | bytes 7864324
  96.7 8.8 %copy-start.46 = (f32[2048]{0:T(1024)S(1)}, f32[2048]{0:T(1024)}, u32[]{:S(2)}) copy-start(f32[2048]{0:T(1024)} %param.21) | copy-start | bytes 24580
  105.7 3.1 collective-permute-start.11
  105.8 31.2 %collective-permute-start.10 = (bf16[320,2048]{1,0:T(8,128)(2,1)S(1)}, bf16[320,2048]{1,0:T(8,128)(2,1)S(1)}, u32[]{:S(2)}, u32[]{:S(2)}) collective-permute-start(bf16[320,2048]{1,0:T(8,128)(2,1)S(1)} %multiply_convert_fusion.xa_ref.refs_0_), channel_id=1, source_target_pairs={{0,2},{1,3},{2,0},{3,1},{4,6},{5,7},{6,4},{7,5},{8,10},{9,11},{10,... | collective-permute-start | bytes 3932168 | tf_op jit(solution)/shard_map/ppermute | solution.py:706
  137.0 3.0 collective-permute-start.12
  164.5 64.7 %collective-permute-start.14 = (bf16[4,256,1408]{2,1,0:T(8,128)(2,1)}, bf16[4,256,1408]{2,1,0:T(8,128)(2,1)S(1)}, u32[]{:S(2)}, u32[]{:S(2)}) collective-permute-start(bf16[4,256,1408]{2,1,0:T(8,128)(2,1)} %weight_grad.8), channel_id=1, source_target_pairs={{0,4},{4,0},{8,12},{12,8},{16,20},{20,16},{24,28},{28,24},{1,5},{5... | collective-permute-start | bytes 8650760 | tf_op jit(solution)/shard_map/ppermute | solution.py:706
  180.5 44.2 %collective-permute-start.13 = (bf16[320,2048]{1,0:T(8,128)(2,1)}, bf16[320,2048]{1,0:T(8,128)(2,1)}, u32[]{:S(2)}, u32[]{:S(2)}) collective-permute-start(bf16[320,2048]{1,0:T(8,128)(2,1)} %pair_sum.11), channel_id=1, source_target_pairs={{0,2},{1,3},{2,0},{3,1},{4,6},{5,7},{6,4},{7,5},{8,10},{9,11},{10,... | collective-permute-start | bytes 3932168 | tf_op jit(solution)/shard_map/ppermute | solution.py:706
  190.8 72.5 %collective-permute-start.16 = (bf16[4,256,1408]{2,1,0:T(8,128)(2,1)}, bf16[4,256,1408]{2,1,0:T(8,128)(2,1)}, u32[]{:S(2)}, u32[]{:S(2)}) collective-permute-start(bf16[4,256,1408]{2,1,0:T(8,128)(2,1)} %weight_grad.11), channel_id=1, source_target_pairs={{0,8},{4,12},{8,0},{12,4},{16,24},{20,28},{24,16},{28,20},{1,9},{5... | collective-permute-start | bytes 8650760 | tf_op jit(solution)/shard_map/ppermute | solution.py:706
  229.2 65.9 %collective-permute-start.19 = (bf16[4,256,1408]{2,1,0:T(8,128)(2,1)}, bf16[4,256,1408]{2,1,0:T(8,128)(2,1)}, u32[]{:S(2)}, u32[]{:S(2)}) collective-permute-start(bf16[4,256,1408]{2,1,0:T(8,128)(2,1)} %weight_grad.9), channel_id=1, source_target_pairs={{0,4},{4,0},{8,12},{12,8},{16,20},{20,16},{24,28},{28,24},{1,5},{5... | collective-permute-start | bytes 8650760 | tf_op jit(solution)/shard_map/ppermute | solution.py:706
  234.6 23.9 %collective-permute-start.17 = (bf16[320,2048]{1,0:T(8,128)(2,1)}, bf16[320,2048]{1,0:T(8,128)(2,1)}, u32[]{:S(2)}, u32[]{:S(2)}) collective-permute-start(bf16[320,2048]{1,0:T(8,128)(2,1)} %get-tuple-element.171.refs_0_), channel_id=1, source_target_pairs={{0,1},{1,0},{2,3},{3,2},{4,5},{5,4},{6,7},{7,6},{8,9},{9,8},{10,11... | collective-permute-start | bytes 3932168 | tf_op jit(solution)/shard_map/ppermute | solution.py:706
  234.6 31.5 %collective-permute-start.15 = (bf16[320,2048]{1,0:T(8,128)(2,1)}, bf16[320,2048]{1,0:T(8,128)(2,1)}, u32[]{:S(2)}, u32[]{:S(2)}) collective-permute-start(bf16[320,2048]{1,0:T(8,128)(2,1)} %get-tuple-element.171.refs_0_), channel_id=1, source_target_pairs={{0,2},{1,3},{2,0},{3,1},{4,6},{5,7},{6,4},{7,5},{8,10},{9,11},{10,... | collective-permute-start | bytes 3932168 | tf_op jit(solution)/shard_map/ppermute | solution.py:706
  238.6 56.5 %collective-permute-start.20 = (bf16[2,256,1408]{2,1,0:T(8,128)(2,1)}, bf16[2,256,1408]{2,1,0:T(8,128)(2,1)}, u32[]{:S(2)}, u32[]{:S(2)}) collective-permute-start(bf16[2,256,1408]{2,1,0:T(8,128)(2,1)} %get-tuple-element.179), channel_id=1, source_target_pairs={{0,8},{4,12},{8,0},{12,4},{16,24},{20,28},{24,16},{28,20},{1,9},{5... | collective-permute-start | bytes 4325384 | tf_op jit(solution)/shard_map/ppermute | solution.py:706
  263.3 13.0 %copy-start.2 = (bf16[4,256,1408]{2,1,0:T(8,128)(2,1)S(1)}, bf16[4,256,1408]{2,1,0:T(8,128)(2,1)}, u32[]{:S(2)}) copy-start(bf16[4,256,1408]{2,1,0:T(8,128)(2,1)} %weight_grad.12.own_away.own_kept) | copy-start | bytes 8650756
  266.1 14.8 %collective-permute-start.18 = (bf16[320,2048]{1,0:T(8,128)(2,1)}, bf16[320,2048]{1,0:T(8,128)(2,1)}, u32[]{:S(2)}, u32[]{:S(2)}) collective-permute-start(bf16[320,2048]{1,0:T(8,128)(2,1)} %collective-permute-done.15.refs_0_.refs_2_), channel_id=1, source_target_pairs={{0,1},{1,0},{2,3},{3,2},{4,5},{5,4},{6,7},{7,6},{8,9},{9,8},{10,11... | collective-permute-start | bytes 3932168 | tf_op jit(solution)/shard_map/ppermute | solution.py:706
  266.1 61.8 %collective-permute-start.21 = (bf16[320,2048]{1,0:T(8,128)(2,1)}, bf16[320,2048]{1,0:T(8,128)(2,1)}, u32[]{:S(2)}, u32[]{:S(2)}) collective-permute-start(bf16[320,2048]{1,0:T(8,128)(2,1)} %pair_sum.13), channel_id=1, source_target_pairs={{0,2},{1,3},{2,0},{3,1},{4,6},{5,7},{6,4},{7,5},{8,10},{9,11},{10,... | collective-permute-start | bytes 3932168 | tf_op jit(solution)/shard_map/ppermute | solution.py:706
  280.4 80.4 %collective-permute-start.24 = (bf16[2,256,1408]{2,1,0:T(8,128)(2,1)}, bf16[2,256,1408]{2,1,0:T(8,128)(2,1)}, u32[]{:S(2)}, u32[]{:S(2)}) collective-permute-start(bf16[2,256,1408]{2,1,0:T(8,128)(2,1)} %get-tuple-element.210), channel_id=1, source_target_pairs={{0,4},{4,0},{8,12},{12,8},{16,20},{20,16},{24,28},{28,24},{1,5},{5... | collective-permute-start | bytes 4325384 | tf_op jit(solution)/shard_map/ppermute | solution.py:706
  285.7 9.4 %copy-start.1 = (bf16[4,256,1408]{2,1,0:T(8,128)(2,1)S(1)}, bf16[4,256,1408]{2,1,0:T(8,128)(2,1)}, u32[]{:S(2)}) copy-start(bf16[4,256,1408]{2,1,0:T(8,128)(2,1)} %weight_grad.13.own_away.own_kept) | copy-start | bytes 8650756
  299.5 61.2 %collective-permute-start.23 = (bf16[2,256,1408]{2,1,0:T(8,128)(2,1)}, bf16[2,256,1408]{2,1,0:T(8,128)(2,1)S(1)}, u32[]{:S(2)}, u32[]{:S(2)}) collective-permute-start(bf16[2,256,1408]{2,1,0:T(8,128)(2,1)} %get-tuple-element.207), channel_id=1, source_target_pairs={{0,8},{4,12},{8,0},{12,4},{16,24},{20,28},{24,16},{28,20},{1,9},{5... | collective-permute-start | bytes 4325384 | tf_op jit(solution)/shard_map/ppermute | solution.py:706
  303.7 44.1 %collective-permute-start.22 = (bf16[1,256,1408]{2,1,0:T(8,128)(2,1)S(1)}, bf16[1,256,1408]{2,1,0:T(8,128)(2,1)S(1)}, u32[]{:S(2)}, u32[]{:S(2)}) collective-permute-start(bf16[1,256,1408]{2,1,0:T(8,128)(2,1)S(1)} %get-tuple-element.198), channel_id=1, source_target_pairs={{0,16},{4,20},{8,24},{12,28},{16,0},{20,4},{24,8},{28,12},{1,17},{... | collective-permute-start | bytes 2162696 | tf_op jit(solution)/shard_map/ppermute | solution.py:706
  327.9 32.9 %collective-permute-start.25 = (bf16[4,256,512]{2,1,0:T(8,128)(2,1)}, bf16[4,256,512]{2,1,0:T(8,128)(2,1)}, u32[]{:S(2)}, u32[]{:S(2)}) collective-permute-start(bf16[4,256,512]{2,1,0:T(8,128)(2,1)} %get-tuple-element.211), channel_id=1, source_target_pairs={{0,4},{4,0},{8,12},{12,8},{16,20},{20,16},{24,28},{28,24},{1,5},{5... | collective-permute-start | bytes 3145736 | tf_op jit(solution)/shard_map/ppermute | solution.py:706
  348.6 12.2 %copy-start.4 = (bf16[2,256,1408]{2,1,0:T(8,128)(2,1)S(1)}, bf16[2,256,1408]{2,1,0:T(8,128)(2,1)}, u32[]{:S(2)}) copy-start(bf16[2,256,1408]{2,1,0:T(8,128)(2,1)} %copy-done.3) | copy-start | bytes 4325380
  358.7 31.2 %collective-permute-start.26 = (bf16[320,2048]{1,0:T(8,128)(2,1)}, bf16[320,2048]{1,0:T(8,128)(2,1)}, u32[]{:S(2)}, u32[]{:S(2)}) collective-permute-start(bf16[320,2048]{1,0:T(8,128)(2,1)} %pair_sum.14), channel_id=1, source_target_pairs={{0,2},{1,3},{2,0},{3,1},{4,6},{5,7},{6,4},{7,5},{8,10},{9,11},{10,... | collective-permute-start | bytes 3932168 | tf_op jit(solution)/shard_map/ppermute | solution.py:706
  359.3 33.1 %collective-permute-start.29 = (bf16[4,256,512]{2,1,0:T(8,128)(2,1)}, bf16[4,256,512]{2,1,0:T(8,128)(2,1)}, u32[]{:S(2)}, u32[]{:S(2)}) collective-permute-start(bf16[4,256,512]{2,1,0:T(8,128)(2,1)} %get-tuple-element.221), channel_id=1, source_target_pairs={{0,4},{4,0},{8,12},{12,8},{16,20},{20,16},{24,28},{28,24},{1,5},{5... | collective-permute-start | bytes 3145736 | tf_op jit(solution)/shard_map/ppermute | solution.py:706
  360.8 6.9 %copy-start.22 = (f32[320,2048]{1,0:T(8,128)S(1)}, f32[320,2048]{1,0:T(8,128)}, u32[]{:S(2)}) copy-start(f32[320,2048]{1,0:T(8,128)} %copy-done.20) | copy-start | bytes 7864324
  364.3 35.0 %collective-permute-start.28 = (bf16[1,256,1408]{2,1,0:T(8,128)(2,1)}, bf16[1,256,1408]{2,1,0:T(8,128)(2,1)}, u32[]{:S(2)}, u32[]{:S(2)}) collective-permute-start(bf16[1,256,1408]{2,1,0:T(8,128)(2,1)} %get-tuple-element.220), channel_id=1, source_target_pairs={{0,16},{4,20},{8,24},{12,28},{16,0},{20,4},{24,8},{28,12},{1,17},{... | collective-permute-start | bytes 2162696 | tf_op jit(solution)/shard_map/ppermute | solution.py:706
  372.2 22.0 %collective-permute-start.27 = (bf16[2,256,512]{2,1,0:T(8,128)(2,1)S(1)}, bf16[2,256,512]{2,1,0:T(8,128)(2,1)S(1)}, u32[]{:S(2)}, u32[]{:S(2)}) collective-permute-start(bf16[2,256,512]{2,1,0:T(8,128)(2,1)S(1)} %get-tuple-element.217), channel_id=1, source_target_pairs={{0,8},{4,12},{8,0},{12,4},{16,24},{20,28},{24,16},{28,20},{1,9},{5... | collective-permute-start | bytes 1572872 | tf_op jit(solution)/shard_map/ppermute | solution.py:706
  373.7 10.8 %copy-start.14 = (bf16[1,256,1408]{2,1,0:T(8,128)(2,1)}, bf16[1,256,1408]{2,1,0:T(8,128)(2,1)S(1)}, u32[]{:S(2)}) copy-start(bf16[1,256,1408]{2,1,0:T(8,128)(2,1)S(1)} %get-tuple-element.226.refs_0_) | copy-start | bytes 2162692
  384.6 14.7 %copy-start.28 = (bf16[320,2048]{1,0:T(8,128)(2,1)S(1)}, bf16[320,2048]{1,0:T(8,128)(2,1)}, u32[]{:S(2)}) copy-start(bf16[320,2048]{1,0:T(8,128)(2,1)} %param.14) | copy-start | bytes 3932164
  384.6 14.7 %copy-start.47 = (f32[2048]{0:T(1024)S(1)}, f32[2048]{0:T(1024)}, u32[]{:S(2)}) copy-start(f32[2048]{0:T(1024)} %param.16) | copy-start | bytes 24580
  392.4 11.1 %copy-start.29 = (f32[320,2048]{1,0:T(8,128)}, f32[320,2048]{1,0:T(8,128)S(1)}, u32[]{:S(2)}) copy-start(f32[320,2048]{1,0:T(8,128)S(1)} %convert_add_fusion.1) | copy-start | bytes 7864324
  (33 other events, 100.7 us)

commit v10 on v7

--- a/solution.py
+++ b/solution.py
@@ -556,8 +556,14 @@
     for m in range(ones, ones + twos):
         for c in (1, 0):
             stage[m, "z", c] = send(away[m].at[side(z2, c)], first[m].at[c], "dp", 2)
-    for m in range(ones):
-        stage[m, "last"] = send(away[m], first[m], "dp", 4)
+    pieces = 4
+    tile = own[0].shape[1] // pieces
+
+    def send_piece(m, index):
+        rows = pl.ds(index * tile, tile)
+        stage[m, "piece", index] = send(away[m].at[0, rows, :], first[m].at[0, rows, :], "dp", 4)
+
+    send_piece(0, 0)
 
     def send_all(m):
         for a in (1, 0):
@@ -603,7 +609,11 @@
             dst[...] = total
 
     def finish(m):
-        stage[m, "last"].wait_recv()
+        if m < ones:
+            for index in range(pieces):
+                stage[m, "piece", index].wait_recv()
+        else:
+            stage[m, "last"].wait_recv()
         if m < ones:
             outs[m][...] = wide(own[m][0]) + wide(first[m][0])
         elif m < ones + twos:
@@ -616,6 +626,7 @@
     from_x(q, 1, 1)
     from_x(q, 1, 0)
     from_near(out, 0)
+    send_piece(up, 1)
     from_x(q, 0, 1)
     from_x(q, 0, 0)
     done_ref[...] = (wide(ready_ref[0]) + wide(got_ref[0])).T
@@ -623,11 +634,13 @@
     from_near(q, 1)
     from_x(k, 1, 0)
     from_near(q, 0)
+    send_piece(up, 2)
     from_x(k, 0, 1)
     from_x(k, 0, 0)
     gain_hop(2)
     from_x(v, 1, 1)
     from_near(k, 1)
+    send_piece(up, 3)
     from_x(v, 1, 0)
     from_near(k, 0)
     gain_hop(3)
@@ -655,7 +668,7 @@
         flat[m] = flat[m][::-1]
     any_space = pl.BlockSpec(memory_space=pl.ANY)
     inside = pl.BlockSpec(memory_space=pltpu.VMEM)
-    count = len(ones) + 3 * len(twos) + 7 * len(threes) + 5
+    count = 4 * len(ones) + 3 * len(twos) + 7 * len(threes) + 5
     result = pl.pallas_call(
         functools.partial(last_body, len(ones), len(twos), len(threes)),
         in_specs=[any_space] * (2 * len(mats)) + [inside] * 3,

time: 504 us -> 508 us (level)
  no operation moved by 1% of the time
where the time goes in v10:
time: 508 us; the launch traced here: 503 us
  Pallas kernels  381 us (75%)
  starting transfers between devices  36.3 us (7%)
  other arithmetic  32.9 us (6%)
  waiting for transfers between devices  29.3 us (6%)
  local copies, waits for them, and re-layouts  21.6 us (4%)
    pallas_call x1, Pallas kernels, last_stages(): pl.pallas_call(functools.partial(last_body, len(ones), len(twos), len(thr...  96.1 us
    pallas_call x8, Pallas kernels, pair_sum(): pl.pallas_call(functools.partial(pair_body, [(len(left), dims) for left,...  83.5 us
    pallas_call x8, Pallas kernels, grad_call(): pl.pallas_call(functools.partial(grad_body, len(pieces), widths, low, sid...  77.1 us
    ppermute x28, starting transfers between devices, exchange(): lax.ppermute(values, axis, [(rank, rank ^ bit) for rank in range(size)])  36.3 us
    pallas_call x2, Pallas kernels, mlp_pair(): pl.pallas_call(mlp_body, grid=(pl.cdiv(width, tile),), in_specs=[whole(xa...  29.4 us
    ppermute x28, waiting for transfers between devices, exchange(): lax.ppermute(values, axis, [(rank, rank ^ bit) for rank in range(size)])  29.3 us
    pallas_call x4, Pallas kernels, project(): pl.pallas_call(functools.partial(project_body, [(len(left), dims) for lef...  26.5 us
    pallas_call x1, Pallas kernels, attend_back(): pl.pallas_call(attend_back_body, grid_spec=pltpu.PrefetchScalarGridSpec(n...  21.7 us
  transfers between devices with their start and end apart: 28, of which 12 were waited for; matrix products, arithmetic and copies ran while one was open for 4% of the time, Pallas kernels for 52%

profile of v10, /device:TPU:0, one launch (start us, length us, event | category | flops | bytes accessed | tf_op | source)
XLA Modules:
  0.0 503.0 jit_solution(18171788122904521893)
XLA Ops:
  4.6 2.6 collective-permute-start
  9.6 2.4 fusion.13
  16.1 2.0 collective-permute-done.2
  18.1 2.6 collective-permute-start.3
  25.4 9.4 %qkv.2 = (bf16[640,512]{1,0:T(8,128)(2,1)}, bf16[640,512]{1,0:T(8,128)(2,1)}, bf16[640,512]{1,0:T(8,128)(2,1)}) custom-call(s32[1]{0:T(128)} %bitcast.rank_ref, bf16[320,2048]{1,0:T(8,128)(2,1)} %copy-done.30, bf16[320,2048]{1,0:T(8,128)(2,1)} %copy-done.33, f32[1280,128]{1,0:T(8,128)} %pad_maximum_fusion.cos_ref, f32[1280,128]{1,0:T(8,128)} %get-tuple-element.245.sin_ref, ...), custom_call_target="tpu_custom_call" | custom-call | flops 4026531 | bytes 8912 | tf_op jit(solution)/shard_map/qkv/pallas_call | solution.py:67
  40.1 8.8 %qkv.3 = (bf16[640,512]{1,0:T(8,128)(2,1)}, bf16[640,512]{1,0:T(8,128)(2,1)}, bf16[640,512]{1,0:T(8,128)(2,1)}) custom-call(s32[1]{0:T(128)} %bitcast.rank_ref, bf16[320,2048]{1,0:T(8,128)(2,1)} %collective-permute-done.xa_ref.refs_2_, bf16[320,2048]{1,0:T(8,128)(2,1)} %collective-permute-done.5.xb_ref.refs_3_, f32[1280,128]{1,0:T(8,128)} %pad_maximum_fusion.cos_ref, ...), custom_call_target="tpu_custom_call" | custom-call | flops 4026531 | bytes 8912 | tf_op jit(solution)/shard_map/qkv/pallas_call | solution.py:67
  48.9 14.6 %attend.1 = (bf16[640,512]{1,0:T(8,128)(2,1)}, bf16[640,512]{1,0:T(8,128)(2,1)}, f32[4,1,1280]{2,1,0:T(1,128)}) custom-call(s32[1]{0:T(128)} %bitcast.rank_ref, bf16[640,512]{1,0:T(8,128)(2,1)} %get-tuple-element.125.qn, bf16[640,512]{1,0:T(8,128)(2,1)} %get-tuple-element.127.qf, bf16[640,512]{1,0:T(8,128)(2,1)} %get-tuple-element.128.kn, ...), custom_call_target="tpu_custom_call" | custom-call | flops 6710886 | bytes 5242 | tf_op jit(solution)/shard_map/attend/pallas_call | solution.py:128
  63.5 6.9 %pair_sum.8 = bf16[320,2048]{1,0:T(8,128)(2,1)} custom-call(bf16[640,512]{1,0:T(8,128)(2,1)} %get-tuple-element.134.refs_0_.refs_5_, bf16[512,2048]{1,0:T(8,128)(2,1)} %refs_2_.7), custom_call_target="tpu_custom_call" | custom-call | flops 1342177 | bytes 5373 | tf_op jit(solution)/shard_map/pair_sum/pallas_call | solution.py:478
  72.4 7.4 %pair_sum.9 = f32[320,2048]{1,0:T(8,128)} custom-call(bf16[640,512]{1,0:T(8,128)(2,1)} %get-tuple-element.138.refs_0_.refs_4_, bf16[512,2048]{1,0:T(8,128)(2,1)} %refs_2_.7), custom_call_target="tpu_custom_call" | custom-call | flops 1342177 | bytes 5373 | tf_op jit(solution)/shard_map/pair_sum/pallas_call | solution.py:478
  79.8 8.4 %project.4.dm_ref = f32[640,1408]{1,0:T(8,128)} custom-call(bf16[320,2048]{1,0:T(8,128)(2,1)} %copy-done.27, bf16[320,2048]{1,0:T(8,128)(2,1)} %copy-done.29, bf16[1408,2048]{1,0:T(8,128)(2,1)} %refs_1_.13), custom_call_target="tpu_custom_call" | custom-call | flops 3690987 | bytes 10190 | tf_op jit(solution)/shard_map/project/pallas_call | solution.py:414
  88.1 8.6 %project.5.dm_ref = f32[640,1408]{1,0:T(8,128)} custom-call(bf16[320,2048]{1,0:T(8,128)(2,1)} %copy-done.28, bf16[320,2048]{1,0:T(8,128)(2,1)} %collective-permute-done.9.refs_1_.refs_3_, bf16[1408,2048]{1,0:T(8,128)(2,1)} %refs_1_.13), custom_call_target="tpu_custom_call" | custom-call | flops 3690987 | bytes 10190 | tf_op jit(solution)/shard_map/project/pallas_call | solution.py:414
  96.7 5.3 %collective-permute-done.8 = bf16[320,2048]{1,0:T(8,128)(2,1)} collective-permute-done((bf16[320,2048]{1,0:T(8,128)(2,1)}, bf16[320,2048]{1,0:T(8,128)(2,1)}, u32[]{:S(2)}, u32[]{:S(2)}) %collective-permute-start.8) | collective-permute-done | bytes 1310752 | tf_op jit(solution)/shard_map/ppermute | solution.py:728
  109.9 14.8 %mlp.2 = (bf16[640,1408]{1,0:T(8,128)(2,1)}, bf16[640,1408]{1,0:T(8,128)(2,1)}, bf16[640,1408]{1,0:T(8,128)(2,1)}) custom-call(bf16[320,2048]{1,0:T(8,128)(2,1)} %copy-done.20, bf16[320,2048]{1,0:T(8,128)(2,1)} %copy-done.21, f32[640,1408]{1,0:T(8,128)} %project.4.dm_ref, bf16[2048,1408]{1,0:T(8,128)(2,1)} %refs_1_.12, bf16[2048,1408]{1,0:T(8,128)(2,1)} %refs_3_.5), custom_call_target="tpu_custom_call" | custom-call | flops 7381975 | bytes 23166 | tf_op jit(solution)/shard_map/mlp/pallas_call | solution.py:234
  124.7 10.0 %pair_sum.10 = f32[320,2048]{1,0:T(8,128)} custom-call(bf16[640,1408]{1,0:T(8,128)(2,1)} %get-tuple-element.160.refs_0_.refs_4_, bf16[1408,2048]{1,0:T(8,128)(2,1)} %refs_1_.13), custom_call_target="tpu_custom_call" | custom-call | flops 3690987 | bytes 10190 | tf_op jit(solution)/shard_map/pair_sum/pallas_call | solution.py:478
  134.6 2.3 collective-permute-done.10.xa_ref.refs_2_
  137.0 3.0 collective-permute-done.12.xb_ref.refs_3_
  141.1 14.6 %mlp.3 = (bf16[640,1408]{1,0:T(8,128)(2,1)}, bf16[640,1408]{1,0:T(8,128)(2,1)}, bf16[640,1408]{1,0:T(8,128)(2,1)}) custom-call(bf16[320,2048]{1,0:T(8,128)(2,1)} %copy-done.22, bf16[320,2048]{1,0:T(8,128)(2,1)} %copy-done.23, f32[640,1408]{1,0:T(8,128)} %project.5.dm_ref, bf16[2048,1408]{1,0:T(8,128)(2,1)} %refs_1_.12, bf16[2048,1408]{1,0:T(8,128)(2,1)} %refs_3_.5), custom_call_target="tpu_custom_call" | custom-call | flops 7381975 | bytes 23166 | tf_op jit(solution)/shard_map/mlp/pallas_call | solution.py:234
  155.7 8.7 %weight_grad.8 = bf16[4,256,1408]{2,1,0:T(8,128)(2,1)} custom-call(s32[1]{0:T(128)} %bitcast.7.rank_ref._, bf16[320,2048]{1,0:T(8,128)(2,1)} %copy-done.27, bf16[320,2048]{1,0:T(8,128)(2,1)} %copy-done.29, bf16[320,2048]{1,0:T(8,128)(2,1)} %copy-done.28, bf16[320,2048]{1,0:T(8,128)(2,1)} %collective-permute-done.9.refs_1_.refs_3_, ...), custom_call_target="tpu_custom_call" | custom-call | flops 3690987 | bytes 9109 | tf_op jit(solution)/shard_map/weight_grad/pallas_call | solution.py:324
  166.1 14.3 %pair_sum.11 = bf16[320,2048]{1,0:T(8,128)(2,1)} custom-call(bf16[640,1408]{1,0:T(8,128)(2,1)} %get-tuple-element.154.refs_0_.refs_5_, bf16[2048,1408]{1,0:T(8,128)(2,1)} %refs_1_.12, bf16[640,1408]{1,0:T(8,128)(2,1)} %get-tuple-element.155.refs_2_.refs_5_, bf16[2048,1408]{1,0:T(8,128)(2,1)} %refs_3_.5), custom_call_target="tpu_custom_call" | custom-call | flops 7381975 | bytes 17760 | tf_op jit(solution)/shard_map/pair_sum/pallas_call | solution.py:478
  182.0 8.7 %weight_grad.11 = bf16[4,256,1408]{2,1,0:T(8,128)(2,1)} custom-call(s32[1]{0:T(128)} %bitcast.7.rank_ref._, bf16[320,2048]{1,0:T(8,128)(2,1)} %copy-done.20, bf16[320,2048]{1,0:T(8,128)(2,1)} %copy-done.21, bf16[320,2048]{1,0:T(8,128)(2,1)} %copy-done.22, bf16[320,2048]{1,0:T(8,128)(2,1)} %copy-done.23, ...), custom_call_target="tpu_custom_call" | custom-call | flops 3690987 | bytes 9109 | tf_op jit(solution)/shard_map/weight_grad/pallas_call | solution.py:324
  192.2 8.7 %weight_grad.10.own_away.own_kept = bf16[4,256,1408]{2,1,0:T(8,128)(2,1)} custom-call(s32[1]{0:T(128)} %bitcast.7.rank_ref._, bf16[320,2048]{1,0:T(8,128)(2,1)} %copy-done.27, bf16[320,2048]{1,0:T(8,128)(2,1)} %copy-done.29, bf16[320,2048]{1,0:T(8,128)(2,1)} %copy-done.28, bf16[320,2048]{1,0:T(8,128)(2,1)} %collective-permute-done.9.refs_1_.refs_3_, ...), custom_call_target="tpu_custom_call" | custom-call | flops 3690987 | bytes 9109 | tf_op jit(solution)/shard_map/weight_grad/pallas_call | solution.py:324
  201.0 8.7 %weight_grad.9 = bf16[4,256,1408]{2,1,0:T(8,128)(2,1)} custom-call(s32[1]{0:T(128)} %bitcast.7.rank_ref._, bf16[320,2048]{1,0:T(8,128)(2,1)} %copy-done.20, bf16[320,2048]{1,0:T(8,128)(2,1)} %copy-done.21, bf16[320,2048]{1,0:T(8,128)(2,1)} %copy-done.22, bf16[320,2048]{1,0:T(8,128)(2,1)} %copy-done.23, bf16[640,1408]{1,0:T(8,128)(2,1)} %get-tuple-element.171.refs_2_.refs_4_, ...), custom_call_target="tpu_custom_call" | custom-call | flops 3690987 | bytes 9109 | tf_op jit(solution)/shard_map/weight_grad/pallas_call | solution.py:324
  209.7 14.9 %pair_sum.12 = f32[320,2048]{1,0:T(8,128)} custom-call(bf16[640,1408]{1,0:T(8,128)(2,1)} %get-tuple-element.164.refs_0_.refs_4_, bf16[2048,1408]{1,0:T(8,128)(2,1)} %refs_1_.12, bf16[640,1408]{1,0:T(8,128)(2,1)} %get-tuple-element.171.refs_2_.refs_4_, bf16[2048,1408]{1,0:T(8,128)(2,1)} %refs_3_.5), custom_call_target="tpu_custom_call" | custom-call | flops 7381975 | bytes 17760 | tf_op jit(solution)/shard_map/pair_sum/pallas_call | solution.py:478
  224.6 2.6 convert_add_fusion.2
  227.2 1.9 collective-permute-done.14.got_away.got_kept
  231.7 2.8 fusion.16
  240.1 9.6 %pair_sum.13 = bf16[320,2048]{1,0:T(8,128)(2,1)} custom-call(bf16[640,1408]{1,0:T(8,128)(2,1)} %get-tuple-element.163.refs_5_.refs_0_, bf16[1408,2048]{1,0:T(8,128)(2,1)} %refs_1_.13), custom_call_target="tpu_custom_call" | custom-call | flops 3690987 | bytes 10190 | tf_op jit(solution)/shard_map/pair_sum/pallas_call | solution.py:478
  249.6 8.8 %weight_grad.12.own_away.own_kept = bf16[4,256,1408]{2,1,0:T(8,128)(2,1)} custom-call(s32[1]{0:T(128)} %bitcast.7.rank_ref._, bf16[320,2048]{1,0:T(8,128)(2,1)} %copy-done.20, bf16[320,2048]{1,0:T(8,128)(2,1)} %copy-done.21, bf16[320,2048]{1,0:T(8,128)(2,1)} %copy-done.22, bf16[320,2048]{1,0:T(8,128)(2,1)} %copy-done.23, ...), custom_call_target="tpu_custom_call" | custom-call | flops 3690987 | bytes 9109 | tf_op jit(solution)/shard_map/weight_grad/pallas_call | solution.py:324
  258.4 4.8 project.6.gn
  263.2 2.8 collective-permute-done.15.refs_0_.refs_2_
  267.5 8.7 %weight_grad.13.own_away.own_kept = bf16[4,256,1408]{2,1,0:T(8,128)(2,1)} custom-call(s32[1]{0:T(128)} %bitcast.7.rank_ref._, bf16[320,2048]{1,0:T(8,128)(2,1)} %copy-done.20, bf16[320,2048]{1,0:T(8,128)(2,1)} %copy-done.21, bf16[320,2048]{1,0:T(8,128)(2,1)} %copy-done.22, bf16[320,2048]{1,0:T(8,128)(2,1)} %copy-done.23, ...), custom_call_target="tpu_custom_call" | custom-call | flops 3690987 | bytes 9109 | tf_op jit(solution)/shard_map/weight_grad/pallas_call | solution.py:324
  276.2 2.9 merge.9
  280.7 4.8 project.7.gf
  285.5 9.4 %weight_grad.14 = (bf16[4,256,512]{2,1,0:T(8,128)(2,1)}, bf16[4,256,512]{2,1,0:T(8,128)(2,1)}) custom-call(s32[1]{0:T(128)} %bitcast.7.rank_ref._, bf16[320,2048]{1,0:T(8,128)(2,1)} %get-tuple-element.162.refs_0_, bf16[320,2048]{1,0:T(8,128)(2,1)} %collective-permute-done.17.refs_1_, bf16[320,2048]{1,0:T(8,128)(2,1)} %collective-permute-done.15.refs_0_.refs_2_, ...), custom_call_target="tpu_custom_call" | custom-call | flops 2684354 | bytes 8650 | tf_op jit(solution)/shard_map/weight_grad/pallas_call | solution.py:324
  295.0 3.3 merge.8
  301.0 2.4 merge.10
  304.2 2.6 collective-permute-start.24
  306.8 21.7 %attend_back.1 = (bf16[640,512]{1,0:T(8,128)(2,1)}, bf16[640,512]{1,0:T(8,128)(2,1)}, bf16[640,512]{1,0:T(8,128)(2,1)}, bf16[640,512]{1,0:T(8,128)(2,1)}, bf16[6...) custom-call(s32[1]{0:T(128)} %bitcast.rank_ref, bf16[640,512]{1,0:T(8,128)(2,1)} %get-tuple-element.125.qn, ...), custom_call_target="tpu_custom_call" | custom-call | flops 16777216 | bytes 10485 | tf_op jit(solution)/shard_map/attend_back/pallas_call | solution.py:191
  328.5 10.1 %pair_sum.14 = bf16[320,2048]{1,0:T(8,128)(2,1)} custom-call(bf16[640,512]{1,0:T(8,128)(2,1)} %get-tuple-element.184.refs_0_.refs_5_, bf16[2048,512]{1,0:T(8,128)(2,1)} %refs_1_.15, bf16[640,512]{1,0:T(8,128)(2,1)} %get-tuple-element.185.refs_2_.refs_7_, bf16[2048,512]{1,0:T(8,128)(2,1)} %refs_3_.7, bf16[640,512]{1,0:T(8,128)(2,1)} %get-tuple-element.186.refs_4_.refs_9_, ...), custom_call_target="tpu_custom_call" | custom-call | flops 4026531 | bytes 10878 | tf_op jit(solution)/shard_map/pair_sum/pallas_call | solution.py:478
  341.8 6.0 %collective-permute-done.24.refs_11_ = bf16[1,256,1408]{2,1,0:T(8,128)(2,1)} collective-permute-done((bf16[1,256,1408]{2,1,0:T(8,128)(2,1)}, bf16[1,256,1408]{2,1,0:T(8,128)(2,1)}, u32[]{:S(2)}, u32[]{:S(2)}) %collective-permute-start.24) | collective-permute-done | bytes 720928 | tf_op jit(solution)/shard_map/ppermute | solution.py:728
  348.5 2.5 merge.11
  351.9 2.6 collective-permute-start.27
  354.5 3.1 add_convert_fusion
  359.7 10.4 %pair_sum.15 = f32[320,2048]{1,0:T(8,128)} custom-call(bf16[640,512]{1,0:T(8,128)(2,1)} %get-tuple-element.196.refs_0_.refs_4_, bf16[2048,512]{1,0:T(8,128)(2,1)} %refs_1_.15, bf16[640,512]{1,0:T(8,128)(2,1)} %get-tuple-element.197.refs_2_.refs_6_, bf16[2048,512]{1,0:T(8,128)(2,1)} %refs_3_.7, bf16[640,512]{1,0:T(8,128)(2,1)} %get-tuple-element.198.refs_4_.refs_8_, ...), custom_call_target="tpu_custom_call" | custom-call | flops 4026531 | bytes 10878 | tf_op jit(solution)/shard_map/pair_sum/pallas_call | solution.py:478
  370.1 15.3 %weight_grad.15 = (bf16[4,256,512]{2,1,0:T(8,128)(2,1)}, bf16[4,256,512]{2,1,0:T(8,128)(2,1)}, bf16[4,256,512]{2,1,0:T(8,128)(2,1)}, bf16[4,256,512]{2,1,0:T(8,1...) custom-call(s32[1]{0:T(128)} %bitcast.7.rank_ref._, bf16[320,2048]{1,0:T(8,128)(2,1)} %copy-done.30, ...), custom_call_target="tpu_custom_call" | custom-call | flops 8053063 | bytes 15466 | tf_op jit(solution)/shard_map/weight_grad/pallas_call | solution.py:324
  385.5 2.5 convert_add_fusion.1
  393.8 96.1 %last_stages.1 = (f32[256,1408]{1,0:T(8,128)}, f32[512,256]{1,0:T(8,128)}, f32[256,512]{1,0:T(8,128)}, f32[256,512]{1,0:T(8,128)}, f32[256,512]{1,0:T(8,128)}, /*index=5*/f32[1408,256]{1,0:T(8,128)}, f32[2,2048]{1,0:T(2,128)}) custom-call(bf16[1,256,1408]{2,1,0:T(8,128)(2,1)} %copy-done.13, bf16[2,256,512]{2,1,0:T(8,128)(2,1)} %copy-done.15, ...), custom_call_target="tpu_custom_call" | custom-call | flops 16777 | bytes 33554 | tf_op jit(solution)/shard_map/last_stages/pallas_call | solution.py:672
  489.9 4.8 fusion.8
  (188 shorter events, 71.6 us)
Async XLA Ops:
  0.6 6.6 %copy-start.48 = (s32[1,3]{1,0:T(1,128)S(1)}, s32[1,3]{1,0:T(1,128)}, u32[]{:S(2)}) copy-start(s32[1,3]{1,0:T(1,128)} %param.25) | copy-start | bytes 40
  0.7 6.9 %copy-start.46 = (s32[1,1280]{1,0:T(1,128)S(1)}, s32[1,1280]{1,0:T(1,128)}, u32[]{:S(2)}) copy-start(s32[1,1280]{1,0:T(1,128)} %param.27) | copy-start | bytes 15364
  0.7 7.1 %copy-start.47 = (s32[1,3]{1,0:T(1,128)S(1)}, s32[1,3]{1,0:T(1,128)}, u32[]{:S(2)}) copy-start(s32[1,3]{1,0:T(1,128)} %param.26) | copy-start | bytes 40
  4.1 10.4 %copy-start.30 = (bf16[320,2048]{1,0:T(8,128)(2,1)}, bf16[320,2048]{1,0:T(8,128)(2,1)S(1)}, u32[]{:S(2)}) copy-start(bf16[320,2048]{1,0:T(8,128)(2,1)S(1)} %fusion.4.xa_ref.refs_0_) | copy-start | bytes 3932164
  4.1 20.3 %collective-permute-start.4 = (bf16[320,2048]{1,0:T(8,128)(2,1)S(1)}, bf16[320,2048]{1,0:T(8,128)(2,1)S(1)}, u32[]{:S(2)}, u32[]{:S(2)}) collective-permute-start(bf16[320,2048]{1,0:T(8,128)(2,1)S(1)} %fusion.4.xa_ref.refs_0_), channel_id=1, source_target_pairs={{0,1},{1,0},{2,3},{3,2},{4,5},{5,4},{6,7},{7,6},{8,9},{9,8},{10,11... | collective-permute-start | bytes 3932168 | tf_op jit(solution)/shard_map/ppermute | solution.py:728
  4.6 32.1 %collective-permute-start = (bf16[320,2048]{1,0:T(8,128)(2,1)S(1)}, bf16[320,2048]{1,0:T(8,128)(2,1)}, u32[]{:S(2)}, u32[]{:S(2)}) collective-permute-start(bf16[320,2048]{1,0:T(8,128)(2,1)S(1)} %fusion.4.xa_ref.refs_0_), channel_id=1, source_target_pairs={{0,2},{1,3},{2,0},{3,1},{4,6},{5,7},{6,4},{7,5},{8,10},{9,11},{10,... | collective-permute-start | bytes 3932168 | tf_op jit(solution)/shard_map/ppermute | solution.py:728
  8.0 6.5 %collective-permute-start.1 = (f32[8]{0:T(128)S(1)}, f32[8]{0:T(128)S(1)}, u32[]{:S(2)}, u32[]{:S(2)}) collective-permute-start(f32[8]{0:T(128)S(1)} %select_reduce_fusion.1), channel_id=1, source_target_pairs={{0,4},{4,0},{8,12},{12,8},{16,20},{20,16},{24,28},{28,24},{1,5},{5... | collective-permute-start | bytes 104 | tf_op jit(solution)/shard_map/ppermute | solution.py:728
  9.5 14.5 %copy-start.34 = (bf16[320,2048]{1,0:T(8,128)(2,1)S(1)}, bf16[320,2048]{1,0:T(8,128)(2,1)}, u32[]{:S(2)}) copy-start(bf16[320,2048]{1,0:T(8,128)(2,1)} %param.15) | copy-start | bytes 3932164
  14.5 3.6 collective-permute-start.2
  18.1 4.5 collective-permute-start.3
  24.3 14.1 %copy-start.27 = (bf16[320,2048]{1,0:T(8,128)(2,1)}, bf16[320,2048]{1,0:T(8,128)(2,1)S(1)}, u32[]{:S(2)}) copy-start(bf16[320,2048]{1,0:T(8,128)(2,1)S(1)} %fusion.12.refs_0_) | copy-start | bytes 3932164
  36.7 3.4 collective-permute-start.5
  36.7 33.7 %collective-permute-start.7 = (bf16[320,2048]{1,0:T(8,128)(2,1)S(1)}, bf16[320,2048]{1,0:T(8,128)(2,1)S(1)}, u32[]{:S(2)}, u32[]{:S(2)}) collective-permute-start(bf16[320,2048]{1,0:T(8,128)(2,1)S(1)} %fusion.12.refs_0_), channel_id=1, source_target_pairs={{0,2},{1,3},{2,0},{3,1},{4,6},{5,7},{6,4},{7,5},{8,10},{9,11},{10,... | collective-permute-start | bytes 3932168 | tf_op jit(solution)/shard_map/ppermute | solution.py:728
  38.4 32.0 %collective-permute-start.6 = (bf16[320,2048]{1,0:T(8,128)(2,1)S(1)}, bf16[320,2048]{1,0:T(8,128)(2,1)S(1)}, u32[]{:S(2)}, u32[]{:S(2)}) collective-permute-start(bf16[320,2048]{1,0:T(8,128)(2,1)S(1)} %fusion.12.refs_0_), channel_id=1, source_target_pairs={{0,1},{1,0},{2,3},{3,2},{4,5},{5,4},{6,7},{7,6},{8,9},{9,8},{10,11... | collective-permute-start | bytes 3932168 | tf_op jit(solution)/shard_map/ppermute | solution.py:728
  70.4 9.3 %copy-start.28 = (bf16[320,2048]{1,0:T(8,128)(2,1)}, bf16[320,2048]{1,0:T(8,128)(2,1)S(1)}, u32[]{:S(2)}) copy-start(bf16[320,2048]{1,0:T(8,128)(2,1)S(1)} %collective-permute-done.7.refs_0_.refs_2_) | copy-start | bytes 3932164
  70.4 9.3 %copy-start.29 = (bf16[320,2048]{1,0:T(8,128)(2,1)}, bf16[320,2048]{1,0:T(8,128)(2,1)S(1)}, u32[]{:S(2)}) copy-start(bf16[320,2048]{1,0:T(8,128)(2,1)S(1)} %collective-permute-done.6.refs_1_) | copy-start | bytes 3932164
  70.4 17.7 %collective-permute-start.9 = (bf16[320,2048]{1,0:T(8,128)(2,1)S(1)}, bf16[320,2048]{1,0:T(8,128)(2,1)}, u32[]{:S(2)}, u32[]{:S(2)}) collective-permute-start(bf16[320,2048]{1,0:T(8,128)(2,1)S(1)} %collective-permute-done.7.refs_0_.refs_2_), channel_id=1, source_target_pairs={{0,1},{1,0},{2,3},{3,2},{4,5},{5,4},{6,7},{7,6},{8,9},{9,8},{10,11... | collective-permute-start | bytes 3932168 | tf_op jit(solution)/shard_map/ppermute | solution.py:728
  70.6 31.4 %collective-permute-start.8 = (bf16[320,2048]{1,0:T(8,128)(2,1)}, bf16[320,2048]{1,0:T(8,128)(2,1)}, u32[]{:S(2)}, u32[]{:S(2)}) collective-permute-start(bf16[320,2048]{1,0:T(8,128)(2,1)} %pair_sum.8), channel_id=1, source_target_pairs={{0,2},{1,3},{2,0},{3,1},{4,6},{5,7},{6,4},{7,5},{8,10},{9,11},{10,... | collective-permute-start | bytes 3932168 | tf_op jit(solution)/shard_map/ppermute | solution.py:728
  88.1 13.9 %copy-start.24 = (bf16[320,2048]{1,0:T(8,128)(2,1)S(1)}, bf16[320,2048]{1,0:T(8,128)(2,1)}, u32[]{:S(2)}) copy-start(bf16[320,2048]{1,0:T(8,128)(2,1)} %param.14) | copy-start | bytes 3932164
  88.1 13.9 %copy-start.32 = (f32[320,2048]{1,0:T(8,128)S(1)}, f32[320,2048]{1,0:T(8,128)}, u32[]{:S(2)}) copy-start(f32[320,2048]{1,0:T(8,128)} %pair_sum.9) | copy-start | bytes 7864324
  96.7 8.8 %copy-start.44 = (f32[2048]{0:T(1024)S(1)}, f32[2048]{0:T(1024)}, u32[]{:S(2)}) copy-start(f32[2048]{0:T(1024)} %param.21) | copy-start | bytes 24580
  105.7 3.1 collective-permute-start.11
  105.8 31.2 %collective-permute-start.10 = (bf16[320,2048]{1,0:T(8,128)(2,1)S(1)}, bf16[320,2048]{1,0:T(8,128)(2,1)S(1)}, u32[]{:S(2)}, u32[]{:S(2)}) collective-permute-start(bf16[320,2048]{1,0:T(8,128)(2,1)S(1)} %multiply_convert_fusion.xa_ref.refs_0_), channel_id=1, source_target_pairs={{0,2},{1,3},{2,0},{3,1},{4,6},{5,7},{6,4},{7,5},{8,10},{9,11},{10,... | collective-permute-start | bytes 3932168 | tf_op jit(solution)/shard_map/ppermute | solution.py:728
  137.0 3.0 collective-permute-start.12
  164.4 64.7 %collective-permute-start.14 = (bf16[4,256,1408]{2,1,0:T(8,128)(2,1)}, bf16[4,256,1408]{2,1,0:T(8,128)(2,1)S(1)}, u32[]{:S(2)}, u32[]{:S(2)}) collective-permute-start(bf16[4,256,1408]{2,1,0:T(8,128)(2,1)} %weight_grad.8), channel_id=1, source_target_pairs={{0,4},{4,0},{8,12},{12,8},{16,20},{20,16},{24,28},{28,24},{1,5},{5... | collective-permute-start | bytes 8650760 | tf_op jit(solution)/shard_map/ppermute | solution.py:728
  180.4 44.2 %collective-permute-start.13 = (bf16[320,2048]{1,0:T(8,128)(2,1)}, bf16[320,2048]{1,0:T(8,128)(2,1)}, u32[]{:S(2)}, u32[]{:S(2)}) collective-permute-start(bf16[320,2048]{1,0:T(8,128)(2,1)} %pair_sum.11), channel_id=1, source_target_pairs={{0,2},{1,3},{2,0},{3,1},{4,6},{5,7},{6,4},{7,5},{8,10},{9,11},{10,... | collective-permute-start | bytes 3932168 | tf_op jit(solution)/shard_map/ppermute | solution.py:728
  190.7 72.6 %collective-permute-start.16 = (bf16[4,256,1408]{2,1,0:T(8,128)(2,1)}, bf16[4,256,1408]{2,1,0:T(8,128)(2,1)}, u32[]{:S(2)}, u32[]{:S(2)}) collective-permute-start(bf16[4,256,1408]{2,1,0:T(8,128)(2,1)} %weight_grad.11), channel_id=1, source_target_pairs={{0,8},{4,12},{8,0},{12,4},{16,24},{20,28},{24,16},{28,20},{1,9},{5... | collective-permute-start | bytes 8650760 | tf_op jit(solution)/shard_map/ppermute | solution.py:728
  224.6 6.3 %copy-start.18 = (f32[320,2048]{1,0:T(8,128)S(1)}, f32[320,2048]{1,0:T(8,128)}, u32[]{:S(2)}) copy-start(f32[320,2048]{1,0:T(8,128)} %copy-done.17) | copy-start | bytes 7864324
  229.1 65.8 %collective-permute-start.19 = (bf16[4,256,1408]{2,1,0:T(8,128)(2,1)}, bf16[4,256,1408]{2,1,0:T(8,128)(2,1)}, u32[]{:S(2)}, u32[]{:S(2)}) collective-permute-start(bf16[4,256,1408]{2,1,0:T(8,128)(2,1)} %weight_grad.9), channel_id=1, source_target_pairs={{0,4},{4,0},{8,12},{12,8},{16,20},{20,16},{24,28},{28,24},{1,5},{5... | collective-permute-start | bytes 8650760 | tf_op jit(solution)/shard_map/ppermute | solution.py:728
  234.5 24.0 %collective-permute-start.17 = (bf16[320,2048]{1,0:T(8,128)(2,1)}, bf16[320,2048]{1,0:T(8,128)(2,1)}, u32[]{:S(2)}, u32[]{:S(2)}) collective-permute-start(bf16[320,2048]{1,0:T(8,128)(2,1)} %get-tuple-element.162.refs_0_), channel_id=1, source_target_pairs={{0,1},{1,0},{2,3},{3,2},{4,5},{5,4},{6,7},{7,6},{8,9},{9,8},{10,11... | collective-permute-start | bytes 3932168 | tf_op jit(solution)/shard_map/ppermute | solution.py:728
  234.5 31.5 %collective-permute-start.15 = (bf16[320,2048]{1,0:T(8,128)(2,1)}, bf16[320,2048]{1,0:T(8,128)(2,1)}, u32[]{:S(2)}, u32[]{:S(2)}) collective-permute-start(bf16[320,2048]{1,0:T(8,128)(2,1)} %get-tuple-element.162.refs_0_), channel_id=1, source_target_pairs={{0,2},{1,3},{2,0},{3,1},{4,6},{5,7},{6,4},{7,5},{8,10},{9,11},{10,... | collective-permute-start | bytes 3932168 | tf_op jit(solution)/shard_map/ppermute | solution.py:728
  238.5 56.5 %collective-permute-start.20 = (bf16[2,256,1408]{2,1,0:T(8,128)(2,1)}, bf16[2,256,1408]{2,1,0:T(8,128)(2,1)}, u32[]{:S(2)}, u32[]{:S(2)}) collective-permute-start(bf16[2,256,1408]{2,1,0:T(8,128)(2,1)} %get-tuple-element.170), channel_id=1, source_target_pairs={{0,8},{4,12},{8,0},{12,4},{16,24},{20,28},{24,16},{28,20},{1,9},{5... | collective-permute-start | bytes 4325384 | tf_op jit(solution)/shard_map/ppermute | solution.py:728
  263.2 13.0 %copy-start.2 = (bf16[4,256,1408]{2,1,0:T(8,128)(2,1)S(1)}, bf16[4,256,1408]{2,1,0:T(8,128)(2,1)}, u32[]{:S(2)}) copy-start(bf16[4,256,1408]{2,1,0:T(8,128)(2,1)} %weight_grad.12.own_away.own_kept) | copy-start | bytes 8650756
  266.0 14.7 %collective-permute-start.18 = (bf16[320,2048]{1,0:T(8,128)(2,1)}, bf16[320,2048]{1,0:T(8,128)(2,1)}, u32[]{:S(2)}, u32[]{:S(2)}) collective-permute-start(bf16[320,2048]{1,0:T(8,128)(2,1)} %collective-permute-done.15.refs_0_.refs_2_), channel_id=1, source_target_pairs={{0,1},{1,0},{2,3},{3,2},{4,5},{5,4},{6,7},{7,6},{8,9},{9,8},{10,11... | collective-permute-start | bytes 3932168 | tf_op jit(solution)/shard_map/ppermute | solution.py:728
  266.0 62.6 %collective-permute-start.21 = (bf16[320,2048]{1,0:T(8,128)(2,1)}, bf16[320,2048]{1,0:T(8,128)(2,1)}, u32[]{:S(2)}, u32[]{:S(2)}) collective-permute-start(bf16[320,2048]{1,0:T(8,128)(2,1)} %pair_sum.13), channel_id=1, source_target_pairs={{0,2},{1,3},{2,0},{3,1},{4,6},{5,7},{6,4},{7,5},{8,10},{9,11},{10,... | collective-permute-start | bytes 3932168 | tf_op jit(solution)/shard_map/ppermute | solution.py:728
  280.2 61.6 %collective-permute-start.23 = (bf16[2,256,1408]{2,1,0:T(8,128)(2,1)}, bf16[2,256,1408]{2,1,0:T(8,128)(2,1)}, u32[]{:S(2)}, u32[]{:S(2)}) collective-permute-start(bf16[2,256,1408]{2,1,0:T(8,128)(2,1)} %get-tuple-element.192), channel_id=1, source_target_pairs={{0,4},{4,0},{8,12},{12,8},{16,20},{20,16},{24,28},{28,24},{1,5},{5... | collective-permute-start | bytes 4325384 | tf_op jit(solution)/shard_map/ppermute | solution.py:728
  285.5 9.5 %copy-start.1 = (bf16[4,256,1408]{2,1,0:T(8,128)(2,1)S(1)}, bf16[4,256,1408]{2,1,0:T(8,128)(2,1)}, u32[]{:S(2)}) copy-start(bf16[4,256,1408]{2,1,0:T(8,128)(2,1)} %weight_grad.13.own_away.own_kept) | copy-start | bytes 8650756
  295.0 6.0 %copy-start.8 = (bf16[2,256,1408]{2,1,0:T(8,128)(2,1)S(1)}, bf16[2,256,1408]{2,1,0:T(8,128)(2,1)}, u32[]{:S(2)}) copy-start(bf16[2,256,1408]{2,1,0:T(8,128)(2,1)} %copy-done.7) | copy-start | bytes 4325380
  299.4 49.1 %collective-permute-start.22 = (bf16[2,256,1408]{2,1,0:T(8,128)(2,1)}, bf16[2,256,1408]{2,1,0:T(8,128)(2,1)S(1)}, u32[]{:S(2)}, u32[]{:S(2)}) collective-permute-start(bf16[2,256,1408]{2,1,0:T(8,128)(2,1)} %get-tuple-element.189), channel_id=1, source_target_pairs={{0,8},{4,12},{8,0},{12,4},{16,24},{20,28},{24,16},{28,20},{1,9},{5... | collective-permute-start | bytes 4325384 | tf_op jit(solution)/shard_map/ppermute | solution.py:728
  304.2 43.5 %collective-permute-start.24 = (bf16[1,256,1408]{2,1,0:T(8,128)(2,1)}, bf16[1,256,1408]{2,1,0:T(8,128)(2,1)}, u32[]{:S(2)}, u32[]{:S(2)}) collective-permute-start(bf16[1,256,1408]{2,1,0:T(8,128)(2,1)} %get-tuple-element.195), channel_id=1, source_target_pairs={{0,16},{4,20},{8,24},{12,28},{16,0},{20,4},{24,8},{28,12},{1,17},{... | collective-permute-start | bytes 2162696 | tf_op jit(solution)/shard_map/ppermute | solution.py:728
  328.5 20.0 %copy-start.4 = (bf16[2,256,1408]{2,1,0:T(8,128)(2,1)S(1)}, bf16[2,256,1408]{2,1,0:T(8,128)(2,1)}, u32[]{:S(2)}) copy-start(bf16[2,256,1408]{2,1,0:T(8,128)(2,1)} %copy-done.3) | copy-start | bytes 4325380
  338.7 46.8 %collective-permute-start.25 = (bf16[320,2048]{1,0:T(8,128)(2,1)}, bf16[320,2048]{1,0:T(8,128)(2,1)}, u32[]{:S(2)}, u32[]{:S(2)}) collective-permute-start(bf16[320,2048]{1,0:T(8,128)(2,1)} %pair_sum.14), channel_id=1, source_target_pairs={{0,2},{1,3},{2,0},{3,1},{4,6},{5,7},{6,4},{7,5},{8,10},{9,11},{10,... | collective-permute-start | bytes 3932168 | tf_op jit(solution)/shard_map/ppermute | solution.py:728
  340.3 47.8 %collective-permute-start.26 = (bf16[4,256,512]{2,1,0:T(8,128)(2,1)}, bf16[4,256,512]{2,1,0:T(8,128)(2,1)}, u32[]{:S(2)}, u32[]{:S(2)}) collective-permute-start(bf16[4,256,512]{2,1,0:T(8,128)(2,1)} %get-tuple-element.199), channel_id=1, source_target_pairs={{0,4},{4,0},{8,12},{12,8},{16,20},{20,16},{24,28},{28,24},{1,5},{5... | collective-permute-start | bytes 3145736 | tf_op jit(solution)/shard_map/ppermute | solution.py:728
  348.5 6.0 %copy-start.19 = (f32[320,2048]{1,0:T(8,128)S(1)}, f32[320,2048]{1,0:T(8,128)}, u32[]{:S(2)}) copy-start(f32[320,2048]{1,0:T(8,128)} %copy-done.17) | copy-start | bytes 7864324
  348.5 6.0 %copy-start.31 = (f32[320,2048]{1,0:T(8,128)S(1)}, f32[320,2048]{1,0:T(8,128)}, u32[]{:S(2)}) copy-start(f32[320,2048]{1,0:T(8,128)} %pair_sum.10) | copy-start | bytes 7864324
  351.9 5.7 %copy-start.6 = (bf16[2,256,1408]{2,1,0:T(8,128)(2,1)S(1)}, bf16[2,256,1408]{2,1,0:T(8,128)(2,1)}, u32[]{:S(2)}) copy-start(bf16[2,256,1408]{2,1,0:T(8,128)(2,1)} %copy-done.5) | copy-start | bytes 4325380
  351.9 36.1 %collective-permute-start.27 = (bf16[1,256,1408]{2,1,0:T(8,128)(2,1)}, bf16[1,256,1408]{2,1,0:T(8,128)(2,1)S(1)}, u32[]{:S(2)}, u32[]{:S(2)}) collective-permute-start(bf16[1,256,1408]{2,1,0:T(8,128)(2,1)} %get-tuple-element.202), channel_id=1, source_target_pairs={{0,16},{4,20},{8,24},{12,28},{16,0},{20,4},{24,8},{28,12},{1,17},{... | collective-permute-start | bytes 2162696 | tf_op jit(solution)/shard_map/ppermute | solution.py:728
  494.8 5.0 %copy-start.40 = (f32[512,256]{1,0:T(8,128)S(1)}, f32[512,256]{1,0:T(8,128)}, u32[]{:S(2)}) copy-start(f32[512,256]{1,0:T(8,128)} %get-tuple-element.268) | copy-start | bytes 1572868
  (29 other events, 67.6 us)
